TPU v7x, 32 devices: a whole 2x2x4 slice. The times are simulated.
32 devices in a mesh: dp: 4 (over z), expert: 8 (over y, x, core).
Axes of the slice: x: 2, y: 2, z: 4, core: 2. Of those that a mesh axis runs over, the one named last changes fastest.
Arguments:
- tokens: bfloat16 [8, 512, 2048], P('expert', 'dp'), may hold values from -12 to 12
- routes: int32 [8, 512, 2], P('expert', 'dp'), may hold values from 0 to 7, all different within a row; in each aligned block of 128 rows (0 to 127, 128 to 255, ..., all dimensions but the last counted through in order) at most 40 rows name the same one
- gate_code: int32 [8, 512, 2], P('expert', 'dp'), may hold values from 0 to 15
- gate_table: float32 [16], replicated, may hold values from 0.1 to 1
- w_gate: bfloat16 [8, 2048, 704], P('expert'), may hold values from -0.125 to 0.125
- w_up: bfloat16 [8, 2048, 704], P('expert'), may hold values from -0.125 to 0.125
- w_down: bfloat16 [8, 704, 2048], P('expert'), may hold values from -0.7 to 0.7
- norm_gain: float32 [2048], replicated, may hold values from 0.25 to 1.75
Outputs:
- relaid_out: bfloat16 [8, 512, 2048], P('expert', None, 'dp')
Inputs may be any that keep to these rules, and one draw needn't show every extreme that they name: Within the 128 tokens of one device (aligned blocks of positions) no expert is named by more than 40 routes, a bound that some block reaches; a token's two experts differ.
All inputs are finite; a program needn't handle non-finite values.
Results may differ from a plain program's by a relative error of at most 0.0064.
Values may be sent and summed in bfloat16 or wider, within the bound.
No kernel may reach another device: no remote copies, remote signals or barrier semaphores. Data moves between devices by JAX's collectives and lax.ppermute only.
A program may use at most 64 MiB of HBM per device.

v0:
```python
import functools

import jax
import jax.numpy as jnp
from jax import lax
from jax.experimental import pallas as pl
from jax.experimental.pallas import tpu as pltpu
from jax.sharding import PartitionSpec as P


epsilon = 1e-06


F32 = jnp.float32
BF16 = jnp.bfloat16


def expert_ffn(slot_block, w_gate, w_up, w_down):
    shape_in = slot_block.shape
    flat_rows = slot_block.reshape(-1, shape_in[-1])
    gate_act = jnp.dot(flat_rows, w_gate[0], preferred_element_type=F32)
    up_act = jnp.dot(flat_rows, w_up[0], preferred_element_type=F32)
    hidden = (jax.nn.silu(gate_act) * up_act).astype(BF16)
    result = jnp.dot(hidden, w_down[0], preferred_element_type=F32).astype(BF16)
    return result.reshape(shape_in)


def lookup(codes, gate_table):
    levels = gate_table.shape[0]
    match = codes[:, None] == jnp.arange(levels, dtype=jnp.int32)[None, :]
    return jnp.sum(jnp.where(match, gate_table[None, :], 0.0), axis=1)


def combine_pairs(outputs, weights):
    combined = outputs[:, 0] * weights[:, 0:1] + outputs[:, 1] * weights[:, 1:2]
    rounded = lax.optimization_barrier(combined.astype(BF16))
    return rounded.astype(F32)


def local_general(tokens, routes, gate_code, gate_table, w_gate, w_up, w_down, norm_gain):
    own_rows = tokens[0]
    tok_count, feat_width = own_rows.shape
    experts = w_gate.shape[0] * lax.axis_size("expert")
    capacity = 5 * tok_count // (2 * experts)
    route_ids = routes[0].reshape(-1)
    onehot = (route_ids[:, None] == jnp.arange(experts, dtype=jnp.int32)[None, :]).astype(jnp.int32)
    slot_pos = jnp.sum((jnp.cumsum(onehot, axis=0) - onehot) * onehot, axis=1)
    position = route_ids * capacity + slot_pos
    owner_row = (
        jnp.zeros((experts * capacity,), jnp.int32)
        .at[position]
        .set(jnp.arange(2 * tok_count, dtype=jnp.int32) // 2)
    )
    filled = jnp.zeros((experts * capacity,), jnp.bool_).at[position].set(True)
    buffer = jnp.where(filled[:, None], own_rows[owner_row], jnp.zeros((), BF16))
    buffer = buffer.reshape(experts, capacity, feat_width)
    level_ids = gate_code[0].reshape(-1)
    received = lax.all_to_all(buffer, "expert", split_axis=0, concat_axis=0, tiled=True)
    expert_out = expert_ffn(received, w_gate, w_up, w_down)
    returned = lax.all_to_all(expert_out, "expert", split_axis=0, concat_axis=0, tiled=True)
    outputs = (
        returned.reshape(-1, feat_width)[position]
        .astype(F32)
        .reshape(tok_count, 2, feat_width)
    )
    weights = lookup(level_ids, gate_table).reshape(tok_count, 2)
    widened = combine_pairs(outputs, weights)
    inv_rms = lax.rsqrt(jnp.mean(widened * widened, axis=1, keepdims=True) + epsilon)
    normed = (widened * inv_rms * norm_gain[None, :]).astype(BF16)
    relaid = lax.all_to_all(normed, "dp", split_axis=1, concat_axis=0, tiled=True)
    return relaid[None]


def vmem():
    return pl.BlockSpec(memory_space=pltpu.VMEM)


def slot_rows(route_rows, experts, me):
    tok = route_rows.shape[1]
    ids = lax.broadcasted_iota(jnp.int32, (experts, tok), 0) ^ me
    named = (route_rows[0:1, :] == ids) | (route_rows[1:2, :] == ids)
    earlier = lax.broadcasted_iota(jnp.int32, (tok, tok), 0) < lax.broadcasted_iota(
        jnp.int32, (tok, tok), 1
    )
    count = jnp.dot(
        named.astype(F32).astype(BF16), earlier.astype(F32).astype(BF16),
        preferred_element_type=F32,
    )
    return jnp.where(named, count.astype(jnp.int32), -1), ids


def dispatch_body(experts, capacity, route_hbm, tok_hbm, *refs):
    *out_refs, route_ref, tok_ref, sems = refs
    copies = [
        pltpu.make_async_copy(route_hbm, route_ref, sems.at[0]),
        pltpu.make_async_copy(tok_hbm, tok_ref, sems.at[1]),
    ]
    for copy in copies:
        copy.start()
    me = lax.axis_index("expert")
    tok, width = tok_ref.shape
    lane = lax.broadcasted_iota(jnp.int32, (capacity, tok), 0)
    copies[0].wait()
    slots, _ = slot_rows(route_ref[...], experts, me)
    pick = jnp.concatenate(
        [(lane == slots[j : j + 1, :]).astype(F32) for j in range(experts)], axis=0
    ).astype(BF16)
    copies[1].wait()
    tile = 256
    for col in range(0, width, tile):
        rows = jnp.dot(pick, tok_ref[:, col : col + tile], preferred_element_type=F32)
        rows = rows.astype(BF16)
        for j in range(experts):
            out_refs[j][:, col : col + tile] = rows[j * capacity : (j + 1) * capacity, :]


def dispatch(route_rows, own_rows, experts, capacity):
    width = own_rows.shape[1]
    return pl.pallas_call(
        functools.partial(dispatch_body, experts, capacity),
        out_shape=[jax.ShapeDtypeStruct((capacity, width), BF16)] * experts,
        in_specs=[pl.BlockSpec(memory_space=pltpu.HBM)] * 2,
        out_specs=[vmem()] * experts,
        scratch_shapes=[
            pltpu.VMEM(route_rows.shape, jnp.int32),
            pltpu.VMEM(own_rows.shape, BF16),
            pltpu.SemaphoreType.DMA((2,)),
        ],
        name="dispatch",
        cost_estimate=pl.CostEstimate(flops=10**8, transcendentals=0, bytes_accessed=2 * 10**6),
        compiler_params=pltpu.CompilerParams(vmem_limit_bytes=16 * 2**20),
    )(route_rows, own_rows)


def selector_body(experts, capacity, route_ref, code_ref, table_ref, *refs):
    sources, (sel_ref, weight_ref), copied, sems = refs[:3], refs[3:5], refs[5:8], refs[8]
    copies = [
        pltpu.make_async_copy(src, dst, sems.at[i])
        for i, (src, dst) in enumerate(zip(sources, copied))
    ]
    for copy in copies:
        copy.start()
    me = lax.axis_index("expert")
    rows = route_ref[...]
    slots, ids = slot_rows(rows, experts, me)
    tok = rows.shape[1]
    lane = lax.broadcasted_iota(jnp.int32, (capacity, tok), 0)
    for r in range(2):
        mine = jnp.where(rows[r : r + 1, :] == ids, slots, -1)
        pick = jnp.concatenate(
            [(lane == mine[j : j + 1, :]).astype(F32) for j in range(experts)], axis=0
        )
        sel_ref[r * tok : (r + 1) * tok, :] = pick.T.astype(BF16)
        codes = code_ref[r : r + 1, :]
        weights = jnp.zeros((1, tok), F32)
        for level in range(table_ref.shape[0]):
            weights = jnp.where(codes == level, table_ref[level], weights)
        weight_ref[r] = jnp.broadcast_to(weights, (tok, tok)).T
    for copy in copies:
        copy.wait()


def selector(route_rows, code_rows, gate_table, matrices, experts, capacity):
    tok = route_rows.shape[1]
    return pl.pallas_call(
        functools.partial(selector_body, experts, capacity),
        out_shape=[
            jax.ShapeDtypeStruct((2 * tok, experts * capacity), BF16),
            jax.ShapeDtypeStruct((2, tok, tok), F32),
        ]
        + [jax.ShapeDtypeStruct(m.shape, m.dtype) for m in matrices],
        in_specs=[vmem(), vmem(), pl.BlockSpec(memory_space=pltpu.SMEM)]
        + [pl.BlockSpec(memory_space=pltpu.HBM)] * 3,
        out_specs=[vmem()] * 5,
        scratch_shapes=[pltpu.SemaphoreType.DMA((3,))],
        name="selector",
        cost_estimate=pl.CostEstimate(flops=10**7, transcendentals=0, bytes_accessed=10**7),
        compiler_params=pltpu.CompilerParams(vmem_limit_bytes=24 * 2**20),
    )(route_rows, code_rows, gate_table, *matrices)


def half_start(which, width):
    own = lax.axis_index("dp") // (lax.axis_size("dp") // 2)
    return (own if which else 1 - own) * width


def write_down(hid_ref, down_ref, start, out_refs):
    capacity, width = out_refs[0].shape
    tile = 256
    for col in range(0, width, tile):
        cols = pl.ds(pl.multiple_of(start + col, tile), tile)
        rows = jnp.dot(hid_ref[...], down_ref[:, cols], preferred_element_type=F32).astype(BF16)
        for j, out in enumerate(out_refs):
            out[:, col : col + tile] = rows[j * capacity : (j + 1) * capacity, :]


def expert_body(count, *refs):
    blocks, (gate_ref, up_ref, down_ref) = refs[:count], refs[count : count + 3]
    hid_ref, x_ref, outs = refs[count + 3], refs[-1], refs[count + 4 : -1]
    capacity = blocks[0].shape[0]
    for j, block in enumerate(blocks):
        x_ref[j * capacity : (j + 1) * capacity, :] = block[...]
    hid = gate_ref.shape[0]
    tile = 256
    over = (((1,), (1,)), ((), ()))
    for low in range(0, hid, tile):
        high = min(hid, low + tile)
        gate = lax.dot_general(x_ref[...], gate_ref[low:high, :], over, preferred_element_type=F32)
        up = lax.dot_general(x_ref[...], up_ref[low:high, :], over, preferred_element_type=F32)
        hid_ref[:, low:high] = (gate / (1.0 + jnp.exp(-gate)) * up).astype(BF16)
    write_down(hid_ref, down_ref, half_start(0, outs[0].shape[1]), outs)


def expert_far(blocks, gate_rows, up_rows, down_rows):
    count = len(blocks)
    capacity, width = blocks[0].shape
    rows, hid = capacity * count, gate_rows.shape[0]
    out_width = down_rows.shape[1] // 2
    hidden, *outs = pl.pallas_call(
        functools.partial(expert_body, count),
        out_shape=[jax.ShapeDtypeStruct((rows, hid), BF16)]
        + [jax.ShapeDtypeStruct((capacity, out_width), BF16)] * count,
        in_specs=[vmem()] * (count + 3),
        out_specs=[vmem()] * (count + 1),
        scratch_shapes=[pltpu.VMEM((rows, width), BF16)],
        cost_estimate=pl.CostEstimate(
            flops=5 * rows * hid * width, transcendentals=rows * hid, bytes_accessed=8 * 10**6
        ),
        compiler_params=pltpu.CompilerParams(vmem_limit_bytes=24 * 2**20),
    )(*blocks, gate_rows, up_rows, down_rows)
    return hidden, outs


def near_body(hid_ref, down_ref, *out_refs):
    write_down(hid_ref, down_ref, half_start(1, out_refs[0].shape[1]), out_refs)


def expert_near(hidden, down_rows, count):
    rows, hid = hidden.shape
    width = down_rows.shape[1] // 2
    return pl.pallas_call(
        near_body,
        out_shape=[jax.ShapeDtypeStruct((rows // count, width), BF16)] * count,
        in_specs=[vmem()] * 2,
        out_specs=[vmem()] * count,
        cost_estimate=pl.CostEstimate(
            flops=2 * rows * hid * width, transcendentals=0, bytes_accessed=3 * 10**6
        ),
        compiler_params=pltpu.CompilerParams(vmem_limit_bytes=16 * 2**20),
    )(hidden, down_rows)


def combine_body(has_prior, chunk, *refs):
    if has_prior:
        sel_ref, weight_ref, prior_ref, *rest = refs
    else:
        sel_ref, weight_ref, *rest = refs
        prior_ref = None
    y_ref = rest[-1]
    sum_ref = rest[-2]
    capacity = rest[0].shape[0]
    experts = y_ref.shape[0] // capacity
    blocks, outs = rest[:experts], rest[experts:-2]
    low = lax.axis_index("dp") % len(outs)
    for j, block in enumerate(blocks):
        y_ref[j * capacity : (j + 1) * capacity, :] = block[...]
    tok = weight_ref.shape[1]
    lanes = weight_ref.shape[2]
    tile = 256
    squares = jnp.zeros((tok, lanes), F32)
    for q, out in enumerate(outs):
        start = (low ^ q) * chunk
        for col in range(0, chunk, tile):
            cols = pl.ds(pl.multiple_of(start + col, tile), tile)
            picked = jnp.dot(sel_ref[...], y_ref[:, cols], preferred_element_type=F32)
            for at in range(0, tile, lanes):
                first = picked[:tok, at : at + lanes] * weight_ref[0]
                second = picked[tok:, at : at + lanes] * weight_ref[1]
                rounded = (first + second).astype(BF16)
                out[:, col + at : col + at + lanes] = rounded
                wide = rounded.astype(F32)
                squares = squares + wide * wide
    total = jnp.sum(squares.T, axis=0, keepdims=True)
    total = jnp.broadcast_to(total, sum_ref.shape)
    if prior_ref is not None:
        total = total + prior_ref[...]
    sum_ref[...] = total


def combine_half(select, weights, prior, blocks, chunk):
    capacity, width = blocks[0].shape
    rows = capacity * len(blocks)
    tok = weights.shape[1]
    heads = [select, weights] + ([] if prior is None else [prior])
    return pl.pallas_call(
        functools.partial(combine_body, prior is not None, chunk),
        out_shape=[jax.ShapeDtypeStruct((tok, chunk), BF16)] * (width // chunk)
        + [jax.ShapeDtypeStruct((8, tok), F32)],
        in_specs=[vmem()] * (len(heads) + len(blocks)),
        out_specs=[vmem()] * (width // chunk + 1),
        scratch_shapes=[pltpu.VMEM((rows, width), BF16)],
        cost_estimate=pl.CostEstimate(
            flops=4 * tok * rows * width, transcendentals=0, bytes_accessed=2 * 10**6
        ),
        compiler_params=pltpu.CompilerParams(vmem_limit_bytes=12 * 2**20),
    )(*heads, *blocks)


def gain_body(gain_ref, out_ref):
    width = out_ref.shape[1]
    start = pl.multiple_of(lax.axis_index("dp") * width, 128)
    out_ref[...] = jnp.broadcast_to(gain_ref[:, pl.ds(start, width)], out_ref.shape)


def own_gain(norm_gain, chunk):
    return pl.pallas_call(
        gain_body,
        out_shape=jax.ShapeDtypeStruct((8, chunk), F32),
        in_specs=[vmem()],
        out_specs=vmem(),
        name="gain",
        cost_estimate=pl.CostEstimate(flops=10**4, transcendentals=0, bytes_accessed=10**4),
        compiler_params=pltpu.CompilerParams(vmem_limit_bytes=2**20),
    )(norm_gain[None, :])


def finish_body(feat_width, *refs):
    out_ref = refs[-1]
    gain_ref = refs[-2]
    ways = (len(refs) - 2) // 2
    chunks, sums = refs[:ways], refs[ways : 2 * ways]
    me = lax.axis_index("dp")
    tok = chunks[0].shape[0]
    gain = gain_ref[0:1, :]
    for k in range(ways):
        inv = lax.rsqrt(sums[k][0:1, :] * (1.0 / feat_width) + epsilon)
        column = jnp.broadcast_to(inv, (tok, tok)).T[:, 0:1]
        value = chunks[k][...].astype(F32) * column * gain
        out_ref[pl.ds(pl.multiple_of((me ^ k) * tok, tok), tok), :] = value.astype(BF16)


def finish(chunks, sums, gain, feat_width):
    tok, width = chunks[0].shape
    return pl.pallas_call(
        functools.partial(finish_body, feat_width),
        out_shape=jax.ShapeDtypeStruct((tok * len(chunks), width), BF16),
        in_specs=[vmem()] * (2 * len(chunks) + 1),
        out_specs=vmem(),
        name="finish",
        cost_estimate=pl.CostEstimate(flops=10**6, transcendentals=0, bytes_accessed=10**6),
        compiler_params=pltpu.CompilerParams(vmem_limit_bytes=8 * 2**20),
    )(*chunks, *sums, gain)


def swap(value, axis, offset):
    size = lax.axis_size(axis)
    return lax.ppermute(value, axis, [(i, i ^ offset) for i in range(size)])


def swap_each(values, axis):
    moved = {}
    for k, value in values.items():
        moved[k] = swap(value, axis, k) if k else value
    return moved


def local_fast(tokens, routes, gate_code, gate_table, w_gate, w_up, w_down, norm_gain):
    return fast_steps(tokens, routes, gate_code, gate_table, w_gate, w_up, w_down, norm_gain)


def fast_steps(tokens, routes, gate_code, gate_table, w_gate, w_up, w_down, norm_gain):
    own_rows = tokens[0]
    tok, feat_width = own_rows.shape
    experts = lax.axis_size("expert")
    ways = lax.axis_size("dp")
    half = ways // 2
    capacity = 5 * tok // (2 * experts)
    chunk = feat_width // ways
    links = [bin(k >> 1).count("1") for k in range(experts)]
    first = [k for k in range(experts - 1, -1, -1) if links[k] != 1]
    second = [k for k in range(experts) if links[k] == 1]

    route_rows = routes[0].T
    blocks = dispatch(route_rows, own_rows, experts, capacity)
    got_a = swap_each({k: blocks[k] for k in first}, "expert")
    got_b = swap_each({k: blocks[k] for k in second}, "expert")
    select, weights, gate_rows, up_rows, down_rows = selector(
        route_rows, gate_code[0].T, gate_table,
        (w_gate[0].T, w_up[0].T, w_down[0]), experts, capacity,
    )

    hid_a, far_a = expert_far([got_a[k] for k in first], gate_rows, up_rows, down_rows)
    far = swap_each(dict(zip(first, far_a)), "expert")
    near_a = expert_near(hid_a, down_rows, len(first))
    hid_b, far_b = expert_far([got_b[k] for k in second], gate_rows, up_rows, down_rows)
    far |= swap_each(dict(zip(second, far_b)), "expert")
    near_b = expert_near(hid_b, down_rows, len(second))
    near = swap_each(dict(zip(first, near_a)), "expert")
    near |= swap_each(dict(zip(second, near_b)), "expert")

    order = range(experts)
    *far_chunks, part = combine_half(select, weights, None, [far[k] for k in order], chunk)
    chunks = swap_each({half + q: c for q, c in enumerate(far_chunks)}, "dp")
    gain = own_gain(norm_gain, chunk)
    *near_chunks, total = combine_half(select, weights, part, [near[k] for k in order], chunk)
    sums = swap_each({k: total for k in range(ways - 1, -1, -1)}, "dp")
    chunks |= swap_each({q: c for q, c in enumerate(near_chunks)}, "dp")
    mine = range(ways)
    return finish([chunks[k] for k in mine], [sums[k] for k in mine], gain, feat_width)[None]


def solution(mesh):
    in_specs = (
        P("expert", "dp", None),
        P("expert", "dp", None),
        P("expert", "dp", None),
        P(),
        P("expert", None, None),
        P("expert", None, None),
        P("expert", None, None),
        P(),
    )
    out_specs = P("expert", None, "dp")

    def whole(tokens, routes, gate_code, gate_table, w_gate, w_up, w_down, norm_gain):
        args = (tokens, routes, gate_code, gate_table, w_gate, w_up, w_down, norm_gain)
        experts, ways = mesh.shape["expert"], mesh.shape["dp"]
        tok, feat = tokens.shape[1] // ways, tokens.shape[2]
        power = experts & (experts - 1) == 0 and ways & (ways - 1) == 0
        fits = power and 4 <= experts <= 8 and 2 <= ways <= 4
        fits = fits and tok % 128 == 0 and w_gate.shape[0] == experts
        fits = fits and 5 * tok % (16 * experts) == 0 and feat % (256 * ways) == 0
        body = local_fast if fits else local_general
        f = jax.shard_map(body, mesh=mesh, in_specs=in_specs, out_specs=out_specs, check_vma=False)
        return f(*args)

    return whole
```

profile of v0, /device:TPU:0, one launch (start us, length us, event | category | flops | bytes accessed | tf_op | source)
XLA Modules:
  0.0 70.5 jit_solution(17752831504869835387)
XLA Ops:
  0.0 1.0 %copy-done.3 = bf16[1,128,2048]{2,1,0:T(8,128)(2,1)S(1)} copy-done((bf16[1,128,2048]{2,1,0:T(8,128)(2,1)S(1)}, bf16[1,128,2048]{2,1,0:T(8,128)(2,1)}, u32[]{:S(2)}) %copy-start.3) | copy-done | bytes 524312
  1.0 0.7 copy-done.5
  1.7 0.7 dispatch.1
  2.4 3.4 %collective-permute-start = (bf16[40,2048]{1,0:T(8,128)(2,1)S(1)}, bf16[40,2048]{1,0:T(8,128)(2,1)S(1)}, u32[]{:S(2)}, u32[]{:S(2)}) collective-permute-start(bf16[40,2048]{1,0:T(8,128)(2,1)S(1)} %get-tuple-element.44), channel_id=1, source_target_pairs={{0,7},{1,6},{2,5},{3,4},{4,3},{5,2},{6,1},{7,0},{8,15},{9,14},{10,... | collective-permute-start | bytes 491528 | tf_op jit(solution)/shard_map/ppermute | solution.py:357
  5.9 0.6 collective-permute-start.1
  6.5 0.0 collective-permute-start.2
  6.5 1.7 %collective-permute-start.4 = (bf16[40,2048]{1,0:T(8,128)(2,1)S(1)}, bf16[40,2048]{1,0:T(8,128)(2,1)S(1)}, u32[]{:S(2)}, u32[]{:S(2)}) collective-permute-start(bf16[40,2048]{1,0:T(8,128)(2,1)S(1)} %get-tuple-element.53), channel_id=1, source_target_pairs={{0,2},{1,3},{2,0},{3,1},{4,6},{5,7},{6,4},{7,5},{8,10},{9,11},{10,... | collective-permute-start | bytes 491528 | tf_op jit(solution)/shard_map/ppermute | solution.py:357
  8.2 0.1 collective-permute-start.5
  8.4 2.1 %collective-permute-done.refs_0_ = bf16[40,2048]{1,0:T(8,128)(2,1)S(1)} collective-permute-done((bf16[40,2048]{1,0:T(8,128)(2,1)S(1)}, bf16[40,2048]{1,0:T(8,128)(2,1)S(1)}, u32[]{:S(2)}, u32[]{:S(2)}) %collective-permute-start) | collective-permute-done | bytes 163872 | tf_op jit(solution)/shard_map/ppermute | solution.py:357
  10.4 2.4 %collective-permute-start.6 = (bf16[40,2048]{1,0:T(8,128)(2,1)S(1)}, bf16[40,2048]{1,0:T(8,128)(2,1)S(1)}, u32[]{:S(2)}, u32[]{:S(2)}) collective-permute-start(bf16[40,2048]{1,0:T(8,128)(2,1)S(1)} %get-tuple-element.55), channel_id=1, source_target_pairs={{0,4},{1,5},{2,6},{3,7},{4,0},{5,1},{6,2},{7,3},{8,12},{9,13},{10,... | collective-permute-start | bytes 491528 | tf_op jit(solution)/shard_map/ppermute | solution.py:357
  12.9 1.8 %collective-permute-done.1.refs_1_ = bf16[40,2048]{1,0:T(8,128)(2,1)S(1)} collective-permute-done((bf16[40,2048]{1,0:T(8,128)(2,1)S(1)}, bf16[40,2048]{1,0:T(8,128)(2,1)S(1)}, u32[]{:S(2)}, u32[]{:S(2)}) %collective-permute-start.1) | collective-permute-done | bytes 163872 | tf_op jit(solution)/shard_map/ppermute | solution.py:357
  14.7 1.4 %collective-permute-start.7 = (bf16[40,2048]{1,0:T(8,128)(2,1)S(1)}, bf16[40,2048]{1,0:T(8,128)(2,1)S(1)}, u32[]{:S(2)}, u32[]{:S(2)}) collective-permute-start(bf16[40,2048]{1,0:T(8,128)(2,1)S(1)} %get-tuple-element.56), channel_id=1, source_target_pairs={{0,5},{1,4},{2,7},{3,6},{4,1},{5,0},{6,3},{7,2},{8,13},{9,12},{10,... | collective-permute-start | bytes 491528 | tf_op jit(solution)/shard_map/ppermute | solution.py:357
  16.1 1.8 %copy-done = bf16[1,2048,704]{1,2,0:T(8,128)(2,1)S(1)} copy-done((bf16[1,2048,704]{1,2,0:T(8,128)(2,1)S(1)}, bf16[1,2048,704]{1,2,0:T(8,128)(2,1)}, u32[]{:S(2)}) %copy-start) | copy-done | bytes 2883608
  17.9 1.8 %copy-done.1 = bf16[1,2048,704]{1,2,0:T(8,128)(2,1)S(1)} copy-done((bf16[1,2048,704]{1,2,0:T(8,128)(2,1)S(1)}, bf16[1,2048,704]{1,2,0:T(8,128)(2,1)}, u32[]{:S(2)}) %copy-start.1) | copy-done | bytes 2883608
  19.7 1.8 %copy-done.2 = bf16[1,704,2048]{2,1,0:T(8,128)(2,1)S(1)} copy-done((bf16[1,704,2048]{2,1,0:T(8,128)(2,1)S(1)}, bf16[1,704,2048]{2,1,0:T(8,128)(2,1)}, u32[]{:S(2)}) %copy-start.2) | copy-done | bytes 2883608
  21.6 0.7 copy-done.6
  22.2 0.7 copy-done.7
  22.9 0.7 copy-done.8
  23.6 1.4 %selector.1 = (bf16[256,320]{1,0:T(8,128)(2,1)S(1)}, f32[2,128,128]{2,1,0:T(8,128)S(1)}, bf16[704,2048]{1,0:T(8,128)(2,1)S(1)}, bf16[704,2048]{1,0:T(8,128)(2,1)S(1)}, bf16[704,2048]{1,0:T(8,128)(2,1)S(1)}) custom-call(s32[2,128]{1,0:T(2,128)S(1)} %bitcast.22, s32[2,128]{1,0:T(2,128)S(1)} %bitcast.23, f32[16]{0:T(128)S(1)} %copy-done.8, ...), custom_call_target="tpu_custom_call" | custom-call | flops 10000000 | bytes 10000000 | tf_op jit(solution)/shard_map/selector/pallas_call | solution.py:165
  25.0 0.0 collective-permute-done.2.refs_2_
  25.0 2.3 %shard_map.82 = (bf16[160,704]{1,0:T(8,128)(2,1)S(1)}, bf16[40,1024]{1,0:T(8,128)(2,1)S(1)}, bf16[40,1024]{1,0:T(8,128)(2,1)S(1)}, bf16[40,1024]{1,0:T(8,128)(2,1)S(1)}, bf16[40,1024]{1,0:T(8,128)(2,1)S(1)}) custom-call(bf16[40,2048]{1,0:T(8,128)(2,1)S(1)} %collective-permute-done.refs_0_, bf16[40,2048]{1,0:T(8,128)(2,1)S(1)} %collective-permute-done.1.refs_1_, ...), custom_call_target="tpu_custom_call" | custom-call | flops 1153433600 | bytes 8000000 | tf_op jit(solution)/shard_map/pallas_call | solution.py:219
  27.4 0.6 collective-permute-start.3
  27.9 0.0 collective-permute-done.4.refs_0_
  27.9 0.0 collective-permute-done.5.refs_1_
  27.9 0.0 collective-permute-done.6.refs_2_
  27.9 0.0 collective-permute-done.7.refs_3_
  27.9 2.3 %shard_map.83 = (bf16[160,704]{1,0:T(8,128)(2,1)S(1)}, bf16[40,1024]{1,0:T(8,128)(2,1)S(1)}, bf16[40,1024]{1,0:T(8,128)(2,1)S(1)}, bf16[40,1024]{1,0:T(8,128)(2,1)S(1)}, bf16[40,1024]{1,0:T(8,128)(2,1)S(1)}) custom-call(bf16[40,2048]{1,0:T(8,128)(2,1)S(1)} %collective-permute-done.4.refs_0_, bf16[40,2048]{1,0:T(8,128)(2,1)S(1)} %collective-permute-done.5.refs_1_, ...), custom_call_target="tpu_custom_call" | custom-call | flops 1153433600 | bytes 8000000 | tf_op jit(solution)/shard_map/pallas_call | solution.py:219
  30.3 1.6 %collective-permute-start.8 = (bf16[40,1024]{1,0:T(8,128)(2,1)S(1)}, bf16[40,1024]{1,0:T(8,128)(2,1)S(1)}, u32[]{:S(2)}, u32[]{:S(2)}) collective-permute-start(bf16[40,1024]{1,0:T(8,128)(2,1)S(1)} %get-tuple-element.57), channel_id=1, source_target_pairs={{0,2},{1,3},{2,0},{3,1},{4,6},{5,7},{6,4},{7,5},{8,10},{9,11},{10,... | collective-permute-start | bytes 245768 | tf_op jit(solution)/shard_map/ppermute | solution.py:357
  31.8 0.0 collective-permute-start.9
  31.8 0.5 collective-permute-start.10
  32.4 1.5 %collective-permute-start.11 = (bf16[40,1024]{1,0:T(8,128)(2,1)S(1)}, bf16[40,1024]{1,0:T(8,128)(2,1)S(1)}, u32[]{:S(2)}, u32[]{:S(2)}) collective-permute-start(bf16[40,1024]{1,0:T(8,128)(2,1)S(1)} %get-tuple-element.60), channel_id=1, source_target_pairs={{0,5},{1,4},{2,7},{3,6},{4,1},{5,0},{6,3},{7,2},{8,13},{9,12},{10,... | collective-permute-start | bytes 245768 | tf_op jit(solution)/shard_map/ppermute | solution.py:357
  33.8 0.4 shard_map.85
  34.3 0.0 copy-start.4
  34.3 0.5 shard_map.86
  34.8 0.0 collective-permute-done.3.refs_3_
  34.8 1.5 %collective-permute-start.12 = (bf16[40,1024]{1,0:T(8,128)(2,1)S(1)}, bf16[40,1024]{1,0:T(8,128)(2,1)S(1)}, u32[]{:S(2)}, u32[]{:S(2)}) collective-permute-start(bf16[40,1024]{1,0:T(8,128)(2,1)S(1)} %get-tuple-element.61), channel_id=1, source_target_pairs={{0,6},{1,7},{2,4},{3,5},{4,2},{5,3},{6,0},{7,1},{8,14},{9,15},{10,... | collective-permute-start | bytes 245768 | tf_op jit(solution)/shard_map/ppermute | solution.py:357
  36.3 0.0 collective-permute-done.8.refs_4_
  36.3 1.0 %collective-permute-start.13 = (bf16[40,1024]{1,0:T(8,128)(2,1)S(1)}, bf16[40,1024]{1,0:T(8,128)(2,1)S(1)}, u32[]{:S(2)}, u32[]{:S(2)}) collective-permute-start(bf16[40,1024]{1,0:T(8,128)(2,1)S(1)} %get-tuple-element.62), channel_id=1, source_target_pairs={{0,7},{1,6},{2,5},{3,4},{4,3},{5,2},{6,1},{7,0},{8,15},{9,14},{10,... | collective-permute-start | bytes 245768 | tf_op jit(solution)/shard_map/ppermute | solution.py:357
  37.3 0.6 collective-permute-start.14
  37.9 1.5 %collective-permute-start.15 = (bf16[40,1024]{1,0:T(8,128)(2,1)S(1)}, bf16[40,1024]{1,0:T(8,128)(2,1)S(1)}, u32[]{:S(2)}, u32[]{:S(2)}) collective-permute-start(bf16[40,1024]{1,0:T(8,128)(2,1)S(1)} %get-tuple-element.68), channel_id=1, source_target_pairs={{0,2},{1,3},{2,0},{3,1},{4,6},{5,7},{6,4},{7,5},{8,10},{9,11},{10,... | collective-permute-start | bytes 245768 | tf_op jit(solution)/shard_map/ppermute | solution.py:357
  39.4 3.4 %collective-permute-start.16 = (bf16[40,1024]{1,0:T(8,128)(2,1)S(1)}, bf16[40,1024]{1,0:T(8,128)(2,1)S(1)}, u32[]{:S(2)}, u32[]{:S(2)}) collective-permute-start(bf16[40,1024]{1,0:T(8,128)(2,1)S(1)} %get-tuple-element.69), channel_id=1, source_target_pairs={{0,3},{1,2},{2,1},{3,0},{4,7},{5,6},{6,5},{7,4},{8,11},{9,10},{10,... | collective-permute-start | bytes 245768 | tf_op jit(solution)/shard_map/ppermute | solution.py:357
  42.8 0.0 collective-permute-done.12.refs_8_
  42.8 0.9 %collective-permute-start.17 = (bf16[40,1024]{1,0:T(8,128)(2,1)S(1)}, bf16[40,1024]{1,0:T(8,128)(2,1)S(1)}, u32[]{:S(2)}, u32[]{:S(2)}) collective-permute-start(bf16[40,1024]{1,0:T(8,128)(2,1)S(1)} %get-tuple-element.70), channel_id=1, source_target_pairs={{0,4},{1,5},{2,6},{3,7},{4,0},{5,1},{6,2},{7,3},{8,12},{9,13},{10,... | collective-permute-start | bytes 245768 | tf_op jit(solution)/shard_map/ppermute | solution.py:357
  43.7 1.7 %collective-permute-start.19 = (bf16[40,1024]{1,0:T(8,128)(2,1)S(1)}, bf16[40,1024]{1,0:T(8,128)(2,1)S(1)}, u32[]{:S(2)}, u32[]{:S(2)}) collective-permute-start(bf16[40,1024]{1,0:T(8,128)(2,1)S(1)} %get-tuple-element.72), channel_id=1, source_target_pairs={{0,6},{1,7},{2,4},{3,5},{4,2},{5,3},{6,0},{7,1},{8,14},{9,15},{10,... | collective-permute-start | bytes 245768 | tf_op jit(solution)/shard_map/ppermute | solution.py:357
  45.4 1.9 %collective-permute-start.20 = (bf16[40,1024]{1,0:T(8,128)(2,1)S(1)}, bf16[40,1024]{1,0:T(8,128)(2,1)S(1)}, u32[]{:S(2)}, u32[]{:S(2)}) collective-permute-start(bf16[40,1024]{1,0:T(8,128)(2,1)S(1)} %get-tuple-element.73), channel_id=1, source_target_pairs={{0,7},{1,6},{2,5},{3,4},{4,3},{5,2},{6,1},{7,0},{8,15},{9,14},{10,... | collective-permute-start | bytes 245768 | tf_op jit(solution)/shard_map/ppermute | solution.py:357
  47.2 0.6 shard_map.84
  47.8 0.0 collective-permute-done.16.refs_6_
  47.8 0.0 collective-permute-done.17.refs_7_
  47.8 4.1 %collective-permute-done.18.refs_8_ = bf16[40,1024]{1,0:T(8,128)(2,1)S(1)} collective-permute-done((bf16[40,1024]{1,0:T(8,128)(2,1)S(1)}, bf16[40,1024]{1,0:T(8,128)(2,1)S(1)}, u32[]{:S(2)}, u32[]{:S(2)}) %collective-permute-start.18) | collective-permute-done | bytes 81952 | tf_op jit(solution)/shard_map/ppermute | solution.py:357
  51.9 0.0 collective-permute-done.19.refs_9_
  51.9 0.0 collective-permute-done.20.refs_10_
  51.9 0.6 shard_map.87
  52.5 1.6 %collective-permute-start.21 = (bf16[128,512]{1,0:T(8,128)(2,1)S(1)}, bf16[128,512]{1,0:T(8,128)(2,1)S(1)}, u32[]{:S(2)}, u32[]{:S(2)}) collective-permute-start(bf16[128,512]{1,0:T(8,128)(2,1)S(1)} %get-tuple-element.75), channel_id=1, source_target_pairs={{0,8},{8,0},{16,24},{24,16},{1,9},{9,1},{17,25},{25,17},{2,10},{10... | collective-permute-start | bytes 393224 | tf_op jit(solution)/shard_map/ppermute | solution.py:357
  54.2 2.6 %collective-permute-start.22 = (bf16[128,512]{1,0:T(8,128)(2,1)S(1)}, bf16[128,512]{1,0:T(8,128)(2,1)S(1)}, u32[]{:S(2)}, u32[]{:S(2)}) collective-permute-start(bf16[128,512]{1,0:T(8,128)(2,1)S(1)} %get-tuple-element.76), channel_id=1, source_target_pairs={{0,16},{8,24},{16,0},{24,8},{1,17},{9,25},{17,1},{25,9},{2,18},{10... | collective-permute-start | bytes 393224 | tf_op jit(solution)/shard_map/ppermute | solution.py:357
  56.8 0.2 collective-permute-start.23
  57.0 0.7 collective-permute-start.24
  57.7 3.5 %collective-permute-start.25 = (f32[8,128]{1,0:T(8,128)S(1)}, f32[8,128]{1,0:T(8,128)S(1)}, u32[]{:S(2)}, u32[]{:S(2)}) collective-permute-start(f32[8,128]{1,0:T(8,128)S(1)} %get-tuple-element.78.refs_4_), channel_id=1, source_target_pairs={{0,16},{8,24},{16,0},{24,8},{1,17},{9,25},{17,1},{25,9},{2,18},{10... | collective-permute-start | bytes 12296 | tf_op jit(solution)/shard_map/ppermute | solution.py:357
  61.2 2.1 %collective-permute-done.24.refs_5_ = f32[8,128]{1,0:T(8,128)S(1)} collective-permute-done((f32[8,128]{1,0:T(8,128)S(1)}, f32[8,128]{1,0:T(8,128)S(1)}, u32[]{:S(2)}, u32[]{:S(2)}) %collective-permute-start.24) | collective-permute-done | bytes 4128 | tf_op jit(solution)/shard_map/ppermute | solution.py:357
  63.3 2.5 %collective-permute-start.26 = (f32[8,128]{1,0:T(8,128)S(1)}, f32[8,128]{1,0:T(8,128)S(1)}, u32[]{:S(2)}, u32[]{:S(2)}) collective-permute-start(f32[8,128]{1,0:T(8,128)S(1)} %get-tuple-element.78.refs_4_), channel_id=1, source_target_pairs={{0,24},{8,16},{16,8},{24,0},{1,25},{9,17},{17,9},{25,1},{2,26},{10... | collective-permute-start | bytes 12296 | tf_op jit(solution)/shard_map/ppermute | solution.py:357
  65.8 3.6 %collective-permute-done.25.refs_6_ = f32[8,128]{1,0:T(8,128)S(1)} collective-permute-done((f32[8,128]{1,0:T(8,128)S(1)}, f32[8,128]{1,0:T(8,128)S(1)}, u32[]{:S(2)}, u32[]{:S(2)}) %collective-permute-start.25) | collective-permute-done | bytes 4128 | tf_op jit(solution)/shard_map/ppermute | solution.py:357
  69.4 0.0 collective-permute-done.26.refs_7_
  69.4 0.0 collective-permute-done.21.refs_1_
  69.4 0.0 collective-permute-done.22.refs_2_
  69.4 1.1 %finish.1 = bf16[512,512]{1,0:T(8,128)(2,1)} custom-call(bf16[128,512]{1,0:T(8,128)(2,1)S(1)} %get-tuple-element.74.refs_0_, bf16[128,512]{1,0:T(8,128)(2,1)S(1)} %collective-permute-done.21.refs_1_, bf16[128,512]{1,0:T(8,128)(2,1)S(1)} %collective-permute-done.22.refs_2_, bf16[128,512]{1,0:T(8,128)(2,1)S(1)} %collective-permute-done.23.refs_3_, ...), custom_call_target="tpu_custom_call" | custom-call | flops 1000000 | bytes 1000000 | tf_op jit(solution)/shard_map/finish/pallas_call | solution.py:344
  (18 shorter events, 0.0 us)
Async XLA Ops:
  0.0 1.0 %copy-start.3 = (bf16[1,128,2048]{2,1,0:T(8,128)(2,1)S(1)}, bf16[1,128,2048]{2,1,0:T(8,128)(2,1)}, u32[]{:S(2)}) copy-start(bf16[1,128,2048]{2,1,0:T(8,128)(2,1)} %param.8) | copy-start | bytes 1572868
  1.0 0.7 copy-start.5
  2.4 8.0 %collective-permute-start = (bf16[40,2048]{1,0:T(8,128)(2,1)S(1)}, bf16[40,2048]{1,0:T(8,128)(2,1)S(1)}, u32[]{:S(2)}, u32[]{:S(2)}) collective-permute-start(bf16[40,2048]{1,0:T(8,128)(2,1)S(1)} %get-tuple-element.44), channel_id=1, source_target_pairs={{0,7},{1,6},{2,5},{3,4},{4,3},{5,2},{6,1},{7,0},{8,15},{9,14},{10,... | collective-permute-start | bytes 491528 | tf_op jit(solution)/shard_map/ppermute | solution.py:357
  5.9 8.9 %collective-permute-start.1 = (bf16[40,2048]{1,0:T(8,128)(2,1)S(1)}, bf16[40,2048]{1,0:T(8,128)(2,1)S(1)}, u32[]{:S(2)}, u32[]{:S(2)}) collective-permute-start(bf16[40,2048]{1,0:T(8,128)(2,1)S(1)} %get-tuple-element.45), channel_id=1, source_target_pairs={{0,6},{1,7},{2,4},{3,5},{4,2},{5,3},{6,0},{7,1},{8,14},{9,15},{10,... | collective-permute-start | bytes 491528 | tf_op jit(solution)/shard_map/ppermute | solution.py:357
  6.5 18.5 %collective-permute-start.2 = (bf16[40,2048]{1,0:T(8,128)(2,1)S(1)}, bf16[40,2048]{1,0:T(8,128)(2,1)S(1)}, u32[]{:S(2)}, u32[]{:S(2)}) collective-permute-start(bf16[40,2048]{1,0:T(8,128)(2,1)S(1)} %get-tuple-element.46), channel_id=1, source_target_pairs={{0,1},{1,0},{2,3},{3,2},{4,5},{5,4},{6,7},{7,6},{8,9},{9,8},{10,11... | collective-permute-start | bytes 491528 | tf_op jit(solution)/shard_map/ppermute | solution.py:357
  6.5 21.4 %collective-permute-start.4 = (bf16[40,2048]{1,0:T(8,128)(2,1)S(1)}, bf16[40,2048]{1,0:T(8,128)(2,1)S(1)}, u32[]{:S(2)}, u32[]{:S(2)}) collective-permute-start(bf16[40,2048]{1,0:T(8,128)(2,1)S(1)} %get-tuple-element.53), channel_id=1, source_target_pairs={{0,2},{1,3},{2,0},{3,1},{4,6},{5,7},{6,4},{7,5},{8,10},{9,11},{10,... | collective-permute-start | bytes 491528 | tf_op jit(solution)/shard_map/ppermute | solution.py:357
  8.2 19.7 %collective-permute-start.5 = (bf16[40,2048]{1,0:T(8,128)(2,1)S(1)}, bf16[40,2048]{1,0:T(8,128)(2,1)S(1)}, u32[]{:S(2)}, u32[]{:S(2)}) collective-permute-start(bf16[40,2048]{1,0:T(8,128)(2,1)S(1)} %get-tuple-element.54), channel_id=1, source_target_pairs={{0,3},{1,2},{2,1},{3,0},{4,7},{5,6},{6,5},{7,4},{8,11},{9,10},{10,... | collective-permute-start | bytes 491528 | tf_op jit(solution)/shard_map/ppermute | solution.py:357
  10.4 17.5 %collective-permute-start.6 = (bf16[40,2048]{1,0:T(8,128)(2,1)S(1)}, bf16[40,2048]{1,0:T(8,128)(2,1)S(1)}, u32[]{:S(2)}, u32[]{:S(2)}) collective-permute-start(bf16[40,2048]{1,0:T(8,128)(2,1)S(1)} %get-tuple-element.55), channel_id=1, source_target_pairs={{0,4},{1,5},{2,6},{3,7},{4,0},{5,1},{6,2},{7,3},{8,12},{9,13},{10,... | collective-permute-start | bytes 491528 | tf_op jit(solution)/shard_map/ppermute | solution.py:357
  14.7 13.2 %collective-permute-start.7 = (bf16[40,2048]{1,0:T(8,128)(2,1)S(1)}, bf16[40,2048]{1,0:T(8,128)(2,1)S(1)}, u32[]{:S(2)}, u32[]{:S(2)}) collective-permute-start(bf16[40,2048]{1,0:T(8,128)(2,1)S(1)} %get-tuple-element.56), channel_id=1, source_target_pairs={{0,5},{1,4},{2,7},{3,6},{4,1},{5,0},{6,3},{7,2},{8,13},{9,12},{10,... | collective-permute-start | bytes 491528 | tf_op jit(solution)/shard_map/ppermute | solution.py:357
  16.1 1.8 %copy-start = (bf16[1,2048,704]{1,2,0:T(8,128)(2,1)S(1)}, bf16[1,2048,704]{1,2,0:T(8,128)(2,1)}, u32[]{:S(2)}) copy-start(bf16[1,2048,704]{1,2,0:T(8,128)(2,1)} %param.12) | copy-start | bytes 8650756
  17.9 1.8 %copy-start.1 = (bf16[1,2048,704]{1,2,0:T(8,128)(2,1)S(1)}, bf16[1,2048,704]{1,2,0:T(8,128)(2,1)}, u32[]{:S(2)}) copy-start(bf16[1,2048,704]{1,2,0:T(8,128)(2,1)} %param.13) | copy-start | bytes 8650756
  19.7 1.8 %copy-start.2 = (bf16[1,704,2048]{2,1,0:T(8,128)(2,1)S(1)}, bf16[1,704,2048]{2,1,0:T(8,128)(2,1)}, u32[]{:S(2)}) copy-start(bf16[1,704,2048]{2,1,0:T(8,128)(2,1)} %param.14) | copy-start | bytes 8650756
  21.6 0.7 copy-start.6
  22.2 0.7 copy-start.7
  22.9 0.7 copy-start.8
  27.4 7.4 %collective-permute-start.3 = (bf16[40,1024]{1,0:T(8,128)(2,1)S(1)}, bf16[40,1024]{1,0:T(8,128)(2,1)S(1)}, u32[]{:S(2)}, u32[]{:S(2)}) collective-permute-start(bf16[40,1024]{1,0:T(8,128)(2,1)S(1)} %get-tuple-element.52), channel_id=1, source_target_pairs={{0,1},{1,0},{2,3},{3,2},{4,5},{5,4},{6,7},{7,6},{8,9},{9,8},{10,11... | collective-permute-start | bytes 245768 | tf_op jit(solution)/shard_map/ppermute | solution.py:357
  30.3 6.0 %collective-permute-start.8 = (bf16[40,1024]{1,0:T(8,128)(2,1)S(1)}, bf16[40,1024]{1,0:T(8,128)(2,1)S(1)}, u32[]{:S(2)}, u32[]{:S(2)}) collective-permute-start(bf16[40,1024]{1,0:T(8,128)(2,1)S(1)} %get-tuple-element.57), channel_id=1, source_target_pairs={{0,2},{1,3},{2,0},{3,1},{4,6},{5,7},{6,4},{7,5},{8,10},{9,11},{10,... | collective-permute-start | bytes 245768 | tf_op jit(solution)/shard_map/ppermute | solution.py:357
  31.8 5.4 %collective-permute-start.9 = (bf16[40,1024]{1,0:T(8,128)(2,1)S(1)}, bf16[40,1024]{1,0:T(8,128)(2,1)S(1)}, u32[]{:S(2)}, u32[]{:S(2)}) collective-permute-start(bf16[40,1024]{1,0:T(8,128)(2,1)S(1)} %get-tuple-element.58), channel_id=1, source_target_pairs={{0,3},{1,2},{2,1},{3,0},{4,7},{5,6},{6,5},{7,4},{8,11},{9,10},{10,... | collective-permute-start | bytes 245768 | tf_op jit(solution)/shard_map/ppermute | solution.py:357
  31.8 6.1 %collective-permute-start.10 = (bf16[40,1024]{1,0:T(8,128)(2,1)S(1)}, bf16[40,1024]{1,0:T(8,128)(2,1)S(1)}, u32[]{:S(2)}, u32[]{:S(2)}) collective-permute-start(bf16[40,1024]{1,0:T(8,128)(2,1)S(1)} %get-tuple-element.59), channel_id=1, source_target_pairs={{0,4},{1,5},{2,6},{3,7},{4,0},{5,1},{6,2},{7,3},{8,12},{9,13},{10,... | collective-permute-start | bytes 245768 | tf_op jit(solution)/shard_map/ppermute | solution.py:357
  32.4 7.0 %collective-permute-start.11 = (bf16[40,1024]{1,0:T(8,128)(2,1)S(1)}, bf16[40,1024]{1,0:T(8,128)(2,1)S(1)}, u32[]{:S(2)}, u32[]{:S(2)}) collective-permute-start(bf16[40,1024]{1,0:T(8,128)(2,1)S(1)} %get-tuple-element.60), channel_id=1, source_target_pairs={{0,5},{1,4},{2,7},{3,6},{4,1},{5,0},{6,3},{7,2},{8,13},{9,12},{10,... | collective-permute-start | bytes 245768 | tf_op jit(solution)/shard_map/ppermute | solution.py:357
  34.3 31.5 %copy-start.4 = (f32[2048]{0:T(1024)S(1)}, f32[2048]{0:T(1024)}, u32[]{:S(2)}) copy-start(f32[2048]{0:T(1024)} %param.15) | copy-start | bytes 24580
  34.8 8.0 %collective-permute-start.12 = (bf16[40,1024]{1,0:T(8,128)(2,1)S(1)}, bf16[40,1024]{1,0:T(8,128)(2,1)S(1)}, u32[]{:S(2)}, u32[]{:S(2)}) collective-permute-start(bf16[40,1024]{1,0:T(8,128)(2,1)S(1)} %get-tuple-element.61), channel_id=1, source_target_pairs={{0,6},{1,7},{2,4},{3,5},{4,2},{5,3},{6,0},{7,1},{8,14},{9,15},{10,... | collective-permute-start | bytes 245768 | tf_op jit(solution)/shard_map/ppermute | solution.py:357
  36.3 7.4 %collective-permute-start.13 = (bf16[40,1024]{1,0:T(8,128)(2,1)S(1)}, bf16[40,1024]{1,0:T(8,128)(2,1)S(1)}, u32[]{:S(2)}, u32[]{:S(2)}) collective-permute-start(bf16[40,1024]{1,0:T(8,128)(2,1)S(1)} %get-tuple-element.62), channel_id=1, source_target_pairs={{0,7},{1,6},{2,5},{3,4},{4,3},{5,2},{6,1},{7,0},{8,15},{9,14},{10,... | collective-permute-start | bytes 245768 | tf_op jit(solution)/shard_map/ppermute | solution.py:357
  37.3 6.4 %collective-permute-start.14 = (bf16[40,1024]{1,0:T(8,128)(2,1)S(1)}, bf16[40,1024]{1,0:T(8,128)(2,1)S(1)}, u32[]{:S(2)}, u32[]{:S(2)}) collective-permute-start(bf16[40,1024]{1,0:T(8,128)(2,1)S(1)} %get-tuple-element.66), channel_id=1, source_target_pairs={{0,1},{1,0},{2,3},{3,2},{4,5},{5,4},{6,7},{7,6},{8,9},{9,8},{10,11... | collective-permute-start | bytes 245768 | tf_op jit(solution)/shard_map/ppermute | solution.py:357
  37.9 7.5 %collective-permute-start.15 = (bf16[40,1024]{1,0:T(8,128)(2,1)S(1)}, bf16[40,1024]{1,0:T(8,128)(2,1)S(1)}, u32[]{:S(2)}, u32[]{:S(2)}) collective-permute-start(bf16[40,1024]{1,0:T(8,128)(2,1)S(1)} %get-tuple-element.68), channel_id=1, source_target_pairs={{0,2},{1,3},{2,0},{3,1},{4,6},{5,7},{6,4},{7,5},{8,10},{9,11},{10,... | collective-permute-start | bytes 245768 | tf_op jit(solution)/shard_map/ppermute | solution.py:357
  39.4 8.4 %collective-permute-start.16 = (bf16[40,1024]{1,0:T(8,128)(2,1)S(1)}, bf16[40,1024]{1,0:T(8,128)(2,1)S(1)}, u32[]{:S(2)}, u32[]{:S(2)}) collective-permute-start(bf16[40,1024]{1,0:T(8,128)(2,1)S(1)} %get-tuple-element.69), channel_id=1, source_target_pairs={{0,3},{1,2},{2,1},{3,0},{4,7},{5,6},{6,5},{7,4},{8,11},{9,10},{10,... | collective-permute-start | bytes 245768 | tf_op jit(solution)/shard_map/ppermute | solution.py:357
  42.8 5.0 %collective-permute-start.17 = (bf16[40,1024]{1,0:T(8,128)(2,1)S(1)}, bf16[40,1024]{1,0:T(8,128)(2,1)S(1)}, u32[]{:S(2)}, u32[]{:S(2)}) collective-permute-start(bf16[40,1024]{1,0:T(8,128)(2,1)S(1)} %get-tuple-element.70), channel_id=1, source_target_pairs={{0,4},{1,5},{2,6},{3,7},{4,0},{5,1},{6,2},{7,3},{8,12},{9,13},{10,... | collective-permute-start | bytes 245768 | tf_op jit(solution)/shard_map/ppermute | solution.py:357
  43.7 8.3 %collective-permute-start.18 = (bf16[40,1024]{1,0:T(8,128)(2,1)S(1)}, bf16[40,1024]{1,0:T(8,128)(2,1)S(1)}, u32[]{:S(2)}, u32[]{:S(2)}) collective-permute-start(bf16[40,1024]{1,0:T(8,128)(2,1)S(1)} %get-tuple-element.71), channel_id=1, source_target_pairs={{0,5},{1,4},{2,7},{3,6},{4,1},{5,0},{6,3},{7,2},{8,13},{9,12},{10,... | collective-permute-start | bytes 245768 | tf_op jit(solution)/shard_map/ppermute | solution.py:357
  43.7 8.2 %collective-permute-start.19 = (bf16[40,1024]{1,0:T(8,128)(2,1)S(1)}, bf16[40,1024]{1,0:T(8,128)(2,1)S(1)}, u32[]{:S(2)}, u32[]{:S(2)}) collective-permute-start(bf16[40,1024]{1,0:T(8,128)(2,1)S(1)} %get-tuple-element.72), channel_id=1, source_target_pairs={{0,6},{1,7},{2,4},{3,5},{4,2},{5,3},{6,0},{7,1},{8,14},{9,15},{10,... | collective-permute-start | bytes 245768 | tf_op jit(solution)/shard_map/ppermute | solution.py:357
  45.4 6.6 %collective-permute-start.20 = (bf16[40,1024]{1,0:T(8,128)(2,1)S(1)}, bf16[40,1024]{1,0:T(8,128)(2,1)S(1)}, u32[]{:S(2)}, u32[]{:S(2)}) collective-permute-start(bf16[40,1024]{1,0:T(8,128)(2,1)S(1)} %get-tuple-element.73), channel_id=1, source_target_pairs={{0,7},{1,6},{2,5},{3,4},{4,3},{5,2},{6,1},{7,0},{8,15},{9,14},{10,... | collective-permute-start | bytes 245768 | tf_op jit(solution)/shard_map/ppermute | solution.py:357
  52.5 16.9 %collective-permute-start.21 = (bf16[128,512]{1,0:T(8,128)(2,1)S(1)}, bf16[128,512]{1,0:T(8,128)(2,1)S(1)}, u32[]{:S(2)}, u32[]{:S(2)}) collective-permute-start(bf16[128,512]{1,0:T(8,128)(2,1)S(1)} %get-tuple-element.75), channel_id=1, source_target_pairs={{0,8},{8,0},{16,24},{24,16},{1,9},{9,1},{17,25},{25,17},{2,10},{10... | collective-permute-start | bytes 393224 | tf_op jit(solution)/shard_map/ppermute | solution.py:357
  54.2 15.2 %collective-permute-start.22 = (bf16[128,512]{1,0:T(8,128)(2,1)S(1)}, bf16[128,512]{1,0:T(8,128)(2,1)S(1)}, u32[]{:S(2)}, u32[]{:S(2)}) collective-permute-start(bf16[128,512]{1,0:T(8,128)(2,1)S(1)} %get-tuple-element.76), channel_id=1, source_target_pairs={{0,16},{8,24},{16,0},{24,8},{1,17},{9,25},{17,1},{25,9},{2,18},{10... | collective-permute-start | bytes 393224 | tf_op jit(solution)/shard_map/ppermute | solution.py:357
  56.8 12.6 %collective-permute-start.23 = (bf16[128,512]{1,0:T(8,128)(2,1)S(1)}, bf16[128,512]{1,0:T(8,128)(2,1)S(1)}, u32[]{:S(2)}, u32[]{:S(2)}) collective-permute-start(bf16[128,512]{1,0:T(8,128)(2,1)S(1)} %get-tuple-element.77), channel_id=1, source_target_pairs={{0,24},{8,16},{16,8},{24,0},{1,25},{9,17},{17,9},{25,1},{2,26},{10... | collective-permute-start | bytes 393224 | tf_op jit(solution)/shard_map/ppermute | solution.py:357
  57.0 6.3 %collective-permute-start.24 = (f32[8,128]{1,0:T(8,128)S(1)}, f32[8,128]{1,0:T(8,128)S(1)}, u32[]{:S(2)}, u32[]{:S(2)}) collective-permute-start(f32[8,128]{1,0:T(8,128)S(1)} %get-tuple-element.78.refs_4_), channel_id=1, source_target_pairs={{0,8},{8,0},{16,24},{24,16},{1,9},{9,1},{17,25},{25,17},{2,10},{10... | collective-permute-start | bytes 12296 | tf_op jit(solution)/shard_map/ppermute | solution.py:357
  57.7 11.7 %collective-permute-start.25 = (f32[8,128]{1,0:T(8,128)S(1)}, f32[8,128]{1,0:T(8,128)S(1)}, u32[]{:S(2)}, u32[]{:S(2)}) collective-permute-start(f32[8,128]{1,0:T(8,128)S(1)} %get-tuple-element.78.refs_4_), channel_id=1, source_target_pairs={{0,16},{8,24},{16,0},{24,8},{1,17},{9,25},{17,1},{25,9},{2,18},{10... | collective-permute-start | bytes 12296 | tf_op jit(solution)/shard_map/ppermute | solution.py:357
  63.3 6.1 %collective-permute-start.26 = (f32[8,128]{1,0:T(8,128)S(1)}, f32[8,128]{1,0:T(8,128)S(1)}, u32[]{:S(2)}, u32[]{:S(2)}) collective-permute-start(f32[8,128]{1,0:T(8,128)S(1)} %get-tuple-element.78.refs_4_), channel_id=1, source_target_pairs={{0,24},{8,16},{16,8},{24,0},{1,25},{9,17},{17,9},{25,1},{2,26},{10... | collective-permute-start | bytes 12296 | tf_op jit(solution)/shard_map/ppermute | solution.py:357
where the time goes:
time: 70.9 us; the launch traced here: 70.5 us
  starting transfers between devices  37.3 us (53%)
  waiting for transfers between devices  13.8 us (19%)
  Pallas kernels  10 us (14%)
  local copies, waits for them, and re-layouts  9.18 us (13%)
    ppermute x27, starting transfers between devices, swap(): return lax.ppermute(value, axis, [(i, i ^ offset) for i in range(size)])  37.3 us
    ppermute x27, waiting for transfers between devices, swap(): return lax.ppermute(value, axis, [(i, i ^ offset) for i in range(size)])  13.8 us
    unnamed x18, local copies, waits for them, and re-layouts  9.18 us
    pallas_call x2, Pallas kernels, expert_far(): pl.pallas_call(functools.partial(expert_body, count), out_shape=[jax.Shap...  4.67 us
    pallas_call x1, Pallas kernels, selector(): pl.pallas_call(functools.partial(selector_body, experts, capacity), out_s...  1.42 us
  transfers between devices with their start and end apart: 27, of which 5 were waited for; matrix products, arithmetic and copies ran while one was open for 0% of the time, Pallas kernels for 11%

commit v1 on v0

v1 whole, which is shorter than its diff:
```python
import functools

import jax
import jax.numpy as jnp
from jax import lax
from jax.experimental import pallas as pl
from jax.experimental.pallas import tpu as pltpu
from jax.sharding import PartitionSpec as P


epsilon = 1e-06


F32 = jnp.float32
BF16 = jnp.bfloat16


def expert_ffn(slot_block, w_gate, w_up, w_down):
    shape_in = slot_block.shape
    flat_rows = slot_block.reshape(-1, shape_in[-1])
    gate_act = jnp.dot(flat_rows, w_gate[0], preferred_element_type=F32)
    up_act = jnp.dot(flat_rows, w_up[0], preferred_element_type=F32)
    hidden = (jax.nn.silu(gate_act) * up_act).astype(BF16)
    result = jnp.dot(hidden, w_down[0], preferred_element_type=F32).astype(BF16)
    return result.reshape(shape_in)


def lookup(codes, gate_table):
    levels = gate_table.shape[0]
    match = codes[:, None] == jnp.arange(levels, dtype=jnp.int32)[None, :]
    return jnp.sum(jnp.where(match, gate_table[None, :], 0.0), axis=1)


def combine_pairs(outputs, weights):
    combined = outputs[:, 0] * weights[:, 0:1] + outputs[:, 1] * weights[:, 1:2]
    rounded = lax.optimization_barrier(combined.astype(BF16))
    return rounded.astype(F32)


def local_general(tokens, routes, gate_code, gate_table, w_gate, w_up, w_down, norm_gain):
    own_rows = tokens[0]
    tok_count, feat_width = own_rows.shape
    experts = w_gate.shape[0] * lax.axis_size("expert")
    capacity = 5 * tok_count // (2 * experts)
    route_ids = routes[0].reshape(-1)
    onehot = (route_ids[:, None] == jnp.arange(experts, dtype=jnp.int32)[None, :]).astype(jnp.int32)
    slot_pos = jnp.sum((jnp.cumsum(onehot, axis=0) - onehot) * onehot, axis=1)
    position = route_ids * capacity + slot_pos
    owner_row = (
        jnp.zeros((experts * capacity,), jnp.int32)
        .at[position]
        .set(jnp.arange(2 * tok_count, dtype=jnp.int32) // 2)
    )
    filled = jnp.zeros((experts * capacity,), jnp.bool_).at[position].set(True)
    buffer = jnp.where(filled[:, None], own_rows[owner_row], jnp.zeros((), BF16))
    buffer = buffer.reshape(experts, capacity, feat_width)
    level_ids = gate_code[0].reshape(-1)
    received = lax.all_to_all(buffer, "expert", split_axis=0, concat_axis=0, tiled=True)
    expert_out = expert_ffn(received, w_gate, w_up, w_down)
    returned = lax.all_to_all(expert_out, "expert", split_axis=0, concat_axis=0, tiled=True)
    outputs = (
        returned.reshape(-1, feat_width)[position]
        .astype(F32)
        .reshape(tok_count, 2, feat_width)
    )
    weights = lookup(level_ids, gate_table).reshape(tok_count, 2)
    widened = combine_pairs(outputs, weights)
    inv_rms = lax.rsqrt(jnp.mean(widened * widened, axis=1, keepdims=True) + epsilon)
    normed = (widened * inv_rms * norm_gain[None, :]).astype(BF16)
    relaid = lax.all_to_all(normed, "dp", split_axis=1, concat_axis=0, tiled=True)
    return relaid[None]


def vmem():
    return pl.BlockSpec(memory_space=pltpu.VMEM)


def slot_rows(route_rows, experts, me):
    tok = route_rows.shape[1]
    ids = lax.broadcasted_iota(jnp.int32, (experts, tok), 0) ^ me
    named = (route_rows[0:1, :] == ids) | (route_rows[1:2, :] == ids)
    earlier = lax.broadcasted_iota(jnp.int32, (tok, tok), 0) < lax.broadcasted_iota(
        jnp.int32, (tok, tok), 1
    )
    count = jnp.dot(
        named.astype(F32).astype(BF16), earlier.astype(F32).astype(BF16),
        preferred_element_type=F32,
    )
    return jnp.where(named, count.astype(jnp.int32), -1), ids


def dispatch_body(experts, capacity, route_hbm, tok_hbm, *refs):
    *out_refs, route_ref, tok_ref, sems = refs
    copies = [
        pltpu.make_async_copy(route_hbm, route_ref, sems.at[0]),
        pltpu.make_async_copy(tok_hbm, tok_ref, sems.at[1]),
    ]
    for copy in copies:
        copy.start()
    me = lax.axis_index("expert")
    tok, width = tok_ref.shape
    lane = lax.broadcasted_iota(jnp.int32, (capacity, tok), 0)
    copies[0].wait()
    slots, _ = slot_rows(route_ref[...], experts, me)
    pick = jnp.concatenate(
        [(lane == slots[j : j + 1, :]).astype(F32) for j in range(experts)], axis=0
    ).astype(BF16)
    copies[1].wait()
    tile = 256
    for col in range(0, width, tile):
        rows = jnp.dot(pick, tok_ref[:, col : col + tile], preferred_element_type=F32)
        rows = rows.astype(BF16)
        for j in range(experts):
            out_refs[j][:, col : col + tile] = rows[j * capacity : (j + 1) * capacity, :]


def dispatch(route_rows, own_rows, experts, capacity):
    width = own_rows.shape[1]
    return pl.pallas_call(
        functools.partial(dispatch_body, experts, capacity),
        out_shape=[jax.ShapeDtypeStruct((capacity, width), BF16)] * experts,
        in_specs=[pl.BlockSpec(memory_space=pltpu.HBM)] * 2,
        out_specs=[vmem()] * experts,
        scratch_shapes=[
            pltpu.VMEM(route_rows.shape, jnp.int32),
            pltpu.VMEM(own_rows.shape, BF16),
            pltpu.SemaphoreType.DMA((2,)),
        ],
        name="dispatch",
        cost_estimate=pl.CostEstimate(flops=10**8, transcendentals=0, bytes_accessed=2 * 10**6),
        compiler_params=pltpu.CompilerParams(vmem_limit_bytes=16 * 2**20),
    )(route_rows, own_rows)


def selector_body(experts, capacity, route_ref, code_ref, table_ref, sel_ref, weight_ref):
    me = lax.axis_index("expert")
    rows = route_ref[...]
    slots, ids = slot_rows(rows, experts, me)
    tok = rows.shape[1]
    lane = lax.broadcasted_iota(jnp.int32, (capacity, tok), 0)
    for r in range(2):
        mine = jnp.where(rows[r : r + 1, :] == ids, slots, -1)
        pick = jnp.concatenate(
            [(lane == mine[j : j + 1, :]).astype(F32) for j in range(experts)], axis=0
        )
        sel_ref[r * tok : (r + 1) * tok, :] = pick.T.astype(BF16)
        codes = code_ref[r : r + 1, :]
        weights = jnp.zeros((1, tok), F32)
        for level in range(table_ref.shape[0]):
            weights = jnp.where(codes == level, table_ref[level], weights)
        weight_ref[r] = jnp.broadcast_to(weights, (tok, tok)).T


def selector(route_rows, code_rows, gate_table, experts, capacity):
    tok = route_rows.shape[1]
    return pl.pallas_call(
        functools.partial(selector_body, experts, capacity),
        out_shape=[
            jax.ShapeDtypeStruct((2 * tok, experts * capacity), BF16),
            jax.ShapeDtypeStruct((2, tok, tok), F32),
        ],
        in_specs=[vmem(), vmem(), pl.BlockSpec(memory_space=pltpu.SMEM)],
        out_specs=[vmem()] * 2,
        name="selector",
        cost_estimate=pl.CostEstimate(flops=2 * 10**10, transcendentals=0, bytes_accessed=10**8),
        compiler_params=pltpu.CompilerParams(vmem_limit_bytes=8 * 2**20),
    )(route_rows, code_rows, gate_table)


def chunk_columns(down_ref, offsets, chunk):
    me, tile = lax.axis_index("dp"), 256
    for q, offset in enumerate(offsets):
        for col in range(0, chunk, tile):
            start = pl.multiple_of((me ^ offset) * chunk + col, tile)
            at = q * chunk + col
            yield slice(at, at + tile), down_ref[:, pl.ds(start, tile)]


def write_down(hid_ref, down_ref, offsets, out_refs):
    capacity, width = out_refs[0].shape
    for cols, weight in chunk_columns(down_ref, offsets, width // len(offsets)):
        rows = jnp.dot(hid_ref[...], weight, preferred_element_type=F32).astype(BF16)
        for j, out in enumerate(out_refs):
            out[:, cols] = rows[j * capacity : (j + 1) * capacity, :]


def expert_body(count, pieces, *refs):
    blocks, (gate_ref, up_ref, down_ref) = refs[:count], refs[count : count + 3]
    hid_ref, x_ref, outs = refs[count + 3], refs[-1], refs[count + 4 : -1]
    capacity = blocks[0].shape[0]
    for j, block in enumerate(blocks):
        x_ref[j * capacity : (j + 1) * capacity, :] = block[...]
    hid = gate_ref.shape[0]
    tile = 256
    over = (((1,), (1,)), ((), ()))
    for low in range(0, hid, tile):
        high = min(hid, low + tile)
        gate = lax.dot_general(x_ref[...], gate_ref[low:high, :], over, preferred_element_type=F32)
        up = lax.dot_general(x_ref[...], up_ref[low:high, :], over, preferred_element_type=F32)
        hid_ref[:, low:high] = (gate / (1.0 + jnp.exp(-gate)) * up).astype(BF16)
    for p, offsets in enumerate(pieces):
        write_down(hid_ref, down_ref, offsets, outs[p * count : (p + 1) * count])


def expert_call(blocks, gate_rows, up_rows, down_rows, pieces, ways):
    count = len(blocks)
    capacity, width = blocks[0].shape
    rows, hid = capacity * count, gate_rows.shape[0]
    chunk = down_rows.shape[1] // ways
    shapes = [
        jax.ShapeDtypeStruct((capacity, chunk * len(offsets)), BF16)
        for offsets in pieces
        for _ in range(count)
    ]
    hidden, *outs = pl.pallas_call(
        functools.partial(expert_body, count, pieces),
        out_shape=[jax.ShapeDtypeStruct((rows, hid), BF16)] + shapes,
        in_specs=[vmem()] * (count + 3),
        out_specs=[vmem()] * (1 + len(shapes)),
        scratch_shapes=[pltpu.VMEM((rows, width), BF16)],
        cost_estimate=pl.CostEstimate(
            flops=5 * rows * hid * width, transcendentals=rows * hid, bytes_accessed=8 * 10**6
        ),
        compiler_params=pltpu.CompilerParams(vmem_limit_bytes=24 * 2**20),
    )(*blocks, gate_rows, up_rows, down_rows)
    return hidden, [outs[p * count : (p + 1) * count] for p in range(len(pieces))]


def down_body(offsets, hid_ref, down_ref, *out_refs):
    write_down(hid_ref, down_ref, offsets, out_refs)


def down_call(hidden, down_rows, count, offsets, ways):
    rows, hid = hidden.shape
    width = down_rows.shape[1] // ways * len(offsets)
    return pl.pallas_call(
        functools.partial(down_body, offsets),
        out_shape=[jax.ShapeDtypeStruct((rows // count, width), BF16)] * count,
        in_specs=[vmem()] * 2,
        out_specs=[vmem()] * count,
        cost_estimate=pl.CostEstimate(
            flops=2 * rows * hid * width, transcendentals=0, bytes_accessed=3 * 10**6
        ),
        compiler_params=pltpu.CompilerParams(vmem_limit_bytes=16 * 2**20),
    )(hidden, down_rows)


def gather_blocks(blocks, y_ref, low):
    capacity, width = blocks[0].shape[0], y_ref.shape[1]
    for j, block in enumerate(blocks):
        start = low if block.shape[1] > width else 0
        y_ref[j * capacity : (j + 1) * capacity, :] = block[:, start : start + width]


def combine_chunk(sel_ref, weight_ref, y_ref, low, out_ref, squares):
    tok, lanes = squares.shape
    chunk, tile = out_ref.shape[1], 256
    for col in range(0, chunk, tile):
        picked = jnp.dot(
            sel_ref[...], y_ref[:, low + col : low + col + tile], preferred_element_type=F32
        )
        for at in range(0, tile, lanes):
            first = picked[:tok, at : at + lanes] * weight_ref[0]
            second = picked[tok:, at : at + lanes] * weight_ref[1]
            rounded = (first + second).astype(BF16)
            out_ref[:, col + at : col + at + lanes] = rounded
            wide = rounded.astype(F32)
            squares = squares + wide * wide
    return squares


def early_body(count, sel_ref, weight_ref, *refs):
    blocks, (out_ref, sum_ref, y_ref) = refs[:count], refs[count:]
    gather_blocks(blocks, y_ref, 0)
    squares = jnp.zeros(sum_ref.shape, F32)
    sum_ref[...] = combine_chunk(sel_ref, weight_ref, y_ref, 0, out_ref, squares)


def combine_early(select, weights, blocks, width):
    rows, tok = blocks[0].shape[0] * len(blocks), weights.shape[1]
    return pl.pallas_call(
        functools.partial(early_body, len(blocks)),
        out_shape=[
            jax.ShapeDtypeStruct((tok, width), BF16),
            jax.ShapeDtypeStruct((tok, weights.shape[2]), F32),
        ],
        in_specs=[vmem()] * (2 + len(blocks)),
        out_specs=[vmem()] * 2,
        scratch_shapes=[pltpu.VMEM((rows, width), BF16)],
        name="combine_early",
        cost_estimate=pl.CostEstimate(
            flops=4 * tok * rows * width, transcendentals=0, bytes_accessed=10**6
        ),
        compiler_params=pltpu.CompilerParams(vmem_limit_bytes=12 * 2**20),
    )(select, weights, *blocks)


def late_body(count, feat_width, sel_ref, weight_ref, part_ref, gain_ref, *refs):
    blocks, y_ref, outs, sum_ref = refs[:count], refs[-1], refs[count:-2], refs[-2]
    chunk = outs[0].shape[1]
    gather_blocks(blocks, y_ref, feat_width - chunk * len(outs))
    squares = part_ref[...]
    for q, out in enumerate(outs):
        squares = combine_chunk(sel_ref, weight_ref, y_ref, q * chunk, out, squares)
    total = jnp.sum(squares, axis=1, keepdims=True)
    tok = total.shape[0]
    sum_ref[...] = jnp.broadcast_to(total, (tok, tok)).T[0:8, :]
    inv = lax.rsqrt(total * (1.0 / feat_width) + epsilon)
    for q, out in enumerate(outs):
        gain = gain_ref[0:1, q * chunk : (q + 1) * chunk]
        out[...] = (out[...].astype(F32) * inv * gain).astype(BF16)


def combine_late(select, weights, part, gain, blocks, chunk, feat_width):
    width = gain.shape[1]
    rows, tok = blocks[0].shape[0] * len(blocks), weights.shape[1]
    return pl.pallas_call(
        functools.partial(late_body, len(blocks), feat_width),
        out_shape=[jax.ShapeDtypeStruct((tok, chunk), BF16)] * (width // chunk)
        + [jax.ShapeDtypeStruct((8, tok), F32)],
        in_specs=[vmem()] * (4 + len(blocks)),
        out_specs=[vmem()] * (width // chunk + 1),
        scratch_shapes=[pltpu.VMEM((rows, width), BF16)],
        name="combine_late",
        cost_estimate=pl.CostEstimate(
            flops=4 * tok * rows * width, transcendentals=0, bytes_accessed=2 * 10**6
        ),
        compiler_params=pltpu.CompilerParams(vmem_limit_bytes=12 * 2**20),
    )(select, weights, part, gain, *blocks)


def gain_body(offsets, gain_ref, out_ref):
    chunk = out_ref.shape[1] // len(offsets)
    me = lax.axis_index("dp")
    for q, offset in enumerate(offsets):
        start = pl.multiple_of((me ^ offset) * chunk, 128)
        row = gain_ref[:, pl.ds(start, chunk)]
        out_ref[:, q * chunk : (q + 1) * chunk] = jnp.broadcast_to(row, (8, chunk))


def gain_of(norm_gain, offsets, chunk):
    return pl.pallas_call(
        functools.partial(gain_body, offsets),
        out_shape=jax.ShapeDtypeStruct((8, chunk * len(offsets)), F32),
        in_specs=[vmem()],
        out_specs=vmem(),
        cost_estimate=pl.CostEstimate(flops=10**4, transcendentals=0, bytes_accessed=10**4),
        compiler_params=pltpu.CompilerParams(vmem_limit_bytes=2**20),
    )(norm_gain[None, :])


def finish_body(feat_width, ready, raw, *refs):
    ways = len(ready) + len(raw)
    chunks, sums = refs[:ways], refs[ways : ways + len(raw)]
    gain_ref, out_ref, scratch, sems = refs[ways + len(raw) :]
    me = lax.axis_index("dp")
    tok = chunks[0].shape[0]

    def put(source, k):
        rows = pl.ds(pl.multiple_of((me ^ k) * tok, tok), tok)
        copy = pltpu.make_async_copy(source, out_ref.at[rows, :], sems.at[k])
        copy.start()
        return copy

    copies = [put(chunks[i], k) for i, k in enumerate(ready)]
    for i, k in enumerate(raw):
        inv = lax.rsqrt(sums[i][0:1, :] * (1.0 / feat_width) + epsilon)
        column = jnp.broadcast_to(inv, (tok, tok)).T[:, 0:1]
        value = chunks[len(ready) + i][...].astype(F32) * column * gain_ref[0:1, :]
        scratch[i] = value.astype(BF16)
        copies.append(put(scratch.at[i], k))
    for copy in copies:
        copy.wait()


def finish(ready, raw, sums, gain, feat_width):
    first = next(iter(ready.values()))
    tok, width = first.shape
    ways = len(ready) + len(raw)
    return pl.pallas_call(
        functools.partial(finish_body, feat_width, tuple(ready), tuple(raw)),
        out_shape=jax.ShapeDtypeStruct((tok * ways, width), BF16),
        in_specs=[vmem()] * (ways + len(raw) + 1),
        out_specs=pl.BlockSpec(memory_space=pltpu.HBM),
        scratch_shapes=[
            pltpu.VMEM((len(raw), tok, width), BF16),
            pltpu.SemaphoreType.DMA((ways,)),
        ],
        name="finish",
        cost_estimate=pl.CostEstimate(flops=10**6, transcendentals=0, bytes_accessed=10**6),
        compiler_params=pltpu.CompilerParams(vmem_limit_bytes=8 * 2**20),
    )(*ready.values(), *raw.values(), *[sums[k] for k in raw], gain)


def swap(value, axis, offset):
    size = lax.axis_size(axis)
    return lax.ppermute(value, axis, [(i, i ^ offset) for i in range(size)])


def swap_each(values, axis):
    moved = {}
    for k, value in values.items():
        moved[k] = swap(value, axis, k) if k else value
    return moved


def local_fast(tokens, routes, gate_code, gate_table, w_gate, w_up, w_down, norm_gain):
    return fast_steps(tokens, routes, gate_code, gate_table, w_gate, w_up, w_down, norm_gain)


def fast_steps(tokens, routes, gate_code, gate_table, w_gate, w_up, w_down, norm_gain):
    own_rows = tokens[0]
    tok, feat_width = own_rows.shape
    experts = lax.axis_size("expert")
    ways = lax.axis_size("dp")
    capacity = 5 * tok // (2 * experts)
    chunk = feat_width // ways
    links = [bin(k >> 1).count("1") for k in range(experts)]
    close = [k for k in range(2, experts) if links[k] == 1] + [1, 0]
    away = [k for k in range(experts) if links[k] == 2]
    early = (ways // 2,)
    late = tuple(k for k in range(ways - 1, -1, -1) if k not in early)

    route_rows = routes[0].T
    blocks = dispatch(
        pltpu.with_memory_space_constraint(route_rows, pltpu.HBM),
        pltpu.with_memory_space_constraint(own_rows, pltpu.HBM),
        experts, capacity,
    )
    near = swap_each({k: blocks[k] for k in close}, "expert")
    far = swap_each({k: blocks[k] for k in away}, "expert")
    select, weights = selector(route_rows, gate_code[0].T, gate_table, experts, capacity)
    matrices = w_gate[0].T, w_up[0].T, w_down[0]

    _, (outputs,) = expert_call([near[k] for k in close], *matrices, (early + late,), ways)
    back = swap_each(dict(zip(close, outputs)), "expert")
    gain_own = gain_of(norm_gain, (0,), chunk)
    hidden, (away_early,) = expert_call([far[k] for k in away], *matrices, (early,), ways)
    got_early = back | swap_each(dict(zip(away, away_early)), "expert")
    away_late = down_call(hidden, matrices[2], len(away), late, ways)
    got_late = back | swap_each(dict(zip(away, away_late)), "expert")

    order = range(experts)
    first, part = combine_early(
        select, weights, [got_early[k] for k in order], chunk
    )
    raw = swap_each({early[0]: first}, "dp")
    gain_late = gain_of(norm_gain, late, chunk)
    *rest, total = combine_late(
        select, weights, part, gain_late, [got_late[k] for k in order], chunk, feat_width
    )
    ready = swap_each(dict(zip(late, rest)), "dp")
    sums = swap_each({k: total for k in early}, "dp")
    return finish(ready, raw, sums, gain_own, feat_width)[None]


def solution(mesh):
    in_specs = (
        P("expert", "dp", None),
        P("expert", "dp", None),
        P("expert", "dp", None),
        P(),
        P("expert", None, None),
        P("expert", None, None),
        P("expert", None, None),
        P(),
    )
    out_specs = P("expert", None, "dp")

    def whole(tokens, routes, gate_code, gate_table, w_gate, w_up, w_down, norm_gain):
        args = (tokens, routes, gate_code, gate_table, w_gate, w_up, w_down, norm_gain)
        experts, ways = mesh.shape["expert"], mesh.shape["dp"]
        tok, feat = tokens.shape[1] // ways, tokens.shape[2]
        power = experts & (experts - 1) == 0 and ways & (ways - 1) == 0
        fits = power and experts == 8 and 2 <= ways <= 4
        fits = fits and tok % 128 == 0 and w_gate.shape[0] == experts
        fits = fits and 5 * tok % (16 * experts) == 0 and feat % (256 * ways) == 0
        body = local_fast if fits else local_general
        f = jax.shard_map(body, mesh=mesh, in_specs=in_specs, out_specs=out_specs, check_vma=False)
        return f(*args)

    return whole
```

time: 70.9 us -> 70 us (0.987)
  waiting for transfers between devices: 13.8 us -> 26.9 us
  starting transfers between devices: 37.3 us -> 27.6 us
  local copies, waits for them, and re-layouts: 9.18 us -> 5.47 us
    ppermute x27 -> x20, waiting for transfers between devices: 13.8 us -> 26.9 us  [swap(): return lax.ppermute(value, axis, [(i, i ^ offset) for i in range(size)])]
    ppermute x27 -> x20, starting transfers between devices: 37.3 us -> 27.6 us  [swap(): return lax.ppermute(value, axis, [(i, i ^ offset) for i in range(size)])]
    unnamed x18, local copies, waits for them, and re-layouts: 9.18 us -> 5.47 us
    pallas_call x1, Pallas kernels: 0.7 us -> 1.57 us  [dispatch(): pl.pallas_call(functools.partial(dispatch_body, experts, capacity), out_s...]
  transfers between devices with their start and end apart: 27 -> 20, of which waited for: 5 -> 6; matrix products, arithmetic and copies ran while one was open for 0% -> 0% of each run, Pallas kernels for 11% -> 9%
where the time goes in v1:
time: 70 us; the launch traced here: 69.7 us
  starting transfers between devices  27.6 us (39%)
  waiting for transfers between devices  26.9 us (38%)
  Pallas kernels  9.63 us (14%)
  local copies, waits for them, and re-layouts  5.47 us (8%)
    ppermute x20, starting transfers between devices, swap(): return lax.ppermute(value, axis, [(i, i ^ offset) for i in range(size)])  27.6 us
    ppermute x20, waiting for transfers between devices, swap(): return lax.ppermute(value, axis, [(i, i ^ offset) for i in range(size)])  26.9 us
    unnamed x18, local copies, waits for them, and re-layouts  5.47 us
    pallas_call x2, Pallas kernels, expert_call(): pl.pallas_call(functools.partial(expert_body, count, pieces), out_shape=[...  4.75 us
    pallas_call x1, Pallas kernels, dispatch(): pl.pallas_call(functools.partial(dispatch_body, experts, capacity), out_s...  1.57 us
  transfers between devices with their start and end apart: 20, of which 6 were waited for; matrix products, arithmetic and copies ran while one was open for 0% of the time, Pallas kernels for 9%

profile of v1, /device:TPU:0, one launch (start us, length us, event | category | flops | bytes accessed | tf_op | source)
XLA Modules:
  0.0 69.7 jit_solution(8915386755840123676)
XLA Ops:
  0.0 1.6 %dispatch.1 = (bf16[40,2048]{1,0:T(8,128)(2,1)S(1)}, bf16[40,2048]{1,0:T(8,128)(2,1)S(1)}, bf16[40,2048]{1,0:T(8,128)(2,1)S(1)}, bf16[40,2048]{1,0:T(8,128)(2,1)...) custom-call(s32[2,128]{1,0:T(2,128)} %bitcast.25, ...), custom_call_target="tpu_custom_call" | custom-call | flops 100000000 | bytes 2000000 | tf_op jit(solution)/shard_map/dispatch/pallas_call | solution.py:119
  1.6 3.0 %collective-permute-start = (bf16[40,2048]{1,0:T(8,128)(2,1)S(1)}, bf16[40,2048]{1,0:T(8,128)(2,1)S(1)}, u32[]{:S(2)}, u32[]{:S(2)}) collective-permute-start(bf16[40,2048]{1,0:T(8,128)(2,1)S(1)} %get-tuple-element.34), channel_id=1, source_target_pairs={{0,2},{1,3},{2,0},{3,1},{4,6},{5,7},{6,4},{7,5},{8,10},{9,11},{10,... | collective-permute-start | bytes 491528 | tf_op jit(solution)/shard_map/ppermute | solution.py:397
  4.6 0.0 collective-permute-start.1
  4.6 1.5 %collective-permute-start.2 = (bf16[40,2048]{1,0:T(8,128)(2,1)S(1)}, bf16[40,2048]{1,0:T(8,128)(2,1)S(1)}, u32[]{:S(2)}, u32[]{:S(2)}) collective-permute-start(bf16[40,2048]{1,0:T(8,128)(2,1)S(1)} %get-tuple-element.36), channel_id=1, source_target_pairs={{0,4},{1,5},{2,6},{3,7},{4,0},{5,1},{6,2},{7,3},{8,12},{9,13},{10,... | collective-permute-start | bytes 491528 | tf_op jit(solution)/shard_map/ppermute | solution.py:397
  6.1 0.3 collective-permute-start.3
  6.4 0.4 collective-permute-start.4
  6.8 2.9 %collective-permute-done.refs_0_ = bf16[40,2048]{1,0:T(8,128)(2,1)S(1)} collective-permute-done((bf16[40,2048]{1,0:T(8,128)(2,1)S(1)}, bf16[40,2048]{1,0:T(8,128)(2,1)S(1)}, u32[]{:S(2)}, u32[]{:S(2)}) %collective-permute-start) | collective-permute-done | bytes 163872 | tf_op jit(solution)/shard_map/ppermute | solution.py:397
  9.7 3.0 %collective-permute-start.10 = (bf16[40,2048]{1,0:T(8,128)(2,1)S(1)}, bf16[40,2048]{1,0:T(8,128)(2,1)S(1)}, u32[]{:S(2)}, u32[]{:S(2)}) collective-permute-start(bf16[40,2048]{1,0:T(8,128)(2,1)S(1)} %get-tuple-element.46), channel_id=1, source_target_pairs={{0,6},{1,7},{2,4},{3,5},{4,2},{5,3},{6,0},{7,1},{8,14},{9,15},{10,... | collective-permute-start | bytes 491528 | tf_op jit(solution)/shard_map/ppermute | solution.py:397
  12.6 0.0 collective-permute-done.1.refs_1_
  12.6 3.2 %collective-permute-start.11 = (bf16[40,2048]{1,0:T(8,128)(2,1)S(1)}, bf16[40,2048]{1,0:T(8,128)(2,1)S(1)}, u32[]{:S(2)}, u32[]{:S(2)}) collective-permute-start(bf16[40,2048]{1,0:T(8,128)(2,1)S(1)} %get-tuple-element.47), channel_id=1, source_target_pairs={{0,7},{1,6},{2,5},{3,4},{4,3},{5,2},{6,1},{7,0},{8,15},{9,14},{10,... | collective-permute-start | bytes 491528 | tf_op jit(solution)/shard_map/ppermute | solution.py:397
  15.9 0.0 collective-permute-done.2.refs_2_
  15.9 5.3 %collective-permute-done.3.refs_3_ = bf16[40,2048]{1,0:T(8,128)(2,1)S(1)} collective-permute-done((bf16[40,2048]{1,0:T(8,128)(2,1)S(1)}, bf16[40,2048]{1,0:T(8,128)(2,1)S(1)}, u32[]{:S(2)}, u32[]{:S(2)}) %collective-permute-start.3) | collective-permute-done | bytes 163872 | tf_op jit(solution)/shard_map/ppermute | solution.py:397
  21.1 0.0 collective-permute-done.4.refs_4_
  21.1 0.0 copy-start
  21.1 1.8 %copy-done = bf16[1,704,2048]{2,1,0:T(8,128)(2,1)S(1)} copy-done((bf16[1,704,2048]{2,1,0:T(8,128)(2,1)S(1)}, bf16[1,704,2048]{2,1,0:T(8,128)(2,1)}, u32[]{:S(2)}) %copy-start) | copy-done | bytes 2883608
  23.0 0.0 copy-start.2
  23.0 1.8 %copy-done.2 = bf16[1,2048,704]{1,2,0:T(8,128)(2,1)S(1)} copy-done((bf16[1,2048,704]{1,2,0:T(8,128)(2,1)S(1)}, bf16[1,2048,704]{1,2,0:T(8,128)(2,1)}, u32[]{:S(2)}) %copy-start.2) | copy-done | bytes 2883608
  24.8 0.0 copy-start.4
  24.8 1.8 %copy-done.4 = bf16[1,2048,704]{1,2,0:T(8,128)(2,1)S(1)} copy-done((bf16[1,2048,704]{1,2,0:T(8,128)(2,1)S(1)}, bf16[1,2048,704]{1,2,0:T(8,128)(2,1)}, u32[]{:S(2)}) %copy-start.4) | copy-done | bytes 2883608
  26.6 0.0 copy-start.1
  26.6 2.7 %shard_map.82 = (bf16[240,704]{1,0:T(8,128)(2,1)}, bf16[40,2048]{1,0:T(8,128)(2,1)S(1)}, bf16[40,2048]{1,0:T(8,128)(2,1)S(1)}, bf16[40,2048]{1,0:T(8,128)(2,1)S(...) custom-call(bf16[40,2048]{1,0:T(8,128)(2,1)S(1)} %collective-permute-done.refs_0_, ...), custom_call_target="tpu_custom_call" | custom-call | flops 1730150400 | bytes 8000000 | tf_op jit(solution)/shard_map/pallas_call | solution.py:215
  29.3 0.4 collective-permute-start.5
  29.7 2.0 %collective-permute-start.6 = (bf16[40,2048]{1,0:T(8,128)(2,1)S(1)}, bf16[40,2048]{1,0:T(8,128)(2,1)S(1)}, u32[]{:S(2)}, u32[]{:S(2)}) collective-permute-start(bf16[40,2048]{1,0:T(8,128)(2,1)S(1)} %get-tuple-element.42), channel_id=1, source_target_pairs={{0,2},{1,3},{2,0},{3,1},{4,6},{5,7},{6,4},{7,5},{8,10},{9,11},{10,... | collective-permute-start | bytes 491528 | tf_op jit(solution)/shard_map/ppermute | solution.py:397
  31.7 0.0 collective-permute-done.10.refs_0_
  31.7 0.0 collective-permute-done.11.refs_1_
  31.7 0.0 copy-done.1
  31.7 0.0 copy-done.3
  31.7 2.0 %shard_map.83 = (bf16[80,704]{1,0:T(8,128)(2,1)S(1)}, bf16[40,512]{1,0:T(8,128)(2,1)S(1)}, bf16[40,512]{1,0:T(8,128)(2,1)S(1)}) custom-call(bf16[40,2048]{1,0:T(8,128)(2,1)S(1)} %collective-permute-done.10.refs_0_, bf16[40,2048]{1,0:T(8,128)(2,1)S(1)} %collective-permute-done.11.refs_1_, bf16[704,2048]{1,0:T(8,128)(2,1)S(1)} %bitcast.20, ...), custom_call_target="tpu_custom_call" | custom-call | flops 576716800 | bytes 8000000 | tf_op jit(solution)/shard_map/pallas_call | solution.py:215
  33.7 0.0 copy-start.6
  33.7 0.0 copy-start.7
  33.8 0.0 copy-start.8
  33.8 1.3 %collective-permute-start.12 = (bf16[40,512]{1,0:T(8,128)(2,1)S(1)}, bf16[40,512]{1,0:T(8,128)(2,1)S(1)}, u32[]{:S(2)}, u32[]{:S(2)}) collective-permute-start(bf16[40,512]{1,0:T(8,128)(2,1)S(1)} %get-tuple-element.48), channel_id=1, source_target_pairs={{0,6},{1,7},{2,4},{3,5},{4,2},{5,3},{6,0},{7,1},{8,14},{9,15},{10,... | collective-permute-start | bytes 122888 | tf_op jit(solution)/shard_map/ppermute | solution.py:397
  35.0 1.2 %collective-permute-start.13 = (bf16[40,512]{1,0:T(8,128)(2,1)S(1)}, bf16[40,512]{1,0:T(8,128)(2,1)S(1)}, u32[]{:S(2)}, u32[]{:S(2)}) collective-permute-start(bf16[40,512]{1,0:T(8,128)(2,1)S(1)} %get-tuple-element.49), channel_id=1, source_target_pairs={{0,7},{1,6},{2,5},{3,4},{4,3},{5,2},{6,1},{7,0},{8,15},{9,14},{10,... | collective-permute-start | bytes 122888 | tf_op jit(solution)/shard_map/ppermute | solution.py:397
  36.2 0.4 collective-permute-start.7
  36.6 0.5 shard_map.85
  37.1 1.6 %collective-permute-done.12.refs_6_ = bf16[40,512]{1,0:T(8,128)(2,1)S(1)} collective-permute-done((bf16[40,512]{1,0:T(8,128)(2,1)S(1)}, bf16[40,512]{1,0:T(8,128)(2,1)S(1)}, u32[]{:S(2)}, u32[]{:S(2)}) %collective-permute-start.12) | collective-permute-done | bytes 40992 | tf_op jit(solution)/shard_map/ppermute | solution.py:397
  38.7 1.5 %collective-permute-start.8 = (bf16[40,2048]{1,0:T(8,128)(2,1)S(1)}, bf16[40,2048]{1,0:T(8,128)(2,1)S(1)}, u32[]{:S(2)}, u32[]{:S(2)}) collective-permute-start(bf16[40,2048]{1,0:T(8,128)(2,1)S(1)} %get-tuple-element.44), channel_id=1, source_target_pairs={{0,4},{1,5},{2,6},{3,7},{4,0},{5,1},{6,2},{7,3},{8,12},{9,13},{10,... | collective-permute-start | bytes 491528 | tf_op jit(solution)/shard_map/ppermute | solution.py:397
  40.3 0.0 collective-permute-done.13.refs_7_
  40.3 0.0 collective-permute-start.9
  40.3 0.0 collective-permute-done.5.refs_1_
  40.3 2.4 %collective-permute-start.14 = (bf16[40,1536]{1,0:T(8,128)(2,1)S(1)}, bf16[40,1536]{1,0:T(8,128)(2,1)S(1)}, u32[]{:S(2)}, u32[]{:S(2)}) collective-permute-start(bf16[40,1536]{1,0:T(8,128)(2,1)S(1)} %get-tuple-element.52), channel_id=1, source_target_pairs={{0,6},{1,7},{2,4},{3,5},{4,2},{5,3},{6,0},{7,1},{8,14},{9,15},{10,... | collective-permute-start | bytes 368648 | tf_op jit(solution)/shard_map/ppermute | solution.py:397
  42.7 0.0 collective-permute-done.6.refs_2_
  42.7 0.4 collective-permute-start.15
  43.1 0.0 copy-done.6
  43.1 0.0 copy-done.7
  43.1 0.0 copy-done.8
  43.2 0.8 %selector.1 = (bf16[256,320]{1,0:T(8,128)(2,1)S(1)}, f32[2,128,128]{2,1,0:T(8,128)S(1)}) custom-call(s32[2,128]{1,0:T(2,128)S(1)} %bitcast.26, s32[2,128]{1,0:T(2,128)S(1)} %bitcast.27, f32[16]{0:T(128)S(1)} %copy-done.8), custom_call_target="tpu_custom_call" | custom-call | flops 20000000000 | bytes 100000000 | tf_op jit(solution)/shard_map/selector/pallas_call | solution.py:156
  44.0 0.0 copy-done.5
  44.0 0.0 collective-permute-done.7.refs_3_
  44.0 6.1 %collective-permute-done.8.refs_4_ = bf16[40,2048]{1,0:T(8,128)(2,1)S(1)} collective-permute-done((bf16[40,2048]{1,0:T(8,128)(2,1)S(1)}, bf16[40,2048]{1,0:T(8,128)(2,1)S(1)}, u32[]{:S(2)}, u32[]{:S(2)}) %collective-permute-start.8) | collective-permute-done | bytes 163872 | tf_op jit(solution)/shard_map/ppermute | solution.py:397
  50.1 1.9 %collective-permute-done.9.refs_5_ = bf16[40,2048]{1,0:T(8,128)(2,1)S(1)} collective-permute-done((bf16[40,2048]{1,0:T(8,128)(2,1)S(1)}, bf16[40,2048]{1,0:T(8,128)(2,1)S(1)}, u32[]{:S(2)}, u32[]{:S(2)}) %collective-permute-start.9) | collective-permute-done | bytes 163872 | tf_op jit(solution)/shard_map/ppermute | solution.py:397
  52.0 0.3 combine_early.1
  52.4 0.0 collective-permute-done.14.refs_6_
  52.4 0.0 collective-permute-done.15.refs_7_
  52.4 0.8 %combine_late.1 = (bf16[128,512]{1,0:T(8,128)(2,1)S(1)}, bf16[128,512]{1,0:T(8,128)(2,1)S(1)}, bf16[128,512]{1,0:T(8,128)(2,1)S(1)}, f32[8,128]{1,0:T(8,128)S(1)}) custom-call(bf16[256,320]{1,0:T(8,128)(2,1)S(1)} %get-tuple-element.32.sel_ref, f32[2,128,128]{2,1,0:T(8,128)S(1)} %get-tuple-element.33.weight_ref, f32[128,128]{1,0:T(8,128)S(1)} %get-tuple-element.50.part_ref, ...), custom_call_target="tpu_custom_call" | custom-call | flops 251658240 | bytes 2000000 | tf_op jit(solution)/shard_map/combine_late/pallas_call | solution.py:317
  53.2 3.7 %collective-permute-start.16 = (bf16[128,512]{1,0:T(8,128)(2,1)S(1)}, bf16[128,512]{1,0:T(8,128)(2,1)S(1)}, u32[]{:S(2)}, u32[]{:S(2)}) collective-permute-start(bf16[128,512]{1,0:T(8,128)(2,1)S(1)} %get-tuple-element.54), channel_id=1, source_target_pairs={{0,24},{8,16},{16,8},{24,0},{1,25},{9,17},{17,9},{25,1},{2,26},{10... | collective-permute-start | bytes 393224 | tf_op jit(solution)/shard_map/ppermute | solution.py:397
  56.9 0.0 collective-permute-start.17
  56.9 0.8 %collective-permute-start.18 = (bf16[128,512]{1,0:T(8,128)(2,1)S(1)}, bf16[128,512]{1,0:T(8,128)(2,1)S(1)}, u32[]{:S(2)}, u32[]{:S(2)}) collective-permute-start(bf16[128,512]{1,0:T(8,128)(2,1)S(1)} %get-tuple-element.57), channel_id=1, source_target_pairs={{0,16},{8,24},{16,0},{24,8},{1,17},{9,25},{17,1},{25,9},{2,18},{10... | collective-permute-start | bytes 393224 | tf_op jit(solution)/shard_map/ppermute | solution.py:397
  57.6 2.2 %collective-permute-start.19 = (f32[8,128]{1,0:T(8,128)S(1)}, f32[8,128]{1,0:T(8,128)S(1)}, u32[]{:S(2)}, u32[]{:S(2)}) collective-permute-start(f32[8,128]{1,0:T(8,128)S(1)} %get-tuple-element.58), channel_id=1, source_target_pairs={{0,16},{8,24},{16,0},{24,8},{1,17},{9,25},{17,1},{25,9},{2,18},{10... | collective-permute-start | bytes 12296 | tf_op jit(solution)/shard_map/ppermute | solution.py:397
  59.8 9.1 %collective-permute-done.19.refs_4_ = f32[8,128]{1,0:T(8,128)S(1)} collective-permute-done((f32[8,128]{1,0:T(8,128)S(1)}, f32[8,128]{1,0:T(8,128)S(1)}, u32[]{:S(2)}, u32[]{:S(2)}) %collective-permute-start.19) | collective-permute-done | bytes 4128 | tf_op jit(solution)/shard_map/ppermute | solution.py:397
  68.9 0.0 collective-permute-done.16.refs_0_
  68.9 0.0 collective-permute-done.17.refs_1_
  68.9 0.0 collective-permute-done.18.refs_3_
  68.9 0.9 %finish.1 = bf16[512,512]{1,0:T(8,128)(2,1)} custom-call(bf16[128,512]{1,0:T(8,128)(2,1)S(1)} %collective-permute-done.16.refs_0_, bf16[128,512]{1,0:T(8,128)(2,1)S(1)} %collective-permute-done.17.refs_1_, bf16[128,512]{1,0:T(8,128)(2,1)S(1)} %get-tuple-element.56.refs_2_, bf16[128,512]{1,0:T(8,128)(2,1)S(1)} %collective-permute-done.18.refs_3_, ...), custom_call_target="tpu_custom_call" | custom-call | flops 1000000 | bytes 1000000 | tf_op jit(solution)/shard_map/finish/pallas_call | solution.py:380
  (4 shorter events, 0.0 us)
Async XLA Ops:
  1.6 8.1 %collective-permute-start = (bf16[40,2048]{1,0:T(8,128)(2,1)S(1)}, bf16[40,2048]{1,0:T(8,128)(2,1)S(1)}, u32[]{:S(2)}, u32[]{:S(2)}) collective-permute-start(bf16[40,2048]{1,0:T(8,128)(2,1)S(1)} %get-tuple-element.34), channel_id=1, source_target_pairs={{0,2},{1,3},{2,0},{3,1},{4,6},{5,7},{6,4},{7,5},{8,10},{9,11},{10,... | collective-permute-start | bytes 491528 | tf_op jit(solution)/shard_map/ppermute | solution.py:397
  4.6 8.0 %collective-permute-start.1 = (bf16[40,2048]{1,0:T(8,128)(2,1)S(1)}, bf16[40,2048]{1,0:T(8,128)(2,1)S(1)}, u32[]{:S(2)}, u32[]{:S(2)}) collective-permute-start(bf16[40,2048]{1,0:T(8,128)(2,1)S(1)} %get-tuple-element.35), channel_id=1, source_target_pairs={{0,3},{1,2},{2,1},{3,0},{4,7},{5,6},{6,5},{7,4},{8,11},{9,10},{10,... | collective-permute-start | bytes 491528 | tf_op jit(solution)/shard_map/ppermute | solution.py:397
  4.6 11.3 %collective-permute-start.2 = (bf16[40,2048]{1,0:T(8,128)(2,1)S(1)}, bf16[40,2048]{1,0:T(8,128)(2,1)S(1)}, u32[]{:S(2)}, u32[]{:S(2)}) collective-permute-start(bf16[40,2048]{1,0:T(8,128)(2,1)S(1)} %get-tuple-element.36), channel_id=1, source_target_pairs={{0,4},{1,5},{2,6},{3,7},{4,0},{5,1},{6,2},{7,3},{8,12},{9,13},{10,... | collective-permute-start | bytes 491528 | tf_op jit(solution)/shard_map/ppermute | solution.py:397
  6.1 15.0 %collective-permute-start.3 = (bf16[40,2048]{1,0:T(8,128)(2,1)S(1)}, bf16[40,2048]{1,0:T(8,128)(2,1)S(1)}, u32[]{:S(2)}, u32[]{:S(2)}) collective-permute-start(bf16[40,2048]{1,0:T(8,128)(2,1)S(1)} %get-tuple-element.37), channel_id=1, source_target_pairs={{0,5},{1,4},{2,7},{3,6},{4,1},{5,0},{6,3},{7,2},{8,13},{9,12},{10,... | collective-permute-start | bytes 491528 | tf_op jit(solution)/shard_map/ppermute | solution.py:397
  6.4 14.7 %collective-permute-start.4 = (bf16[40,2048]{1,0:T(8,128)(2,1)S(1)}, bf16[40,2048]{1,0:T(8,128)(2,1)S(1)}, u32[]{:S(2)}, u32[]{:S(2)}) collective-permute-start(bf16[40,2048]{1,0:T(8,128)(2,1)S(1)} %get-tuple-element.38), channel_id=1, source_target_pairs={{0,1},{1,0},{2,3},{3,2},{4,5},{5,4},{6,7},{7,6},{8,9},{9,8},{10,11... | collective-permute-start | bytes 491528 | tf_op jit(solution)/shard_map/ppermute | solution.py:397
  9.7 22.0 %collective-permute-start.10 = (bf16[40,2048]{1,0:T(8,128)(2,1)S(1)}, bf16[40,2048]{1,0:T(8,128)(2,1)S(1)}, u32[]{:S(2)}, u32[]{:S(2)}) collective-permute-start(bf16[40,2048]{1,0:T(8,128)(2,1)S(1)} %get-tuple-element.46), channel_id=1, source_target_pairs={{0,6},{1,7},{2,4},{3,5},{4,2},{5,3},{6,0},{7,1},{8,14},{9,15},{10,... | collective-permute-start | bytes 491528 | tf_op jit(solution)/shard_map/ppermute | solution.py:397
  12.6 19.0 %collective-permute-start.11 = (bf16[40,2048]{1,0:T(8,128)(2,1)S(1)}, bf16[40,2048]{1,0:T(8,128)(2,1)S(1)}, u32[]{:S(2)}, u32[]{:S(2)}) collective-permute-start(bf16[40,2048]{1,0:T(8,128)(2,1)S(1)} %get-tuple-element.47), channel_id=1, source_target_pairs={{0,7},{1,6},{2,5},{3,4},{4,3},{5,2},{6,1},{7,0},{8,15},{9,14},{10,... | collective-permute-start | bytes 491528 | tf_op jit(solution)/shard_map/ppermute | solution.py:397
  21.1 1.8 %copy-start = (bf16[1,704,2048]{2,1,0:T(8,128)(2,1)S(1)}, bf16[1,704,2048]{2,1,0:T(8,128)(2,1)}, u32[]{:S(2)}) copy-start(bf16[1,704,2048]{2,1,0:T(8,128)(2,1)} %param.14) | copy-start | bytes 8650756
  23.0 1.8 %copy-start.2 = (bf16[1,2048,704]{1,2,0:T(8,128)(2,1)S(1)}, bf16[1,2048,704]{1,2,0:T(8,128)(2,1)}, u32[]{:S(2)}) copy-start(bf16[1,2048,704]{1,2,0:T(8,128)(2,1)} %param.12) | copy-start | bytes 8650756
  24.8 1.8 %copy-start.4 = (bf16[1,2048,704]{1,2,0:T(8,128)(2,1)S(1)}, bf16[1,2048,704]{1,2,0:T(8,128)(2,1)}, u32[]{:S(2)}) copy-start(bf16[1,2048,704]{1,2,0:T(8,128)(2,1)} %param.13) | copy-start | bytes 8650756
  26.6 5.1 %copy-start.1 = (bf16[1,704,2048]{2,1,0:T(8,128)(2,1)S(1)}, bf16[1,704,2048]{2,1,0:T(8,128)(2,1)}, u32[]{:S(2)}) copy-start(bf16[1,704,2048]{2,1,0:T(8,128)(2,1)} %param.14) | copy-start | bytes 8650756
  26.6 5.1 %copy-start.3 = (bf16[1,2048,704]{1,2,0:T(8,128)(2,1)S(1)}, bf16[1,2048,704]{1,2,0:T(8,128)(2,1)}, u32[]{:S(2)}) copy-start(bf16[1,2048,704]{1,2,0:T(8,128)(2,1)} %param.12) | copy-start | bytes 8650756
  29.3 11.0 %collective-permute-start.5 = (bf16[40,2048]{1,0:T(8,128)(2,1)S(1)}, bf16[40,2048]{1,0:T(8,128)(2,1)S(1)}, u32[]{:S(2)}, u32[]{:S(2)}) collective-permute-start(bf16[40,2048]{1,0:T(8,128)(2,1)S(1)} %get-tuple-element.41), channel_id=1, source_target_pairs={{0,1},{1,0},{2,3},{3,2},{4,5},{5,4},{6,7},{7,6},{8,9},{9,8},{10,11... | collective-permute-start | bytes 491528 | tf_op jit(solution)/shard_map/ppermute | solution.py:397
  29.7 13.1 %collective-permute-start.6 = (bf16[40,2048]{1,0:T(8,128)(2,1)S(1)}, bf16[40,2048]{1,0:T(8,128)(2,1)S(1)}, u32[]{:S(2)}, u32[]{:S(2)}) collective-permute-start(bf16[40,2048]{1,0:T(8,128)(2,1)S(1)} %get-tuple-element.42), channel_id=1, source_target_pairs={{0,2},{1,3},{2,0},{3,1},{4,6},{5,7},{6,4},{7,5},{8,10},{9,11},{10,... | collective-permute-start | bytes 491528 | tf_op jit(solution)/shard_map/ppermute | solution.py:397
  33.7 9.4 %copy-start.6 = (s32[1,128,2]{1,2,0:T(2,128)S(1)}, s32[1,128,2]{1,2,0:T(2,128)}, u32[]{:S(2)}) copy-start(s32[1,128,2]{1,2,0:T(2,128)} %param.9) | copy-start | bytes 3076
  33.7 9.4 %copy-start.7 = (s32[1,128,2]{1,2,0:T(2,128)S(1)}, s32[1,128,2]{1,2,0:T(2,128)}, u32[]{:S(2)}) copy-start(s32[1,128,2]{1,2,0:T(2,128)} %param.10) | copy-start | bytes 3076
  33.8 9.4 %copy-start.8 = (f32[16]{0:T(128)S(1)}, f32[16]{0:T(128)}, u32[]{:S(2)}) copy-start(f32[16]{0:T(128)} %table_ref.1) | copy-start | bytes 196
  33.8 5.0 %collective-permute-start.12 = (bf16[40,512]{1,0:T(8,128)(2,1)S(1)}, bf16[40,512]{1,0:T(8,128)(2,1)S(1)}, u32[]{:S(2)}, u32[]{:S(2)}) collective-permute-start(bf16[40,512]{1,0:T(8,128)(2,1)S(1)} %get-tuple-element.48), channel_id=1, source_target_pairs={{0,6},{1,7},{2,4},{3,5},{4,2},{5,3},{6,0},{7,1},{8,14},{9,15},{10,... | collective-permute-start | bytes 122888 | tf_op jit(solution)/shard_map/ppermute | solution.py:397
  35.0 5.2 %collective-permute-start.13 = (bf16[40,512]{1,0:T(8,128)(2,1)S(1)}, bf16[40,512]{1,0:T(8,128)(2,1)S(1)}, u32[]{:S(2)}, u32[]{:S(2)}) collective-permute-start(bf16[40,512]{1,0:T(8,128)(2,1)S(1)} %get-tuple-element.49), channel_id=1, source_target_pairs={{0,7},{1,6},{2,5},{3,4},{4,3},{5,2},{6,1},{7,0},{8,15},{9,14},{10,... | collective-permute-start | bytes 122888 | tf_op jit(solution)/shard_map/ppermute | solution.py:397
  36.2 7.8 %collective-permute-start.7 = (bf16[40,2048]{1,0:T(8,128)(2,1)S(1)}, bf16[40,2048]{1,0:T(8,128)(2,1)S(1)}, u32[]{:S(2)}, u32[]{:S(2)}) collective-permute-start(bf16[40,2048]{1,0:T(8,128)(2,1)S(1)} %get-tuple-element.43), channel_id=1, source_target_pairs={{0,3},{1,2},{2,1},{3,0},{4,7},{5,6},{6,5},{7,4},{8,11},{9,10},{10,... | collective-permute-start | bytes 491528 | tf_op jit(solution)/shard_map/ppermute | solution.py:397
  38.7 11.4 %collective-permute-start.8 = (bf16[40,2048]{1,0:T(8,128)(2,1)S(1)}, bf16[40,2048]{1,0:T(8,128)(2,1)S(1)}, u32[]{:S(2)}, u32[]{:S(2)}) collective-permute-start(bf16[40,2048]{1,0:T(8,128)(2,1)S(1)} %get-tuple-element.44), channel_id=1, source_target_pairs={{0,4},{1,5},{2,6},{3,7},{4,0},{5,1},{6,2},{7,3},{8,12},{9,13},{10,... | collective-permute-start | bytes 491528 | tf_op jit(solution)/shard_map/ppermute | solution.py:397
  40.3 11.8 %collective-permute-start.9 = (bf16[40,2048]{1,0:T(8,128)(2,1)S(1)}, bf16[40,2048]{1,0:T(8,128)(2,1)S(1)}, u32[]{:S(2)}, u32[]{:S(2)}) collective-permute-start(bf16[40,2048]{1,0:T(8,128)(2,1)S(1)} %get-tuple-element.45), channel_id=1, source_target_pairs={{0,5},{1,4},{2,7},{3,6},{4,1},{5,0},{6,3},{7,2},{8,13},{9,12},{10,... | collective-permute-start | bytes 491528 | tf_op jit(solution)/shard_map/ppermute | solution.py:397
  40.3 12.1 %collective-permute-start.14 = (bf16[40,1536]{1,0:T(8,128)(2,1)S(1)}, bf16[40,1536]{1,0:T(8,128)(2,1)S(1)}, u32[]{:S(2)}, u32[]{:S(2)}) collective-permute-start(bf16[40,1536]{1,0:T(8,128)(2,1)S(1)} %get-tuple-element.52), channel_id=1, source_target_pairs={{0,6},{1,7},{2,4},{3,5},{4,2},{5,3},{6,0},{7,1},{8,14},{9,15},{10,... | collective-permute-start | bytes 368648 | tf_op jit(solution)/shard_map/ppermute | solution.py:397
  42.7 9.6 %collective-permute-start.15 = (bf16[40,1536]{1,0:T(8,128)(2,1)S(1)}, bf16[40,1536]{1,0:T(8,128)(2,1)S(1)}, u32[]{:S(2)}, u32[]{:S(2)}) collective-permute-start(bf16[40,1536]{1,0:T(8,128)(2,1)S(1)} %get-tuple-element.53), channel_id=1, source_target_pairs={{0,7},{1,6},{2,5},{3,4},{4,3},{5,2},{6,1},{7,0},{8,15},{9,14},{10,... | collective-permute-start | bytes 368648 | tf_op jit(solution)/shard_map/ppermute | solution.py:397
  43.1 0.8 %copy-start.5 = (f32[2048]{0:T(1024)S(1)}, f32[2048]{0:T(1024)}, u32[]{:S(2)}) copy-start(f32[2048]{0:T(1024)} %param.15) | copy-start | bytes 24580
  53.2 15.7 %collective-permute-start.16 = (bf16[128,512]{1,0:T(8,128)(2,1)S(1)}, bf16[128,512]{1,0:T(8,128)(2,1)S(1)}, u32[]{:S(2)}, u32[]{:S(2)}) collective-permute-start(bf16[128,512]{1,0:T(8,128)(2,1)S(1)} %get-tuple-element.54), channel_id=1, source_target_pairs={{0,24},{8,16},{16,8},{24,0},{1,25},{9,17},{17,9},{25,1},{2,26},{10... | collective-permute-start | bytes 393224 | tf_op jit(solution)/shard_map/ppermute | solution.py:397
  56.9 12.0 %collective-permute-start.17 = (bf16[128,512]{1,0:T(8,128)(2,1)S(1)}, bf16[128,512]{1,0:T(8,128)(2,1)S(1)}, u32[]{:S(2)}, u32[]{:S(2)}) collective-permute-start(bf16[128,512]{1,0:T(8,128)(2,1)S(1)} %get-tuple-element.55), channel_id=1, source_target_pairs={{0,8},{8,0},{16,24},{24,16},{1,9},{9,1},{17,25},{25,17},{2,10},{10... | collective-permute-start | bytes 393224 | tf_op jit(solution)/shard_map/ppermute | solution.py:397
  56.9 12.0 %collective-permute-start.18 = (bf16[128,512]{1,0:T(8,128)(2,1)S(1)}, bf16[128,512]{1,0:T(8,128)(2,1)S(1)}, u32[]{:S(2)}, u32[]{:S(2)}) collective-permute-start(bf16[128,512]{1,0:T(8,128)(2,1)S(1)} %get-tuple-element.57), channel_id=1, source_target_pairs={{0,16},{8,24},{16,0},{24,8},{1,17},{9,25},{17,1},{25,9},{2,18},{10... | collective-permute-start | bytes 393224 | tf_op jit(solution)/shard_map/ppermute | solution.py:397
  57.6 11.2 %collective-permute-start.19 = (f32[8,128]{1,0:T(8,128)S(1)}, f32[8,128]{1,0:T(8,128)S(1)}, u32[]{:S(2)}, u32[]{:S(2)}) collective-permute-start(f32[8,128]{1,0:T(8,128)S(1)} %get-tuple-element.58), channel_id=1, source_target_pairs={{0,16},{8,24},{16,0},{24,8},{1,17},{9,25},{17,1},{25,9},{2,18},{10... | collective-permute-start | bytes 12296 | tf_op jit(solution)/shard_map/ppermute | solution.py:397

commit v2 on v1

--- a/solution.py
+++ b/solution.py
@@ -415,9 +415,8 @@
     ways = lax.axis_size("dp")
     capacity = 5 * tok // (2 * experts)
     chunk = feat_width // ways
-    links = [bin(k >> 1).count("1") for k in range(experts)]
-    close = [k for k in range(2, experts) if links[k] == 1] + [1, 0]
-    away = [k for k in range(experts) if links[k] == 2]
+    close = [4, 5, 2, 3, 1, 0]
+    away = [6, 7]
     early = (ways // 2,)
     late = tuple(k for k in range(ways - 1, -1, -1) if k not in early)
 

time: 70 us -> 63 us (0.900)
  waiting for transfers between devices: 26.9 us -> 21.3 us
  starting transfers between devices: 27.6 us -> 26.3 us
    ppermute x20, waiting for transfers between devices: 26.9 us -> 21.3 us  [swap(): return lax.ppermute(value, axis, [(i, i ^ offset) for i in range(size)])]
    ppermute x20, starting transfers between devices: 27.6 us -> 26.3 us  [swap(): return lax.ppermute(value, axis, [(i, i ^ offset) for i in range(size)])]
  transfers between devices with their start and end apart: 20 -> 20, of which waited for: 6 -> 5; matrix products, arithmetic and copies ran while one was open for 0% -> 0% of each run, Pallas kernels for 9% -> 10%
where the time goes in v2:
time: 63 us; the launch traced here: 62.8 us
  starting transfers between devices  26.3 us (42%)
  waiting for transfers between devices  21.3 us (34%)
  Pallas kernels  9.64 us (15%)
  local copies, waits for them, and re-layouts  5.47 us (9%)
    ppermute x20, starting transfers between devices, swap(): return lax.ppermute(value, axis, [(i, i ^ offset) for i in range(size)])  26.3 us
    ppermute x20, waiting for transfers between devices, swap(): return lax.ppermute(value, axis, [(i, i ^ offset) for i in range(size)])  21.3 us
    unnamed x18, local copies, waits for them, and re-layouts  5.47 us
    pallas_call x2, Pallas kernels, expert_call(): pl.pallas_call(functools.partial(expert_body, count, pieces), out_shape=[...  4.75 us
    pallas_call x1, Pallas kernels, dispatch(): pl.pallas_call(functools.partial(dispatch_body, experts, capacity), out_s...  1.57 us
  transfers between devices with their start and end apart: 20, of which 5 were waited for; matrix products, arithmetic and copies ran while one was open for 0% of the time, Pallas kernels for 10%

profile of v2, /device:TPU:0, one launch (start us, length us, event | category | flops | bytes accessed | tf_op | source)
XLA Modules:
  0.0 62.8 jit_solution(10919427677175048669)
XLA Ops:
  0.0 1.6 %dispatch.1 = (bf16[40,2048]{1,0:T(8,128)(2,1)S(1)}, bf16[40,2048]{1,0:T(8,128)(2,1)S(1)}, bf16[40,2048]{1,0:T(8,128)(2,1)S(1)}, bf16[40,2048]{1,0:T(8,128)(2,1)...) custom-call(s32[2,128]{1,0:T(2,128)} %bitcast.25, ...), custom_call_target="tpu_custom_call" | custom-call | flops 100000000 | bytes 2000000 | tf_op jit(solution)/shard_map/dispatch/pallas_call | solution.py:119
  1.6 3.1 %collective-permute-start = (bf16[40,2048]{1,0:T(8,128)(2,1)S(1)}, bf16[40,2048]{1,0:T(8,128)(2,1)S(1)}, u32[]{:S(2)}, u32[]{:S(2)}) collective-permute-start(bf16[40,2048]{1,0:T(8,128)(2,1)S(1)} %get-tuple-element.34), channel_id=1, source_target_pairs={{0,4},{1,5},{2,6},{3,7},{4,0},{5,1},{6,2},{7,3},{8,12},{9,13},{10,... | collective-permute-start | bytes 491528 | tf_op jit(solution)/shard_map/ppermute | solution.py:397
  4.6 0.0 collective-permute-start.1
  4.6 1.5 %collective-permute-start.2 = (bf16[40,2048]{1,0:T(8,128)(2,1)S(1)}, bf16[40,2048]{1,0:T(8,128)(2,1)S(1)}, u32[]{:S(2)}, u32[]{:S(2)}) collective-permute-start(bf16[40,2048]{1,0:T(8,128)(2,1)S(1)} %get-tuple-element.36), channel_id=1, source_target_pairs={{0,2},{1,3},{2,0},{3,1},{4,6},{5,7},{6,4},{7,5},{8,10},{9,11},{10,... | collective-permute-start | bytes 491528 | tf_op jit(solution)/shard_map/ppermute | solution.py:397
  6.1 0.2 collective-permute-start.3
  6.4 0.4 collective-permute-start.4
  6.8 2.9 %collective-permute-done.refs_0_ = bf16[40,2048]{1,0:T(8,128)(2,1)S(1)} collective-permute-done((bf16[40,2048]{1,0:T(8,128)(2,1)S(1)}, bf16[40,2048]{1,0:T(8,128)(2,1)S(1)}, u32[]{:S(2)}, u32[]{:S(2)}) %collective-permute-start) | collective-permute-done | bytes 163872 | tf_op jit(solution)/shard_map/ppermute | solution.py:397
  9.7 2.9 %collective-permute-start.10 = (bf16[40,2048]{1,0:T(8,128)(2,1)S(1)}, bf16[40,2048]{1,0:T(8,128)(2,1)S(1)}, u32[]{:S(2)}, u32[]{:S(2)}) collective-permute-start(bf16[40,2048]{1,0:T(8,128)(2,1)S(1)} %get-tuple-element.46), channel_id=1, source_target_pairs={{0,6},{1,7},{2,4},{3,5},{4,2},{5,3},{6,0},{7,1},{8,14},{9,15},{10,... | collective-permute-start | bytes 491528 | tf_op jit(solution)/shard_map/ppermute | solution.py:397
  12.6 0.0 collective-permute-done.1.refs_1_
  12.6 2.1 %collective-permute-start.11 = (bf16[40,2048]{1,0:T(8,128)(2,1)S(1)}, bf16[40,2048]{1,0:T(8,128)(2,1)S(1)}, u32[]{:S(2)}, u32[]{:S(2)}) collective-permute-start(bf16[40,2048]{1,0:T(8,128)(2,1)S(1)} %get-tuple-element.47), channel_id=1, source_target_pairs={{0,7},{1,6},{2,5},{3,4},{4,3},{5,2},{6,1},{7,0},{8,15},{9,14},{10,... | collective-permute-start | bytes 491528 | tf_op jit(solution)/shard_map/ppermute | solution.py:397
  14.7 0.0 collective-permute-done.2.refs_2_
  14.7 0.0 collective-permute-done.3.refs_3_
  14.7 0.0 collective-permute-done.4.refs_4_
  14.8 0.0 copy-start
  14.8 1.8 %copy-done = bf16[1,704,2048]{2,1,0:T(8,128)(2,1)S(1)} copy-done((bf16[1,704,2048]{2,1,0:T(8,128)(2,1)S(1)}, bf16[1,704,2048]{2,1,0:T(8,128)(2,1)}, u32[]{:S(2)}) %copy-start) | copy-done | bytes 2883608
  16.6 0.0 copy-start.2
  16.6 1.8 %copy-done.2 = bf16[1,2048,704]{1,2,0:T(8,128)(2,1)S(1)} copy-done((bf16[1,2048,704]{1,2,0:T(8,128)(2,1)S(1)}, bf16[1,2048,704]{1,2,0:T(8,128)(2,1)}, u32[]{:S(2)}) %copy-start.2) | copy-done | bytes 2883608
  18.4 0.0 copy-start.4
  18.4 1.8 %copy-done.4 = bf16[1,2048,704]{1,2,0:T(8,128)(2,1)S(1)} copy-done((bf16[1,2048,704]{1,2,0:T(8,128)(2,1)S(1)}, bf16[1,2048,704]{1,2,0:T(8,128)(2,1)}, u32[]{:S(2)}) %copy-start.4) | copy-done | bytes 2883608
  20.2 0.0 copy-start.1
  20.2 2.7 %shard_map.82 = (bf16[240,704]{1,0:T(8,128)(2,1)}, bf16[40,2048]{1,0:T(8,128)(2,1)S(1)}, bf16[40,2048]{1,0:T(8,128)(2,1)S(1)}, bf16[40,2048]{1,0:T(8,128)(2,1)S(...) custom-call(bf16[40,2048]{1,0:T(8,128)(2,1)S(1)} %collective-permute-done.refs_0_, ...), custom_call_target="tpu_custom_call" | custom-call | flops 1730150400 | bytes 8000000 | tf_op jit(solution)/shard_map/pallas_call | solution.py:215
  22.9 0.3 collective-permute-start.5
  23.2 1.5 %collective-permute-start.6 = (bf16[40,2048]{1,0:T(8,128)(2,1)S(1)}, bf16[40,2048]{1,0:T(8,128)(2,1)S(1)}, u32[]{:S(2)}, u32[]{:S(2)}) collective-permute-start(bf16[40,2048]{1,0:T(8,128)(2,1)S(1)} %get-tuple-element.42), channel_id=1, source_target_pairs={{0,2},{1,3},{2,0},{3,1},{4,6},{5,7},{6,4},{7,5},{8,10},{9,11},{10,... | collective-permute-start | bytes 491528 | tf_op jit(solution)/shard_map/ppermute | solution.py:397
  24.7 0.0 collective-permute-done.10.refs_0_
  24.7 0.0 collective-permute-done.11.refs_1_
  24.7 0.0 copy-done.1
  24.7 0.0 copy-done.3
  24.7 2.0 %shard_map.83 = (bf16[80,704]{1,0:T(8,128)(2,1)S(1)}, bf16[40,512]{1,0:T(8,128)(2,1)S(1)}, bf16[40,512]{1,0:T(8,128)(2,1)S(1)}) custom-call(bf16[40,2048]{1,0:T(8,128)(2,1)S(1)} %collective-permute-done.10.refs_0_, bf16[40,2048]{1,0:T(8,128)(2,1)S(1)} %collective-permute-done.11.refs_1_, bf16[704,2048]{1,0:T(8,128)(2,1)S(1)} %bitcast.20, ...), custom_call_target="tpu_custom_call" | custom-call | flops 576716800 | bytes 8000000 | tf_op jit(solution)/shard_map/pallas_call | solution.py:215
  26.8 0.0 copy-start.6
  26.8 0.0 copy-start.7
  26.8 0.0 copy-start.8
  26.8 1.5 %collective-permute-start.12 = (bf16[40,512]{1,0:T(8,128)(2,1)S(1)}, bf16[40,512]{1,0:T(8,128)(2,1)S(1)}, u32[]{:S(2)}, u32[]{:S(2)}) collective-permute-start(bf16[40,512]{1,0:T(8,128)(2,1)S(1)} %get-tuple-element.48), channel_id=1, source_target_pairs={{0,6},{1,7},{2,4},{3,5},{4,2},{5,3},{6,0},{7,1},{8,14},{9,15},{10,... | collective-permute-start | bytes 122888 | tf_op jit(solution)/shard_map/ppermute | solution.py:397
  28.3 0.6 collective-permute-start.13
  28.9 1.2 %collective-permute-start.7 = (bf16[40,2048]{1,0:T(8,128)(2,1)S(1)}, bf16[40,2048]{1,0:T(8,128)(2,1)S(1)}, u32[]{:S(2)}, u32[]{:S(2)}) collective-permute-start(bf16[40,2048]{1,0:T(8,128)(2,1)S(1)} %get-tuple-element.43), channel_id=1, source_target_pairs={{0,3},{1,2},{2,1},{3,0},{4,7},{5,6},{6,5},{7,4},{8,11},{9,10},{10,... | collective-permute-start | bytes 491528 | tf_op jit(solution)/shard_map/ppermute | solution.py:397
  30.1 0.5 shard_map.85
  30.6 1.2 %collective-permute-done.12.refs_6_ = bf16[40,512]{1,0:T(8,128)(2,1)S(1)} collective-permute-done((bf16[40,512]{1,0:T(8,128)(2,1)S(1)}, bf16[40,512]{1,0:T(8,128)(2,1)S(1)}, u32[]{:S(2)}, u32[]{:S(2)}) %collective-permute-start.12) | collective-permute-done | bytes 40992 | tf_op jit(solution)/shard_map/ppermute | solution.py:397
  31.8 1.9 %collective-permute-start.8 = (bf16[40,2048]{1,0:T(8,128)(2,1)S(1)}, bf16[40,2048]{1,0:T(8,128)(2,1)S(1)}, u32[]{:S(2)}, u32[]{:S(2)}) collective-permute-start(bf16[40,2048]{1,0:T(8,128)(2,1)S(1)} %get-tuple-element.44), channel_id=1, source_target_pairs={{0,4},{1,5},{2,6},{3,7},{4,0},{5,1},{6,2},{7,3},{8,12},{9,13},{10,... | collective-permute-start | bytes 491528 | tf_op jit(solution)/shard_map/ppermute | solution.py:397
  33.7 0.0 collective-permute-done.13.refs_7_
  33.7 0.3 collective-permute-start.9
  34.0 0.0 collective-permute-done.5.refs_1_
  34.0 1.8 %collective-permute-start.14 = (bf16[40,1536]{1,0:T(8,128)(2,1)S(1)}, bf16[40,1536]{1,0:T(8,128)(2,1)S(1)}, u32[]{:S(2)}, u32[]{:S(2)}) collective-permute-start(bf16[40,1536]{1,0:T(8,128)(2,1)S(1)} %get-tuple-element.52), channel_id=1, source_target_pairs={{0,6},{1,7},{2,4},{3,5},{4,2},{5,3},{6,0},{7,1},{8,14},{9,15},{10,... | collective-permute-start | bytes 368648 | tf_op jit(solution)/shard_map/ppermute | solution.py:397
  35.7 0.0 collective-permute-done.6.refs_2_
  35.7 0.5 collective-permute-start.15
  36.2 0.0 copy-done.6
  36.2 0.0 copy-done.7
  36.2 0.0 copy-done.8
  36.2 0.8 %selector.1 = (bf16[256,320]{1,0:T(8,128)(2,1)S(1)}, f32[2,128,128]{2,1,0:T(8,128)S(1)}) custom-call(s32[2,128]{1,0:T(2,128)S(1)} %bitcast.26, s32[2,128]{1,0:T(2,128)S(1)} %bitcast.27, f32[16]{0:T(128)S(1)} %copy-done.8), custom_call_target="tpu_custom_call" | custom-call | flops 20000000000 | bytes 100000000 | tf_op jit(solution)/shard_map/selector/pallas_call | solution.py:156
  37.0 0.0 copy-done.5
  37.0 0.0 collective-permute-done.7.refs_3_
  37.1 6.0 %collective-permute-done.8.refs_4_ = bf16[40,2048]{1,0:T(8,128)(2,1)S(1)} collective-permute-done((bf16[40,2048]{1,0:T(8,128)(2,1)S(1)}, bf16[40,2048]{1,0:T(8,128)(2,1)S(1)}, u32[]{:S(2)}, u32[]{:S(2)}) %collective-permute-start.8) | collective-permute-done | bytes 163872 | tf_op jit(solution)/shard_map/ppermute | solution.py:397
  43.1 2.3 %collective-permute-done.9.refs_5_ = bf16[40,2048]{1,0:T(8,128)(2,1)S(1)} collective-permute-done((bf16[40,2048]{1,0:T(8,128)(2,1)S(1)}, bf16[40,2048]{1,0:T(8,128)(2,1)S(1)}, u32[]{:S(2)}, u32[]{:S(2)}) %collective-permute-start.9) | collective-permute-done | bytes 163872 | tf_op jit(solution)/shard_map/ppermute | solution.py:397
  45.4 0.3 combine_early.1
  45.7 0.0 collective-permute-done.14.refs_6_
  45.8 0.0 collective-permute-done.15.refs_7_
  45.8 0.8 %combine_late.1 = (bf16[128,512]{1,0:T(8,128)(2,1)S(1)}, bf16[128,512]{1,0:T(8,128)(2,1)S(1)}, bf16[128,512]{1,0:T(8,128)(2,1)S(1)}, f32[8,128]{1,0:T(8,128)S(1)}) custom-call(bf16[256,320]{1,0:T(8,128)(2,1)S(1)} %get-tuple-element.32.sel_ref, f32[2,128,128]{2,1,0:T(8,128)S(1)} %get-tuple-element.33.weight_ref, f32[128,128]{1,0:T(8,128)S(1)} %get-tuple-element.50.part_ref, ...), custom_call_target="tpu_custom_call" | custom-call | flops 251658240 | bytes 2000000 | tf_op jit(solution)/shard_map/combine_late/pallas_call | solution.py:317
  46.6 3.7 %collective-permute-start.16 = (bf16[128,512]{1,0:T(8,128)(2,1)S(1)}, bf16[128,512]{1,0:T(8,128)(2,1)S(1)}, u32[]{:S(2)}, u32[]{:S(2)}) collective-permute-start(bf16[128,512]{1,0:T(8,128)(2,1)S(1)} %get-tuple-element.54), channel_id=1, source_target_pairs={{0,24},{8,16},{16,8},{24,0},{1,25},{9,17},{17,9},{25,1},{2,26},{10... | collective-permute-start | bytes 393224 | tf_op jit(solution)/shard_map/ppermute | solution.py:397
  50.2 0.0 collective-permute-start.17
  50.2 0.8 %collective-permute-start.18 = (bf16[128,512]{1,0:T(8,128)(2,1)S(1)}, bf16[128,512]{1,0:T(8,128)(2,1)S(1)}, u32[]{:S(2)}, u32[]{:S(2)}) collective-permute-start(bf16[128,512]{1,0:T(8,128)(2,1)S(1)} %get-tuple-element.57), channel_id=1, source_target_pairs={{0,16},{8,24},{16,0},{24,8},{1,17},{9,25},{17,1},{25,9},{2,18},{10... | collective-permute-start | bytes 393224 | tf_op jit(solution)/shard_map/ppermute | solution.py:397
  51.0 2.1 %collective-permute-start.19 = (f32[8,128]{1,0:T(8,128)S(1)}, f32[8,128]{1,0:T(8,128)S(1)}, u32[]{:S(2)}, u32[]{:S(2)}) collective-permute-start(f32[8,128]{1,0:T(8,128)S(1)} %get-tuple-element.58), channel_id=1, source_target_pairs={{0,16},{8,24},{16,0},{24,8},{1,17},{9,25},{17,1},{25,9},{2,18},{10... | collective-permute-start | bytes 12296 | tf_op jit(solution)/shard_map/ppermute | solution.py:397
  53.2 8.8 %collective-permute-done.19.refs_4_ = f32[8,128]{1,0:T(8,128)S(1)} collective-permute-done((f32[8,128]{1,0:T(8,128)S(1)}, f32[8,128]{1,0:T(8,128)S(1)}, u32[]{:S(2)}, u32[]{:S(2)}) %collective-permute-start.19) | collective-permute-done | bytes 4128 | tf_op jit(solution)/shard_map/ppermute | solution.py:397
  61.9 0.0 collective-permute-done.16.refs_0_
  61.9 0.0 collective-permute-done.17.refs_1_
  61.9 0.0 collective-permute-done.18.refs_3_
  61.9 0.9 %finish.1 = bf16[512,512]{1,0:T(8,128)(2,1)} custom-call(bf16[128,512]{1,0:T(8,128)(2,1)S(1)} %collective-permute-done.16.refs_0_, bf16[128,512]{1,0:T(8,128)(2,1)S(1)} %collective-permute-done.17.refs_1_, bf16[128,512]{1,0:T(8,128)(2,1)S(1)} %get-tuple-element.56.refs_2_, bf16[128,512]{1,0:T(8,128)(2,1)S(1)} %collective-permute-done.18.refs_3_, ...), custom_call_target="tpu_custom_call" | custom-call | flops 1000000 | bytes 1000000 | tf_op jit(solution)/shard_map/finish/pallas_call | solution.py:380
  (4 shorter events, 0.0 us)
Async XLA Ops:
  1.6 8.1 %collective-permute-start = (bf16[40,2048]{1,0:T(8,128)(2,1)S(1)}, bf16[40,2048]{1,0:T(8,128)(2,1)S(1)}, u32[]{:S(2)}, u32[]{:S(2)}) collective-permute-start(bf16[40,2048]{1,0:T(8,128)(2,1)S(1)} %get-tuple-element.34), channel_id=1, source_target_pairs={{0,4},{1,5},{2,6},{3,7},{4,0},{5,1},{6,2},{7,3},{8,12},{9,13},{10,... | collective-permute-start | bytes 491528 | tf_op jit(solution)/shard_map/ppermute | solution.py:397
  4.6 8.0 %collective-permute-start.1 = (bf16[40,2048]{1,0:T(8,128)(2,1)S(1)}, bf16[40,2048]{1,0:T(8,128)(2,1)S(1)}, u32[]{:S(2)}, u32[]{:S(2)}) collective-permute-start(bf16[40,2048]{1,0:T(8,128)(2,1)S(1)} %get-tuple-element.35), channel_id=1, source_target_pairs={{0,5},{1,4},{2,7},{3,6},{4,1},{5,0},{6,3},{7,2},{8,13},{9,12},{10,... | collective-permute-start | bytes 491528 | tf_op jit(solution)/shard_map/ppermute | solution.py:397
  4.6 10.1 %collective-permute-start.2 = (bf16[40,2048]{1,0:T(8,128)(2,1)S(1)}, bf16[40,2048]{1,0:T(8,128)(2,1)S(1)}, u32[]{:S(2)}, u32[]{:S(2)}) collective-permute-start(bf16[40,2048]{1,0:T(8,128)(2,1)S(1)} %get-tuple-element.36), channel_id=1, source_target_pairs={{0,2},{1,3},{2,0},{3,1},{4,6},{5,7},{6,4},{7,5},{8,10},{9,11},{10,... | collective-permute-start | bytes 491528 | tf_op jit(solution)/shard_map/ppermute | solution.py:397
  6.1 8.6 %collective-permute-start.3 = (bf16[40,2048]{1,0:T(8,128)(2,1)S(1)}, bf16[40,2048]{1,0:T(8,128)(2,1)S(1)}, u32[]{:S(2)}, u32[]{:S(2)}) collective-permute-start(bf16[40,2048]{1,0:T(8,128)(2,1)S(1)} %get-tuple-element.37), channel_id=1, source_target_pairs={{0,3},{1,2},{2,1},{3,0},{4,7},{5,6},{6,5},{7,4},{8,11},{9,10},{10,... | collective-permute-start | bytes 491528 | tf_op jit(solution)/shard_map/ppermute | solution.py:397
  6.4 8.4 %collective-permute-start.4 = (bf16[40,2048]{1,0:T(8,128)(2,1)S(1)}, bf16[40,2048]{1,0:T(8,128)(2,1)S(1)}, u32[]{:S(2)}, u32[]{:S(2)}) collective-permute-start(bf16[40,2048]{1,0:T(8,128)(2,1)S(1)} %get-tuple-element.38), channel_id=1, source_target_pairs={{0,1},{1,0},{2,3},{3,2},{4,5},{5,4},{6,7},{7,6},{8,9},{9,8},{10,11... | collective-permute-start | bytes 491528 | tf_op jit(solution)/shard_map/ppermute | solution.py:397
  9.7 15.0 %collective-permute-start.10 = (bf16[40,2048]{1,0:T(8,128)(2,1)S(1)}, bf16[40,2048]{1,0:T(8,128)(2,1)S(1)}, u32[]{:S(2)}, u32[]{:S(2)}) collective-permute-start(bf16[40,2048]{1,0:T(8,128)(2,1)S(1)} %get-tuple-element.46), channel_id=1, source_target_pairs={{0,6},{1,7},{2,4},{3,5},{4,2},{5,3},{6,0},{7,1},{8,14},{9,15},{10,... | collective-permute-start | bytes 491528 | tf_op jit(solution)/shard_map/ppermute | solution.py:397
  12.6 12.1 %collective-permute-start.11 = (bf16[40,2048]{1,0:T(8,128)(2,1)S(1)}, bf16[40,2048]{1,0:T(8,128)(2,1)S(1)}, u32[]{:S(2)}, u32[]{:S(2)}) collective-permute-start(bf16[40,2048]{1,0:T(8,128)(2,1)S(1)} %get-tuple-element.47), channel_id=1, source_target_pairs={{0,7},{1,6},{2,5},{3,4},{4,3},{5,2},{6,1},{7,0},{8,15},{9,14},{10,... | collective-permute-start | bytes 491528 | tf_op jit(solution)/shard_map/ppermute | solution.py:397
  14.8 1.8 %copy-start = (bf16[1,704,2048]{2,1,0:T(8,128)(2,1)S(1)}, bf16[1,704,2048]{2,1,0:T(8,128)(2,1)}, u32[]{:S(2)}) copy-start(bf16[1,704,2048]{2,1,0:T(8,128)(2,1)} %param.14) | copy-start | bytes 8650756
  16.6 1.8 %copy-start.2 = (bf16[1,2048,704]{1,2,0:T(8,128)(2,1)S(1)}, bf16[1,2048,704]{1,2,0:T(8,128)(2,1)}, u32[]{:S(2)}) copy-start(bf16[1,2048,704]{1,2,0:T(8,128)(2,1)} %param.12) | copy-start | bytes 8650756
  18.4 1.8 %copy-start.4 = (bf16[1,2048,704]{1,2,0:T(8,128)(2,1)S(1)}, bf16[1,2048,704]{1,2,0:T(8,128)(2,1)}, u32[]{:S(2)}) copy-start(bf16[1,2048,704]{1,2,0:T(8,128)(2,1)} %param.13) | copy-start | bytes 8650756
  20.2 4.5 %copy-start.1 = (bf16[1,704,2048]{2,1,0:T(8,128)(2,1)S(1)}, bf16[1,704,2048]{2,1,0:T(8,128)(2,1)}, u32[]{:S(2)}) copy-start(bf16[1,704,2048]{2,1,0:T(8,128)(2,1)} %param.14) | copy-start | bytes 8650756
  20.2 4.5 %copy-start.3 = (bf16[1,2048,704]{1,2,0:T(8,128)(2,1)S(1)}, bf16[1,2048,704]{1,2,0:T(8,128)(2,1)}, u32[]{:S(2)}) copy-start(bf16[1,2048,704]{1,2,0:T(8,128)(2,1)} %param.12) | copy-start | bytes 8650756
  22.9 11.0 %collective-permute-start.5 = (bf16[40,2048]{1,0:T(8,128)(2,1)S(1)}, bf16[40,2048]{1,0:T(8,128)(2,1)S(1)}, u32[]{:S(2)}, u32[]{:S(2)}) collective-permute-start(bf16[40,2048]{1,0:T(8,128)(2,1)S(1)} %get-tuple-element.41), channel_id=1, source_target_pairs={{0,1},{1,0},{2,3},{3,2},{4,5},{5,4},{6,7},{7,6},{8,9},{9,8},{10,11... | collective-permute-start | bytes 491528 | tf_op jit(solution)/shard_map/ppermute | solution.py:397
  23.2 12.5 %collective-permute-start.6 = (bf16[40,2048]{1,0:T(8,128)(2,1)S(1)}, bf16[40,2048]{1,0:T(8,128)(2,1)S(1)}, u32[]{:S(2)}, u32[]{:S(2)}) collective-permute-start(bf16[40,2048]{1,0:T(8,128)(2,1)S(1)} %get-tuple-element.42), channel_id=1, source_target_pairs={{0,2},{1,3},{2,0},{3,1},{4,6},{5,7},{6,4},{7,5},{8,10},{9,11},{10,... | collective-permute-start | bytes 491528 | tf_op jit(solution)/shard_map/ppermute | solution.py:397
  26.8 9.4 %copy-start.6 = (s32[1,128,2]{1,2,0:T(2,128)S(1)}, s32[1,128,2]{1,2,0:T(2,128)}, u32[]{:S(2)}) copy-start(s32[1,128,2]{1,2,0:T(2,128)} %param.9) | copy-start | bytes 3076
  26.8 9.4 %copy-start.7 = (s32[1,128,2]{1,2,0:T(2,128)S(1)}, s32[1,128,2]{1,2,0:T(2,128)}, u32[]{:S(2)}) copy-start(s32[1,128,2]{1,2,0:T(2,128)} %param.10) | copy-start | bytes 3076
  26.8 9.4 %copy-start.8 = (f32[16]{0:T(128)S(1)}, f32[16]{0:T(128)}, u32[]{:S(2)}) copy-start(f32[16]{0:T(128)} %table_ref.1) | copy-start | bytes 196
  26.8 5.0 %collective-permute-start.12 = (bf16[40,512]{1,0:T(8,128)(2,1)S(1)}, bf16[40,512]{1,0:T(8,128)(2,1)S(1)}, u32[]{:S(2)}, u32[]{:S(2)}) collective-permute-start(bf16[40,512]{1,0:T(8,128)(2,1)S(1)} %get-tuple-element.48), channel_id=1, source_target_pairs={{0,6},{1,7},{2,4},{3,5},{4,2},{5,3},{6,0},{7,1},{8,14},{9,15},{10,... | collective-permute-start | bytes 122888 | tf_op jit(solution)/shard_map/ppermute | solution.py:397
  28.3 5.4 %collective-permute-start.13 = (bf16[40,512]{1,0:T(8,128)(2,1)S(1)}, bf16[40,512]{1,0:T(8,128)(2,1)S(1)}, u32[]{:S(2)}, u32[]{:S(2)}) collective-permute-start(bf16[40,512]{1,0:T(8,128)(2,1)S(1)} %get-tuple-element.49), channel_id=1, source_target_pairs={{0,7},{1,6},{2,5},{3,4},{4,3},{5,2},{6,1},{7,0},{8,15},{9,14},{10,... | collective-permute-start | bytes 122888 | tf_op jit(solution)/shard_map/ppermute | solution.py:397
  28.9 8.2 %collective-permute-start.7 = (bf16[40,2048]{1,0:T(8,128)(2,1)S(1)}, bf16[40,2048]{1,0:T(8,128)(2,1)S(1)}, u32[]{:S(2)}, u32[]{:S(2)}) collective-permute-start(bf16[40,2048]{1,0:T(8,128)(2,1)S(1)} %get-tuple-element.43), channel_id=1, source_target_pairs={{0,3},{1,2},{2,1},{3,0},{4,7},{5,6},{6,5},{7,4},{8,11},{9,10},{10,... | collective-permute-start | bytes 491528 | tf_op jit(solution)/shard_map/ppermute | solution.py:397
  31.8 11.3 %collective-permute-start.8 = (bf16[40,2048]{1,0:T(8,128)(2,1)S(1)}, bf16[40,2048]{1,0:T(8,128)(2,1)S(1)}, u32[]{:S(2)}, u32[]{:S(2)}) collective-permute-start(bf16[40,2048]{1,0:T(8,128)(2,1)S(1)} %get-tuple-element.44), channel_id=1, source_target_pairs={{0,4},{1,5},{2,6},{3,7},{4,0},{5,1},{6,2},{7,3},{8,12},{9,13},{10,... | collective-permute-start | bytes 491528 | tf_op jit(solution)/shard_map/ppermute | solution.py:397
  33.7 11.8 %collective-permute-start.9 = (bf16[40,2048]{1,0:T(8,128)(2,1)S(1)}, bf16[40,2048]{1,0:T(8,128)(2,1)S(1)}, u32[]{:S(2)}, u32[]{:S(2)}) collective-permute-start(bf16[40,2048]{1,0:T(8,128)(2,1)S(1)} %get-tuple-element.45), channel_id=1, source_target_pairs={{0,5},{1,4},{2,7},{3,6},{4,1},{5,0},{6,3},{7,2},{8,13},{9,12},{10,... | collective-permute-start | bytes 491528 | tf_op jit(solution)/shard_map/ppermute | solution.py:397
  34.0 11.8 %collective-permute-start.14 = (bf16[40,1536]{1,0:T(8,128)(2,1)S(1)}, bf16[40,1536]{1,0:T(8,128)(2,1)S(1)}, u32[]{:S(2)}, u32[]{:S(2)}) collective-permute-start(bf16[40,1536]{1,0:T(8,128)(2,1)S(1)} %get-tuple-element.52), channel_id=1, source_target_pairs={{0,6},{1,7},{2,4},{3,5},{4,2},{5,3},{6,0},{7,1},{8,14},{9,15},{10,... | collective-permute-start | bytes 368648 | tf_op jit(solution)/shard_map/ppermute | solution.py:397
  35.7 10.0 %collective-permute-start.15 = (bf16[40,1536]{1,0:T(8,128)(2,1)S(1)}, bf16[40,1536]{1,0:T(8,128)(2,1)S(1)}, u32[]{:S(2)}, u32[]{:S(2)}) collective-permute-start(bf16[40,1536]{1,0:T(8,128)(2,1)S(1)} %get-tuple-element.53), channel_id=1, source_target_pairs={{0,7},{1,6},{2,5},{3,4},{4,3},{5,2},{6,1},{7,0},{8,15},{9,14},{10,... | collective-permute-start | bytes 368648 | tf_op jit(solution)/shard_map/ppermute | solution.py:397
  36.2 0.8 %copy-start.5 = (f32[2048]{0:T(1024)S(1)}, f32[2048]{0:T(1024)}, u32[]{:S(2)}) copy-start(f32[2048]{0:T(1024)} %param.15) | copy-start | bytes 24580
  46.6 15.4 %collective-permute-start.16 = (bf16[128,512]{1,0:T(8,128)(2,1)S(1)}, bf16[128,512]{1,0:T(8,128)(2,1)S(1)}, u32[]{:S(2)}, u32[]{:S(2)}) collective-permute-start(bf16[128,512]{1,0:T(8,128)(2,1)S(1)} %get-tuple-element.54), channel_id=1, source_target_pairs={{0,24},{8,16},{16,8},{24,0},{1,25},{9,17},{17,9},{25,1},{2,26},{10... | collective-permute-start | bytes 393224 | tf_op jit(solution)/shard_map/ppermute | solution.py:397
  50.2 11.7 %collective-permute-start.17 = (bf16[128,512]{1,0:T(8,128)(2,1)S(1)}, bf16[128,512]{1,0:T(8,128)(2,1)S(1)}, u32[]{:S(2)}, u32[]{:S(2)}) collective-permute-start(bf16[128,512]{1,0:T(8,128)(2,1)S(1)} %get-tuple-element.55), channel_id=1, source_target_pairs={{0,8},{8,0},{16,24},{24,16},{1,9},{9,1},{17,25},{25,17},{2,10},{10... | collective-permute-start | bytes 393224 | tf_op jit(solution)/shard_map/ppermute | solution.py:397
  50.2 11.7 %collective-permute-start.18 = (bf16[128,512]{1,0:T(8,128)(2,1)S(1)}, bf16[128,512]{1,0:T(8,128)(2,1)S(1)}, u32[]{:S(2)}, u32[]{:S(2)}) collective-permute-start(bf16[128,512]{1,0:T(8,128)(2,1)S(1)} %get-tuple-element.57), channel_id=1, source_target_pairs={{0,16},{8,24},{16,0},{24,8},{1,17},{9,25},{17,1},{25,9},{2,18},{10... | collective-permute-start | bytes 393224 | tf_op jit(solution)/shard_map/ppermute | solution.py:397
  51.0 10.9 %collective-permute-start.19 = (f32[8,128]{1,0:T(8,128)S(1)}, f32[8,128]{1,0:T(8,128)S(1)}, u32[]{:S(2)}, u32[]{:S(2)}) collective-permute-start(f32[8,128]{1,0:T(8,128)S(1)} %get-tuple-element.58), channel_id=1, source_target_pairs={{0,16},{8,24},{16,0},{24,8},{1,17},{9,25},{17,1},{25,9},{2,18},{10... | collective-permute-start | bytes 12296 | tf_op jit(solution)/shard_map/ppermute | solution.py:397

commit v3 on v2

--- a/solution.py
+++ b/solution.py
@@ -167,24 +167,25 @@
     )(route_rows, code_rows, gate_table)
 
 
-def chunk_columns(down_ref, offsets, chunk):
+def chunk_columns(down_ref, offset, chunk):
     me, tile = lax.axis_index("dp"), 256
-    for q, offset in enumerate(offsets):
-        for col in range(0, chunk, tile):
-            start = pl.multiple_of((me ^ offset) * chunk + col, tile)
-            at = q * chunk + col
-            yield slice(at, at + tile), down_ref[:, pl.ds(start, tile)]
-
-
-def write_down(hid_ref, down_ref, offsets, out_refs):
-    capacity, width = out_refs[0].shape
-    for cols, weight in chunk_columns(down_ref, offsets, width // len(offsets)):
-        rows = jnp.dot(hid_ref[...], weight, preferred_element_type=F32).astype(BF16)
-        for j, out in enumerate(out_refs):
-            out[:, cols] = rows[j * capacity : (j + 1) * capacity, :]
-
-
-def expert_body(count, pieces, *refs):
+    for col in range(0, chunk, tile):
+        start = pl.multiple_of((me ^ offset) * chunk + col, tile)
+        yield col, tile, down_ref[:, pl.ds(start, tile)]
+
+
+def write_down(hid_ref, down_ref, chunk, plan, out_refs):
+    for offset in dict.fromkeys(k for _, offsets in plan for k in offsets):
+        for col, tile, weight in chunk_columns(down_ref, offset, chunk):
+            rows = jnp.dot(hid_ref[...], weight, preferred_element_type=F32).astype(BF16)
+            for (j, offsets), out in zip(plan, out_refs):
+                if offset in offsets:
+                    capacity = out.shape[0]
+                    at = offsets.index(offset) * chunk + col
+                    out[:, at : at + tile] = rows[j * capacity : (j + 1) * capacity, :]
+
+
+def expert_body(count, chunk, plan, *refs):
     blocks, (gate_ref, up_ref, down_ref) = refs[:count], refs[count : count + 3]
     hid_ref, x_ref, outs = refs[count + 3], refs[-1], refs[count + 4 : -1]
     capacity = blocks[0].shape[0]
@@ -198,22 +199,16 @@
         gate = lax.dot_general(x_ref[...], gate_ref[low:high, :], over, preferred_element_type=F32)
         up = lax.dot_general(x_ref[...], up_ref[low:high, :], over, preferred_element_type=F32)
         hid_ref[:, low:high] = (gate / (1.0 + jnp.exp(-gate)) * up).astype(BF16)
-    for p, offsets in enumerate(pieces):
-        write_down(hid_ref, down_ref, offsets, outs[p * count : (p + 1) * count])
-
-
-def expert_call(blocks, gate_rows, up_rows, down_rows, pieces, ways):
+    write_down(hid_ref, down_ref, chunk, plan, outs)
+
+
+def expert_call(blocks, gate_rows, up_rows, down_rows, plan, chunk):
     count = len(blocks)
     capacity, width = blocks[0].shape
     rows, hid = capacity * count, gate_rows.shape[0]
-    chunk = down_rows.shape[1] // ways
-    shapes = [
-        jax.ShapeDtypeStruct((capacity, chunk * len(offsets)), BF16)
-        for offsets in pieces
-        for _ in range(count)
-    ]
-    hidden, *outs = pl.pallas_call(
-        functools.partial(expert_body, count, pieces),
+    shapes = [jax.ShapeDtypeStruct((capacity, chunk * len(offsets)), BF16) for _, offsets in plan]
+    return pl.pallas_call(
+        functools.partial(expert_body, count, chunk, plan),
         out_shape=[jax.ShapeDtypeStruct((rows, hid), BF16)] + shapes,
         in_specs=[vmem()] * (count + 3),
         out_specs=[vmem()] * (1 + len(shapes)),
@@ -223,23 +218,23 @@
         ),
         compiler_params=pltpu.CompilerParams(vmem_limit_bytes=24 * 2**20),
     )(*blocks, gate_rows, up_rows, down_rows)
-    return hidden, [outs[p * count : (p + 1) * count] for p in range(len(pieces))]
-
-
-def down_body(offsets, hid_ref, down_ref, *out_refs):
-    write_down(hid_ref, down_ref, offsets, out_refs)
-
-
-def down_call(hidden, down_rows, count, offsets, ways):
+
+
+def down_body(chunk, plan, hid_ref, down_ref, *out_refs):
+    write_down(hid_ref, down_ref, chunk, plan, out_refs)
+
+
+def down_call(hidden, down_rows, count, plan, chunk):
     rows, hid = hidden.shape
-    width = down_rows.shape[1] // ways * len(offsets)
-    return pl.pallas_call(
-        functools.partial(down_body, offsets),
-        out_shape=[jax.ShapeDtypeStruct((rows // count, width), BF16)] * count,
+    return pl.pallas_call(
+        functools.partial(down_body, chunk, plan),
+        out_shape=[
+            jax.ShapeDtypeStruct((rows // count, chunk * len(offsets)), BF16) for _, offsets in plan
+        ],
         in_specs=[vmem()] * 2,
-        out_specs=[vmem()] * count,
+        out_specs=[vmem()] * len(plan),
         cost_estimate=pl.CostEstimate(
-            flops=2 * rows * hid * width, transcendentals=0, bytes_accessed=3 * 10**6
+            flops=2 * rows * hid * chunk, transcendentals=0, bytes_accessed=3 * 10**6
         ),
         compiler_params=pltpu.CompilerParams(vmem_limit_bytes=16 * 2**20),
     )(hidden, down_rows)
@@ -415,10 +410,10 @@
     ways = lax.axis_size("dp")
     capacity = 5 * tok // (2 * experts)
     chunk = feat_width // ways
-    close = [4, 5, 2, 3, 1, 0]
-    away = [6, 7]
-    early = (ways // 2,)
-    late = tuple(k for k in range(ways - 1, -1, -1) if k not in early)
+    along_y, along_x, own, away = [4, 5], [2, 3], [1, 0], [6, 7]
+    close = along_y + along_x + own
+    early = (ways - 1,)
+    late = tuple(range(ways - 2, -1, -1))
 
     route_rows = routes[0].T
     blocks = dispatch(
@@ -431,13 +426,22 @@
     select, weights = selector(route_rows, gate_code[0].T, gate_table, experts, capacity)
     matrices = w_gate[0].T, w_up[0].T, w_down[0]
 
-    _, (outputs,) = expert_call([near[k] for k in close], *matrices, (early + late,), ways)
-    back = swap_each(dict(zip(close, outputs)), "expert")
+    plan = [(close.index(k), early) for k in along_y]
+    plan += [(close.index(k), early + late) for k in along_x + own]
+    plan += [(close.index(k), late) for k in along_y]
+    _, *outputs = expert_call([near[k] for k in close], *matrices, plan, chunk)
+    y_early, x_whole, own_whole, y_late = outputs[:2], outputs[2:4], outputs[4:6], outputs[6:]
+    got_early = swap_each(dict(zip(along_y, y_early)), "expert")
+    whole = swap_each(dict(zip(along_x, x_whole)), "expert")
+    whole |= swap_each(dict(zip(own, own_whole)), "expert")
+    got_late = swap_each(dict(zip(along_y, y_late)), "expert")
     gain_own = gain_of(norm_gain, (0,), chunk)
-    hidden, (away_early,) = expert_call([far[k] for k in away], *matrices, (early,), ways)
-    got_early = back | swap_each(dict(zip(away, away_early)), "expert")
-    away_late = down_call(hidden, matrices[2], len(away), late, ways)
-    got_late = back | swap_each(dict(zip(away, away_late)), "expert")
+    plan = [(j, early) for j in range(len(away))]
+    hidden, *away_early = expert_call([far[k] for k in away], *matrices, plan, chunk)
+    got_early |= whole | swap_each(dict(zip(away, away_early)), "expert")
+    plan = [(j, late) for j in range(len(away))]
+    away_late = down_call(hidden, matrices[2], len(away), plan, chunk)
+    got_late |= whole | swap_each(dict(zip(away, away_late)), "expert")
 
     order = range(experts)
     first, part = combine_early(

time: 63 us -> 61.7 us (0.979)
  the two profiles are of different devices: /device:TPU:0 before, /device:TPU:17 now
where the time goes in v3:
time: 61.7 us; the launch traced here: 61.5 us
  waiting for transfers between devices  24 us (39%)
  starting transfers between devices  22.2 us (36%)
  Pallas kernels  9.64 us (16%)
  local copies, waits for them, and re-layouts  5.47 us (9%)
    ppermute x22, waiting for transfers between devices, swap(): return lax.ppermute(value, axis, [(i, i ^ offset) for i in range(size)])  24 us
    ppermute x22, starting transfers between devices, swap(): return lax.ppermute(value, axis, [(i, i ^ offset) for i in range(size)])  22.2 us
    unnamed x18, local copies, waits for them, and re-layouts  5.47 us
    pallas_call x2, Pallas kernels, expert_call(): pl.pallas_call(functools.partial(expert_body, count, chunk, plan), out_sh...  4.74 us
    pallas_call x1, Pallas kernels, dispatch(): pl.pallas_call(functools.partial(dispatch_body, experts, capacity), out_s...  1.58 us
  transfers between devices with their start and end apart: 22, of which 7 were waited for; matrix products, arithmetic and copies ran while one was open for 0% of the time, Pallas kernels for 10%

profile of v3, /device:TPU:17, one launch (start us, length us, event | category | flops | bytes accessed | tf_op | source)
XLA Modules:
  0.0 61.5 jit_solution(10232590299016491904)
XLA Ops:
  0.0 1.6 %dispatch.1 = (bf16[40,2048]{1,0:T(8,128)(2,1)S(1)}, bf16[40,2048]{1,0:T(8,128)(2,1)S(1)}, bf16[40,2048]{1,0:T(8,128)(2,1)S(1)}, bf16[40,2048]{1,0:T(8,128)(2,1)...) custom-call(s32[2,128]{1,0:T(2,128)} %bitcast.25, ...), custom_call_target="tpu_custom_call" | custom-call | flops 100000000 | bytes 2000000 | tf_op jit(solution)/shard_map/dispatch/pallas_call | solution.py:119
  1.6 1.3 %collective-permute-start = (bf16[40,2048]{1,0:T(8,128)(2,1)S(1)}, bf16[40,2048]{1,0:T(8,128)(2,1)S(1)}, u32[]{:S(2)}, u32[]{:S(2)}) collective-permute-start(bf16[40,2048]{1,0:T(8,128)(2,1)S(1)} %get-tuple-element.36), channel_id=1, source_target_pairs={{0,4},{1,5},{2,6},{3,7},{4,0},{5,1},{6,2},{7,3},{8,12},{9,13},{10,... | collective-permute-start | bytes 491528 | tf_op jit(solution)/shard_map/ppermute | solution.py:392
  2.9 1.1 %collective-permute-start.1 = (bf16[40,2048]{1,0:T(8,128)(2,1)S(1)}, bf16[40,2048]{1,0:T(8,128)(2,1)S(1)}, u32[]{:S(2)}, u32[]{:S(2)}) collective-permute-start(bf16[40,2048]{1,0:T(8,128)(2,1)S(1)} %get-tuple-element.37), channel_id=1, source_target_pairs={{0,5},{1,4},{2,7},{3,6},{4,1},{5,0},{6,3},{7,2},{8,13},{9,12},{10,... | collective-permute-start | bytes 491528 | tf_op jit(solution)/shard_map/ppermute | solution.py:392
  4.0 1.2 %collective-permute-start.2 = (bf16[40,2048]{1,0:T(8,128)(2,1)S(1)}, bf16[40,2048]{1,0:T(8,128)(2,1)S(1)}, u32[]{:S(2)}, u32[]{:S(2)}) collective-permute-start(bf16[40,2048]{1,0:T(8,128)(2,1)S(1)} %get-tuple-element.38), channel_id=1, source_target_pairs={{0,2},{1,3},{2,0},{3,1},{4,6},{5,7},{6,4},{7,5},{8,10},{9,11},{10,... | collective-permute-start | bytes 491528 | tf_op jit(solution)/shard_map/ppermute | solution.py:392
  5.2 0.3 collective-permute-start.3
  5.5 0.3 collective-permute-start.4
  5.8 0.9 %collective-permute-done.refs_0_ = bf16[40,2048]{1,0:T(8,128)(2,1)S(1)} collective-permute-done((bf16[40,2048]{1,0:T(8,128)(2,1)S(1)}, bf16[40,2048]{1,0:T(8,128)(2,1)S(1)}, u32[]{:S(2)}, u32[]{:S(2)}) %collective-permute-start) | collective-permute-done | bytes 163872 | tf_op jit(solution)/shard_map/ppermute | solution.py:392
  6.7 2.2 %collective-permute-start.10 = (bf16[40,2048]{1,0:T(8,128)(2,1)S(1)}, bf16[40,2048]{1,0:T(8,128)(2,1)S(1)}, u32[]{:S(2)}, u32[]{:S(2)}) collective-permute-start(bf16[40,2048]{1,0:T(8,128)(2,1)S(1)} %get-tuple-element.48), channel_id=1, source_target_pairs={{0,6},{1,7},{2,4},{3,5},{4,2},{5,3},{6,0},{7,1},{8,14},{9,15},{10,... | collective-permute-start | bytes 491528 | tf_op jit(solution)/shard_map/ppermute | solution.py:392
  8.9 2.5 %collective-permute-done.1.refs_1_ = bf16[40,2048]{1,0:T(8,128)(2,1)S(1)} collective-permute-done((bf16[40,2048]{1,0:T(8,128)(2,1)S(1)}, bf16[40,2048]{1,0:T(8,128)(2,1)S(1)}, u32[]{:S(2)}, u32[]{:S(2)}) %collective-permute-start.1) | collective-permute-done | bytes 163872 | tf_op jit(solution)/shard_map/ppermute | solution.py:392
  11.4 1.3 %collective-permute-start.11 = (bf16[40,2048]{1,0:T(8,128)(2,1)S(1)}, bf16[40,2048]{1,0:T(8,128)(2,1)S(1)}, u32[]{:S(2)}, u32[]{:S(2)}) collective-permute-start(bf16[40,2048]{1,0:T(8,128)(2,1)S(1)} %get-tuple-element.49), channel_id=1, source_target_pairs={{0,7},{1,6},{2,5},{3,4},{4,3},{5,2},{6,1},{7,0},{8,15},{9,14},{10,... | collective-permute-start | bytes 491528 | tf_op jit(solution)/shard_map/ppermute | solution.py:392
  12.7 0.0 collective-permute-done.2.refs_2_
  12.7 1.0 %collective-permute-done.3.refs_3_ = bf16[40,2048]{1,0:T(8,128)(2,1)S(1)} collective-permute-done((bf16[40,2048]{1,0:T(8,128)(2,1)S(1)}, bf16[40,2048]{1,0:T(8,128)(2,1)S(1)}, u32[]{:S(2)}, u32[]{:S(2)}) %collective-permute-start.3) | collective-permute-done | bytes 163872 | tf_op jit(solution)/shard_map/ppermute | solution.py:392
  13.7 0.0 collective-permute-done.4.refs_4_
  13.7 1.8 %copy-done = bf16[1,704,2048]{2,1,0:T(8,128)(2,1)S(1)} copy-done((bf16[1,704,2048]{2,1,0:T(8,128)(2,1)S(1)}, bf16[1,704,2048]{2,1,0:T(8,128)(2,1)}, u32[]{:S(2)}) %copy-start) | copy-done | bytes 2883608
  15.6 1.8 %copy-done.2 = bf16[1,2048,704]{1,2,0:T(8,128)(2,1)S(1)} copy-done((bf16[1,2048,704]{1,2,0:T(8,128)(2,1)S(1)}, bf16[1,2048,704]{1,2,0:T(8,128)(2,1)}, u32[]{:S(2)}) %copy-start.2) | copy-done | bytes 2883608
  17.4 1.8 %copy-done.4 = bf16[1,2048,704]{1,2,0:T(8,128)(2,1)S(1)} copy-done((bf16[1,2048,704]{1,2,0:T(8,128)(2,1)S(1)}, bf16[1,2048,704]{1,2,0:T(8,128)(2,1)}, u32[]{:S(2)}) %copy-start.4) | copy-done | bytes 2883608
  19.2 2.7 %shard_map.82 = (bf16[240,704]{1,0:T(8,128)(2,1)}, bf16[40,512]{1,0:T(8,128)(2,1)S(1)}, bf16[40,512]{1,0:T(8,128)(2,1)S(1)}, bf16[40,2048]{1,0:T(8,128)(2,1)S(1)...) custom-call(bf16[40,2048]{1,0:T(8,128)(2,1)S(1)} %collective-permute, ...), custom_call_target="tpu_custom_call" | custom-call | flops 1730150400 | bytes 8000000 | tf_op jit(solution)/shard_map/pallas_call | solution.py:210
  21.9 0.2 collective-permute-start.5
  22.1 1.0 %collective-permute-start.6 = (bf16[40,2048]{1,0:T(8,128)(2,1)S(1)}, bf16[40,2048]{1,0:T(8,128)(2,1)S(1)}, u32[]{:S(2)}, u32[]{:S(2)}) collective-permute-start(bf16[40,2048]{1,0:T(8,128)(2,1)S(1)} %get-tuple-element.44), channel_id=1, source_target_pairs={{0,2},{1,3},{2,0},{3,1},{4,6},{5,7},{6,4},{7,5},{8,10},{9,11},{10,... | collective-permute-start | bytes 491528 | tf_op jit(solution)/shard_map/ppermute | solution.py:392
  23.1 1.5 %collective-permute-start.8 = (bf16[40,512]{1,0:T(8,128)(2,1)S(1)}, bf16[40,512]{1,0:T(8,128)(2,1)S(1)}, u32[]{:S(2)}, u32[]{:S(2)}) collective-permute-start(bf16[40,512]{1,0:T(8,128)(2,1)S(1)} %get-tuple-element.46), channel_id=1, source_target_pairs={{0,4},{1,5},{2,6},{3,7},{4,0},{5,1},{6,2},{7,3},{8,12},{9,13},{10,... | collective-permute-start | bytes 122888 | tf_op jit(solution)/shard_map/ppermute | solution.py:392
  24.7 0.0 collective-permute-done.10.refs_0_
  24.7 0.9 %collective-permute-start.9 = (bf16[40,512]{1,0:T(8,128)(2,1)S(1)}, bf16[40,512]{1,0:T(8,128)(2,1)S(1)}, u32[]{:S(2)}, u32[]{:S(2)}) collective-permute-start(bf16[40,512]{1,0:T(8,128)(2,1)S(1)} %get-tuple-element.47), channel_id=1, source_target_pairs={{0,5},{1,4},{2,7},{3,6},{4,1},{5,0},{6,3},{7,2},{8,13},{9,12},{10,... | collective-permute-start | bytes 122888 | tf_op jit(solution)/shard_map/ppermute | solution.py:392
  25.5 0.0 collective-permute-done.11.refs_1_
  25.6 0.0 copy-done.1
  25.6 0.0 copy-done.3
  25.6 2.0 %shard_map.83 = (bf16[80,704]{1,0:T(8,128)(2,1)S(1)}, bf16[40,512]{1,0:T(8,128)(2,1)S(1)}, bf16[40,512]{1,0:T(8,128)(2,1)S(1)}) custom-call(bf16[40,2048]{1,0:T(8,128)(2,1)S(1)} %collective-permute-done.10.refs_0_, bf16[40,2048]{1,0:T(8,128)(2,1)S(1)} %collective-permute-done.11.refs_1_, bf16[704,2048]{1,0:T(8,128)(2,1)S(1)} %bitcast.20, ...), custom_call_target="tpu_custom_call" | custom-call | flops 576716800 | bytes 8000000 | tf_op jit(solution)/shard_map/pallas_call | solution.py:210
  27.6 0.0 copy-start.6
  27.6 0.0 copy-start.7
  27.6 0.0 copy-start.8
  27.6 1.2 %collective-permute-start.12 = (bf16[40,512]{1,0:T(8,128)(2,1)S(1)}, bf16[40,512]{1,0:T(8,128)(2,1)S(1)}, u32[]{:S(2)}, u32[]{:S(2)}) collective-permute-start(bf16[40,512]{1,0:T(8,128)(2,1)S(1)} %get-tuple-element.50), channel_id=1, source_target_pairs={{0,6},{1,7},{2,4},{3,5},{4,2},{5,3},{6,0},{7,1},{8,14},{9,15},{10,... | collective-permute-start | bytes 122888 | tf_op jit(solution)/shard_map/ppermute | solution.py:392
  28.8 0.0 collective-permute-done.8.refs_4_
  28.8 1.2 %collective-permute-start.13 = (bf16[40,512]{1,0:T(8,128)(2,1)S(1)}, bf16[40,512]{1,0:T(8,128)(2,1)S(1)}, u32[]{:S(2)}, u32[]{:S(2)}) collective-permute-start(bf16[40,512]{1,0:T(8,128)(2,1)S(1)} %get-tuple-element.51), channel_id=1, source_target_pairs={{0,7},{1,6},{2,5},{3,4},{4,3},{5,2},{6,1},{7,0},{8,15},{9,14},{10,... | collective-permute-start | bytes 122888 | tf_op jit(solution)/shard_map/ppermute | solution.py:392
  30.1 0.5 shard_map.85
  30.6 0.0 collective-permute-done.9.refs_5_
  30.6 0.6 collective-permute-start.7
  31.2 0.7 %collective-permute-done.12.refs_6_ = bf16[40,512]{1,0:T(8,128)(2,1)S(1)} collective-permute-done((bf16[40,512]{1,0:T(8,128)(2,1)S(1)}, bf16[40,512]{1,0:T(8,128)(2,1)S(1)}, u32[]{:S(2)}, u32[]{:S(2)}) %collective-permute-start.12) | collective-permute-done | bytes 40992 | tf_op jit(solution)/shard_map/ppermute | solution.py:392
  31.9 1.2 %collective-permute-start.14 = (bf16[40,1536]{1,0:T(8,128)(2,1)S(1)}, bf16[40,1536]{1,0:T(8,128)(2,1)S(1)}, u32[]{:S(2)}, u32[]{:S(2)}) collective-permute-start(bf16[40,1536]{1,0:T(8,128)(2,1)S(1)} %get-tuple-element.53), channel_id=1, source_target_pairs={{0,4},{1,5},{2,6},{3,7},{4,0},{5,1},{6,2},{7,3},{8,12},{9,13},{10,... | collective-permute-start | bytes 368648 | tf_op jit(solution)/shard_map/ppermute | solution.py:392
  33.1 0.1 collective-permute-done.13.refs_7_
  33.2 1.1 %collective-permute-start.15 = (bf16[40,1536]{1,0:T(8,128)(2,1)S(1)}, bf16[40,1536]{1,0:T(8,128)(2,1)S(1)}, u32[]{:S(2)}, u32[]{:S(2)}) collective-permute-start(bf16[40,1536]{1,0:T(8,128)(2,1)S(1)} %get-tuple-element.54), channel_id=1, source_target_pairs={{0,5},{1,4},{2,7},{3,6},{4,1},{5,0},{6,3},{7,2},{8,13},{9,12},{10,... | collective-permute-start | bytes 368648 | tf_op jit(solution)/shard_map/ppermute | solution.py:392
  34.2 0.0 collective-permute-done.5.refs_1_
  34.2 1.3 %collective-permute-start.16 = (bf16[40,1536]{1,0:T(8,128)(2,1)S(1)}, bf16[40,1536]{1,0:T(8,128)(2,1)S(1)}, u32[]{:S(2)}, u32[]{:S(2)}) collective-permute-start(bf16[40,1536]{1,0:T(8,128)(2,1)S(1)} %get-tuple-element.56), channel_id=1, source_target_pairs={{0,6},{1,7},{2,4},{3,5},{4,2},{5,3},{6,0},{7,1},{8,14},{9,15},{10,... | collective-permute-start | bytes 368648 | tf_op jit(solution)/shard_map/ppermute | solution.py:392
  35.6 0.0 collective-permute-done.6.refs_2_
  35.6 1.4 %collective-permute-start.17 = (bf16[40,1536]{1,0:T(8,128)(2,1)S(1)}, bf16[40,1536]{1,0:T(8,128)(2,1)S(1)}, u32[]{:S(2)}, u32[]{:S(2)}) collective-permute-start(bf16[40,1536]{1,0:T(8,128)(2,1)S(1)} %get-tuple-element.57), channel_id=1, source_target_pairs={{0,7},{1,6},{2,5},{3,4},{4,3},{5,2},{6,1},{7,0},{8,15},{9,14},{10,... | collective-permute-start | bytes 368648 | tf_op jit(solution)/shard_map/ppermute | solution.py:392
  36.9 0.0 copy-done.6
  36.9 0.0 copy-done.7
  36.9 0.0 copy-done.8
  37.0 0.8 %selector.1 = (bf16[256,320]{1,0:T(8,128)(2,1)S(1)}, f32[2,128,128]{2,1,0:T(8,128)S(1)}) custom-call(s32[2,128]{1,0:T(2,128)S(1)} %bitcast.26, s32[2,128]{1,0:T(2,128)S(1)} %bitcast.27, f32[16]{0:T(128)S(1)} %copy-done.8), custom_call_target="tpu_custom_call" | custom-call | flops 20000000000 | bytes 100000000 | tf_op jit(solution)/shard_map/selector/pallas_call | solution.py:156
  37.8 0.0 copy-done.5
  37.8 0.0 collective-permute-done.7.refs_3_
  37.8 0.3 combine_early.1
  38.1 0.0 collective-permute-done.14.refs_4_
  38.2 6.7 %collective-permute-done.15.refs_5_ = bf16[40,1536]{1,0:T(8,128)(2,1)S(1)} collective-permute-done((bf16[40,1536]{1,0:T(8,128)(2,1)S(1)}, bf16[40,1536]{1,0:T(8,128)(2,1)S(1)}, u32[]{:S(2)}, u32[]{:S(2)}) %collective-permute-start.15) | collective-permute-done | bytes 122912 | tf_op jit(solution)/shard_map/ppermute | solution.py:392
  44.8 0.0 collective-permute-done.16.refs_6_
  44.8 0.0 collective-permute-done.17.refs_7_
  44.8 0.8 %combine_late.1 = (bf16[128,512]{1,0:T(8,128)(2,1)S(1)}, bf16[128,512]{1,0:T(8,128)(2,1)S(1)}, bf16[128,512]{1,0:T(8,128)(2,1)S(1)}, f32[8,128]{1,0:T(8,128)S(1)}) custom-call(bf16[256,320]{1,0:T(8,128)(2,1)S(1)} %get-tuple-element.34.sel_ref, f32[2,128,128]{2,1,0:T(8,128)S(1)} %get-tuple-element.35.weight_ref, f32[128,128]{1,0:T(8,128)S(1)} %get-tuple-element.52.part_ref, ...), custom_call_target="tpu_custom_call" | custom-call | flops 251658240 | bytes 2000000 | tf_op jit(solution)/shard_map/combine_late/pallas_call | solution.py:312
  45.6 0.1 collective-permute-start.18
  45.7 1.3 %collective-permute-start.19 = (bf16[128,512]{1,0:T(8,128)(2,1)S(1)}, bf16[128,512]{1,0:T(8,128)(2,1)S(1)}, u32[]{:S(2)}, u32[]{:S(2)}) collective-permute-start(bf16[128,512]{1,0:T(8,128)(2,1)S(1)} %get-tuple-element.59), channel_id=1, source_target_pairs={{0,8},{8,0},{16,24},{24,16},{1,9},{9,1},{17,25},{25,17},{2,10},{10... | collective-permute-start | bytes 393224 | tf_op jit(solution)/shard_map/ppermute | solution.py:392
  47.0 1.3 %collective-permute-start.20 = (bf16[128,512]{1,0:T(8,128)(2,1)S(1)}, bf16[128,512]{1,0:T(8,128)(2,1)S(1)}, u32[]{:S(2)}, u32[]{:S(2)}) collective-permute-start(bf16[128,512]{1,0:T(8,128)(2,1)S(1)} %get-tuple-element.61), channel_id=1, source_target_pairs={{0,24},{8,16},{16,8},{24,0},{1,25},{9,17},{17,9},{25,1},{2,26},{10... | collective-permute-start | bytes 393224 | tf_op jit(solution)/shard_map/ppermute | solution.py:392
  48.3 0.2 collective-permute-start.21
  48.5 12.1 %collective-permute-done.21.refs_4_ = f32[8,128]{1,0:T(8,128)S(1)} collective-permute-done((f32[8,128]{1,0:T(8,128)S(1)}, f32[8,128]{1,0:T(8,128)S(1)}, u32[]{:S(2)}, u32[]{:S(2)}) %collective-permute-start.21) | collective-permute-done | bytes 4128 | tf_op jit(solution)/shard_map/ppermute | solution.py:392
  60.6 0.0 collective-permute-done.18.refs_0_
  60.6 0.0 collective-permute-done.19.refs_1_
  60.6 0.0 collective-permute-done.20.refs_3_
  60.6 0.9 %finish.1 = bf16[512,512]{1,0:T(8,128)(2,1)} custom-call(bf16[128,512]{1,0:T(8,128)(2,1)S(1)} %collective-permute-done.18.refs_0_, bf16[128,512]{1,0:T(8,128)(2,1)S(1)} %collective-permute-done.19.refs_1_, bf16[128,512]{1,0:T(8,128)(2,1)S(1)} %get-tuple-element.60.refs_2_, bf16[128,512]{1,0:T(8,128)(2,1)S(1)} %collective-permute-done.20.refs_3_, ...), custom_call_target="tpu_custom_call" | custom-call | flops 1000000 | bytes 1000000 | tf_op jit(solution)/shard_map/finish/pallas_call | solution.py:375
  (8 shorter events, 0.0 us)
Async XLA Ops:
  1.6 5.1 %collective-permute-start = (bf16[40,2048]{1,0:T(8,128)(2,1)S(1)}, bf16[40,2048]{1,0:T(8,128)(2,1)S(1)}, u32[]{:S(2)}, u32[]{:S(2)}) collective-permute-start(bf16[40,2048]{1,0:T(8,128)(2,1)S(1)} %get-tuple-element.36), channel_id=1, source_target_pairs={{0,4},{1,5},{2,6},{3,7},{4,0},{5,1},{6,2},{7,3},{8,12},{9,13},{10,... | collective-permute-start | bytes 491528 | tf_op jit(solution)/shard_map/ppermute | solution.py:392
  2.9 8.5 %collective-permute-start.1 = (bf16[40,2048]{1,0:T(8,128)(2,1)S(1)}, bf16[40,2048]{1,0:T(8,128)(2,1)S(1)}, u32[]{:S(2)}, u32[]{:S(2)}) collective-permute-start(bf16[40,2048]{1,0:T(8,128)(2,1)S(1)} %get-tuple-element.37), channel_id=1, source_target_pairs={{0,5},{1,4},{2,7},{3,6},{4,1},{5,0},{6,3},{7,2},{8,13},{9,12},{10,... | collective-permute-start | bytes 491528 | tf_op jit(solution)/shard_map/ppermute | solution.py:392
  4.0 8.7 %collective-permute-start.2 = (bf16[40,2048]{1,0:T(8,128)(2,1)S(1)}, bf16[40,2048]{1,0:T(8,128)(2,1)S(1)}, u32[]{:S(2)}, u32[]{:S(2)}) collective-permute-start(bf16[40,2048]{1,0:T(8,128)(2,1)S(1)} %get-tuple-element.38), channel_id=1, source_target_pairs={{0,2},{1,3},{2,0},{3,1},{4,6},{5,7},{6,4},{7,5},{8,10},{9,11},{10,... | collective-permute-start | bytes 491528 | tf_op jit(solution)/shard_map/ppermute | solution.py:392
  5.2 8.6 %collective-permute-start.3 = (bf16[40,2048]{1,0:T(8,128)(2,1)S(1)}, bf16[40,2048]{1,0:T(8,128)(2,1)S(1)}, u32[]{:S(2)}, u32[]{:S(2)}) collective-permute-start(bf16[40,2048]{1,0:T(8,128)(2,1)S(1)} %get-tuple-element.39), channel_id=1, source_target_pairs={{0,3},{1,2},{2,1},{3,0},{4,7},{5,6},{6,5},{7,4},{8,11},{9,10},{10,... | collective-permute-start | bytes 491528 | tf_op jit(solution)/shard_map/ppermute | solution.py:392
  5.5 8.3 %collective-permute-start.4 = (bf16[40,2048]{1,0:T(8,128)(2,1)S(1)}, bf16[40,2048]{1,0:T(8,128)(2,1)S(1)}, u32[]{:S(2)}, u32[]{:S(2)}) collective-permute-start(bf16[40,2048]{1,0:T(8,128)(2,1)S(1)} %get-tuple-element.40), channel_id=1, source_target_pairs={{0,1},{1,0},{2,3},{3,2},{4,5},{5,4},{6,7},{7,6},{8,9},{9,8},{10,11... | collective-permute-start | bytes 491528 | tf_op jit(solution)/shard_map/ppermute | solution.py:392
  6.7 18.0 %collective-permute-start.10 = (bf16[40,2048]{1,0:T(8,128)(2,1)S(1)}, bf16[40,2048]{1,0:T(8,128)(2,1)S(1)}, u32[]{:S(2)}, u32[]{:S(2)}) collective-permute-start(bf16[40,2048]{1,0:T(8,128)(2,1)S(1)} %get-tuple-element.48), channel_id=1, source_target_pairs={{0,6},{1,7},{2,4},{3,5},{4,2},{5,3},{6,0},{7,1},{8,14},{9,15},{10,... | collective-permute-start | bytes 491528 | tf_op jit(solution)/shard_map/ppermute | solution.py:392
  11.4 14.2 %collective-permute-start.11 = (bf16[40,2048]{1,0:T(8,128)(2,1)S(1)}, bf16[40,2048]{1,0:T(8,128)(2,1)S(1)}, u32[]{:S(2)}, u32[]{:S(2)}) collective-permute-start(bf16[40,2048]{1,0:T(8,128)(2,1)S(1)} %get-tuple-element.49), channel_id=1, source_target_pairs={{0,7},{1,6},{2,5},{3,4},{4,3},{5,2},{6,1},{7,0},{8,15},{9,14},{10,... | collective-permute-start | bytes 491528 | tf_op jit(solution)/shard_map/ppermute | solution.py:392
  13.7 1.8 %copy-start = (bf16[1,704,2048]{2,1,0:T(8,128)(2,1)S(1)}, bf16[1,704,2048]{2,1,0:T(8,128)(2,1)}, u32[]{:S(2)}) copy-start(bf16[1,704,2048]{2,1,0:T(8,128)(2,1)} %param.14) | copy-start | bytes 8650756
  15.6 1.8 %copy-start.2 = (bf16[1,2048,704]{1,2,0:T(8,128)(2,1)S(1)}, bf16[1,2048,704]{1,2,0:T(8,128)(2,1)}, u32[]{:S(2)}) copy-start(bf16[1,2048,704]{1,2,0:T(8,128)(2,1)} %param.12) | copy-start | bytes 8650756
  17.4 1.8 %copy-start.4 = (bf16[1,2048,704]{1,2,0:T(8,128)(2,1)S(1)}, bf16[1,2048,704]{1,2,0:T(8,128)(2,1)}, u32[]{:S(2)}) copy-start(bf16[1,2048,704]{1,2,0:T(8,128)(2,1)} %param.13) | copy-start | bytes 8650756
  19.2 6.4 %copy-start.1 = (bf16[1,704,2048]{2,1,0:T(8,128)(2,1)S(1)}, bf16[1,704,2048]{2,1,0:T(8,128)(2,1)}, u32[]{:S(2)}) copy-start(bf16[1,704,2048]{2,1,0:T(8,128)(2,1)} %param.14) | copy-start | bytes 8650756
  19.2 6.4 %copy-start.3 = (bf16[1,2048,704]{1,2,0:T(8,128)(2,1)S(1)}, bf16[1,2048,704]{1,2,0:T(8,128)(2,1)}, u32[]{:S(2)}) copy-start(bf16[1,2048,704]{1,2,0:T(8,128)(2,1)} %param.12) | copy-start | bytes 8650756
  21.9 12.3 %collective-permute-start.5 = (bf16[40,2048]{1,0:T(8,128)(2,1)S(1)}, bf16[40,2048]{1,0:T(8,128)(2,1)S(1)}, u32[]{:S(2)}, u32[]{:S(2)}) collective-permute-start(bf16[40,2048]{1,0:T(8,128)(2,1)S(1)} %get-tuple-element.43), channel_id=1, source_target_pairs={{0,1},{1,0},{2,3},{3,2},{4,5},{5,4},{6,7},{7,6},{8,9},{9,8},{10,11... | collective-permute-start | bytes 491528 | tf_op jit(solution)/shard_map/ppermute | solution.py:392
  22.1 13.5 %collective-permute-start.6 = (bf16[40,2048]{1,0:T(8,128)(2,1)S(1)}, bf16[40,2048]{1,0:T(8,128)(2,1)S(1)}, u32[]{:S(2)}, u32[]{:S(2)}) collective-permute-start(bf16[40,2048]{1,0:T(8,128)(2,1)S(1)} %get-tuple-element.44), channel_id=1, source_target_pairs={{0,2},{1,3},{2,0},{3,1},{4,6},{5,7},{6,4},{7,5},{8,10},{9,11},{10,... | collective-permute-start | bytes 491528 | tf_op jit(solution)/shard_map/ppermute | solution.py:392
  23.1 5.7 %collective-permute-start.8 = (bf16[40,512]{1,0:T(8,128)(2,1)S(1)}, bf16[40,512]{1,0:T(8,128)(2,1)S(1)}, u32[]{:S(2)}, u32[]{:S(2)}) collective-permute-start(bf16[40,512]{1,0:T(8,128)(2,1)S(1)} %get-tuple-element.46), channel_id=1, source_target_pairs={{0,4},{1,5},{2,6},{3,7},{4,0},{5,1},{6,2},{7,3},{8,12},{9,13},{10,... | collective-permute-start | bytes 122888 | tf_op jit(solution)/shard_map/ppermute | solution.py:392
  24.7 5.9 %collective-permute-start.9 = (bf16[40,512]{1,0:T(8,128)(2,1)S(1)}, bf16[40,512]{1,0:T(8,128)(2,1)S(1)}, u32[]{:S(2)}, u32[]{:S(2)}) collective-permute-start(bf16[40,512]{1,0:T(8,128)(2,1)S(1)} %get-tuple-element.47), channel_id=1, source_target_pairs={{0,5},{1,4},{2,7},{3,6},{4,1},{5,0},{6,3},{7,2},{8,13},{9,12},{10,... | collective-permute-start | bytes 122888 | tf_op jit(solution)/shard_map/ppermute | solution.py:392
  27.6 9.3 %copy-start.6 = (s32[1,128,2]{1,2,0:T(2,128)S(1)}, s32[1,128,2]{1,2,0:T(2,128)}, u32[]{:S(2)}) copy-start(s32[1,128,2]{1,2,0:T(2,128)} %param.9) | copy-start | bytes 3076
  27.6 9.3 %copy-start.7 = (s32[1,128,2]{1,2,0:T(2,128)S(1)}, s32[1,128,2]{1,2,0:T(2,128)}, u32[]{:S(2)}) copy-start(s32[1,128,2]{1,2,0:T(2,128)} %param.10) | copy-start | bytes 3076
  27.6 9.3 %copy-start.8 = (f32[16]{0:T(128)S(1)}, f32[16]{0:T(128)}, u32[]{:S(2)}) copy-start(f32[16]{0:T(128)} %table_ref.1) | copy-start | bytes 196
  27.6 4.2 %collective-permute-start.12 = (bf16[40,512]{1,0:T(8,128)(2,1)S(1)}, bf16[40,512]{1,0:T(8,128)(2,1)S(1)}, u32[]{:S(2)}, u32[]{:S(2)}) collective-permute-start(bf16[40,512]{1,0:T(8,128)(2,1)S(1)} %get-tuple-element.50), channel_id=1, source_target_pairs={{0,6},{1,7},{2,4},{3,5},{4,2},{5,3},{6,0},{7,1},{8,14},{9,15},{10,... | collective-permute-start | bytes 122888 | tf_op jit(solution)/shard_map/ppermute | solution.py:392
  28.8 4.3 %collective-permute-start.13 = (bf16[40,512]{1,0:T(8,128)(2,1)S(1)}, bf16[40,512]{1,0:T(8,128)(2,1)S(1)}, u32[]{:S(2)}, u32[]{:S(2)}) collective-permute-start(bf16[40,512]{1,0:T(8,128)(2,1)S(1)} %get-tuple-element.51), channel_id=1, source_target_pairs={{0,7},{1,6},{2,5},{3,4},{4,3},{5,2},{6,1},{7,0},{8,15},{9,14},{10,... | collective-permute-start | bytes 122888 | tf_op jit(solution)/shard_map/ppermute | solution.py:392
  30.6 7.2 %collective-permute-start.7 = (bf16[40,2048]{1,0:T(8,128)(2,1)S(1)}, bf16[40,2048]{1,0:T(8,128)(2,1)S(1)}, u32[]{:S(2)}, u32[]{:S(2)}) collective-permute-start(bf16[40,2048]{1,0:T(8,128)(2,1)S(1)} %get-tuple-element.45), channel_id=1, source_target_pairs={{0,3},{1,2},{2,1},{3,0},{4,7},{5,6},{6,5},{7,4},{8,11},{9,10},{10,... | collective-permute-start | bytes 491528 | tf_op jit(solution)/shard_map/ppermute | solution.py:392
  31.9 6.3 %collective-permute-start.14 = (bf16[40,1536]{1,0:T(8,128)(2,1)S(1)}, bf16[40,1536]{1,0:T(8,128)(2,1)S(1)}, u32[]{:S(2)}, u32[]{:S(2)}) collective-permute-start(bf16[40,1536]{1,0:T(8,128)(2,1)S(1)} %get-tuple-element.53), channel_id=1, source_target_pairs={{0,4},{1,5},{2,6},{3,7},{4,0},{5,1},{6,2},{7,3},{8,12},{9,13},{10,... | collective-permute-start | bytes 368648 | tf_op jit(solution)/shard_map/ppermute | solution.py:392
  33.2 11.7 %collective-permute-start.15 = (bf16[40,1536]{1,0:T(8,128)(2,1)S(1)}, bf16[40,1536]{1,0:T(8,128)(2,1)S(1)}, u32[]{:S(2)}, u32[]{:S(2)}) collective-permute-start(bf16[40,1536]{1,0:T(8,128)(2,1)S(1)} %get-tuple-element.54), channel_id=1, source_target_pairs={{0,5},{1,4},{2,7},{3,6},{4,1},{5,0},{6,3},{7,2},{8,13},{9,12},{10,... | collective-permute-start | bytes 368648 | tf_op jit(solution)/shard_map/ppermute | solution.py:392
  34.2 10.6 %collective-permute-start.16 = (bf16[40,1536]{1,0:T(8,128)(2,1)S(1)}, bf16[40,1536]{1,0:T(8,128)(2,1)S(1)}, u32[]{:S(2)}, u32[]{:S(2)}) collective-permute-start(bf16[40,1536]{1,0:T(8,128)(2,1)S(1)} %get-tuple-element.56), channel_id=1, source_target_pairs={{0,6},{1,7},{2,4},{3,5},{4,2},{5,3},{6,0},{7,1},{8,14},{9,15},{10,... | collective-permute-start | bytes 368648 | tf_op jit(solution)/shard_map/ppermute | solution.py:392
  35.6 9.3 %collective-permute-start.17 = (bf16[40,1536]{1,0:T(8,128)(2,1)S(1)}, bf16[40,1536]{1,0:T(8,128)(2,1)S(1)}, u32[]{:S(2)}, u32[]{:S(2)}) collective-permute-start(bf16[40,1536]{1,0:T(8,128)(2,1)S(1)} %get-tuple-element.57), channel_id=1, source_target_pairs={{0,7},{1,6},{2,5},{3,4},{4,3},{5,2},{6,1},{7,0},{8,15},{9,14},{10,... | collective-permute-start | bytes 368648 | tf_op jit(solution)/shard_map/ppermute | solution.py:392
  36.9 0.8 %copy-start.5 = (f32[2048]{0:T(1024)S(1)}, f32[2048]{0:T(1024)}, u32[]{:S(2)}) copy-start(f32[2048]{0:T(1024)} %param.15) | copy-start | bytes 24580
  45.6 15.0 %collective-permute-start.18 = (bf16[128,512]{1,0:T(8,128)(2,1)S(1)}, bf16[128,512]{1,0:T(8,128)(2,1)S(1)}, u32[]{:S(2)}, u32[]{:S(2)}) collective-permute-start(bf16[128,512]{1,0:T(8,128)(2,1)S(1)} %get-tuple-element.58), channel_id=1, source_target_pairs={{0,16},{8,24},{16,0},{24,8},{1,17},{9,25},{17,1},{25,9},{2,18},{10... | collective-permute-start | bytes 393224 | tf_op jit(solution)/shard_map/ppermute | solution.py:392
  45.7 14.9 %collective-permute-start.19 = (bf16[128,512]{1,0:T(8,128)(2,1)S(1)}, bf16[128,512]{1,0:T(8,128)(2,1)S(1)}, u32[]{:S(2)}, u32[]{:S(2)}) collective-permute-start(bf16[128,512]{1,0:T(8,128)(2,1)S(1)} %get-tuple-element.59), channel_id=1, source_target_pairs={{0,8},{8,0},{16,24},{24,16},{1,9},{9,1},{17,25},{25,17},{2,10},{10... | collective-permute-start | bytes 393224 | tf_op jit(solution)/shard_map/ppermute | solution.py:392
  47.0 13.6 %collective-permute-start.20 = (bf16[128,512]{1,0:T(8,128)(2,1)S(1)}, bf16[128,512]{1,0:T(8,128)(2,1)S(1)}, u32[]{:S(2)}, u32[]{:S(2)}) collective-permute-start(bf16[128,512]{1,0:T(8,128)(2,1)S(1)} %get-tuple-element.61), channel_id=1, source_target_pairs={{0,24},{8,16},{16,8},{24,0},{1,25},{9,17},{17,9},{25,1},{2,26},{10... | collective-permute-start | bytes 393224 | tf_op jit(solution)/shard_map/ppermute | solution.py:392
  48.3 12.3 %collective-permute-start.21 = (f32[8,128]{1,0:T(8,128)S(1)}, f32[8,128]{1,0:T(8,128)S(1)}, u32[]{:S(2)}, u32[]{:S(2)}) collective-permute-start(f32[8,128]{1,0:T(8,128)S(1)} %get-tuple-element.62), channel_id=1, source_target_pairs={{0,24},{8,16},{16,8},{24,0},{1,25},{9,17},{17,9},{25,1},{2,26},{10... | collective-permute-start | bytes 12296 | tf_op jit(solution)/shard_map/ppermute | solution.py:392

commit v4 on v3

--- a/solution.py
+++ b/solution.py
@@ -69,6 +69,9 @@
     normed = (widened * inv_rms * norm_gain[None, :]).astype(BF16)
     relaid = lax.all_to_all(normed, "dp", split_axis=1, concat_axis=0, tiled=True)
     return relaid[None]
+
+
+CLOSE, AWAY = [4, 2, 5, 3, 1], [6, 7]
 
 
 def vmem():
@@ -410,10 +413,9 @@
     ways = lax.axis_size("dp")
     capacity = 5 * tok // (2 * experts)
     chunk = feat_width // ways
-    along_y, along_x, own, away = [4, 5], [2, 3], [1, 0], [6, 7]
-    close = along_y + along_x + own
-    early = (ways - 1,)
-    late = tuple(range(ways - 2, -1, -1))
+    close, away = CLOSE + [0], AWAY
+    early = (ways // 2,)
+    late = tuple(k for k in range(ways - 1, -1, -1) if k not in early)
 
     route_rows = routes[0].T
     blocks = dispatch(
@@ -426,22 +428,16 @@
     select, weights = selector(route_rows, gate_code[0].T, gate_table, experts, capacity)
     matrices = w_gate[0].T, w_up[0].T, w_down[0]
 
-    plan = [(close.index(k), early) for k in along_y]
-    plan += [(close.index(k), early + late) for k in along_x + own]
-    plan += [(close.index(k), late) for k in along_y]
+    plan = [(j, early + late) for j in range(len(close))]
     _, *outputs = expert_call([near[k] for k in close], *matrices, plan, chunk)
-    y_early, x_whole, own_whole, y_late = outputs[:2], outputs[2:4], outputs[4:6], outputs[6:]
-    got_early = swap_each(dict(zip(along_y, y_early)), "expert")
-    whole = swap_each(dict(zip(along_x, x_whole)), "expert")
-    whole |= swap_each(dict(zip(own, own_whole)), "expert")
-    got_late = swap_each(dict(zip(along_y, y_late)), "expert")
+    back = swap_each(dict(zip(close, outputs)), "expert")
     gain_own = gain_of(norm_gain, (0,), chunk)
     plan = [(j, early) for j in range(len(away))]
     hidden, *away_early = expert_call([far[k] for k in away], *matrices, plan, chunk)
-    got_early |= whole | swap_each(dict(zip(away, away_early)), "expert")
+    got_early = back | swap_each(dict(zip(away, away_early)), "expert")
     plan = [(j, late) for j in range(len(away))]
     away_late = down_call(hidden, matrices[2], len(away), plan, chunk)
-    got_late |= whole | swap_each(dict(zip(away, away_late)), "expert")
+    got_late = back | swap_each(dict(zip(away, away_late)), "expert")
 
     order = range(experts)
     first, part = combine_early(

time: 61.7 us -> 62 us (level)
  the two profiles are of different devices: /device:TPU:17 before, /device:TPU:0 now
where the time goes in v4:
time: 62 us; the launch traced here: 61.7 us
  starting transfers between devices  25.4 us (41%)
  waiting for transfers between devices  21.1 us (34%)
  Pallas kernels  9.64 us (16%)
  local copies, waits for them, and re-layouts  5.47 us (9%)
    ppermute x20, starting transfers between devices, swap(): return lax.ppermute(value, axis, [(i, i ^ offset) for i in range(size)])  25.4 us
    ppermute x20, waiting for transfers between devices, swap(): return lax.ppermute(value, axis, [(i, i ^ offset) for i in range(size)])  21.1 us
    unnamed x18, local copies, waits for them, and re-layouts  5.47 us
    pallas_call x2, Pallas kernels, expert_call(): pl.pallas_call(functools.partial(expert_body, count, chunk, plan), out_sh...  4.75 us
    pallas_call x1, Pallas kernels, dispatch(): pl.pallas_call(functools.partial(dispatch_body, experts, capacity), out_s...  1.57 us
  transfers between devices with their start and end apart: 20, of which 5 were waited for; matrix products, arithmetic and copies ran while one was open for 0% of the time, Pallas kernels for 10%

profile of v4, /device:TPU:0, one launch (start us, length us, event | category | flops | bytes accessed | tf_op | source)
XLA Modules:
  0.0 61.7 jit_solution(26041694916719565)
XLA Ops:
  0.0 1.6 %dispatch.1 = (bf16[40,2048]{1,0:T(8,128)(2,1)S(1)}, bf16[40,2048]{1,0:T(8,128)(2,1)S(1)}, bf16[40,2048]{1,0:T(8,128)(2,1)S(1)}, bf16[40,2048]{1,0:T(8,128)(2,1)...) custom-call(s32[2,128]{1,0:T(2,128)} %bitcast.25, ...), custom_call_target="tpu_custom_call" | custom-call | flops 100000000 | bytes 2000000 | tf_op jit(solution)/shard_map/dispatch/pallas_call | solution.py:122
  1.6 3.1 %collective-permute-start = (bf16[40,2048]{1,0:T(8,128)(2,1)S(1)}, bf16[40,2048]{1,0:T(8,128)(2,1)S(1)}, u32[]{:S(2)}, u32[]{:S(2)}) collective-permute-start(bf16[40,2048]{1,0:T(8,128)(2,1)S(1)} %get-tuple-element.34), channel_id=1, source_target_pairs={{0,4},{1,5},{2,6},{3,7},{4,0},{5,1},{6,2},{7,3},{8,12},{9,13},{10,... | collective-permute-start | bytes 491528 | tf_op jit(solution)/shard_map/ppermute | solution.py:395
  4.6 1.5 %collective-permute-start.1 = (bf16[40,2048]{1,0:T(8,128)(2,1)S(1)}, bf16[40,2048]{1,0:T(8,128)(2,1)S(1)}, u32[]{:S(2)}, u32[]{:S(2)}) collective-permute-start(bf16[40,2048]{1,0:T(8,128)(2,1)S(1)} %get-tuple-element.35), channel_id=1, source_target_pairs={{0,2},{1,3},{2,0},{3,1},{4,6},{5,7},{6,4},{7,5},{8,10},{9,11},{10,... | collective-permute-start | bytes 491528 | tf_op jit(solution)/shard_map/ppermute | solution.py:395
  6.1 0.0 collective-permute-start.2
  6.1 0.3 collective-permute-start.3
  6.5 0.3 collective-permute-start.4
  6.8 2.3 %collective-permute-done.refs_0_ = bf16[40,2048]{1,0:T(8,128)(2,1)S(1)} collective-permute-done((bf16[40,2048]{1,0:T(8,128)(2,1)S(1)}, bf16[40,2048]{1,0:T(8,128)(2,1)S(1)}, u32[]{:S(2)}, u32[]{:S(2)}) %collective-permute-start) | collective-permute-done | bytes 163872 | tf_op jit(solution)/shard_map/ppermute | solution.py:395
  9.1 3.6 %collective-permute-start.10 = (bf16[40,2048]{1,0:T(8,128)(2,1)S(1)}, bf16[40,2048]{1,0:T(8,128)(2,1)S(1)}, u32[]{:S(2)}, u32[]{:S(2)}) collective-permute-start(bf16[40,2048]{1,0:T(8,128)(2,1)S(1)} %get-tuple-element.46), channel_id=1, source_target_pairs={{0,6},{1,7},{2,4},{3,5},{4,2},{5,3},{6,0},{7,1},{8,14},{9,15},{10,... | collective-permute-start | bytes 491528 | tf_op jit(solution)/shard_map/ppermute | solution.py:395
  12.6 0.0 collective-permute-done.1.refs_1_
  12.6 0.0 collective-permute-start.11
  12.6 0.0 collective-permute-done.2.refs_2_
  12.7 1.6 %collective-permute-done.3.refs_3_ = bf16[40,2048]{1,0:T(8,128)(2,1)S(1)} collective-permute-done((bf16[40,2048]{1,0:T(8,128)(2,1)S(1)}, bf16[40,2048]{1,0:T(8,128)(2,1)S(1)}, u32[]{:S(2)}, u32[]{:S(2)}) %collective-permute-start.3) | collective-permute-done | bytes 163872 | tf_op jit(solution)/shard_map/ppermute | solution.py:395
  14.2 0.0 collective-permute-done.4.refs_4_
  14.2 0.0 copy-start
  14.2 1.8 %copy-done = bf16[1,704,2048]{2,1,0:T(8,128)(2,1)S(1)} copy-done((bf16[1,704,2048]{2,1,0:T(8,128)(2,1)S(1)}, bf16[1,704,2048]{2,1,0:T(8,128)(2,1)}, u32[]{:S(2)}) %copy-start) | copy-done | bytes 2883608
  16.1 0.0 copy-start.2
  16.1 1.8 %copy-done.2 = bf16[1,2048,704]{1,2,0:T(8,128)(2,1)S(1)} copy-done((bf16[1,2048,704]{1,2,0:T(8,128)(2,1)S(1)}, bf16[1,2048,704]{1,2,0:T(8,128)(2,1)}, u32[]{:S(2)}) %copy-start.2) | copy-done | bytes 2883608
  17.9 0.0 copy-start.4
  17.9 1.8 %copy-done.4 = bf16[1,2048,704]{1,2,0:T(8,128)(2,1)S(1)} copy-done((bf16[1,2048,704]{1,2,0:T(8,128)(2,1)S(1)}, bf16[1,2048,704]{1,2,0:T(8,128)(2,1)}, u32[]{:S(2)}) %copy-start.4) | copy-done | bytes 2883608
  19.7 0.0 copy-start.1
  19.7 2.7 %shard_map.82 = (bf16[240,704]{1,0:T(8,128)(2,1)}, bf16[40,2048]{1,0:T(8,128)(2,1)S(1)}, bf16[40,2048]{1,0:T(8,128)(2,1)S(1)}, bf16[40,2048]{1,0:T(8,128)(2,1)S(...) custom-call(bf16[40,2048]{1,0:T(8,128)(2,1)S(1)} %collective-permute-done.refs_0_, ...), custom_call_target="tpu_custom_call" | custom-call | flops 1730150400 | bytes 8000000 | tf_op jit(solution)/shard_map/pallas_call | solution.py:213
  22.4 0.9 %collective-permute-start.5 = (bf16[40,2048]{1,0:T(8,128)(2,1)S(1)}, bf16[40,2048]{1,0:T(8,128)(2,1)S(1)}, u32[]{:S(2)}, u32[]{:S(2)}) collective-permute-start(bf16[40,2048]{1,0:T(8,128)(2,1)S(1)} %get-tuple-element.41), channel_id=1, source_target_pairs={{0,1},{1,0},{2,3},{3,2},{4,5},{5,4},{6,7},{7,6},{8,9},{9,8},{10,11... | collective-permute-start | bytes 491528 | tf_op jit(solution)/shard_map/ppermute | solution.py:395
  23.3 1.7 %collective-permute-start.6 = (bf16[40,2048]{1,0:T(8,128)(2,1)S(1)}, bf16[40,2048]{1,0:T(8,128)(2,1)S(1)}, u32[]{:S(2)}, u32[]{:S(2)}) collective-permute-start(bf16[40,2048]{1,0:T(8,128)(2,1)S(1)} %get-tuple-element.42), channel_id=1, source_target_pairs={{0,2},{1,3},{2,0},{3,1},{4,6},{5,7},{6,4},{7,5},{8,10},{9,11},{10,... | collective-permute-start | bytes 491528 | tf_op jit(solution)/shard_map/ppermute | solution.py:395
  25.0 0.0 collective-permute-done.10.refs_0_
  25.0 0.0 collective-permute-done.11.refs_1_
  25.0 0.0 copy-done.1
  25.0 0.0 copy-done.3
  25.0 2.0 %shard_map.83 = (bf16[80,704]{1,0:T(8,128)(2,1)S(1)}, bf16[40,512]{1,0:T(8,128)(2,1)S(1)}, bf16[40,512]{1,0:T(8,128)(2,1)S(1)}) custom-call(bf16[40,2048]{1,0:T(8,128)(2,1)S(1)} %collective-permute-done.10.refs_0_, bf16[40,2048]{1,0:T(8,128)(2,1)S(1)} %collective-permute-done.11.refs_1_, bf16[704,2048]{1,0:T(8,128)(2,1)S(1)} %bitcast.20, ...), custom_call_target="tpu_custom_call" | custom-call | flops 576716800 | bytes 8000000 | tf_op jit(solution)/shard_map/pallas_call | solution.py:213
  27.1 0.0 copy-start.6
  27.1 0.0 copy-start.7
  27.1 0.0 copy-start.8
  27.1 0.1 collective-permute-start.12
  27.2 2.0 %collective-permute-start.13 = (bf16[40,512]{1,0:T(8,128)(2,1)S(1)}, bf16[40,512]{1,0:T(8,128)(2,1)S(1)}, u32[]{:S(2)}, u32[]{:S(2)}) collective-permute-start(bf16[40,512]{1,0:T(8,128)(2,1)S(1)} %get-tuple-element.49), channel_id=1, source_target_pairs={{0,7},{1,6},{2,5},{3,4},{4,3},{5,2},{6,1},{7,0},{8,15},{9,14},{10,... | collective-permute-start | bytes 122888 | tf_op jit(solution)/shard_map/ppermute | solution.py:395
  29.1 1.0 %collective-permute-start.7 = (bf16[40,2048]{1,0:T(8,128)(2,1)S(1)}, bf16[40,2048]{1,0:T(8,128)(2,1)S(1)}, u32[]{:S(2)}, u32[]{:S(2)}) collective-permute-start(bf16[40,2048]{1,0:T(8,128)(2,1)S(1)} %get-tuple-element.43), channel_id=1, source_target_pairs={{0,3},{1,2},{2,1},{3,0},{4,7},{5,6},{6,5},{7,4},{8,11},{9,10},{10,... | collective-permute-start | bytes 491528 | tf_op jit(solution)/shard_map/ppermute | solution.py:395
  30.1 0.5 shard_map.85
  30.6 1.9 %collective-permute-done.12.refs_6_ = bf16[40,512]{1,0:T(8,128)(2,1)S(1)} collective-permute-done((bf16[40,512]{1,0:T(8,128)(2,1)S(1)}, bf16[40,512]{1,0:T(8,128)(2,1)S(1)}, u32[]{:S(2)}, u32[]{:S(2)}) %collective-permute-start.12) | collective-permute-done | bytes 40992 | tf_op jit(solution)/shard_map/ppermute | solution.py:395
  32.5 0.0 collective-permute-start.8
  32.5 0.0 collective-permute-done.13.refs_7_
  32.5 0.2 collective-permute-start.9
  32.7 0.0 collective-permute-done.5.refs_1_
  32.7 1.8 %collective-permute-start.14 = (bf16[40,1536]{1,0:T(8,128)(2,1)S(1)}, bf16[40,1536]{1,0:T(8,128)(2,1)S(1)}, u32[]{:S(2)}, u32[]{:S(2)}) collective-permute-start(bf16[40,1536]{1,0:T(8,128)(2,1)S(1)} %get-tuple-element.52), channel_id=1, source_target_pairs={{0,6},{1,7},{2,4},{3,5},{4,2},{5,3},{6,0},{7,1},{8,14},{9,15},{10,... | collective-permute-start | bytes 368648 | tf_op jit(solution)/shard_map/ppermute | solution.py:395
  34.5 0.0 collective-permute-done.6.refs_2_
  34.5 2.4 %collective-permute-start.15 = (bf16[40,1536]{1,0:T(8,128)(2,1)S(1)}, bf16[40,1536]{1,0:T(8,128)(2,1)S(1)}, u32[]{:S(2)}, u32[]{:S(2)}) collective-permute-start(bf16[40,1536]{1,0:T(8,128)(2,1)S(1)} %get-tuple-element.53), channel_id=1, source_target_pairs={{0,7},{1,6},{2,5},{3,4},{4,3},{5,2},{6,1},{7,0},{8,15},{9,14},{10,... | collective-permute-start | bytes 368648 | tf_op jit(solution)/shard_map/ppermute | solution.py:395
  36.9 0.0 copy-done.6
  36.9 0.0 copy-done.7
  36.9 0.0 copy-done.8
  36.9 0.8 %selector.1 = (bf16[256,320]{1,0:T(8,128)(2,1)S(1)}, f32[2,128,128]{2,1,0:T(8,128)S(1)}) custom-call(s32[2,128]{1,0:T(2,128)S(1)} %bitcast.26, s32[2,128]{1,0:T(2,128)S(1)} %bitcast.27, f32[16]{0:T(128)S(1)} %copy-done.8), custom_call_target="tpu_custom_call" | custom-call | flops 20000000000 | bytes 100000000 | tf_op jit(solution)/shard_map/selector/pallas_call | solution.py:159
  37.7 0.0 copy-done.5
  37.8 0.0 collective-permute-done.7.refs_3_
  37.8 6.5 %collective-permute-done.8.refs_4_ = bf16[40,2048]{1,0:T(8,128)(2,1)S(1)} collective-permute-done((bf16[40,2048]{1,0:T(8,128)(2,1)S(1)}, bf16[40,2048]{1,0:T(8,128)(2,1)S(1)}, u32[]{:S(2)}, u32[]{:S(2)}) %collective-permute-start.8) | collective-permute-done | bytes 163872 | tf_op jit(solution)/shard_map/ppermute | solution.py:395
  44.3 0.0 collective-permute-done.9.refs_5_
  44.3 0.3 combine_early.1
  44.6 0.0 collective-permute-done.14.refs_6_
  44.6 0.0 collective-permute-done.15.refs_7_
  44.6 0.8 %combine_late.1 = (bf16[128,512]{1,0:T(8,128)(2,1)S(1)}, bf16[128,512]{1,0:T(8,128)(2,1)S(1)}, bf16[128,512]{1,0:T(8,128)(2,1)S(1)}, f32[8,128]{1,0:T(8,128)S(1)}) custom-call(bf16[256,320]{1,0:T(8,128)(2,1)S(1)} %get-tuple-element.32.sel_ref, f32[2,128,128]{2,1,0:T(8,128)S(1)} %get-tuple-element.33.weight_ref, f32[128,128]{1,0:T(8,128)S(1)} %get-tuple-element.50.part_ref, ...), custom_call_target="tpu_custom_call" | custom-call | flops 251658240 | bytes 2000000 | tf_op jit(solution)/shard_map/combine_late/pallas_call | solution.py:315
  45.4 3.7 %collective-permute-start.16 = (bf16[128,512]{1,0:T(8,128)(2,1)S(1)}, bf16[128,512]{1,0:T(8,128)(2,1)S(1)}, u32[]{:S(2)}, u32[]{:S(2)}) collective-permute-start(bf16[128,512]{1,0:T(8,128)(2,1)S(1)} %get-tuple-element.54), channel_id=1, source_target_pairs={{0,24},{8,16},{16,8},{24,0},{1,25},{9,17},{17,9},{25,1},{2,26},{10... | collective-permute-start | bytes 393224 | tf_op jit(solution)/shard_map/ppermute | solution.py:395
  49.1 0.0 collective-permute-start.17
  49.1 0.8 %collective-permute-start.18 = (bf16[128,512]{1,0:T(8,128)(2,1)S(1)}, bf16[128,512]{1,0:T(8,128)(2,1)S(1)}, u32[]{:S(2)}, u32[]{:S(2)}) collective-permute-start(bf16[128,512]{1,0:T(8,128)(2,1)S(1)} %get-tuple-element.57), channel_id=1, source_target_pairs={{0,16},{8,24},{16,0},{24,8},{1,17},{9,25},{17,1},{25,9},{2,18},{10... | collective-permute-start | bytes 393224 | tf_op jit(solution)/shard_map/ppermute | solution.py:395
  49.9 2.1 %collective-permute-start.19 = (f32[8,128]{1,0:T(8,128)S(1)}, f32[8,128]{1,0:T(8,128)S(1)}, u32[]{:S(2)}, u32[]{:S(2)}) collective-permute-start(f32[8,128]{1,0:T(8,128)S(1)} %get-tuple-element.58), channel_id=1, source_target_pairs={{0,16},{8,24},{16,0},{24,8},{1,17},{9,25},{17,1},{25,9},{2,18},{10... | collective-permute-start | bytes 12296 | tf_op jit(solution)/shard_map/ppermute | solution.py:395
  52.0 8.8 %collective-permute-done.19.refs_4_ = f32[8,128]{1,0:T(8,128)S(1)} collective-permute-done((f32[8,128]{1,0:T(8,128)S(1)}, f32[8,128]{1,0:T(8,128)S(1)}, u32[]{:S(2)}, u32[]{:S(2)}) %collective-permute-start.19) | collective-permute-done | bytes 4128 | tf_op jit(solution)/shard_map/ppermute | solution.py:395
  60.9 0.0 collective-permute-done.16.refs_0_
  60.9 0.0 collective-permute-done.17.refs_1_
  60.9 0.0 collective-permute-done.18.refs_3_
  60.9 0.9 %finish.1 = bf16[512,512]{1,0:T(8,128)(2,1)} custom-call(bf16[128,512]{1,0:T(8,128)(2,1)S(1)} %collective-permute-done.16.refs_0_, bf16[128,512]{1,0:T(8,128)(2,1)S(1)} %collective-permute-done.17.refs_1_, bf16[128,512]{1,0:T(8,128)(2,1)S(1)} %get-tuple-element.56.refs_2_, bf16[128,512]{1,0:T(8,128)(2,1)S(1)} %collective-permute-done.18.refs_3_, ...), custom_call_target="tpu_custom_call" | custom-call | flops 1000000 | bytes 1000000 | tf_op jit(solution)/shard_map/finish/pallas_call | solution.py:378
  (4 shorter events, 0.0 us)
Async XLA Ops:
  1.6 7.5 %collective-permute-start = (bf16[40,2048]{1,0:T(8,128)(2,1)S(1)}, bf16[40,2048]{1,0:T(8,128)(2,1)S(1)}, u32[]{:S(2)}, u32[]{:S(2)}) collective-permute-start(bf16[40,2048]{1,0:T(8,128)(2,1)S(1)} %get-tuple-element.34), channel_id=1, source_target_pairs={{0,4},{1,5},{2,6},{3,7},{4,0},{5,1},{6,2},{7,3},{8,12},{9,13},{10,... | collective-permute-start | bytes 491528 | tf_op jit(solution)/shard_map/ppermute | solution.py:395
  4.6 8.0 %collective-permute-start.1 = (bf16[40,2048]{1,0:T(8,128)(2,1)S(1)}, bf16[40,2048]{1,0:T(8,128)(2,1)S(1)}, u32[]{:S(2)}, u32[]{:S(2)}) collective-permute-start(bf16[40,2048]{1,0:T(8,128)(2,1)S(1)} %get-tuple-element.35), channel_id=1, source_target_pairs={{0,2},{1,3},{2,0},{3,1},{4,6},{5,7},{6,4},{7,5},{8,10},{9,11},{10,... | collective-permute-start | bytes 491528 | tf_op jit(solution)/shard_map/ppermute | solution.py:395
  6.1 6.5 %collective-permute-start.2 = (bf16[40,2048]{1,0:T(8,128)(2,1)S(1)}, bf16[40,2048]{1,0:T(8,128)(2,1)S(1)}, u32[]{:S(2)}, u32[]{:S(2)}) collective-permute-start(bf16[40,2048]{1,0:T(8,128)(2,1)S(1)} %get-tuple-element.36), channel_id=1, source_target_pairs={{0,5},{1,4},{2,7},{3,6},{4,1},{5,0},{6,3},{7,2},{8,13},{9,12},{10,... | collective-permute-start | bytes 491528 | tf_op jit(solution)/shard_map/ppermute | solution.py:395
  6.1 8.1 %collective-permute-start.3 = (bf16[40,2048]{1,0:T(8,128)(2,1)S(1)}, bf16[40,2048]{1,0:T(8,128)(2,1)S(1)}, u32[]{:S(2)}, u32[]{:S(2)}) collective-permute-start(bf16[40,2048]{1,0:T(8,128)(2,1)S(1)} %get-tuple-element.37), channel_id=1, source_target_pairs={{0,3},{1,2},{2,1},{3,0},{4,7},{5,6},{6,5},{7,4},{8,11},{9,10},{10,... | collective-permute-start | bytes 491528 | tf_op jit(solution)/shard_map/ppermute | solution.py:395
  6.5 7.8 %collective-permute-start.4 = (bf16[40,2048]{1,0:T(8,128)(2,1)S(1)}, bf16[40,2048]{1,0:T(8,128)(2,1)S(1)}, u32[]{:S(2)}, u32[]{:S(2)}) collective-permute-start(bf16[40,2048]{1,0:T(8,128)(2,1)S(1)} %get-tuple-element.38), channel_id=1, source_target_pairs={{0,1},{1,0},{2,3},{3,2},{4,5},{5,4},{6,7},{7,6},{8,9},{9,8},{10,11... | collective-permute-start | bytes 491528 | tf_op jit(solution)/shard_map/ppermute | solution.py:395
  9.1 15.9 %collective-permute-start.10 = (bf16[40,2048]{1,0:T(8,128)(2,1)S(1)}, bf16[40,2048]{1,0:T(8,128)(2,1)S(1)}, u32[]{:S(2)}, u32[]{:S(2)}) collective-permute-start(bf16[40,2048]{1,0:T(8,128)(2,1)S(1)} %get-tuple-element.46), channel_id=1, source_target_pairs={{0,6},{1,7},{2,4},{3,5},{4,2},{5,3},{6,0},{7,1},{8,14},{9,15},{10,... | collective-permute-start | bytes 491528 | tf_op jit(solution)/shard_map/ppermute | solution.py:395
  12.6 12.4 %collective-permute-start.11 = (bf16[40,2048]{1,0:T(8,128)(2,1)S(1)}, bf16[40,2048]{1,0:T(8,128)(2,1)S(1)}, u32[]{:S(2)}, u32[]{:S(2)}) collective-permute-start(bf16[40,2048]{1,0:T(8,128)(2,1)S(1)} %get-tuple-element.47), channel_id=1, source_target_pairs={{0,7},{1,6},{2,5},{3,4},{4,3},{5,2},{6,1},{7,0},{8,15},{9,14},{10,... | collective-permute-start | bytes 491528 | tf_op jit(solution)/shard_map/ppermute | solution.py:395
  14.2 1.8 %copy-start = (bf16[1,704,2048]{2,1,0:T(8,128)(2,1)S(1)}, bf16[1,704,2048]{2,1,0:T(8,128)(2,1)}, u32[]{:S(2)}) copy-start(bf16[1,704,2048]{2,1,0:T(8,128)(2,1)} %param.14) | copy-start | bytes 8650756
  16.1 1.8 %copy-start.2 = (bf16[1,2048,704]{1,2,0:T(8,128)(2,1)S(1)}, bf16[1,2048,704]{1,2,0:T(8,128)(2,1)}, u32[]{:S(2)}) copy-start(bf16[1,2048,704]{1,2,0:T(8,128)(2,1)} %param.12) | copy-start | bytes 8650756
  17.9 1.8 %copy-start.4 = (bf16[1,2048,704]{1,2,0:T(8,128)(2,1)S(1)}, bf16[1,2048,704]{1,2,0:T(8,128)(2,1)}, u32[]{:S(2)}) copy-start(bf16[1,2048,704]{1,2,0:T(8,128)(2,1)} %param.13) | copy-start | bytes 8650756
  19.7 5.3 %copy-start.1 = (bf16[1,704,2048]{2,1,0:T(8,128)(2,1)S(1)}, bf16[1,704,2048]{2,1,0:T(8,128)(2,1)}, u32[]{:S(2)}) copy-start(bf16[1,704,2048]{2,1,0:T(8,128)(2,1)} %param.14) | copy-start | bytes 8650756
  19.7 5.3 %copy-start.3 = (bf16[1,2048,704]{1,2,0:T(8,128)(2,1)S(1)}, bf16[1,2048,704]{1,2,0:T(8,128)(2,1)}, u32[]{:S(2)}) copy-start(bf16[1,2048,704]{1,2,0:T(8,128)(2,1)} %param.12) | copy-start | bytes 8650756
  22.4 10.3 %collective-permute-start.5 = (bf16[40,2048]{1,0:T(8,128)(2,1)S(1)}, bf16[40,2048]{1,0:T(8,128)(2,1)S(1)}, u32[]{:S(2)}, u32[]{:S(2)}) collective-permute-start(bf16[40,2048]{1,0:T(8,128)(2,1)S(1)} %get-tuple-element.41), channel_id=1, source_target_pairs={{0,1},{1,0},{2,3},{3,2},{4,5},{5,4},{6,7},{7,6},{8,9},{9,8},{10,11... | collective-permute-start | bytes 491528 | tf_op jit(solution)/shard_map/ppermute | solution.py:395
  23.3 11.2 %collective-permute-start.6 = (bf16[40,2048]{1,0:T(8,128)(2,1)S(1)}, bf16[40,2048]{1,0:T(8,128)(2,1)S(1)}, u32[]{:S(2)}, u32[]{:S(2)}) collective-permute-start(bf16[40,2048]{1,0:T(8,128)(2,1)S(1)} %get-tuple-element.42), channel_id=1, source_target_pairs={{0,2},{1,3},{2,0},{3,1},{4,6},{5,7},{6,4},{7,5},{8,10},{9,11},{10,... | collective-permute-start | bytes 491528 | tf_op jit(solution)/shard_map/ppermute | solution.py:395
  27.1 9.8 %copy-start.6 = (s32[1,128,2]{1,2,0:T(2,128)S(1)}, s32[1,128,2]{1,2,0:T(2,128)}, u32[]{:S(2)}) copy-start(s32[1,128,2]{1,2,0:T(2,128)} %param.9) | copy-start | bytes 3076
  27.1 9.8 %copy-start.7 = (s32[1,128,2]{1,2,0:T(2,128)S(1)}, s32[1,128,2]{1,2,0:T(2,128)}, u32[]{:S(2)}) copy-start(s32[1,128,2]{1,2,0:T(2,128)} %param.10) | copy-start | bytes 3076
  27.1 9.8 %copy-start.8 = (f32[16]{0:T(128)S(1)}, f32[16]{0:T(128)}, u32[]{:S(2)}) copy-start(f32[16]{0:T(128)} %table_ref.1) | copy-start | bytes 196
  27.1 5.4 %collective-permute-start.12 = (bf16[40,512]{1,0:T(8,128)(2,1)S(1)}, bf16[40,512]{1,0:T(8,128)(2,1)S(1)}, u32[]{:S(2)}, u32[]{:S(2)}) collective-permute-start(bf16[40,512]{1,0:T(8,128)(2,1)S(1)} %get-tuple-element.48), channel_id=1, source_target_pairs={{0,6},{1,7},{2,4},{3,5},{4,2},{5,3},{6,0},{7,1},{8,14},{9,15},{10,... | collective-permute-start | bytes 122888 | tf_op jit(solution)/shard_map/ppermute | solution.py:395
  27.2 5.3 %collective-permute-start.13 = (bf16[40,512]{1,0:T(8,128)(2,1)S(1)}, bf16[40,512]{1,0:T(8,128)(2,1)S(1)}, u32[]{:S(2)}, u32[]{:S(2)}) collective-permute-start(bf16[40,512]{1,0:T(8,128)(2,1)S(1)} %get-tuple-element.49), channel_id=1, source_target_pairs={{0,7},{1,6},{2,5},{3,4},{4,3},{5,2},{6,1},{7,0},{8,15},{9,14},{10,... | collective-permute-start | bytes 122888 | tf_op jit(solution)/shard_map/ppermute | solution.py:395
  29.1 8.6 %collective-permute-start.7 = (bf16[40,2048]{1,0:T(8,128)(2,1)S(1)}, bf16[40,2048]{1,0:T(8,128)(2,1)S(1)}, u32[]{:S(2)}, u32[]{:S(2)}) collective-permute-start(bf16[40,2048]{1,0:T(8,128)(2,1)S(1)} %get-tuple-element.43), channel_id=1, source_target_pairs={{0,3},{1,2},{2,1},{3,0},{4,7},{5,6},{6,5},{7,4},{8,11},{9,10},{10,... | collective-permute-start | bytes 491528 | tf_op jit(solution)/shard_map/ppermute | solution.py:395
  32.5 11.8 %collective-permute-start.8 = (bf16[40,2048]{1,0:T(8,128)(2,1)S(1)}, bf16[40,2048]{1,0:T(8,128)(2,1)S(1)}, u32[]{:S(2)}, u32[]{:S(2)}) collective-permute-start(bf16[40,2048]{1,0:T(8,128)(2,1)S(1)} %get-tuple-element.44), channel_id=1, source_target_pairs={{0,4},{1,5},{2,6},{3,7},{4,0},{5,1},{6,2},{7,3},{8,12},{9,13},{10,... | collective-permute-start | bytes 491528 | tf_op jit(solution)/shard_map/ppermute | solution.py:395
  32.5 11.8 %collective-permute-start.9 = (bf16[40,2048]{1,0:T(8,128)(2,1)S(1)}, bf16[40,2048]{1,0:T(8,128)(2,1)S(1)}, u32[]{:S(2)}, u32[]{:S(2)}) collective-permute-start(bf16[40,2048]{1,0:T(8,128)(2,1)S(1)} %get-tuple-element.45), channel_id=1, source_target_pairs={{0,5},{1,4},{2,7},{3,6},{4,1},{5,0},{6,3},{7,2},{8,13},{9,12},{10,... | collective-permute-start | bytes 491528 | tf_op jit(solution)/shard_map/ppermute | solution.py:395
  32.7 11.9 %collective-permute-start.14 = (bf16[40,1536]{1,0:T(8,128)(2,1)S(1)}, bf16[40,1536]{1,0:T(8,128)(2,1)S(1)}, u32[]{:S(2)}, u32[]{:S(2)}) collective-permute-start(bf16[40,1536]{1,0:T(8,128)(2,1)S(1)} %get-tuple-element.52), channel_id=1, source_target_pairs={{0,6},{1,7},{2,4},{3,5},{4,2},{5,3},{6,0},{7,1},{8,14},{9,15},{10,... | collective-permute-start | bytes 368648 | tf_op jit(solution)/shard_map/ppermute | solution.py:395
  34.5 10.1 %collective-permute-start.15 = (bf16[40,1536]{1,0:T(8,128)(2,1)S(1)}, bf16[40,1536]{1,0:T(8,128)(2,1)S(1)}, u32[]{:S(2)}, u32[]{:S(2)}) collective-permute-start(bf16[40,1536]{1,0:T(8,128)(2,1)S(1)} %get-tuple-element.53), channel_id=1, source_target_pairs={{0,7},{1,6},{2,5},{3,4},{4,3},{5,2},{6,1},{7,0},{8,15},{9,14},{10,... | collective-permute-start | bytes 368648 | tf_op jit(solution)/shard_map/ppermute | solution.py:395
  36.9 0.8 %copy-start.5 = (f32[2048]{0:T(1024)S(1)}, f32[2048]{0:T(1024)}, u32[]{:S(2)}) copy-start(f32[2048]{0:T(1024)} %param.15) | copy-start | bytes 24580
  45.4 15.5 %collective-permute-start.16 = (bf16[128,512]{1,0:T(8,128)(2,1)S(1)}, bf16[128,512]{1,0:T(8,128)(2,1)S(1)}, u32[]{:S(2)}, u32[]{:S(2)}) collective-permute-start(bf16[128,512]{1,0:T(8,128)(2,1)S(1)} %get-tuple-element.54), channel_id=1, source_target_pairs={{0,24},{8,16},{16,8},{24,0},{1,25},{9,17},{17,9},{25,1},{2,26},{10... | collective-permute-start | bytes 393224 | tf_op jit(solution)/shard_map/ppermute | solution.py:395
  49.1 11.8 %collective-permute-start.17 = (bf16[128,512]{1,0:T(8,128)(2,1)S(1)}, bf16[128,512]{1,0:T(8,128)(2,1)S(1)}, u32[]{:S(2)}, u32[]{:S(2)}) collective-permute-start(bf16[128,512]{1,0:T(8,128)(2,1)S(1)} %get-tuple-element.55), channel_id=1, source_target_pairs={{0,8},{8,0},{16,24},{24,16},{1,9},{9,1},{17,25},{25,17},{2,10},{10... | collective-permute-start | bytes 393224 | tf_op jit(solution)/shard_map/ppermute | solution.py:395
  49.1 11.8 %collective-permute-start.18 = (bf16[128,512]{1,0:T(8,128)(2,1)S(1)}, bf16[128,512]{1,0:T(8,128)(2,1)S(1)}, u32[]{:S(2)}, u32[]{:S(2)}) collective-permute-start(bf16[128,512]{1,0:T(8,128)(2,1)S(1)} %get-tuple-element.57), channel_id=1, source_target_pairs={{0,16},{8,24},{16,0},{24,8},{1,17},{9,25},{17,1},{25,9},{2,18},{10... | collective-permute-start | bytes 393224 | tf_op jit(solution)/shard_map/ppermute | solution.py:395
  49.9 11.0 %collective-permute-start.19 = (f32[8,128]{1,0:T(8,128)S(1)}, f32[8,128]{1,0:T(8,128)S(1)}, u32[]{:S(2)}, u32[]{:S(2)}) collective-permute-start(f32[8,128]{1,0:T(8,128)S(1)} %get-tuple-element.58), channel_id=1, source_target_pairs={{0,16},{8,24},{16,0},{24,8},{1,17},{9,25},{17,1},{25,9},{2,18},{10... | collective-permute-start | bytes 12296 | tf_op jit(solution)/shard_map/ppermute | solution.py:395

commit v5 on v4

--- a/solution.py
+++ b/solution.py
@@ -414,8 +414,8 @@
     capacity = 5 * tok // (2 * experts)
     chunk = feat_width // ways
     close, away = CLOSE + [0], AWAY
-    early = (ways // 2,)
-    late = tuple(k for k in range(ways - 1, -1, -1) if k not in early)
+    early = (ways - 1,)
+    late = tuple(range(ways - 2, -1, -1))
 
     route_rows = routes[0].T
     blocks = dispatch(
@@ -471,7 +471,7 @@
         experts, ways = mesh.shape["expert"], mesh.shape["dp"]
         tok, feat = tokens.shape[1] // ways, tokens.shape[2]
         power = experts & (experts - 1) == 0 and ways & (ways - 1) == 0
-        fits = power and experts == 8 and 2 <= ways <= 4
+        fits = power and experts == 8 and ways == 4
         fits = fits and tok % 128 == 0 and w_gate.shape[0] == experts
         fits = fits and 5 * tok % (16 * experts) == 0 and feat % (256 * ways) == 0
         body = local_fast if fits else local_general

time: 62 us -> 61.2 us (0.987)
  the two profiles are of different devices: /device:TPU:0 before, /device:TPU:17 now
where the time goes in v5:
time: 61.2 us; the launch traced here: 61 us
  waiting for transfers between devices  25.6 us (42%)
  starting transfers between devices  20.1 us (33%)
  Pallas kernels  9.65 us (16%)
  local copies, waits for them, and re-layouts  5.47 us (9%)
    ppermute x20, waiting for transfers between devices, swap(): return lax.ppermute(value, axis, [(i, i ^ offset) for i in range(size)])  25.6 us
    ppermute x20, starting transfers between devices, swap(): return lax.ppermute(value, axis, [(i, i ^ offset) for i in range(size)])  20.1 us
    unnamed x18, local copies, waits for them, and re-layouts  5.47 us
    pallas_call x2, Pallas kernels, expert_call(): pl.pallas_call(functools.partial(expert_body, count, chunk, plan), out_sh...  4.74 us
    pallas_call x1, Pallas kernels, dispatch(): pl.pallas_call(functools.partial(dispatch_body, experts, capacity), out_s...  1.58 us
  transfers between devices with their start and end apart: 20, of which 5 were waited for; matrix products, arithmetic and copies ran while one was open for 0% of the time, Pallas kernels for 11%

profile of v5, /device:TPU:17, one launch (start us, length us, event | category | flops | bytes accessed | tf_op | source)
XLA Modules:
  0.0 61.0 jit_solution(9126057910653276528)
XLA Ops:
  0.0 1.6 %dispatch.1 = (bf16[40,2048]{1,0:T(8,128)(2,1)S(1)}, bf16[40,2048]{1,0:T(8,128)(2,1)S(1)}, bf16[40,2048]{1,0:T(8,128)(2,1)S(1)}, bf16[40,2048]{1,0:T(8,128)(2,1)...) custom-call(s32[2,128]{1,0:T(2,128)} %bitcast.25, ...), custom_call_target="tpu_custom_call" | custom-call | flops 100000000 | bytes 2000000 | tf_op jit(solution)/shard_map/dispatch/pallas_call | solution.py:122
  1.6 1.3 %collective-permute-start = (bf16[40,2048]{1,0:T(8,128)(2,1)S(1)}, bf16[40,2048]{1,0:T(8,128)(2,1)S(1)}, u32[]{:S(2)}, u32[]{:S(2)}) collective-permute-start(bf16[40,2048]{1,0:T(8,128)(2,1)S(1)} %get-tuple-element.34), channel_id=1, source_target_pairs={{0,4},{1,5},{2,6},{3,7},{4,0},{5,1},{6,2},{7,3},{8,12},{9,13},{10,... | collective-permute-start | bytes 491528 | tf_op jit(solution)/shard_map/ppermute | solution.py:395
  2.9 1.2 %collective-permute-start.1 = (bf16[40,2048]{1,0:T(8,128)(2,1)S(1)}, bf16[40,2048]{1,0:T(8,128)(2,1)S(1)}, u32[]{:S(2)}, u32[]{:S(2)}) collective-permute-start(bf16[40,2048]{1,0:T(8,128)(2,1)S(1)} %get-tuple-element.35), channel_id=1, source_target_pairs={{0,2},{1,3},{2,0},{3,1},{4,6},{5,7},{6,4},{7,5},{8,10},{9,11},{10,... | collective-permute-start | bytes 491528 | tf_op jit(solution)/shard_map/ppermute | solution.py:395
  4.1 1.3 %collective-permute-start.2 = (bf16[40,2048]{1,0:T(8,128)(2,1)S(1)}, bf16[40,2048]{1,0:T(8,128)(2,1)S(1)}, u32[]{:S(2)}, u32[]{:S(2)}) collective-permute-start(bf16[40,2048]{1,0:T(8,128)(2,1)S(1)} %get-tuple-element.36), channel_id=1, source_target_pairs={{0,5},{1,4},{2,7},{3,6},{4,1},{5,0},{6,3},{7,2},{8,13},{9,12},{10,... | collective-permute-start | bytes 491528 | tf_op jit(solution)/shard_map/ppermute | solution.py:395
  5.4 0.0 collective-permute-start.3
  5.5 0.6 %collective-permute-start.4 = (bf16[40,2048]{1,0:T(8,128)(2,1)S(1)}, bf16[40,2048]{1,0:T(8,128)(2,1)S(1)}, u32[]{:S(2)}, u32[]{:S(2)}) collective-permute-start(bf16[40,2048]{1,0:T(8,128)(2,1)S(1)} %get-tuple-element.38), channel_id=1, source_target_pairs={{0,1},{1,0},{2,3},{3,2},{4,5},{5,4},{6,7},{7,6},{8,9},{9,8},{10,11... | collective-permute-start | bytes 491528 | tf_op jit(solution)/shard_map/ppermute | solution.py:395
  6.1 0.6 %collective-permute-done.refs_0_ = bf16[40,2048]{1,0:T(8,128)(2,1)S(1)} collective-permute-done((bf16[40,2048]{1,0:T(8,128)(2,1)S(1)}, bf16[40,2048]{1,0:T(8,128)(2,1)S(1)}, u32[]{:S(2)}, u32[]{:S(2)}) %collective-permute-start) | collective-permute-done | bytes 163872 | tf_op jit(solution)/shard_map/ppermute | solution.py:395
  6.7 2.2 %collective-permute-start.10 = (bf16[40,2048]{1,0:T(8,128)(2,1)S(1)}, bf16[40,2048]{1,0:T(8,128)(2,1)S(1)}, u32[]{:S(2)}, u32[]{:S(2)}) collective-permute-start(bf16[40,2048]{1,0:T(8,128)(2,1)S(1)} %get-tuple-element.46), channel_id=1, source_target_pairs={{0,6},{1,7},{2,4},{3,5},{4,2},{5,3},{6,0},{7,1},{8,14},{9,15},{10,... | collective-permute-start | bytes 491528 | tf_op jit(solution)/shard_map/ppermute | solution.py:395
  8.9 0.0 collective-permute-done.1.refs_1_
  8.9 2.8 %collective-permute-start.11 = (bf16[40,2048]{1,0:T(8,128)(2,1)S(1)}, bf16[40,2048]{1,0:T(8,128)(2,1)S(1)}, u32[]{:S(2)}, u32[]{:S(2)}) collective-permute-start(bf16[40,2048]{1,0:T(8,128)(2,1)S(1)} %get-tuple-element.47), channel_id=1, source_target_pairs={{0,7},{1,6},{2,5},{3,4},{4,3},{5,2},{6,1},{7,0},{8,15},{9,14},{10,... | collective-permute-start | bytes 491528 | tf_op jit(solution)/shard_map/ppermute | solution.py:395
  11.7 0.0 collective-permute-done.2.refs_2_
  11.7 2.1 %collective-permute-done.3.refs_3_ = bf16[40,2048]{1,0:T(8,128)(2,1)S(1)} collective-permute-done((bf16[40,2048]{1,0:T(8,128)(2,1)S(1)}, bf16[40,2048]{1,0:T(8,128)(2,1)S(1)}, u32[]{:S(2)}, u32[]{:S(2)}) %collective-permute-start.3) | collective-permute-done | bytes 163872 | tf_op jit(solution)/shard_map/ppermute | solution.py:395
  13.8 0.0 collective-permute-done.4.refs_4_
  13.8 0.0 copy-start
  13.8 1.8 %copy-done = bf16[1,704,2048]{2,1,0:T(8,128)(2,1)S(1)} copy-done((bf16[1,704,2048]{2,1,0:T(8,128)(2,1)S(1)}, bf16[1,704,2048]{2,1,0:T(8,128)(2,1)}, u32[]{:S(2)}) %copy-start) | copy-done | bytes 2883608
  15.6 0.0 copy-start.2
  15.6 1.8 %copy-done.2 = bf16[1,2048,704]{1,2,0:T(8,128)(2,1)S(1)} copy-done((bf16[1,2048,704]{1,2,0:T(8,128)(2,1)S(1)}, bf16[1,2048,704]{1,2,0:T(8,128)(2,1)}, u32[]{:S(2)}) %copy-start.2) | copy-done | bytes 2883608
  17.4 0.0 copy-start.4
  17.4 1.8 %copy-done.4 = bf16[1,2048,704]{1,2,0:T(8,128)(2,1)S(1)} copy-done((bf16[1,2048,704]{1,2,0:T(8,128)(2,1)S(1)}, bf16[1,2048,704]{1,2,0:T(8,128)(2,1)}, u32[]{:S(2)}) %copy-start.4) | copy-done | bytes 2883608
  19.2 0.0 copy-start.1
  19.2 2.7 %shard_map.82 = (bf16[240,704]{1,0:T(8,128)(2,1)}, bf16[40,2048]{1,0:T(8,128)(2,1)S(1)}, bf16[40,2048]{1,0:T(8,128)(2,1)S(1)}, bf16[40,2048]{1,0:T(8,128)(2,1)S(...) custom-call(bf16[40,2048]{1,0:T(8,128)(2,1)S(1)} %collective-permute-done.refs_0_, ...), custom_call_target="tpu_custom_call" | custom-call | flops 1730150400 | bytes 8000000 | tf_op jit(solution)/shard_map/pallas_call | solution.py:213
  22.0 0.0 collective-permute-start.5
  22.0 1.5 %collective-permute-start.6 = (bf16[40,2048]{1,0:T(8,128)(2,1)S(1)}, bf16[40,2048]{1,0:T(8,128)(2,1)S(1)}, u32[]{:S(2)}, u32[]{:S(2)}) collective-permute-start(bf16[40,2048]{1,0:T(8,128)(2,1)S(1)} %get-tuple-element.42), channel_id=1, source_target_pairs={{0,2},{1,3},{2,0},{3,1},{4,6},{5,7},{6,4},{7,5},{8,10},{9,11},{10,... | collective-permute-start | bytes 491528 | tf_op jit(solution)/shard_map/ppermute | solution.py:395
  23.4 0.0 collective-permute-done.10.refs_0_
  23.4 0.0 collective-permute-done.11.refs_1_
  23.4 0.0 copy-done.1
  23.4 0.0 copy-done.3
  23.4 2.0 %shard_map.83 = (bf16[80,704]{1,0:T(8,128)(2,1)S(1)}, bf16[40,512]{1,0:T(8,128)(2,1)S(1)}, bf16[40,512]{1,0:T(8,128)(2,1)S(1)}) custom-call(bf16[40,2048]{1,0:T(8,128)(2,1)S(1)} %collective-permute-done.10.refs_0_, bf16[40,2048]{1,0:T(8,128)(2,1)S(1)} %collective-permute-done.11.refs_1_, bf16[704,2048]{1,0:T(8,128)(2,1)S(1)} %bitcast.20, ...), custom_call_target="tpu_custom_call" | custom-call | flops 576716800 | bytes 8000000 | tf_op jit(solution)/shard_map/pallas_call | solution.py:213
  25.5 0.0 copy-start.6
  25.5 0.0 copy-start.7
  25.5 0.0 copy-start.8
  25.5 0.1 collective-permute-start.12
  25.6 3.3 %collective-permute-start.13 = (bf16[40,512]{1,0:T(8,128)(2,1)S(1)}, bf16[40,512]{1,0:T(8,128)(2,1)S(1)}, u32[]{:S(2)}, u32[]{:S(2)}) collective-permute-start(bf16[40,512]{1,0:T(8,128)(2,1)S(1)} %get-tuple-element.49), channel_id=1, source_target_pairs={{0,7},{1,6},{2,5},{3,4},{4,3},{5,2},{6,1},{7,0},{8,15},{9,14},{10,... | collective-permute-start | bytes 122888 | tf_op jit(solution)/shard_map/ppermute | solution.py:395
  28.9 0.0 collective-permute-start.7
  28.9 0.5 shard_map.85
  29.4 0.0 collective-permute-done.12.refs_6_
  29.4 0.3 collective-permute-start.8
  29.8 2.1 %collective-permute-done.13.refs_7_ = bf16[40,512]{1,0:T(8,128)(2,1)S(1)} collective-permute-done((bf16[40,512]{1,0:T(8,128)(2,1)S(1)}, bf16[40,512]{1,0:T(8,128)(2,1)S(1)}, u32[]{:S(2)}, u32[]{:S(2)}) %collective-permute-start.13) | collective-permute-done | bytes 40992 | tf_op jit(solution)/shard_map/ppermute | solution.py:395
  31.9 1.4 %collective-permute-start.9 = (bf16[40,2048]{1,0:T(8,128)(2,1)S(1)}, bf16[40,2048]{1,0:T(8,128)(2,1)S(1)}, u32[]{:S(2)}, u32[]{:S(2)}) collective-permute-start(bf16[40,2048]{1,0:T(8,128)(2,1)S(1)} %get-tuple-element.45), channel_id=1, source_target_pairs={{0,5},{1,4},{2,7},{3,6},{4,1},{5,0},{6,3},{7,2},{8,13},{9,12},{10,... | collective-permute-start | bytes 491528 | tf_op jit(solution)/shard_map/ppermute | solution.py:395
  33.3 0.0 collective-permute-done.5.refs_1_
  33.3 0.1 collective-permute-start.14
  33.5 0.0 collective-permute-done.6.refs_2_
  33.5 1.0 %collective-permute-start.15 = (bf16[40,1536]{1,0:T(8,128)(2,1)S(1)}, bf16[40,1536]{1,0:T(8,128)(2,1)S(1)}, u32[]{:S(2)}, u32[]{:S(2)}) collective-permute-start(bf16[40,1536]{1,0:T(8,128)(2,1)S(1)} %get-tuple-element.53), channel_id=1, source_target_pairs={{0,7},{1,6},{2,5},{3,4},{4,3},{5,2},{6,1},{7,0},{8,15},{9,14},{10,... | collective-permute-start | bytes 368648 | tf_op jit(solution)/shard_map/ppermute | solution.py:395
  34.4 0.0 copy-done.6
  34.5 0.0 copy-done.7
  34.5 0.0 copy-done.8
  34.5 0.8 %selector.1 = (bf16[256,320]{1,0:T(8,128)(2,1)S(1)}, f32[2,128,128]{2,1,0:T(8,128)S(1)}) custom-call(s32[2,128]{1,0:T(2,128)S(1)} %bitcast.26, s32[2,128]{1,0:T(2,128)S(1)} %bitcast.27, f32[16]{0:T(128)S(1)} %copy-done.8), custom_call_target="tpu_custom_call" | custom-call | flops 20000000000 | bytes 100000000 | tf_op jit(solution)/shard_map/selector/pallas_call | solution.py:159
  35.3 0.0 copy-done.5
  35.3 0.0 collective-permute-done.7.refs_3_
  35.3 0.0 collective-permute-done.8.refs_4_
  35.3 9.2 %collective-permute-done.9.refs_5_ = bf16[40,2048]{1,0:T(8,128)(2,1)S(1)} collective-permute-done((bf16[40,2048]{1,0:T(8,128)(2,1)S(1)}, bf16[40,2048]{1,0:T(8,128)(2,1)S(1)}, u32[]{:S(2)}, u32[]{:S(2)}) %collective-permute-start.9) | collective-permute-done | bytes 163872 | tf_op jit(solution)/shard_map/ppermute | solution.py:395
  44.5 0.3 combine_early.1
  44.9 0.0 collective-permute-done.14.refs_6_
  44.9 0.0 collective-permute-done.15.refs_7_
  44.9 0.8 %combine_late.1 = (bf16[128,512]{1,0:T(8,128)(2,1)S(1)}, bf16[128,512]{1,0:T(8,128)(2,1)S(1)}, bf16[128,512]{1,0:T(8,128)(2,1)S(1)}, f32[8,128]{1,0:T(8,128)S(1)}) custom-call(bf16[256,320]{1,0:T(8,128)(2,1)S(1)} %get-tuple-element.32.sel_ref, f32[2,128,128]{2,1,0:T(8,128)S(1)} %get-tuple-element.33.weight_ref, f32[128,128]{1,0:T(8,128)S(1)} %get-tuple-element.50.part_ref, ...), custom_call_target="tpu_custom_call" | custom-call | flops 251658240 | bytes 2000000 | tf_op jit(solution)/shard_map/combine_late/pallas_call | solution.py:315
  45.7 0.1 collective-permute-start.16
  45.8 1.3 %collective-permute-start.17 = (bf16[128,512]{1,0:T(8,128)(2,1)S(1)}, bf16[128,512]{1,0:T(8,128)(2,1)S(1)}, u32[]{:S(2)}, u32[]{:S(2)}) collective-permute-start(bf16[128,512]{1,0:T(8,128)(2,1)S(1)} %get-tuple-element.55), channel_id=1, source_target_pairs={{0,8},{8,0},{16,24},{24,16},{1,9},{9,1},{17,25},{25,17},{2,10},{10... | collective-permute-start | bytes 393224 | tf_op jit(solution)/shard_map/ppermute | solution.py:395
  47.1 1.3 %collective-permute-start.18 = (bf16[128,512]{1,0:T(8,128)(2,1)S(1)}, bf16[128,512]{1,0:T(8,128)(2,1)S(1)}, u32[]{:S(2)}, u32[]{:S(2)}) collective-permute-start(bf16[128,512]{1,0:T(8,128)(2,1)S(1)} %get-tuple-element.57), channel_id=1, source_target_pairs={{0,24},{8,16},{16,8},{24,0},{1,25},{9,17},{17,9},{25,1},{2,26},{10... | collective-permute-start | bytes 393224 | tf_op jit(solution)/shard_map/ppermute | solution.py:395
  48.4 0.2 collective-permute-start.19
  48.6 11.5 %collective-permute-done.19.refs_4_ = f32[8,128]{1,0:T(8,128)S(1)} collective-permute-done((f32[8,128]{1,0:T(8,128)S(1)}, f32[8,128]{1,0:T(8,128)S(1)}, u32[]{:S(2)}, u32[]{:S(2)}) %collective-permute-start.19) | collective-permute-done | bytes 4128 | tf_op jit(solution)/shard_map/ppermute | solution.py:395
  60.1 0.0 collective-permute-done.16.refs_0_
  60.1 0.0 collective-permute-done.17.refs_1_
  60.1 0.0 collective-permute-done.18.refs_3_
  60.1 0.9 %finish.1 = bf16[512,512]{1,0:T(8,128)(2,1)} custom-call(bf16[128,512]{1,0:T(8,128)(2,1)S(1)} %collective-permute-done.16.refs_0_, bf16[128,512]{1,0:T(8,128)(2,1)S(1)} %collective-permute-done.17.refs_1_, bf16[128,512]{1,0:T(8,128)(2,1)S(1)} %get-tuple-element.56.refs_2_, bf16[128,512]{1,0:T(8,128)(2,1)S(1)} %collective-permute-done.18.refs_3_, ...), custom_call_target="tpu_custom_call" | custom-call | flops 1000000 | bytes 1000000 | tf_op jit(solution)/shard_map/finish/pallas_call | solution.py:378
  (4 shorter events, 0.0 us)
Async XLA Ops:
  1.6 5.1 %collective-permute-start = (bf16[40,2048]{1,0:T(8,128)(2,1)S(1)}, bf16[40,2048]{1,0:T(8,128)(2,1)S(1)}, u32[]{:S(2)}, u32[]{:S(2)}) collective-permute-start(bf16[40,2048]{1,0:T(8,128)(2,1)S(1)} %get-tuple-element.34), channel_id=1, source_target_pairs={{0,4},{1,5},{2,6},{3,7},{4,0},{5,1},{6,2},{7,3},{8,12},{9,13},{10,... | collective-permute-start | bytes 491528 | tf_op jit(solution)/shard_map/ppermute | solution.py:395
  2.9 6.0 %collective-permute-start.1 = (bf16[40,2048]{1,0:T(8,128)(2,1)S(1)}, bf16[40,2048]{1,0:T(8,128)(2,1)S(1)}, u32[]{:S(2)}, u32[]{:S(2)}) collective-permute-start(bf16[40,2048]{1,0:T(8,128)(2,1)S(1)} %get-tuple-element.35), channel_id=1, source_target_pairs={{0,2},{1,3},{2,0},{3,1},{4,6},{5,7},{6,4},{7,5},{8,10},{9,11},{10,... | collective-permute-start | bytes 491528 | tf_op jit(solution)/shard_map/ppermute | solution.py:395
  4.1 7.6 %collective-permute-start.2 = (bf16[40,2048]{1,0:T(8,128)(2,1)S(1)}, bf16[40,2048]{1,0:T(8,128)(2,1)S(1)}, u32[]{:S(2)}, u32[]{:S(2)}) collective-permute-start(bf16[40,2048]{1,0:T(8,128)(2,1)S(1)} %get-tuple-element.36), channel_id=1, source_target_pairs={{0,5},{1,4},{2,7},{3,6},{4,1},{5,0},{6,3},{7,2},{8,13},{9,12},{10,... | collective-permute-start | bytes 491528 | tf_op jit(solution)/shard_map/ppermute | solution.py:395
  5.4 8.3 %collective-permute-start.3 = (bf16[40,2048]{1,0:T(8,128)(2,1)S(1)}, bf16[40,2048]{1,0:T(8,128)(2,1)S(1)}, u32[]{:S(2)}, u32[]{:S(2)}) collective-permute-start(bf16[40,2048]{1,0:T(8,128)(2,1)S(1)} %get-tuple-element.37), channel_id=1, source_target_pairs={{0,3},{1,2},{2,1},{3,0},{4,7},{5,6},{6,5},{7,4},{8,11},{9,10},{10,... | collective-permute-start | bytes 491528 | tf_op jit(solution)/shard_map/ppermute | solution.py:395
  5.5 8.3 %collective-permute-start.4 = (bf16[40,2048]{1,0:T(8,128)(2,1)S(1)}, bf16[40,2048]{1,0:T(8,128)(2,1)S(1)}, u32[]{:S(2)}, u32[]{:S(2)}) collective-permute-start(bf16[40,2048]{1,0:T(8,128)(2,1)S(1)} %get-tuple-element.38), channel_id=1, source_target_pairs={{0,1},{1,0},{2,3},{3,2},{4,5},{5,4},{6,7},{7,6},{8,9},{9,8},{10,11... | collective-permute-start | bytes 491528 | tf_op jit(solution)/shard_map/ppermute | solution.py:395
  6.7 16.7 %collective-permute-start.10 = (bf16[40,2048]{1,0:T(8,128)(2,1)S(1)}, bf16[40,2048]{1,0:T(8,128)(2,1)S(1)}, u32[]{:S(2)}, u32[]{:S(2)}) collective-permute-start(bf16[40,2048]{1,0:T(8,128)(2,1)S(1)} %get-tuple-element.46), channel_id=1, source_target_pairs={{0,6},{1,7},{2,4},{3,5},{4,2},{5,3},{6,0},{7,1},{8,14},{9,15},{10,... | collective-permute-start | bytes 491528 | tf_op jit(solution)/shard_map/ppermute | solution.py:395
  8.9 14.5 %collective-permute-start.11 = (bf16[40,2048]{1,0:T(8,128)(2,1)S(1)}, bf16[40,2048]{1,0:T(8,128)(2,1)S(1)}, u32[]{:S(2)}, u32[]{:S(2)}) collective-permute-start(bf16[40,2048]{1,0:T(8,128)(2,1)S(1)} %get-tuple-element.47), channel_id=1, source_target_pairs={{0,7},{1,6},{2,5},{3,4},{4,3},{5,2},{6,1},{7,0},{8,15},{9,14},{10,... | collective-permute-start | bytes 491528 | tf_op jit(solution)/shard_map/ppermute | solution.py:395
  13.8 1.8 %copy-start = (bf16[1,704,2048]{2,1,0:T(8,128)(2,1)S(1)}, bf16[1,704,2048]{2,1,0:T(8,128)(2,1)}, u32[]{:S(2)}) copy-start(bf16[1,704,2048]{2,1,0:T(8,128)(2,1)} %param.14) | copy-start | bytes 8650756
  15.6 1.8 %copy-start.2 = (bf16[1,2048,704]{1,2,0:T(8,128)(2,1)S(1)}, bf16[1,2048,704]{1,2,0:T(8,128)(2,1)}, u32[]{:S(2)}) copy-start(bf16[1,2048,704]{1,2,0:T(8,128)(2,1)} %param.12) | copy-start | bytes 8650756
  17.4 1.8 %copy-start.4 = (bf16[1,2048,704]{1,2,0:T(8,128)(2,1)S(1)}, bf16[1,2048,704]{1,2,0:T(8,128)(2,1)}, u32[]{:S(2)}) copy-start(bf16[1,2048,704]{1,2,0:T(8,128)(2,1)} %param.13) | copy-start | bytes 8650756
  19.2 4.2 %copy-start.1 = (bf16[1,704,2048]{2,1,0:T(8,128)(2,1)S(1)}, bf16[1,704,2048]{2,1,0:T(8,128)(2,1)}, u32[]{:S(2)}) copy-start(bf16[1,704,2048]{2,1,0:T(8,128)(2,1)} %param.14) | copy-start | bytes 8650756
  19.2 4.2 %copy-start.3 = (bf16[1,2048,704]{1,2,0:T(8,128)(2,1)S(1)}, bf16[1,2048,704]{1,2,0:T(8,128)(2,1)}, u32[]{:S(2)}) copy-start(bf16[1,2048,704]{1,2,0:T(8,128)(2,1)} %param.12) | copy-start | bytes 8650756
  22.0 11.4 %collective-permute-start.5 = (bf16[40,2048]{1,0:T(8,128)(2,1)S(1)}, bf16[40,2048]{1,0:T(8,128)(2,1)S(1)}, u32[]{:S(2)}, u32[]{:S(2)}) collective-permute-start(bf16[40,2048]{1,0:T(8,128)(2,1)S(1)} %get-tuple-element.41), channel_id=1, source_target_pairs={{0,1},{1,0},{2,3},{3,2},{4,5},{5,4},{6,7},{7,6},{8,9},{9,8},{10,11... | collective-permute-start | bytes 491528 | tf_op jit(solution)/shard_map/ppermute | solution.py:395
  22.0 11.5 %collective-permute-start.6 = (bf16[40,2048]{1,0:T(8,128)(2,1)S(1)}, bf16[40,2048]{1,0:T(8,128)(2,1)S(1)}, u32[]{:S(2)}, u32[]{:S(2)}) collective-permute-start(bf16[40,2048]{1,0:T(8,128)(2,1)S(1)} %get-tuple-element.42), channel_id=1, source_target_pairs={{0,2},{1,3},{2,0},{3,1},{4,6},{5,7},{6,4},{7,5},{8,10},{9,11},{10,... | collective-permute-start | bytes 491528 | tf_op jit(solution)/shard_map/ppermute | solution.py:395
  25.5 9.0 %copy-start.6 = (s32[1,128,2]{1,2,0:T(2,128)S(1)}, s32[1,128,2]{1,2,0:T(2,128)}, u32[]{:S(2)}) copy-start(s32[1,128,2]{1,2,0:T(2,128)} %param.9) | copy-start | bytes 3076
  25.5 9.0 %copy-start.7 = (s32[1,128,2]{1,2,0:T(2,128)S(1)}, s32[1,128,2]{1,2,0:T(2,128)}, u32[]{:S(2)}) copy-start(s32[1,128,2]{1,2,0:T(2,128)} %param.10) | copy-start | bytes 3076
  25.5 8.9 %copy-start.8 = (f32[16]{0:T(128)S(1)}, f32[16]{0:T(128)}, u32[]{:S(2)}) copy-start(f32[16]{0:T(128)} %table_ref.1) | copy-start | bytes 196
  25.5 3.9 %collective-permute-start.12 = (bf16[40,512]{1,0:T(8,128)(2,1)S(1)}, bf16[40,512]{1,0:T(8,128)(2,1)S(1)}, u32[]{:S(2)}, u32[]{:S(2)}) collective-permute-start(bf16[40,512]{1,0:T(8,128)(2,1)S(1)} %get-tuple-element.48), channel_id=1, source_target_pairs={{0,6},{1,7},{2,4},{3,5},{4,2},{5,3},{6,0},{7,1},{8,14},{9,15},{10,... | collective-permute-start | bytes 122888 | tf_op jit(solution)/shard_map/ppermute | solution.py:395
  25.6 6.3 %collective-permute-start.13 = (bf16[40,512]{1,0:T(8,128)(2,1)S(1)}, bf16[40,512]{1,0:T(8,128)(2,1)S(1)}, u32[]{:S(2)}, u32[]{:S(2)}) collective-permute-start(bf16[40,512]{1,0:T(8,128)(2,1)S(1)} %get-tuple-element.49), channel_id=1, source_target_pairs={{0,7},{1,6},{2,5},{3,4},{4,3},{5,2},{6,1},{7,0},{8,15},{9,14},{10,... | collective-permute-start | bytes 122888 | tf_op jit(solution)/shard_map/ppermute | solution.py:395
  28.9 6.4 %collective-permute-start.7 = (bf16[40,2048]{1,0:T(8,128)(2,1)S(1)}, bf16[40,2048]{1,0:T(8,128)(2,1)S(1)}, u32[]{:S(2)}, u32[]{:S(2)}) collective-permute-start(bf16[40,2048]{1,0:T(8,128)(2,1)S(1)} %get-tuple-element.43), channel_id=1, source_target_pairs={{0,3},{1,2},{2,1},{3,0},{4,7},{5,6},{6,5},{7,4},{8,11},{9,10},{10,... | collective-permute-start | bytes 491528 | tf_op jit(solution)/shard_map/ppermute | solution.py:395
  29.4 5.9 %collective-permute-start.8 = (bf16[40,2048]{1,0:T(8,128)(2,1)S(1)}, bf16[40,2048]{1,0:T(8,128)(2,1)S(1)}, u32[]{:S(2)}, u32[]{:S(2)}) collective-permute-start(bf16[40,2048]{1,0:T(8,128)(2,1)S(1)} %get-tuple-element.44), channel_id=1, source_target_pairs={{0,4},{1,5},{2,6},{3,7},{4,0},{5,1},{6,2},{7,3},{8,12},{9,13},{10,... | collective-permute-start | bytes 491528 | tf_op jit(solution)/shard_map/ppermute | solution.py:395
  31.9 12.7 %collective-permute-start.9 = (bf16[40,2048]{1,0:T(8,128)(2,1)S(1)}, bf16[40,2048]{1,0:T(8,128)(2,1)S(1)}, u32[]{:S(2)}, u32[]{:S(2)}) collective-permute-start(bf16[40,2048]{1,0:T(8,128)(2,1)S(1)} %get-tuple-element.45), channel_id=1, source_target_pairs={{0,5},{1,4},{2,7},{3,6},{4,1},{5,0},{6,3},{7,2},{8,13},{9,12},{10,... | collective-permute-start | bytes 491528 | tf_op jit(solution)/shard_map/ppermute | solution.py:395
  33.3 11.5 %collective-permute-start.14 = (bf16[40,1536]{1,0:T(8,128)(2,1)S(1)}, bf16[40,1536]{1,0:T(8,128)(2,1)S(1)}, u32[]{:S(2)}, u32[]{:S(2)}) collective-permute-start(bf16[40,1536]{1,0:T(8,128)(2,1)S(1)} %get-tuple-element.52), channel_id=1, source_target_pairs={{0,6},{1,7},{2,4},{3,5},{4,2},{5,3},{6,0},{7,1},{8,14},{9,15},{10,... | collective-permute-start | bytes 368648 | tf_op jit(solution)/shard_map/ppermute | solution.py:395
  33.5 11.4 %collective-permute-start.15 = (bf16[40,1536]{1,0:T(8,128)(2,1)S(1)}, bf16[40,1536]{1,0:T(8,128)(2,1)S(1)}, u32[]{:S(2)}, u32[]{:S(2)}) collective-permute-start(bf16[40,1536]{1,0:T(8,128)(2,1)S(1)} %get-tuple-element.53), channel_id=1, source_target_pairs={{0,7},{1,6},{2,5},{3,4},{4,3},{5,2},{6,1},{7,0},{8,15},{9,14},{10,... | collective-permute-start | bytes 368648 | tf_op jit(solution)/shard_map/ppermute | solution.py:395
  34.5 0.8 %copy-start.5 = (f32[2048]{0:T(1024)S(1)}, f32[2048]{0:T(1024)}, u32[]{:S(2)}) copy-start(f32[2048]{0:T(1024)} %param.15) | copy-start | bytes 24580
  45.7 14.4 %collective-permute-start.16 = (bf16[128,512]{1,0:T(8,128)(2,1)S(1)}, bf16[128,512]{1,0:T(8,128)(2,1)S(1)}, u32[]{:S(2)}, u32[]{:S(2)}) collective-permute-start(bf16[128,512]{1,0:T(8,128)(2,1)S(1)} %get-tuple-element.54), channel_id=1, source_target_pairs={{0,16},{8,24},{16,0},{24,8},{1,17},{9,25},{17,1},{25,9},{2,18},{10... | collective-permute-start | bytes 393224 | tf_op jit(solution)/shard_map/ppermute | solution.py:395
  45.8 14.3 %collective-permute-start.17 = (bf16[128,512]{1,0:T(8,128)(2,1)S(1)}, bf16[128,512]{1,0:T(8,128)(2,1)S(1)}, u32[]{:S(2)}, u32[]{:S(2)}) collective-permute-start(bf16[128,512]{1,0:T(8,128)(2,1)S(1)} %get-tuple-element.55), channel_id=1, source_target_pairs={{0,8},{8,0},{16,24},{24,16},{1,9},{9,1},{17,25},{25,17},{2,10},{10... | collective-permute-start | bytes 393224 | tf_op jit(solution)/shard_map/ppermute | solution.py:395
  47.1 13.0 %collective-permute-start.18 = (bf16[128,512]{1,0:T(8,128)(2,1)S(1)}, bf16[128,512]{1,0:T(8,128)(2,1)S(1)}, u32[]{:S(2)}, u32[]{:S(2)}) collective-permute-start(bf16[128,512]{1,0:T(8,128)(2,1)S(1)} %get-tuple-element.57), channel_id=1, source_target_pairs={{0,24},{8,16},{16,8},{24,0},{1,25},{9,17},{17,9},{25,1},{2,26},{10... | collective-permute-start | bytes 393224 | tf_op jit(solution)/shard_map/ppermute | solution.py:395
  48.4 11.7 %collective-permute-start.19 = (f32[8,128]{1,0:T(8,128)S(1)}, f32[8,128]{1,0:T(8,128)S(1)}, u32[]{:S(2)}, u32[]{:S(2)}) collective-permute-start(f32[8,128]{1,0:T(8,128)S(1)} %get-tuple-element.58), channel_id=1, source_target_pairs={{0,24},{8,16},{16,8},{24,0},{1,25},{9,17},{17,9},{25,1},{2,26},{10... | collective-permute-start | bytes 12296 | tf_op jit(solution)/shard_map/ppermute | solution.py:395

commit v6 on v4

--- a/solution.py
+++ b/solution.py
@@ -71,7 +71,7 @@
     return relaid[None]
 
 
-CLOSE, AWAY = [4, 2, 5, 3, 1], [6, 7]
+OUT, BACK, AWAY = [2, 4, 3, 5, 1], [4, 2, 5, 3, 1], [6, 7]
 
 
 def vmem():
@@ -413,7 +413,7 @@
     ways = lax.axis_size("dp")
     capacity = 5 * tok // (2 * experts)
     chunk = feat_width // ways
-    close, away = CLOSE + [0], AWAY
+    close, away = BACK + [0], AWAY
     early = (ways // 2,)
     late = tuple(k for k in range(ways - 1, -1, -1) if k not in early)
 
@@ -423,7 +423,7 @@
         pltpu.with_memory_space_constraint(own_rows, pltpu.HBM),
         experts, capacity,
     )
-    near = swap_each({k: blocks[k] for k in close}, "expert")
+    near = swap_each({k: blocks[k] for k in OUT + [0]}, "expert")
     far = swap_each({k: blocks[k] for k in away}, "expert")
     select, weights = selector(route_rows, gate_code[0].T, gate_table, experts, capacity)
     matrices = w_gate[0].T, w_up[0].T, w_down[0]
@@ -471,7 +471,7 @@
         experts, ways = mesh.shape["expert"], mesh.shape["dp"]
         tok, feat = tokens.shape[1] // ways, tokens.shape[2]
         power = experts & (experts - 1) == 0 and ways & (ways - 1) == 0
-        fits = power and experts == 8 and 2 <= ways <= 4
+        fits = power and experts == 8 and ways == 4
         fits = fits and tok % 128 == 0 and w_gate.shape[0] == experts
         fits = fits and 5 * tok % (16 * experts) == 0 and feat % (256 * ways) == 0
         body = local_fast if fits else local_general

time: 62 us -> 62 us (level)
  no operation moved by 1% of the time
where the time goes in v6:
time: 62 us; the launch traced here: 61.7 us
  starting transfers between devices  25.4 us (41%)
  waiting for transfers between devices  21.1 us (34%)
  Pallas kernels  9.64 us (16%)
  local copies, waits for them, and re-layouts  5.47 us (9%)
    ppermute x20, starting transfers between devices, swap(): return lax.ppermute(value, axis, [(i, i ^ offset) for i in range(size)])  25.4 us
    ppermute x20, waiting for transfers between devices, swap(): return lax.ppermute(value, axis, [(i, i ^ offset) for i in range(size)])  21.1 us
    unnamed x18, local copies, waits for them, and re-layouts  5.47 us
    pallas_call x2, Pallas kernels, expert_call(): pl.pallas_call(functools.partial(expert_body, count, chunk, plan), out_sh...  4.75 us
    pallas_call x1, Pallas kernels, dispatch(): pl.pallas_call(functools.partial(dispatch_body, experts, capacity), out_s...  1.57 us
  transfers between devices with their start and end apart: 20, of which 5 were waited for; matrix products, arithmetic and copies ran while one was open for 0% of the time, Pallas kernels for 10%

profile of v6, /device:TPU:0, one launch (start us, length us, event | category | flops | bytes accessed | tf_op | source)
XLA Modules:
  0.0 61.7 jit_solution(26041694916719565)
XLA Ops:
  0.0 1.6 %dispatch.1 = (bf16[40,2048]{1,0:T(8,128)(2,1)S(1)}, bf16[40,2048]{1,0:T(8,128)(2,1)S(1)}, bf16[40,2048]{1,0:T(8,128)(2,1)S(1)}, bf16[40,2048]{1,0:T(8,128)(2,1)...) custom-call(s32[2,128]{1,0:T(2,128)} %bitcast.25, ...), custom_call_target="tpu_custom_call" | custom-call | flops 100000000 | bytes 2000000 | tf_op jit(solution)/shard_map/dispatch/pallas_call | solution.py:122
  1.6 3.1 %collective-permute-start = (bf16[40,2048]{1,0:T(8,128)(2,1)S(1)}, bf16[40,2048]{1,0:T(8,128)(2,1)S(1)}, u32[]{:S(2)}, u32[]{:S(2)}) collective-permute-start(bf16[40,2048]{1,0:T(8,128)(2,1)S(1)} %get-tuple-element.34), channel_id=1, source_target_pairs={{0,4},{1,5},{2,6},{3,7},{4,0},{5,1},{6,2},{7,3},{8,12},{9,13},{10,... | collective-permute-start | bytes 491528 | tf_op jit(solution)/shard_map/ppermute | solution.py:395
  4.6 1.5 %collective-permute-start.1 = (bf16[40,2048]{1,0:T(8,128)(2,1)S(1)}, bf16[40,2048]{1,0:T(8,128)(2,1)S(1)}, u32[]{:S(2)}, u32[]{:S(2)}) collective-permute-start(bf16[40,2048]{1,0:T(8,128)(2,1)S(1)} %get-tuple-element.35), channel_id=1, source_target_pairs={{0,2},{1,3},{2,0},{3,1},{4,6},{5,7},{6,4},{7,5},{8,10},{9,11},{10,... | collective-permute-start | bytes 491528 | tf_op jit(solution)/shard_map/ppermute | solution.py:395
  6.1 0.0 collective-permute-start.2
  6.1 0.3 collective-permute-start.3
  6.5 0.3 collective-permute-start.4
  6.8 2.3 %collective-permute-done.refs_0_ = bf16[40,2048]{1,0:T(8,128)(2,1)S(1)} collective-permute-done((bf16[40,2048]{1,0:T(8,128)(2,1)S(1)}, bf16[40,2048]{1,0:T(8,128)(2,1)S(1)}, u32[]{:S(2)}, u32[]{:S(2)}) %collective-permute-start) | collective-permute-done | bytes 163872 | tf_op jit(solution)/shard_map/ppermute | solution.py:395
  9.1 3.6 %collective-permute-start.10 = (bf16[40,2048]{1,0:T(8,128)(2,1)S(1)}, bf16[40,2048]{1,0:T(8,128)(2,1)S(1)}, u32[]{:S(2)}, u32[]{:S(2)}) collective-permute-start(bf16[40,2048]{1,0:T(8,128)(2,1)S(1)} %get-tuple-element.46), channel_id=1, source_target_pairs={{0,6},{1,7},{2,4},{3,5},{4,2},{5,3},{6,0},{7,1},{8,14},{9,15},{10,... | collective-permute-start | bytes 491528 | tf_op jit(solution)/shard_map/ppermute | solution.py:395
  12.6 0.0 collective-permute-done.1.refs_1_
  12.6 0.0 collective-permute-start.11
  12.6 0.0 collective-permute-done.2.refs_2_
  12.7 1.6 %collective-permute-done.3.refs_3_ = bf16[40,2048]{1,0:T(8,128)(2,1)S(1)} collective-permute-done((bf16[40,2048]{1,0:T(8,128)(2,1)S(1)}, bf16[40,2048]{1,0:T(8,128)(2,1)S(1)}, u32[]{:S(2)}, u32[]{:S(2)}) %collective-permute-start.3) | collective-permute-done | bytes 163872 | tf_op jit(solution)/shard_map/ppermute | solution.py:395
  14.2 0.0 collective-permute-done.4.refs_4_
  14.2 0.0 copy-start
  14.2 1.8 %copy-done = bf16[1,704,2048]{2,1,0:T(8,128)(2,1)S(1)} copy-done((bf16[1,704,2048]{2,1,0:T(8,128)(2,1)S(1)}, bf16[1,704,2048]{2,1,0:T(8,128)(2,1)}, u32[]{:S(2)}) %copy-start) | copy-done | bytes 2883608
  16.1 0.0 copy-start.2
  16.1 1.8 %copy-done.2 = bf16[1,2048,704]{1,2,0:T(8,128)(2,1)S(1)} copy-done((bf16[1,2048,704]{1,2,0:T(8,128)(2,1)S(1)}, bf16[1,2048,704]{1,2,0:T(8,128)(2,1)}, u32[]{:S(2)}) %copy-start.2) | copy-done | bytes 2883608
  17.9 0.0 copy-start.4
  17.9 1.8 %copy-done.4 = bf16[1,2048,704]{1,2,0:T(8,128)(2,1)S(1)} copy-done((bf16[1,2048,704]{1,2,0:T(8,128)(2,1)S(1)}, bf16[1,2048,704]{1,2,0:T(8,128)(2,1)}, u32[]{:S(2)}) %copy-start.4) | copy-done | bytes 2883608
  19.7 0.0 copy-start.1
  19.7 2.7 %shard_map.82 = (bf16[240,704]{1,0:T(8,128)(2,1)}, bf16[40,2048]{1,0:T(8,128)(2,1)S(1)}, bf16[40,2048]{1,0:T(8,128)(2,1)S(1)}, bf16[40,2048]{1,0:T(8,128)(2,1)S(...) custom-call(bf16[40,2048]{1,0:T(8,128)(2,1)S(1)} %collective-permute-done.refs_0_, ...), custom_call_target="tpu_custom_call" | custom-call | flops 1730150400 | bytes 8000000 | tf_op jit(solution)/shard_map/pallas_call | solution.py:213
  22.4 0.9 %collective-permute-start.5 = (bf16[40,2048]{1,0:T(8,128)(2,1)S(1)}, bf16[40,2048]{1,0:T(8,128)(2,1)S(1)}, u32[]{:S(2)}, u32[]{:S(2)}) collective-permute-start(bf16[40,2048]{1,0:T(8,128)(2,1)S(1)} %get-tuple-element.41), channel_id=1, source_target_pairs={{0,1},{1,0},{2,3},{3,2},{4,5},{5,4},{6,7},{7,6},{8,9},{9,8},{10,11... | collective-permute-start | bytes 491528 | tf_op jit(solution)/shard_map/ppermute | solution.py:395
  23.3 1.7 %collective-permute-start.6 = (bf16[40,2048]{1,0:T(8,128)(2,1)S(1)}, bf16[40,2048]{1,0:T(8,128)(2,1)S(1)}, u32[]{:S(2)}, u32[]{:S(2)}) collective-permute-start(bf16[40,2048]{1,0:T(8,128)(2,1)S(1)} %get-tuple-element.42), channel_id=1, source_target_pairs={{0,2},{1,3},{2,0},{3,1},{4,6},{5,7},{6,4},{7,5},{8,10},{9,11},{10,... | collective-permute-start | bytes 491528 | tf_op jit(solution)/shard_map/ppermute | solution.py:395
  25.0 0.0 collective-permute-done.10.refs_0_
  25.0 0.0 collective-permute-done.11.refs_1_
  25.0 0.0 copy-done.1
  25.0 0.0 copy-done.3
  25.0 2.0 %shard_map.83 = (bf16[80,704]{1,0:T(8,128)(2,1)S(1)}, bf16[40,512]{1,0:T(8,128)(2,1)S(1)}, bf16[40,512]{1,0:T(8,128)(2,1)S(1)}) custom-call(bf16[40,2048]{1,0:T(8,128)(2,1)S(1)} %collective-permute-done.10.refs_0_, bf16[40,2048]{1,0:T(8,128)(2,1)S(1)} %collective-permute-done.11.refs_1_, bf16[704,2048]{1,0:T(8,128)(2,1)S(1)} %bitcast.20, ...), custom_call_target="tpu_custom_call" | custom-call | flops 576716800 | bytes 8000000 | tf_op jit(solution)/shard_map/pallas_call | solution.py:213
  27.1 0.0 copy-start.6
  27.1 0.0 copy-start.7
  27.1 0.0 copy-start.8
  27.1 0.1 collective-permute-start.12
  27.2 2.0 %collective-permute-start.13 = (bf16[40,512]{1,0:T(8,128)(2,1)S(1)}, bf16[40,512]{1,0:T(8,128)(2,1)S(1)}, u32[]{:S(2)}, u32[]{:S(2)}) collective-permute-start(bf16[40,512]{1,0:T(8,128)(2,1)S(1)} %get-tuple-element.49), channel_id=1, source_target_pairs={{0,7},{1,6},{2,5},{3,4},{4,3},{5,2},{6,1},{7,0},{8,15},{9,14},{10,... | collective-permute-start | bytes 122888 | tf_op jit(solution)/shard_map/ppermute | solution.py:395
  29.1 1.0 %collective-permute-start.7 = (bf16[40,2048]{1,0:T(8,128)(2,1)S(1)}, bf16[40,2048]{1,0:T(8,128)(2,1)S(1)}, u32[]{:S(2)}, u32[]{:S(2)}) collective-permute-start(bf16[40,2048]{1,0:T(8,128)(2,1)S(1)} %get-tuple-element.43), channel_id=1, source_target_pairs={{0,3},{1,2},{2,1},{3,0},{4,7},{5,6},{6,5},{7,4},{8,11},{9,10},{10,... | collective-permute-start | bytes 491528 | tf_op jit(solution)/shard_map/ppermute | solution.py:395
  30.1 0.5 shard_map.85
  30.6 1.9 %collective-permute-done.12.refs_6_ = bf16[40,512]{1,0:T(8,128)(2,1)S(1)} collective-permute-done((bf16[40,512]{1,0:T(8,128)(2,1)S(1)}, bf16[40,512]{1,0:T(8,128)(2,1)S(1)}, u32[]{:S(2)}, u32[]{:S(2)}) %collective-permute-start.12) | collective-permute-done | bytes 40992 | tf_op jit(solution)/shard_map/ppermute | solution.py:395
  32.5 0.0 collective-permute-start.8
  32.5 0.0 collective-permute-done.13.refs_7_
  32.5 0.2 collective-permute-start.9
  32.7 0.0 collective-permute-done.5.refs_1_
  32.7 1.8 %collective-permute-start.14 = (bf16[40,1536]{1,0:T(8,128)(2,1)S(1)}, bf16[40,1536]{1,0:T(8,128)(2,1)S(1)}, u32[]{:S(2)}, u32[]{:S(2)}) collective-permute-start(bf16[40,1536]{1,0:T(8,128)(2,1)S(1)} %get-tuple-element.52), channel_id=1, source_target_pairs={{0,6},{1,7},{2,4},{3,5},{4,2},{5,3},{6,0},{7,1},{8,14},{9,15},{10,... | collective-permute-start | bytes 368648 | tf_op jit(solution)/shard_map/ppermute | solution.py:395
  34.5 0.0 collective-permute-done.6.refs_2_
  34.5 2.4 %collective-permute-start.15 = (bf16[40,1536]{1,0:T(8,128)(2,1)S(1)}, bf16[40,1536]{1,0:T(8,128)(2,1)S(1)}, u32[]{:S(2)}, u32[]{:S(2)}) collective-permute-start(bf16[40,1536]{1,0:T(8,128)(2,1)S(1)} %get-tuple-element.53), channel_id=1, source_target_pairs={{0,7},{1,6},{2,5},{3,4},{4,3},{5,2},{6,1},{7,0},{8,15},{9,14},{10,... | collective-permute-start | bytes 368648 | tf_op jit(solution)/shard_map/ppermute | solution.py:395
  36.9 0.0 copy-done.6
  36.9 0.0 copy-done.7
  36.9 0.0 copy-done.8
  36.9 0.8 %selector.1 = (bf16[256,320]{1,0:T(8,128)(2,1)S(1)}, f32[2,128,128]{2,1,0:T(8,128)S(1)}) custom-call(s32[2,128]{1,0:T(2,128)S(1)} %bitcast.26, s32[2,128]{1,0:T(2,128)S(1)} %bitcast.27, f32[16]{0:T(128)S(1)} %copy-done.8), custom_call_target="tpu_custom_call" | custom-call | flops 20000000000 | bytes 100000000 | tf_op jit(solution)/shard_map/selector/pallas_call | solution.py:159
  37.7 0.0 copy-done.5
  37.8 0.0 collective-permute-done.7.refs_3_
  37.8 6.5 %collective-permute-done.8.refs_4_ = bf16[40,2048]{1,0:T(8,128)(2,1)S(1)} collective-permute-done((bf16[40,2048]{1,0:T(8,128)(2,1)S(1)}, bf16[40,2048]{1,0:T(8,128)(2,1)S(1)}, u32[]{:S(2)}, u32[]{:S(2)}) %collective-permute-start.8) | collective-permute-done | bytes 163872 | tf_op jit(solution)/shard_map/ppermute | solution.py:395
  44.3 0.0 collective-permute-done.9.refs_5_
  44.3 0.3 combine_early.1
  44.6 0.0 collective-permute-done.14.refs_6_
  44.6 0.0 collective-permute-done.15.refs_7_
  44.6 0.8 %combine_late.1 = (bf16[128,512]{1,0:T(8,128)(2,1)S(1)}, bf16[128,512]{1,0:T(8,128)(2,1)S(1)}, bf16[128,512]{1,0:T(8,128)(2,1)S(1)}, f32[8,128]{1,0:T(8,128)S(1)}) custom-call(bf16[256,320]{1,0:T(8,128)(2,1)S(1)} %get-tuple-element.32.sel_ref, f32[2,128,128]{2,1,0:T(8,128)S(1)} %get-tuple-element.33.weight_ref, f32[128,128]{1,0:T(8,128)S(1)} %get-tuple-element.50.part_ref, ...), custom_call_target="tpu_custom_call" | custom-call | flops 251658240 | bytes 2000000 | tf_op jit(solution)/shard_map/combine_late/pallas_call | solution.py:315
  45.4 3.7 %collective-permute-start.16 = (bf16[128,512]{1,0:T(8,128)(2,1)S(1)}, bf16[128,512]{1,0:T(8,128)(2,1)S(1)}, u32[]{:S(2)}, u32[]{:S(2)}) collective-permute-start(bf16[128,512]{1,0:T(8,128)(2,1)S(1)} %get-tuple-element.54), channel_id=1, source_target_pairs={{0,24},{8,16},{16,8},{24,0},{1,25},{9,17},{17,9},{25,1},{2,26},{10... | collective-permute-start | bytes 393224 | tf_op jit(solution)/shard_map/ppermute | solution.py:395
  49.1 0.0 collective-permute-start.17
  49.1 0.8 %collective-permute-start.18 = (bf16[128,512]{1,0:T(8,128)(2,1)S(1)}, bf16[128,512]{1,0:T(8,128)(2,1)S(1)}, u32[]{:S(2)}, u32[]{:S(2)}) collective-permute-start(bf16[128,512]{1,0:T(8,128)(2,1)S(1)} %get-tuple-element.57), channel_id=1, source_target_pairs={{0,16},{8,24},{16,0},{24,8},{1,17},{9,25},{17,1},{25,9},{2,18},{10... | collective-permute-start | bytes 393224 | tf_op jit(solution)/shard_map/ppermute | solution.py:395
  49.9 2.1 %collective-permute-start.19 = (f32[8,128]{1,0:T(8,128)S(1)}, f32[8,128]{1,0:T(8,128)S(1)}, u32[]{:S(2)}, u32[]{:S(2)}) collective-permute-start(f32[8,128]{1,0:T(8,128)S(1)} %get-tuple-element.58), channel_id=1, source_target_pairs={{0,16},{8,24},{16,0},{24,8},{1,17},{9,25},{17,1},{25,9},{2,18},{10... | collective-permute-start | bytes 12296 | tf_op jit(solution)/shard_map/ppermute | solution.py:395
  52.0 8.8 %collective-permute-done.19.refs_4_ = f32[8,128]{1,0:T(8,128)S(1)} collective-permute-done((f32[8,128]{1,0:T(8,128)S(1)}, f32[8,128]{1,0:T(8,128)S(1)}, u32[]{:S(2)}, u32[]{:S(2)}) %collective-permute-start.19) | collective-permute-done | bytes 4128 | tf_op jit(solution)/shard_map/ppermute | solution.py:395
  60.9 0.0 collective-permute-done.16.refs_0_
  60.9 0.0 collective-permute-done.17.refs_1_
  60.9 0.0 collective-permute-done.18.refs_3_
  60.9 0.9 %finish.1 = bf16[512,512]{1,0:T(8,128)(2,1)} custom-call(bf16[128,512]{1,0:T(8,128)(2,1)S(1)} %collective-permute-done.16.refs_0_, bf16[128,512]{1,0:T(8,128)(2,1)S(1)} %collective-permute-done.17.refs_1_, bf16[128,512]{1,0:T(8,128)(2,1)S(1)} %get-tuple-element.56.refs_2_, bf16[128,512]{1,0:T(8,128)(2,1)S(1)} %collective-permute-done.18.refs_3_, ...), custom_call_target="tpu_custom_call" | custom-call | flops 1000000 | bytes 1000000 | tf_op jit(solution)/shard_map/finish/pallas_call | solution.py:378
  (4 shorter events, 0.0 us)
Async XLA Ops:
  1.6 7.5 %collective-permute-start = (bf16[40,2048]{1,0:T(8,128)(2,1)S(1)}, bf16[40,2048]{1,0:T(8,128)(2,1)S(1)}, u32[]{:S(2)}, u32[]{:S(2)}) collective-permute-start(bf16[40,2048]{1,0:T(8,128)(2,1)S(1)} %get-tuple-element.34), channel_id=1, source_target_pairs={{0,4},{1,5},{2,6},{3,7},{4,0},{5,1},{6,2},{7,3},{8,12},{9,13},{10,... | collective-permute-start | bytes 491528 | tf_op jit(solution)/shard_map/ppermute | solution.py:395
  4.6 8.0 %collective-permute-start.1 = (bf16[40,2048]{1,0:T(8,128)(2,1)S(1)}, bf16[40,2048]{1,0:T(8,128)(2,1)S(1)}, u32[]{:S(2)}, u32[]{:S(2)}) collective-permute-start(bf16[40,2048]{1,0:T(8,128)(2,1)S(1)} %get-tuple-element.35), channel_id=1, source_target_pairs={{0,2},{1,3},{2,0},{3,1},{4,6},{5,7},{6,4},{7,5},{8,10},{9,11},{10,... | collective-permute-start | bytes 491528 | tf_op jit(solution)/shard_map/ppermute | solution.py:395
  6.1 6.5 %collective-permute-start.2 = (bf16[40,2048]{1,0:T(8,128)(2,1)S(1)}, bf16[40,2048]{1,0:T(8,128)(2,1)S(1)}, u32[]{:S(2)}, u32[]{:S(2)}) collective-permute-start(bf16[40,2048]{1,0:T(8,128)(2,1)S(1)} %get-tuple-element.36), channel_id=1, source_target_pairs={{0,5},{1,4},{2,7},{3,6},{4,1},{5,0},{6,3},{7,2},{8,13},{9,12},{10,... | collective-permute-start | bytes 491528 | tf_op jit(solution)/shard_map/ppermute | solution.py:395
  6.1 8.1 %collective-permute-start.3 = (bf16[40,2048]{1,0:T(8,128)(2,1)S(1)}, bf16[40,2048]{1,0:T(8,128)(2,1)S(1)}, u32[]{:S(2)}, u32[]{:S(2)}) collective-permute-start(bf16[40,2048]{1,0:T(8,128)(2,1)S(1)} %get-tuple-element.37), channel_id=1, source_target_pairs={{0,3},{1,2},{2,1},{3,0},{4,7},{5,6},{6,5},{7,4},{8,11},{9,10},{10,... | collective-permute-start | bytes 491528 | tf_op jit(solution)/shard_map/ppermute | solution.py:395
  6.5 7.8 %collective-permute-start.4 = (bf16[40,2048]{1,0:T(8,128)(2,1)S(1)}, bf16[40,2048]{1,0:T(8,128)(2,1)S(1)}, u32[]{:S(2)}, u32[]{:S(2)}) collective-permute-start(bf16[40,2048]{1,0:T(8,128)(2,1)S(1)} %get-tuple-element.38), channel_id=1, source_target_pairs={{0,1},{1,0},{2,3},{3,2},{4,5},{5,4},{6,7},{7,6},{8,9},{9,8},{10,11... | collective-permute-start | bytes 491528 | tf_op jit(solution)/shard_map/ppermute | solution.py:395
  9.1 15.9 %collective-permute-start.10 = (bf16[40,2048]{1,0:T(8,128)(2,1)S(1)}, bf16[40,2048]{1,0:T(8,128)(2,1)S(1)}, u32[]{:S(2)}, u32[]{:S(2)}) collective-permute-start(bf16[40,2048]{1,0:T(8,128)(2,1)S(1)} %get-tuple-element.46), channel_id=1, source_target_pairs={{0,6},{1,7},{2,4},{3,5},{4,2},{5,3},{6,0},{7,1},{8,14},{9,15},{10,... | collective-permute-start | bytes 491528 | tf_op jit(solution)/shard_map/ppermute | solution.py:395
  12.6 12.4 %collective-permute-start.11 = (bf16[40,2048]{1,0:T(8,128)(2,1)S(1)}, bf16[40,2048]{1,0:T(8,128)(2,1)S(1)}, u32[]{:S(2)}, u32[]{:S(2)}) collective-permute-start(bf16[40,2048]{1,0:T(8,128)(2,1)S(1)} %get-tuple-element.47), channel_id=1, source_target_pairs={{0,7},{1,6},{2,5},{3,4},{4,3},{5,2},{6,1},{7,0},{8,15},{9,14},{10,... | collective-permute-start | bytes 491528 | tf_op jit(solution)/shard_map/ppermute | solution.py:395
  14.2 1.8 %copy-start = (bf16[1,704,2048]{2,1,0:T(8,128)(2,1)S(1)}, bf16[1,704,2048]{2,1,0:T(8,128)(2,1)}, u32[]{:S(2)}) copy-start(bf16[1,704,2048]{2,1,0:T(8,128)(2,1)} %param.14) | copy-start | bytes 8650756
  16.1 1.8 %copy-start.2 = (bf16[1,2048,704]{1,2,0:T(8,128)(2,1)S(1)}, bf16[1,2048,704]{1,2,0:T(8,128)(2,1)}, u32[]{:S(2)}) copy-start(bf16[1,2048,704]{1,2,0:T(8,128)(2,1)} %param.12) | copy-start | bytes 8650756
  17.9 1.8 %copy-start.4 = (bf16[1,2048,704]{1,2,0:T(8,128)(2,1)S(1)}, bf16[1,2048,704]{1,2,0:T(8,128)(2,1)}, u32[]{:S(2)}) copy-start(bf16[1,2048,704]{1,2,0:T(8,128)(2,1)} %param.13) | copy-start | bytes 8650756
  19.7 5.3 %copy-start.1 = (bf16[1,704,2048]{2,1,0:T(8,128)(2,1)S(1)}, bf16[1,704,2048]{2,1,0:T(8,128)(2,1)}, u32[]{:S(2)}) copy-start(bf16[1,704,2048]{2,1,0:T(8,128)(2,1)} %param.14) | copy-start | bytes 8650756
  19.7 5.3 %copy-start.3 = (bf16[1,2048,704]{1,2,0:T(8,128)(2,1)S(1)}, bf16[1,2048,704]{1,2,0:T(8,128)(2,1)}, u32[]{:S(2)}) copy-start(bf16[1,2048,704]{1,2,0:T(8,128)(2,1)} %param.12) | copy-start | bytes 8650756
  22.4 10.3 %collective-permute-start.5 = (bf16[40,2048]{1,0:T(8,128)(2,1)S(1)}, bf16[40,2048]{1,0:T(8,128)(2,1)S(1)}, u32[]{:S(2)}, u32[]{:S(2)}) collective-permute-start(bf16[40,2048]{1,0:T(8,128)(2,1)S(1)} %get-tuple-element.41), channel_id=1, source_target_pairs={{0,1},{1,0},{2,3},{3,2},{4,5},{5,4},{6,7},{7,6},{8,9},{9,8},{10,11... | collective-permute-start | bytes 491528 | tf_op jit(solution)/shard_map/ppermute | solution.py:395
  23.3 11.2 %collective-permute-start.6 = (bf16[40,2048]{1,0:T(8,128)(2,1)S(1)}, bf16[40,2048]{1,0:T(8,128)(2,1)S(1)}, u32[]{:S(2)}, u32[]{:S(2)}) collective-permute-start(bf16[40,2048]{1,0:T(8,128)(2,1)S(1)} %get-tuple-element.42), channel_id=1, source_target_pairs={{0,2},{1,3},{2,0},{3,1},{4,6},{5,7},{6,4},{7,5},{8,10},{9,11},{10,... | collective-permute-start | bytes 491528 | tf_op jit(solution)/shard_map/ppermute | solution.py:395
  27.1 9.8 %copy-start.6 = (s32[1,128,2]{1,2,0:T(2,128)S(1)}, s32[1,128,2]{1,2,0:T(2,128)}, u32[]{:S(2)}) copy-start(s32[1,128,2]{1,2,0:T(2,128)} %param.9) | copy-start | bytes 3076
  27.1 9.8 %copy-start.7 = (s32[1,128,2]{1,2,0:T(2,128)S(1)}, s32[1,128,2]{1,2,0:T(2,128)}, u32[]{:S(2)}) copy-start(s32[1,128,2]{1,2,0:T(2,128)} %param.10) | copy-start | bytes 3076
  27.1 9.8 %copy-start.8 = (f32[16]{0:T(128)S(1)}, f32[16]{0:T(128)}, u32[]{:S(2)}) copy-start(f32[16]{0:T(128)} %table_ref.1) | copy-start | bytes 196
  27.1 5.4 %collective-permute-start.12 = (bf16[40,512]{1,0:T(8,128)(2,1)S(1)}, bf16[40,512]{1,0:T(8,128)(2,1)S(1)}, u32[]{:S(2)}, u32[]{:S(2)}) collective-permute-start(bf16[40,512]{1,0:T(8,128)(2,1)S(1)} %get-tuple-element.48), channel_id=1, source_target_pairs={{0,6},{1,7},{2,4},{3,5},{4,2},{5,3},{6,0},{7,1},{8,14},{9,15},{10,... | collective-permute-start | bytes 122888 | tf_op jit(solution)/shard_map/ppermute | solution.py:395
  27.2 5.3 %collective-permute-start.13 = (bf16[40,512]{1,0:T(8,128)(2,1)S(1)}, bf16[40,512]{1,0:T(8,128)(2,1)S(1)}, u32[]{:S(2)}, u32[]{:S(2)}) collective-permute-start(bf16[40,512]{1,0:T(8,128)(2,1)S(1)} %get-tuple-element.49), channel_id=1, source_target_pairs={{0,7},{1,6},{2,5},{3,4},{4,3},{5,2},{6,1},{7,0},{8,15},{9,14},{10,... | collective-permute-start | bytes 122888 | tf_op jit(solution)/shard_map/ppermute | solution.py:395
  29.1 8.6 %collective-permute-start.7 = (bf16[40,2048]{1,0:T(8,128)(2,1)S(1)}, bf16[40,2048]{1,0:T(8,128)(2,1)S(1)}, u32[]{:S(2)}, u32[]{:S(2)}) collective-permute-start(bf16[40,2048]{1,0:T(8,128)(2,1)S(1)} %get-tuple-element.43), channel_id=1, source_target_pairs={{0,3},{1,2},{2,1},{3,0},{4,7},{5,6},{6,5},{7,4},{8,11},{9,10},{10,... | collective-permute-start | bytes 491528 | tf_op jit(solution)/shard_map/ppermute | solution.py:395
  32.5 11.8 %collective-permute-start.8 = (bf16[40,2048]{1,0:T(8,128)(2,1)S(1)}, bf16[40,2048]{1,0:T(8,128)(2,1)S(1)}, u32[]{:S(2)}, u32[]{:S(2)}) collective-permute-start(bf16[40,2048]{1,0:T(8,128)(2,1)S(1)} %get-tuple-element.44), channel_id=1, source_target_pairs={{0,4},{1,5},{2,6},{3,7},{4,0},{5,1},{6,2},{7,3},{8,12},{9,13},{10,... | collective-permute-start | bytes 491528 | tf_op jit(solution)/shard_map/ppermute | solution.py:395
  32.5 11.8 %collective-permute-start.9 = (bf16[40,2048]{1,0:T(8,128)(2,1)S(1)}, bf16[40,2048]{1,0:T(8,128)(2,1)S(1)}, u32[]{:S(2)}, u32[]{:S(2)}) collective-permute-start(bf16[40,2048]{1,0:T(8,128)(2,1)S(1)} %get-tuple-element.45), channel_id=1, source_target_pairs={{0,5},{1,4},{2,7},{3,6},{4,1},{5,0},{6,3},{7,2},{8,13},{9,12},{10,... | collective-permute-start | bytes 491528 | tf_op jit(solution)/shard_map/ppermute | solution.py:395
  32.7 11.9 %collective-permute-start.14 = (bf16[40,1536]{1,0:T(8,128)(2,1)S(1)}, bf16[40,1536]{1,0:T(8,128)(2,1)S(1)}, u32[]{:S(2)}, u32[]{:S(2)}) collective-permute-start(bf16[40,1536]{1,0:T(8,128)(2,1)S(1)} %get-tuple-element.52), channel_id=1, source_target_pairs={{0,6},{1,7},{2,4},{3,5},{4,2},{5,3},{6,0},{7,1},{8,14},{9,15},{10,... | collective-permute-start | bytes 368648 | tf_op jit(solution)/shard_map/ppermute | solution.py:395
  34.5 10.1 %collective-permute-start.15 = (bf16[40,1536]{1,0:T(8,128)(2,1)S(1)}, bf16[40,1536]{1,0:T(8,128)(2,1)S(1)}, u32[]{:S(2)}, u32[]{:S(2)}) collective-permute-start(bf16[40,1536]{1,0:T(8,128)(2,1)S(1)} %get-tuple-element.53), channel_id=1, source_target_pairs={{0,7},{1,6},{2,5},{3,4},{4,3},{5,2},{6,1},{7,0},{8,15},{9,14},{10,... | collective-permute-start | bytes 368648 | tf_op jit(solution)/shard_map/ppermute | solution.py:395
  36.9 0.8 %copy-start.5 = (f32[2048]{0:T(1024)S(1)}, f32[2048]{0:T(1024)}, u32[]{:S(2)}) copy-start(f32[2048]{0:T(1024)} %param.15) | copy-start | bytes 24580
  45.4 15.5 %collective-permute-start.16 = (bf16[128,512]{1,0:T(8,128)(2,1)S(1)}, bf16[128,512]{1,0:T(8,128)(2,1)S(1)}, u32[]{:S(2)}, u32[]{:S(2)}) collective-permute-start(bf16[128,512]{1,0:T(8,128)(2,1)S(1)} %get-tuple-element.54), channel_id=1, source_target_pairs={{0,24},{8,16},{16,8},{24,0},{1,25},{9,17},{17,9},{25,1},{2,26},{10... | collective-permute-start | bytes 393224 | tf_op jit(solution)/shard_map/ppermute | solution.py:395
  49.1 11.8 %collective-permute-start.17 = (bf16[128,512]{1,0:T(8,128)(2,1)S(1)}, bf16[128,512]{1,0:T(8,128)(2,1)S(1)}, u32[]{:S(2)}, u32[]{:S(2)}) collective-permute-start(bf16[128,512]{1,0:T(8,128)(2,1)S(1)} %get-tuple-element.55), channel_id=1, source_target_pairs={{0,8},{8,0},{16,24},{24,16},{1,9},{9,1},{17,25},{25,17},{2,10},{10... | collective-permute-start | bytes 393224 | tf_op jit(solution)/shard_map/ppermute | solution.py:395
  49.1 11.8 %collective-permute-start.18 = (bf16[128,512]{1,0:T(8,128)(2,1)S(1)}, bf16[128,512]{1,0:T(8,128)(2,1)S(1)}, u32[]{:S(2)}, u32[]{:S(2)}) collective-permute-start(bf16[128,512]{1,0:T(8,128)(2,1)S(1)} %get-tuple-element.57), channel_id=1, source_target_pairs={{0,16},{8,24},{16,0},{24,8},{1,17},{9,25},{17,1},{25,9},{2,18},{10... | collective-permute-start | bytes 393224 | tf_op jit(solution)/shard_map/ppermute | solution.py:395
  49.9 11.0 %collective-permute-start.19 = (f32[8,128]{1,0:T(8,128)S(1)}, f32[8,128]{1,0:T(8,128)S(1)}, u32[]{:S(2)}, u32[]{:S(2)}) collective-permute-start(f32[8,128]{1,0:T(8,128)S(1)} %get-tuple-element.58), channel_id=1, source_target_pairs={{0,16},{8,24},{16,0},{24,8},{1,17},{9,25},{17,1},{25,9},{2,18},{10... | collective-permute-start | bytes 12296 | tf_op jit(solution)/shard_map/ppermute | solution.py:395

commit v7 on v4

--- a/solution.py
+++ b/solution.py
@@ -94,27 +94,31 @@
 
 def dispatch_body(experts, capacity, route_hbm, tok_hbm, *refs):
     *out_refs, route_ref, tok_ref, sems = refs
-    copies = [
-        pltpu.make_async_copy(route_hbm, route_ref, sems.at[0]),
-        pltpu.make_async_copy(tok_hbm, tok_ref, sems.at[1]),
-    ]
-    for copy in copies:
-        copy.start()
+    tok, width = tok_ref.shape
+    pieces = sems.shape[0] - 1
+    step = width // pieces
+    route_copy = pltpu.make_async_copy(route_hbm, route_ref, sems.at[pieces])
+    route_copy.start()
+    copies = []
+    for p in range(pieces):
+        cols = pl.ds(p * step, step)
+        copies.append(pltpu.make_async_copy(tok_hbm.at[:, cols], tok_ref.at[:, cols], sems.at[p]))
+        copies[-1].start()
     me = lax.axis_index("expert")
-    tok, width = tok_ref.shape
     lane = lax.broadcasted_iota(jnp.int32, (capacity, tok), 0)
-    copies[0].wait()
+    route_copy.wait()
     slots, _ = slot_rows(route_ref[...], experts, me)
     pick = jnp.concatenate(
         [(lane == slots[j : j + 1, :]).astype(F32) for j in range(experts)], axis=0
     ).astype(BF16)
-    copies[1].wait()
     tile = 256
-    for col in range(0, width, tile):
-        rows = jnp.dot(pick, tok_ref[:, col : col + tile], preferred_element_type=F32)
-        rows = rows.astype(BF16)
-        for j in range(experts):
-            out_refs[j][:, col : col + tile] = rows[j * capacity : (j + 1) * capacity, :]
+    for p, copy in enumerate(copies):
+        copy.wait()
+        for col in range(p * step, (p + 1) * step, tile):
+            rows = jnp.dot(pick, tok_ref[:, col : col + tile], preferred_element_type=F32)
+            rows = rows.astype(BF16)
+            for j in range(experts):
+                out_refs[j][:, col : col + tile] = rows[j * capacity : (j + 1) * capacity, :]
 
 
 def dispatch(route_rows, own_rows, experts, capacity):
@@ -127,7 +131,7 @@
         scratch_shapes=[
             pltpu.VMEM(route_rows.shape, jnp.int32),
             pltpu.VMEM(own_rows.shape, BF16),
-            pltpu.SemaphoreType.DMA((2,)),
+            pltpu.SemaphoreType.DMA((5,)),
         ],
         name="dispatch",
         cost_estimate=pl.CostEstimate(flops=10**8, transcendentals=0, bytes_accessed=2 * 10**6),
@@ -135,7 +139,8 @@
     )(route_rows, own_rows)
 
 
-def selector_body(experts, capacity, route_ref, code_ref, table_ref, sel_ref, weight_ref):
+def selector_body(experts, capacity, route_ref, code_ref, table_ref, *refs):
+    sel_ref, close_ref, away_ref, weight_ref = refs
     me = lax.axis_index("expert")
     rows = route_ref[...]
     slots, ids = slot_rows(rows, experts, me)
@@ -146,7 +151,11 @@
         pick = jnp.concatenate(
             [(lane == mine[j : j + 1, :]).astype(F32) for j in range(experts)], axis=0
         )
-        sel_ref[r * tok : (r + 1) * tok, :] = pick.T.astype(BF16)
+        held = slice(r * tok, (r + 1) * tok)
+        split = close_ref.shape[1]
+        sel_ref[held, :] = pick.T.astype(BF16)
+        close_ref[held, :] = pick[:split].T.astype(BF16)
+        away_ref[held, :] = pick[split:].T.astype(BF16)
         codes = code_ref[r : r + 1, :]
         weights = jnp.zeros((1, tok), F32)
         for level in range(table_ref.shape[0]):
@@ -156,14 +165,15 @@
 
 def selector(route_rows, code_rows, gate_table, experts, capacity):
     tok = route_rows.shape[1]
+    counts = (experts, experts - len(AWAY), len(AWAY))
     return pl.pallas_call(
         functools.partial(selector_body, experts, capacity),
         out_shape=[
-            jax.ShapeDtypeStruct((2 * tok, experts * capacity), BF16),
+            *[jax.ShapeDtypeStruct((2 * tok, n * capacity), BF16) for n in counts],
             jax.ShapeDtypeStruct((2, tok, tok), F32),
         ],
         in_specs=[vmem(), vmem(), pl.BlockSpec(memory_space=pltpu.SMEM)],
-        out_specs=[vmem()] * 2,
+        out_specs=[vmem()] * 4,
         name="selector",
         cost_estimate=pl.CostEstimate(flops=2 * 10**10, transcendentals=0, bytes_accessed=10**8),
         compiler_params=pltpu.CompilerParams(vmem_limit_bytes=8 * 2**20),
@@ -250,28 +260,25 @@
         y_ref[j * capacity : (j + 1) * capacity, :] = block[:, start : start + width]
 
 
-def combine_chunk(sel_ref, weight_ref, y_ref, low, out_ref, squares):
-    tok, lanes = squares.shape
-    chunk, tile = out_ref.shape[1], 256
-    for col in range(0, chunk, tile):
-        picked = jnp.dot(
-            sel_ref[...], y_ref[:, low + col : low + col + tile], preferred_element_type=F32
-        )
-        for at in range(0, tile, lanes):
-            first = picked[:tok, at : at + lanes] * weight_ref[0]
-            second = picked[tok:, at : at + lanes] * weight_ref[1]
-            rounded = (first + second).astype(BF16)
-            out_ref[:, col + at : col + at + lanes] = rounded
-            wide = rounded.astype(F32)
-            squares = squares + wide * wide
-    return squares
+def weighted(sel_ref, weight_ref, y_ref, low, tile):
+    tok, lanes = weight_ref.shape[1:]
+    picked = jnp.dot(sel_ref[...], y_ref[:, low : low + tile], preferred_element_type=F32)
+    for at in range(0, tile, lanes):
+        first = picked[:tok, at : at + lanes] * weight_ref[0]
+        second = picked[tok:, at : at + lanes] * weight_ref[1]
+        yield slice(low + at, low + at + lanes), first + second
 
 
 def early_body(count, sel_ref, weight_ref, *refs):
     blocks, (out_ref, sum_ref, y_ref) = refs[:count], refs[count:]
     gather_blocks(blocks, y_ref, 0)
     squares = jnp.zeros(sum_ref.shape, F32)
-    sum_ref[...] = combine_chunk(sel_ref, weight_ref, y_ref, 0, out_ref, squares)
+    for low in range(0, y_ref.shape[1], 256):
+        for cols, combined in weighted(sel_ref, weight_ref, y_ref, low, 256):
+            rounded = combined.astype(BF16)
+            out_ref[:, cols] = rounded
+            squares = squares + rounded.astype(F32) * rounded.astype(F32)
+    sum_ref[...] = squares
 
 
 def combine_early(select, weights, blocks, width):
@@ -293,13 +300,42 @@
     )(select, weights, *blocks)
 
 
-def late_body(count, feat_width, sel_ref, weight_ref, part_ref, gain_ref, *refs):
+def mid_body(count, low, sel_ref, weight_ref, *refs):
+    blocks, (out_ref, y_ref) = refs[:count], refs[count:]
+    gather_blocks(blocks, y_ref, low)
+    for col in range(0, y_ref.shape[1], 256):
+        for cols, combined in weighted(sel_ref, weight_ref, y_ref, col, 256):
+            out_ref[:, cols] = combined
+
+
+def combine_mid(select, weights, blocks, low):
+    capacity, width = blocks[0].shape
+    rows, tok, width = capacity * len(blocks), weights.shape[1], width - low
+    return pl.pallas_call(
+        functools.partial(mid_body, len(blocks), low),
+        out_shape=jax.ShapeDtypeStruct((tok, width), F32),
+        in_specs=[vmem()] * (2 + len(blocks)),
+        out_specs=vmem(),
+        scratch_shapes=[pltpu.VMEM((rows, width), BF16)],
+        name="combine_mid",
+        cost_estimate=pl.CostEstimate(
+            flops=4 * tok * rows * width, transcendentals=0, bytes_accessed=2 * 10**6
+        ),
+        compiler_params=pltpu.CompilerParams(vmem_limit_bytes=12 * 2**20),
+    )(select, weights, *blocks)
+
+
+def late_body(count, feat_width, sel_ref, weight_ref, begun_ref, part_ref, gain_ref, *refs):
     blocks, y_ref, outs, sum_ref = refs[:count], refs[-1], refs[count:-2], refs[-2]
     chunk = outs[0].shape[1]
-    gather_blocks(blocks, y_ref, feat_width - chunk * len(outs))
+    gather_blocks(blocks, y_ref, 0)
     squares = part_ref[...]
-    for q, out in enumerate(outs):
-        squares = combine_chunk(sel_ref, weight_ref, y_ref, q * chunk, out, squares)
+    for low in range(0, y_ref.shape[1], 256):
+        for cols, combined in weighted(sel_ref, weight_ref, y_ref, low, 256):
+            rounded = (begun_ref[:, cols] + combined).astype(BF16)
+            at = cols.start % chunk
+            outs[cols.start // chunk][:, at : at + cols.stop - cols.start] = rounded
+            squares = squares + rounded.astype(F32) * rounded.astype(F32)
     total = jnp.sum(squares, axis=1, keepdims=True)
     tok = total.shape[0]
     sum_ref[...] = jnp.broadcast_to(total, (tok, tok)).T[0:8, :]
@@ -309,14 +345,14 @@
         out[...] = (out[...].astype(F32) * inv * gain).astype(BF16)
 
 
-def combine_late(select, weights, part, gain, blocks, chunk, feat_width):
-    width = gain.shape[1]
-    rows, tok = blocks[0].shape[0] * len(blocks), weights.shape[1]
+def combine_late(select, weights, begun, part, gain, blocks, chunk, feat_width):
+    capacity, width = blocks[0].shape
+    rows, tok = capacity * len(blocks), weights.shape[1]
     return pl.pallas_call(
         functools.partial(late_body, len(blocks), feat_width),
         out_shape=[jax.ShapeDtypeStruct((tok, chunk), BF16)] * (width // chunk)
         + [jax.ShapeDtypeStruct((8, tok), F32)],
-        in_specs=[vmem()] * (4 + len(blocks)),
+        in_specs=[vmem()] * (5 + len(blocks)),
         out_specs=[vmem()] * (width // chunk + 1),
         scratch_shapes=[pltpu.VMEM((rows, width), BF16)],
         name="combine_late",
@@ -324,7 +360,7 @@
             flops=4 * tok * rows * width, transcendentals=0, bytes_accessed=2 * 10**6
         ),
         compiler_params=pltpu.CompilerParams(vmem_limit_bytes=12 * 2**20),
-    )(select, weights, part, gain, *blocks)
+    )(select, weights, begun, part, gain, *blocks)
 
 
 def gain_body(offsets, gain_ref, out_ref):
@@ -347,47 +383,50 @@
     )(norm_gain[None, :])
 
 
-def finish_body(feat_width, ready, raw, *refs):
-    ways = len(ready) + len(raw)
-    chunks, sums = refs[:ways], refs[ways : ways + len(raw)]
-    gain_ref, out_ref, scratch, sems = refs[ways + len(raw) :]
+def scale_body(feat_width, chunk_ref, sum_ref, gain_ref, out_ref):
+    tok = chunk_ref.shape[0]
+    inv = lax.rsqrt(sum_ref[0:1, :] * (1.0 / feat_width) + epsilon)
+    column = jnp.broadcast_to(inv, (tok, tok)).T[:, 0:1]
+    out_ref[...] = (chunk_ref[...].astype(F32) * column * gain_ref[0:1, :]).astype(BF16)
+
+
+def scale(chunk, total, gain, feat_width):
+    return pl.pallas_call(
+        functools.partial(scale_body, feat_width),
+        out_shape=jax.ShapeDtypeStruct(chunk.shape, BF16),
+        in_specs=[vmem()] * 3,
+        out_specs=vmem(),
+        name="scale",
+        cost_estimate=pl.CostEstimate(flops=10**6, transcendentals=0, bytes_accessed=10**6),
+        compiler_params=pltpu.CompilerParams(vmem_limit_bytes=4 * 2**20),
+    )(chunk, total, gain)
+
+
+def finish_body(*refs):
+    *chunks, out_ref, sems = refs
     me = lax.axis_index("dp")
     tok = chunks[0].shape[0]
-
-    def put(source, k):
+    copies = []
+    for k, chunk in enumerate(chunks):
         rows = pl.ds(pl.multiple_of((me ^ k) * tok, tok), tok)
-        copy = pltpu.make_async_copy(source, out_ref.at[rows, :], sems.at[k])
-        copy.start()
-        return copy
-
-    copies = [put(chunks[i], k) for i, k in enumerate(ready)]
-    for i, k in enumerate(raw):
-        inv = lax.rsqrt(sums[i][0:1, :] * (1.0 / feat_width) + epsilon)
-        column = jnp.broadcast_to(inv, (tok, tok)).T[:, 0:1]
-        value = chunks[len(ready) + i][...].astype(F32) * column * gain_ref[0:1, :]
-        scratch[i] = value.astype(BF16)
-        copies.append(put(scratch.at[i], k))
+        copies.append(pltpu.make_async_copy(chunk, out_ref.at[rows, :], sems.at[k]))
+        copies[-1].start()
     for copy in copies:
         copy.wait()
 
 
-def finish(ready, raw, sums, gain, feat_width):
-    first = next(iter(ready.values()))
-    tok, width = first.shape
-    ways = len(ready) + len(raw)
-    return pl.pallas_call(
-        functools.partial(finish_body, feat_width, tuple(ready), tuple(raw)),
-        out_shape=jax.ShapeDtypeStruct((tok * ways, width), BF16),
-        in_specs=[vmem()] * (ways + len(raw) + 1),
+def finish(chunks):
+    tok, width = chunks[0].shape
+    return pl.pallas_call(
+        finish_body,
+        out_shape=jax.ShapeDtypeStruct((tok * len(chunks), width), BF16),
+        in_specs=[vmem()] * len(chunks),
         out_specs=pl.BlockSpec(memory_space=pltpu.HBM),
-        scratch_shapes=[
-            pltpu.VMEM((len(raw), tok, width), BF16),
-            pltpu.SemaphoreType.DMA((ways,)),
-        ],
+        scratch_shapes=[pltpu.SemaphoreType.DMA((len(chunks),))],
         name="finish",
         cost_estimate=pl.CostEstimate(flops=10**6, transcendentals=0, bytes_accessed=10**6),
-        compiler_params=pltpu.CompilerParams(vmem_limit_bytes=8 * 2**20),
-    )(*ready.values(), *raw.values(), *[sums[k] for k in raw], gain)
+        compiler_params=pltpu.CompilerParams(vmem_limit_bytes=4 * 2**20),
+    )(*chunks)
 
 
 def swap(value, axis, offset):
@@ -425,7 +464,7 @@
     )
     near = swap_each({k: blocks[k] for k in close}, "expert")
     far = swap_each({k: blocks[k] for k in away}, "expert")
-    select, weights = selector(route_rows, gate_code[0].T, gate_table, experts, capacity)
+    select, select_close, select_away, weights = selector(route_rows, gate_code[0].T, gate_table, experts, capacity)
     matrices = w_gate[0].T, w_up[0].T, w_down[0]
 
     plan = [(j, early + late) for j in range(len(close))]
@@ -437,20 +476,24 @@
     got_early = back | swap_each(dict(zip(away, away_early)), "expert")
     plan = [(j, late) for j in range(len(away))]
     away_late = down_call(hidden, matrices[2], len(away), plan, chunk)
-    got_late = back | swap_each(dict(zip(away, away_late)), "expert")
+    got_late = swap_each(dict(zip(away, away_late)), "expert")
 
     order = range(experts)
-    first, part = combine_early(
-        select, weights, [got_early[k] for k in order], chunk
-    )
+    first, part = combine_early(select, weights, [got_early[k] for k in order], chunk)
     raw = swap_each({early[0]: first}, "dp")
     gain_late = gain_of(norm_gain, late, chunk)
+    begun = combine_mid(
+        select_close, weights, [back[k] for k in order if k not in away], chunk * len(early)
+    )
     *rest, total = combine_late(
-        select, weights, part, gain_late, [got_late[k] for k in order], chunk, feat_width
-    )
-    ready = swap_each(dict(zip(late, rest)), "dp")
+        select_away, weights, begun, part, gain_late, [got_late[k] for k in away], chunk,
+        feat_width,
+    )
+    chunks = swap_each(dict(zip(late, rest)), "dp")
     sums = swap_each({k: total for k in early}, "dp")
-    return finish(ready, raw, sums, gain_own, feat_width)[None]
+    for k in early:
+        chunks[k] = scale(raw[k], sums[k], gain_own, feat_width)
+    return finish([chunks[k] for k in range(ways)])[None]
 
 
 def solution(mesh):
@@ -471,7 +514,7 @@
         experts, ways = mesh.shape["expert"], mesh.shape["dp"]
         tok, feat = tokens.shape[1] // ways, tokens.shape[2]
         power = experts & (experts - 1) == 0 and ways & (ways - 1) == 0
-        fits = power and experts == 8 and 2 <= ways <= 4
+        fits = power and experts == 8 and ways == 4
         fits = fits and tok % 128 == 0 and w_gate.shape[0] == experts
         fits = fits and 5 * tok % (16 * experts) == 0 and feat % (256 * ways) == 0
         body = local_fast if fits else local_general

time: 62 us -> 61.6 us (level)
  waiting for transfers between devices: 21.1 us -> 20.4 us
  Pallas kernels: 9.64 us -> 10.3 us
    ppermute x20, waiting for transfers between devices: 21.1 us -> 20.4 us  [swap(): return lax.ppermute(value, axis, [(i, i ^ offset) for i in range(size)])]
    pallas_call x1 -> x3, Pallas kernels: 0.87 us -> 1.39 us  [the longest x1 0.83 us: finish(): pl.pallas_call(finish_body, out_shape=jax.ShapeDtypeStruct((tok * len(chu...]
  transfers between devices with their start and end apart: 20 -> 20, of which waited for: 5 -> 5; matrix products, arithmetic and copies ran while one was open for 0% -> 0% of each run, Pallas kernels for 10% -> 12%
where the time goes in v7:
time: 61.6 us; the launch traced here: 61.3 us
  starting transfers between devices  25 us (41%)
  waiting for transfers between devices  20.4 us (33%)
  Pallas kernels  10.3 us (17%)
  local copies, waits for them, and re-layouts  5.47 us (9%)
    ppermute x20, starting transfers between devices, swap(): return lax.ppermute(value, axis, [(i, i ^ offset) for i in range(size)])  25 us
    ppermute x20, waiting for transfers between devices, swap(): return lax.ppermute(value, axis, [(i, i ^ offset) for i in range(size)])  20.4 us
    unnamed x18, local copies, waits for them, and re-layouts  5.47 us
    pallas_call x2, Pallas kernels, expert_call(): pl.pallas_call(functools.partial(expert_body, count, chunk, plan), out_sh...  4.75 us
    pallas_call x1, Pallas kernels, dispatch(): pl.pallas_call(functools.partial(dispatch_body, experts, capacity), out_s...  1.9 us
  transfers between devices with their start and end apart: 20, of which 5 were waited for; matrix products, arithmetic and copies ran while one was open for 0% of the time, Pallas kernels for 12%

profile of v7, /device:TPU:0, one launch (start us, length us, event | category | flops | bytes accessed | tf_op | source)
XLA Modules:
  0.0 61.3 jit_solution(5857986411218026793)
XLA Ops:
  0.0 1.9 %dispatch.1 = (bf16[40,2048]{1,0:T(8,128)(2,1)S(1)}, bf16[40,2048]{1,0:T(8,128)(2,1)S(1)}, bf16[40,2048]{1,0:T(8,128)(2,1)S(1)}, bf16[40,2048]{1,0:T(8,128)(2,1)...) custom-call(s32[2,128]{1,0:T(2,128)} %bitcast.25, ...), custom_call_target="tpu_custom_call" | custom-call | flops 100000000 | bytes 2000000 | tf_op jit(solution)/shard_map/dispatch/pallas_call | solution.py:126
  1.9 3.1 %collective-permute-start = (bf16[40,2048]{1,0:T(8,128)(2,1)S(1)}, bf16[40,2048]{1,0:T(8,128)(2,1)S(1)}, u32[]{:S(2)}, u32[]{:S(2)}) collective-permute-start(bf16[40,2048]{1,0:T(8,128)(2,1)S(1)} %get-tuple-element.37), channel_id=1, source_target_pairs={{0,4},{1,5},{2,6},{3,7},{4,0},{5,1},{6,2},{7,3},{8,12},{9,13},{10,... | collective-permute-start | bytes 491528 | tf_op jit(solution)/shard_map/ppermute | solution.py:434
  5.0 1.5 %collective-permute-start.1 = (bf16[40,2048]{1,0:T(8,128)(2,1)S(1)}, bf16[40,2048]{1,0:T(8,128)(2,1)S(1)}, u32[]{:S(2)}, u32[]{:S(2)}) collective-permute-start(bf16[40,2048]{1,0:T(8,128)(2,1)S(1)} %get-tuple-element.38), channel_id=1, source_target_pairs={{0,2},{1,3},{2,0},{3,1},{4,6},{5,7},{6,4},{7,5},{8,10},{9,11},{10,... | collective-permute-start | bytes 491528 | tf_op jit(solution)/shard_map/ppermute | solution.py:434
  6.5 0.0 collective-permute-start.2
  6.5 0.3 collective-permute-start.3
  6.8 0.3 collective-permute-start.4
  7.1 2.2 %collective-permute-done.refs_0_ = bf16[40,2048]{1,0:T(8,128)(2,1)S(1)} collective-permute-done((bf16[40,2048]{1,0:T(8,128)(2,1)S(1)}, bf16[40,2048]{1,0:T(8,128)(2,1)S(1)}, u32[]{:S(2)}, u32[]{:S(2)}) %collective-permute-start) | collective-permute-done | bytes 163872 | tf_op jit(solution)/shard_map/ppermute | solution.py:434
  9.3 3.7 %collective-permute-start.10 = (bf16[40,2048]{1,0:T(8,128)(2,1)S(1)}, bf16[40,2048]{1,0:T(8,128)(2,1)S(1)}, u32[]{:S(2)}, u32[]{:S(2)}) collective-permute-start(bf16[40,2048]{1,0:T(8,128)(2,1)S(1)} %get-tuple-element.50), channel_id=1, source_target_pairs={{0,6},{1,7},{2,4},{3,5},{4,2},{5,3},{6,0},{7,1},{8,14},{9,15},{10,... | collective-permute-start | bytes 491528 | tf_op jit(solution)/shard_map/ppermute | solution.py:434
  13.0 0.0 collective-permute-done.1.refs_1_
  13.0 0.0 collective-permute-start.11
  13.0 0.0 collective-permute-done.2.refs_2_
  13.0 1.6 %collective-permute-done.3.refs_3_ = bf16[40,2048]{1,0:T(8,128)(2,1)S(1)} collective-permute-done((bf16[40,2048]{1,0:T(8,128)(2,1)S(1)}, bf16[40,2048]{1,0:T(8,128)(2,1)S(1)}, u32[]{:S(2)}, u32[]{:S(2)}) %collective-permute-start.3) | collective-permute-done | bytes 163872 | tf_op jit(solution)/shard_map/ppermute | solution.py:434
  14.6 0.0 collective-permute-done.4.refs_4_
  14.6 0.0 copy-start
  14.6 1.8 %copy-done = bf16[1,704,2048]{2,1,0:T(8,128)(2,1)S(1)} copy-done((bf16[1,704,2048]{2,1,0:T(8,128)(2,1)S(1)}, bf16[1,704,2048]{2,1,0:T(8,128)(2,1)}, u32[]{:S(2)}) %copy-start) | copy-done | bytes 2883608
  16.4 0.0 copy-start.2
  16.4 1.8 %copy-done.2 = bf16[1,2048,704]{1,2,0:T(8,128)(2,1)S(1)} copy-done((bf16[1,2048,704]{1,2,0:T(8,128)(2,1)S(1)}, bf16[1,2048,704]{1,2,0:T(8,128)(2,1)}, u32[]{:S(2)}) %copy-start.2) | copy-done | bytes 2883608
  18.2 1.8 %copy-done.4 = bf16[1,2048,704]{1,2,0:T(8,128)(2,1)S(1)} copy-done((bf16[1,2048,704]{1,2,0:T(8,128)(2,1)S(1)}, bf16[1,2048,704]{1,2,0:T(8,128)(2,1)}, u32[]{:S(2)}) %copy-start.4) | copy-done | bytes 2883608
  20.0 2.7 %shard_map.82 = (bf16[240,704]{1,0:T(8,128)(2,1)}, bf16[40,2048]{1,0:T(8,128)(2,1)S(1)}, bf16[40,2048]{1,0:T(8,128)(2,1)S(1)}, bf16[40,2048]{1,0:T(8,128)(2,1)S(...) custom-call(bf16[40,2048]{1,0:T(8,128)(2,1)S(1)} %collective-permute-done.refs_0_, ...), custom_call_target="tpu_custom_call" | custom-call | flops 1730150400 | bytes 8000000 | tf_op jit(solution)/shard_map/pallas_call | solution.py:223
  22.7 0.8 %collective-permute-start.5 = (bf16[40,2048]{1,0:T(8,128)(2,1)S(1)}, bf16[40,2048]{1,0:T(8,128)(2,1)S(1)}, u32[]{:S(2)}, u32[]{:S(2)}) collective-permute-start(bf16[40,2048]{1,0:T(8,128)(2,1)S(1)} %get-tuple-element.44), channel_id=1, source_target_pairs={{0,1},{1,0},{2,3},{3,2},{4,5},{5,4},{6,7},{7,6},{8,9},{9,8},{10,11... | collective-permute-start | bytes 491528 | tf_op jit(solution)/shard_map/ppermute | solution.py:434
  23.6 1.8 %collective-permute-start.6 = (bf16[40,2048]{1,0:T(8,128)(2,1)S(1)}, bf16[40,2048]{1,0:T(8,128)(2,1)S(1)}, u32[]{:S(2)}, u32[]{:S(2)}) collective-permute-start(bf16[40,2048]{1,0:T(8,128)(2,1)S(1)} %get-tuple-element.45), channel_id=1, source_target_pairs={{0,2},{1,3},{2,0},{3,1},{4,6},{5,7},{6,4},{7,5},{8,10},{9,11},{10,... | collective-permute-start | bytes 491528 | tf_op jit(solution)/shard_map/ppermute | solution.py:434
  25.3 0.0 collective-permute-done.10.refs_0_
  25.3 0.0 collective-permute-done.11.refs_1_
  25.3 0.0 copy-done.1
  25.3 0.0 copy-done.3
  25.4 2.0 %shard_map.83 = (bf16[80,704]{1,0:T(8,128)(2,1)S(1)}, bf16[40,512]{1,0:T(8,128)(2,1)S(1)}, bf16[40,512]{1,0:T(8,128)(2,1)S(1)}) custom-call(bf16[40,2048]{1,0:T(8,128)(2,1)S(1)} %collective-permute-done.10.refs_0_, bf16[40,2048]{1,0:T(8,128)(2,1)S(1)} %collective-permute-done.11.refs_1_, bf16[704,2048]{1,0:T(8,128)(2,1)S(1)} %bitcast.20, ...), custom_call_target="tpu_custom_call" | custom-call | flops 576716800 | bytes 8000000 | tf_op jit(solution)/shard_map/pallas_call | solution.py:223
  27.4 0.0 copy-start.6
  27.4 0.0 copy-start.7
  27.4 0.0 copy-start.8
  27.4 0.1 collective-permute-start.12
  27.5 2.0 %collective-permute-start.13 = (bf16[40,512]{1,0:T(8,128)(2,1)S(1)}, bf16[40,512]{1,0:T(8,128)(2,1)S(1)}, u32[]{:S(2)}, u32[]{:S(2)}) collective-permute-start(bf16[40,512]{1,0:T(8,128)(2,1)S(1)} %get-tuple-element.53), channel_id=1, source_target_pairs={{0,7},{1,6},{2,5},{3,4},{4,3},{5,2},{6,1},{7,0},{8,15},{9,14},{10,... | collective-permute-start | bytes 122888 | tf_op jit(solution)/shard_map/ppermute | solution.py:434
  29.5 0.9 %collective-permute-start.7 = (bf16[40,2048]{1,0:T(8,128)(2,1)S(1)}, bf16[40,2048]{1,0:T(8,128)(2,1)S(1)}, u32[]{:S(2)}, u32[]{:S(2)}) collective-permute-start(bf16[40,2048]{1,0:T(8,128)(2,1)S(1)} %get-tuple-element.46), channel_id=1, source_target_pairs={{0,3},{1,2},{2,1},{3,0},{4,7},{5,6},{6,5},{7,4},{8,11},{9,10},{10,... | collective-permute-start | bytes 491528 | tf_op jit(solution)/shard_map/ppermute | solution.py:434
  30.4 0.5 shard_map.85
  30.9 1.9 %collective-permute-done.12.refs_6_ = bf16[40,512]{1,0:T(8,128)(2,1)S(1)} collective-permute-done((bf16[40,512]{1,0:T(8,128)(2,1)S(1)}, bf16[40,512]{1,0:T(8,128)(2,1)S(1)}, u32[]{:S(2)}, u32[]{:S(2)}) %collective-permute-start.12) | collective-permute-done | bytes 40992 | tf_op jit(solution)/shard_map/ppermute | solution.py:434
  32.8 0.0 collective-permute-start.8
  32.8 0.0 collective-permute-done.13.refs_7_
  32.9 0.3 collective-permute-start.9
  33.1 0.0 collective-permute-done.5.refs_1_
  33.1 1.7 %collective-permute-start.14 = (bf16[40,1536]{1,0:T(8,128)(2,1)S(1)}, bf16[40,1536]{1,0:T(8,128)(2,1)S(1)}, u32[]{:S(2)}, u32[]{:S(2)}) collective-permute-start(bf16[40,1536]{1,0:T(8,128)(2,1)S(1)} %get-tuple-element.56), channel_id=1, source_target_pairs={{0,6},{1,7},{2,4},{3,5},{4,2},{5,3},{6,0},{7,1},{8,14},{9,15},{10,... | collective-permute-start | bytes 368648 | tf_op jit(solution)/shard_map/ppermute | solution.py:434
  34.9 0.0 collective-permute-done.6.refs_2_
  34.9 2.4 %collective-permute-start.15 = (bf16[40,1536]{1,0:T(8,128)(2,1)S(1)}, bf16[40,1536]{1,0:T(8,128)(2,1)S(1)}, u32[]{:S(2)}, u32[]{:S(2)}) collective-permute-start(bf16[40,1536]{1,0:T(8,128)(2,1)S(1)} %get-tuple-element.57), channel_id=1, source_target_pairs={{0,7},{1,6},{2,5},{3,4},{4,3},{5,2},{6,1},{7,0},{8,15},{9,14},{10,... | collective-permute-start | bytes 368648 | tf_op jit(solution)/shard_map/ppermute | solution.py:434
  37.2 0.0 copy-done.6
  37.3 0.0 copy-done.7
  37.3 0.0 copy-done.8
  37.3 0.9 %selector.1 = (bf16[256,320]{1,0:T(8,128)(2,1)S(1)}, bf16[256,240]{1,0:T(8,128)(2,1)S(1)}, bf16[256,80]{1,0:T(8,128)(2,1)S(1)}, f32[2,128,128]{2,1,0:T(8,128)S(1)}) custom-call(s32[2,128]{1,0:T(2,128)S(1)} %bitcast.26, s32[2,128]{1,0:T(2,128)S(1)} %bitcast.27, f32[16]{0:T(128)S(1)} %copy-done.8), custom_call_target="tpu_custom_call" | custom-call | flops 20000000000 | bytes 100000000 | tf_op jit(solution)/shard_map/selector/pallas_call | solution.py:169
  38.1 0.0 copy-done.5
  38.2 0.0 collective-permute-done.7.refs_3_
  38.2 6.4 %collective-permute-done.8.refs_4_ = bf16[40,2048]{1,0:T(8,128)(2,1)S(1)} collective-permute-done((bf16[40,2048]{1,0:T(8,128)(2,1)S(1)}, bf16[40,2048]{1,0:T(8,128)(2,1)S(1)}, u32[]{:S(2)}, u32[]{:S(2)}) %collective-permute-start.8) | collective-permute-done | bytes 163872 | tf_op jit(solution)/shard_map/ppermute | solution.py:434
  44.6 0.0 collective-permute-done.9.refs_5_
  44.6 0.3 combine_early.1
  44.9 2.6 %collective-permute-start.17 = (bf16[128,512]{1,0:T(8,128)(2,1)S(1)}, bf16[128,512]{1,0:T(8,128)(2,1)S(1)}, u32[]{:S(2)}, u32[]{:S(2)}) collective-permute-start(bf16[128,512]{1,0:T(8,128)(2,1)S(1)} %get-tuple-element.60), channel_id=1, source_target_pairs={{0,16},{8,24},{16,0},{24,8},{1,17},{9,25},{17,1},{25,9},{2,18},{10... | collective-permute-start | bytes 393224 | tf_op jit(solution)/shard_map/ppermute | solution.py:434
  47.6 0.4 combine_mid.1.begun_ref
  48.0 0.0 collective-permute-done.14.refs_0_
  48.0 0.0 collective-permute-done.15.refs_1_
  48.0 0.5 combine_late.1
  48.6 1.6 %collective-permute-start.16 = (bf16[128,512]{1,0:T(8,128)(2,1)S(1)}, bf16[128,512]{1,0:T(8,128)(2,1)S(1)}, u32[]{:S(2)}, u32[]{:S(2)}) collective-permute-start(bf16[128,512]{1,0:T(8,128)(2,1)S(1)} %get-tuple-element.59), channel_id=1, source_target_pairs={{0,8},{8,0},{16,24},{24,16},{1,9},{9,1},{17,25},{25,17},{2,10},{10... | collective-permute-start | bytes 393224 | tf_op jit(solution)/shard_map/ppermute | solution.py:434
  50.2 0.3 collective-permute-start.19
  50.4 1.7 %collective-permute-start.18 = (f32[8,128]{1,0:T(8,128)S(1)}, f32[8,128]{1,0:T(8,128)S(1)}, u32[]{:S(2)}, u32[]{:S(2)}) collective-permute-start(f32[8,128]{1,0:T(8,128)S(1)} %get-tuple-element.61), channel_id=1, source_target_pairs={{0,16},{8,24},{16,0},{24,8},{1,17},{9,25},{17,1},{25,9},{2,18},{10... | collective-permute-start | bytes 12296 | tf_op jit(solution)/shard_map/ppermute | solution.py:434
  52.1 8.2 %collective-permute-done.18.sum_ref = f32[8,128]{1,0:T(8,128)S(1)} collective-permute-done((f32[8,128]{1,0:T(8,128)S(1)}, f32[8,128]{1,0:T(8,128)S(1)}, u32[]{:S(2)}, u32[]{:S(2)}) %collective-permute-start.18) | collective-permute-done | bytes 4128 | tf_op jit(solution)/shard_map/ppermute | solution.py:434
  60.3 0.0 collective-permute-done.17.chunk_ref
  60.3 0.2 scale.1.refs_2_
  60.5 0.0 collective-permute-done.16.refs_1_
  60.5 0.0 collective-permute-done.19.refs_3_
  60.5 0.8 %finish.1 = bf16[512,512]{1,0:T(8,128)(2,1)} custom-call(bf16[128,512]{1,0:T(8,128)(2,1)S(1)} %get-tuple-element.58.refs_0_, bf16[128,512]{1,0:T(8,128)(2,1)S(1)} %collective-permute-done.16.refs_1_, bf16[128,512]{1,0:T(8,128)(2,1)S(1)} %scale.1.refs_2_, bf16[128,512]{1,0:T(8,128)(2,1)S(1)} %collective-permute-done.19.refs_3_), custom_call_target="tpu_custom_call" | custom-call | flops 1000000 | bytes 1000000 | tf_op jit(solution)/shard_map/finish/pallas_call | solution.py:420
  (6 shorter events, 0.0 us)
Async XLA Ops:
  1.9 7.4 %collective-permute-start = (bf16[40,2048]{1,0:T(8,128)(2,1)S(1)}, bf16[40,2048]{1,0:T(8,128)(2,1)S(1)}, u32[]{:S(2)}, u32[]{:S(2)}) collective-permute-start(bf16[40,2048]{1,0:T(8,128)(2,1)S(1)} %get-tuple-element.37), channel_id=1, source_target_pairs={{0,4},{1,5},{2,6},{3,7},{4,0},{5,1},{6,2},{7,3},{8,12},{9,13},{10,... | collective-permute-start | bytes 491528 | tf_op jit(solution)/shard_map/ppermute | solution.py:434
  5.0 8.0 %collective-permute-start.1 = (bf16[40,2048]{1,0:T(8,128)(2,1)S(1)}, bf16[40,2048]{1,0:T(8,128)(2,1)S(1)}, u32[]{:S(2)}, u32[]{:S(2)}) collective-permute-start(bf16[40,2048]{1,0:T(8,128)(2,1)S(1)} %get-tuple-element.38), channel_id=1, source_target_pairs={{0,2},{1,3},{2,0},{3,1},{4,6},{5,7},{6,4},{7,5},{8,10},{9,11},{10,... | collective-permute-start | bytes 491528 | tf_op jit(solution)/shard_map/ppermute | solution.py:434
  6.5 6.5 %collective-permute-start.2 = (bf16[40,2048]{1,0:T(8,128)(2,1)S(1)}, bf16[40,2048]{1,0:T(8,128)(2,1)S(1)}, u32[]{:S(2)}, u32[]{:S(2)}) collective-permute-start(bf16[40,2048]{1,0:T(8,128)(2,1)S(1)} %get-tuple-element.39), channel_id=1, source_target_pairs={{0,5},{1,4},{2,7},{3,6},{4,1},{5,0},{6,3},{7,2},{8,13},{9,12},{10,... | collective-permute-start | bytes 491528 | tf_op jit(solution)/shard_map/ppermute | solution.py:434
  6.5 8.1 %collective-permute-start.3 = (bf16[40,2048]{1,0:T(8,128)(2,1)S(1)}, bf16[40,2048]{1,0:T(8,128)(2,1)S(1)}, u32[]{:S(2)}, u32[]{:S(2)}) collective-permute-start(bf16[40,2048]{1,0:T(8,128)(2,1)S(1)} %get-tuple-element.40), channel_id=1, source_target_pairs={{0,3},{1,2},{2,1},{3,0},{4,7},{5,6},{6,5},{7,4},{8,11},{9,10},{10,... | collective-permute-start | bytes 491528 | tf_op jit(solution)/shard_map/ppermute | solution.py:434
  6.8 7.8 %collective-permute-start.4 = (bf16[40,2048]{1,0:T(8,128)(2,1)S(1)}, bf16[40,2048]{1,0:T(8,128)(2,1)S(1)}, u32[]{:S(2)}, u32[]{:S(2)}) collective-permute-start(bf16[40,2048]{1,0:T(8,128)(2,1)S(1)} %get-tuple-element.41), channel_id=1, source_target_pairs={{0,1},{1,0},{2,3},{3,2},{4,5},{5,4},{6,7},{7,6},{8,9},{9,8},{10,11... | collective-permute-start | bytes 491528 | tf_op jit(solution)/shard_map/ppermute | solution.py:434
  9.3 16.0 %collective-permute-start.10 = (bf16[40,2048]{1,0:T(8,128)(2,1)S(1)}, bf16[40,2048]{1,0:T(8,128)(2,1)S(1)}, u32[]{:S(2)}, u32[]{:S(2)}) collective-permute-start(bf16[40,2048]{1,0:T(8,128)(2,1)S(1)} %get-tuple-element.50), channel_id=1, source_target_pairs={{0,6},{1,7},{2,4},{3,5},{4,2},{5,3},{6,0},{7,1},{8,14},{9,15},{10,... | collective-permute-start | bytes 491528 | tf_op jit(solution)/shard_map/ppermute | solution.py:434
  13.0 12.4 %collective-permute-start.11 = (bf16[40,2048]{1,0:T(8,128)(2,1)S(1)}, bf16[40,2048]{1,0:T(8,128)(2,1)S(1)}, u32[]{:S(2)}, u32[]{:S(2)}) collective-permute-start(bf16[40,2048]{1,0:T(8,128)(2,1)S(1)} %get-tuple-element.51), channel_id=1, source_target_pairs={{0,7},{1,6},{2,5},{3,4},{4,3},{5,2},{6,1},{7,0},{8,15},{9,14},{10,... | collective-permute-start | bytes 491528 | tf_op jit(solution)/shard_map/ppermute | solution.py:434
  14.6 1.8 %copy-start = (bf16[1,704,2048]{2,1,0:T(8,128)(2,1)S(1)}, bf16[1,704,2048]{2,1,0:T(8,128)(2,1)}, u32[]{:S(2)}) copy-start(bf16[1,704,2048]{2,1,0:T(8,128)(2,1)} %param.14) | copy-start | bytes 8650756
  16.4 1.8 %copy-start.2 = (bf16[1,2048,704]{1,2,0:T(8,128)(2,1)S(1)}, bf16[1,2048,704]{1,2,0:T(8,128)(2,1)}, u32[]{:S(2)}) copy-start(bf16[1,2048,704]{1,2,0:T(8,128)(2,1)} %param.12) | copy-start | bytes 8650756
  18.2 1.8 %copy-start.4 = (bf16[1,2048,704]{1,2,0:T(8,128)(2,1)S(1)}, bf16[1,2048,704]{1,2,0:T(8,128)(2,1)}, u32[]{:S(2)}) copy-start(bf16[1,2048,704]{1,2,0:T(8,128)(2,1)} %param.13) | copy-start | bytes 8650756
  20.0 5.3 %copy-start.1 = (bf16[1,704,2048]{2,1,0:T(8,128)(2,1)S(1)}, bf16[1,704,2048]{2,1,0:T(8,128)(2,1)}, u32[]{:S(2)}) copy-start(bf16[1,704,2048]{2,1,0:T(8,128)(2,1)} %param.14) | copy-start | bytes 8650756
  20.0 5.3 %copy-start.3 = (bf16[1,2048,704]{1,2,0:T(8,128)(2,1)S(1)}, bf16[1,2048,704]{1,2,0:T(8,128)(2,1)}, u32[]{:S(2)}) copy-start(bf16[1,2048,704]{1,2,0:T(8,128)(2,1)} %param.12) | copy-start | bytes 8650756
  22.7 10.4 %collective-permute-start.5 = (bf16[40,2048]{1,0:T(8,128)(2,1)S(1)}, bf16[40,2048]{1,0:T(8,128)(2,1)S(1)}, u32[]{:S(2)}, u32[]{:S(2)}) collective-permute-start(bf16[40,2048]{1,0:T(8,128)(2,1)S(1)} %get-tuple-element.44), channel_id=1, source_target_pairs={{0,1},{1,0},{2,3},{3,2},{4,5},{5,4},{6,7},{7,6},{8,9},{9,8},{10,11... | collective-permute-start | bytes 491528 | tf_op jit(solution)/shard_map/ppermute | solution.py:434
  23.6 11.3 %collective-permute-start.6 = (bf16[40,2048]{1,0:T(8,128)(2,1)S(1)}, bf16[40,2048]{1,0:T(8,128)(2,1)S(1)}, u32[]{:S(2)}, u32[]{:S(2)}) collective-permute-start(bf16[40,2048]{1,0:T(8,128)(2,1)S(1)} %get-tuple-element.45), channel_id=1, source_target_pairs={{0,2},{1,3},{2,0},{3,1},{4,6},{5,7},{6,4},{7,5},{8,10},{9,11},{10,... | collective-permute-start | bytes 491528 | tf_op jit(solution)/shard_map/ppermute | solution.py:434
  27.4 9.8 %copy-start.6 = (s32[1,128,2]{1,2,0:T(2,128)S(1)}, s32[1,128,2]{1,2,0:T(2,128)}, u32[]{:S(2)}) copy-start(s32[1,128,2]{1,2,0:T(2,128)} %param.9) | copy-start | bytes 3076
  27.4 9.8 %copy-start.7 = (s32[1,128,2]{1,2,0:T(2,128)S(1)}, s32[1,128,2]{1,2,0:T(2,128)}, u32[]{:S(2)}) copy-start(s32[1,128,2]{1,2,0:T(2,128)} %param.10) | copy-start | bytes 3076
  27.4 9.8 %copy-start.8 = (f32[16]{0:T(128)S(1)}, f32[16]{0:T(128)}, u32[]{:S(2)}) copy-start(f32[16]{0:T(128)} %table_ref.1) | copy-start | bytes 196
  27.4 5.4 %collective-permute-start.12 = (bf16[40,512]{1,0:T(8,128)(2,1)S(1)}, bf16[40,512]{1,0:T(8,128)(2,1)S(1)}, u32[]{:S(2)}, u32[]{:S(2)}) collective-permute-start(bf16[40,512]{1,0:T(8,128)(2,1)S(1)} %get-tuple-element.52), channel_id=1, source_target_pairs={{0,6},{1,7},{2,4},{3,5},{4,2},{5,3},{6,0},{7,1},{8,14},{9,15},{10,... | collective-permute-start | bytes 122888 | tf_op jit(solution)/shard_map/ppermute | solution.py:434
  27.5 5.3 %collective-permute-start.13 = (bf16[40,512]{1,0:T(8,128)(2,1)S(1)}, bf16[40,512]{1,0:T(8,128)(2,1)S(1)}, u32[]{:S(2)}, u32[]{:S(2)}) collective-permute-start(bf16[40,512]{1,0:T(8,128)(2,1)S(1)} %get-tuple-element.53), channel_id=1, source_target_pairs={{0,7},{1,6},{2,5},{3,4},{4,3},{5,2},{6,1},{7,0},{8,15},{9,14},{10,... | collective-permute-start | bytes 122888 | tf_op jit(solution)/shard_map/ppermute | solution.py:434
  29.5 8.7 %collective-permute-start.7 = (bf16[40,2048]{1,0:T(8,128)(2,1)S(1)}, bf16[40,2048]{1,0:T(8,128)(2,1)S(1)}, u32[]{:S(2)}, u32[]{:S(2)}) collective-permute-start(bf16[40,2048]{1,0:T(8,128)(2,1)S(1)} %get-tuple-element.46), channel_id=1, source_target_pairs={{0,3},{1,2},{2,1},{3,0},{4,7},{5,6},{6,5},{7,4},{8,11},{9,10},{10,... | collective-permute-start | bytes 491528 | tf_op jit(solution)/shard_map/ppermute | solution.py:434
  32.8 11.8 %collective-permute-start.8 = (bf16[40,2048]{1,0:T(8,128)(2,1)S(1)}, bf16[40,2048]{1,0:T(8,128)(2,1)S(1)}, u32[]{:S(2)}, u32[]{:S(2)}) collective-permute-start(bf16[40,2048]{1,0:T(8,128)(2,1)S(1)} %get-tuple-element.47), channel_id=1, source_target_pairs={{0,4},{1,5},{2,6},{3,7},{4,0},{5,1},{6,2},{7,3},{8,12},{9,13},{10,... | collective-permute-start | bytes 491528 | tf_op jit(solution)/shard_map/ppermute | solution.py:434
  32.9 11.8 %collective-permute-start.9 = (bf16[40,2048]{1,0:T(8,128)(2,1)S(1)}, bf16[40,2048]{1,0:T(8,128)(2,1)S(1)}, u32[]{:S(2)}, u32[]{:S(2)}) collective-permute-start(bf16[40,2048]{1,0:T(8,128)(2,1)S(1)} %get-tuple-element.48), channel_id=1, source_target_pairs={{0,5},{1,4},{2,7},{3,6},{4,1},{5,0},{6,3},{7,2},{8,13},{9,12},{10,... | collective-permute-start | bytes 491528 | tf_op jit(solution)/shard_map/ppermute | solution.py:434
  33.1 14.9 %collective-permute-start.14 = (bf16[40,1536]{1,0:T(8,128)(2,1)S(1)}, bf16[40,1536]{1,0:T(8,128)(2,1)S(1)}, u32[]{:S(2)}, u32[]{:S(2)}) collective-permute-start(bf16[40,1536]{1,0:T(8,128)(2,1)S(1)} %get-tuple-element.56), channel_id=1, source_target_pairs={{0,6},{1,7},{2,4},{3,5},{4,2},{5,3},{6,0},{7,1},{8,14},{9,15},{10,... | collective-permute-start | bytes 368648 | tf_op jit(solution)/shard_map/ppermute | solution.py:434
  34.9 13.1 %collective-permute-start.15 = (bf16[40,1536]{1,0:T(8,128)(2,1)S(1)}, bf16[40,1536]{1,0:T(8,128)(2,1)S(1)}, u32[]{:S(2)}, u32[]{:S(2)}) collective-permute-start(bf16[40,1536]{1,0:T(8,128)(2,1)S(1)} %get-tuple-element.57), channel_id=1, source_target_pairs={{0,7},{1,6},{2,5},{3,4},{4,3},{5,2},{6,1},{7,0},{8,15},{9,14},{10,... | collective-permute-start | bytes 368648 | tf_op jit(solution)/shard_map/ppermute | solution.py:434
  37.3 0.9 %copy-start.5 = (f32[2048]{0:T(1024)S(1)}, f32[2048]{0:T(1024)}, u32[]{:S(2)}) copy-start(f32[2048]{0:T(1024)} %param.15) | copy-start | bytes 24580
  44.9 15.3 %collective-permute-start.17 = (bf16[128,512]{1,0:T(8,128)(2,1)S(1)}, bf16[128,512]{1,0:T(8,128)(2,1)S(1)}, u32[]{:S(2)}, u32[]{:S(2)}) collective-permute-start(bf16[128,512]{1,0:T(8,128)(2,1)S(1)} %get-tuple-element.60), channel_id=1, source_target_pairs={{0,16},{8,24},{16,0},{24,8},{1,17},{9,25},{17,1},{25,9},{2,18},{10... | collective-permute-start | bytes 393224 | tf_op jit(solution)/shard_map/ppermute | solution.py:434
  48.6 11.9 %collective-permute-start.16 = (bf16[128,512]{1,0:T(8,128)(2,1)S(1)}, bf16[128,512]{1,0:T(8,128)(2,1)S(1)}, u32[]{:S(2)}, u32[]{:S(2)}) collective-permute-start(bf16[128,512]{1,0:T(8,128)(2,1)S(1)} %get-tuple-element.59), channel_id=1, source_target_pairs={{0,8},{8,0},{16,24},{24,16},{1,9},{9,1},{17,25},{25,17},{2,10},{10... | collective-permute-start | bytes 393224 | tf_op jit(solution)/shard_map/ppermute | solution.py:434
  50.2 10.3 %collective-permute-start.19 = (bf16[128,512]{1,0:T(8,128)(2,1)S(1)}, bf16[128,512]{1,0:T(8,128)(2,1)S(1)}, u32[]{:S(2)}, u32[]{:S(2)}) collective-permute-start(bf16[128,512]{1,0:T(8,128)(2,1)S(1)} %get-tuple-element.62), channel_id=1, source_target_pairs={{0,24},{8,16},{16,8},{24,0},{1,25},{9,17},{17,9},{25,1},{2,26},{10... | collective-permute-start | bytes 393224 | tf_op jit(solution)/shard_map/ppermute | solution.py:434
  50.4 9.8 %collective-permute-start.18 = (f32[8,128]{1,0:T(8,128)S(1)}, f32[8,128]{1,0:T(8,128)S(1)}, u32[]{:S(2)}, u32[]{:S(2)}) collective-permute-start(f32[8,128]{1,0:T(8,128)S(1)} %get-tuple-element.61), channel_id=1, source_target_pairs={{0,16},{8,24},{16,0},{24,8},{1,17},{9,25},{17,1},{25,9},{2,18},{10... | collective-permute-start | bytes 12296 | tf_op jit(solution)/shard_map/ppermute | solution.py:434

commit v8 on v7

--- a/solution.py
+++ b/solution.py
@@ -94,31 +94,27 @@
 
 def dispatch_body(experts, capacity, route_hbm, tok_hbm, *refs):
     *out_refs, route_ref, tok_ref, sems = refs
+    copies = [
+        pltpu.make_async_copy(route_hbm, route_ref, sems.at[0]),
+        pltpu.make_async_copy(tok_hbm, tok_ref, sems.at[1]),
+    ]
+    for copy in copies:
+        copy.start()
+    me = lax.axis_index("expert")
     tok, width = tok_ref.shape
-    pieces = sems.shape[0] - 1
-    step = width // pieces
-    route_copy = pltpu.make_async_copy(route_hbm, route_ref, sems.at[pieces])
-    route_copy.start()
-    copies = []
-    for p in range(pieces):
-        cols = pl.ds(p * step, step)
-        copies.append(pltpu.make_async_copy(tok_hbm.at[:, cols], tok_ref.at[:, cols], sems.at[p]))
-        copies[-1].start()
-    me = lax.axis_index("expert")
     lane = lax.broadcasted_iota(jnp.int32, (capacity, tok), 0)
-    route_copy.wait()
+    copies[0].wait()
     slots, _ = slot_rows(route_ref[...], experts, me)
     pick = jnp.concatenate(
         [(lane == slots[j : j + 1, :]).astype(F32) for j in range(experts)], axis=0
     ).astype(BF16)
+    copies[1].wait()
     tile = 256
-    for p, copy in enumerate(copies):
-        copy.wait()
-        for col in range(p * step, (p + 1) * step, tile):
-            rows = jnp.dot(pick, tok_ref[:, col : col + tile], preferred_element_type=F32)
-            rows = rows.astype(BF16)
-            for j in range(experts):
-                out_refs[j][:, col : col + tile] = rows[j * capacity : (j + 1) * capacity, :]
+    for col in range(0, width, tile):
+        rows = jnp.dot(pick, tok_ref[:, col : col + tile], preferred_element_type=F32)
+        rows = rows.astype(BF16)
+        for j in range(experts):
+            out_refs[j][:, col : col + tile] = rows[j * capacity : (j + 1) * capacity, :]
 
 
 def dispatch(route_rows, own_rows, experts, capacity):
@@ -131,7 +127,7 @@
         scratch_shapes=[
             pltpu.VMEM(route_rows.shape, jnp.int32),
             pltpu.VMEM(own_rows.shape, BF16),
-            pltpu.SemaphoreType.DMA((5,)),
+            pltpu.SemaphoreType.DMA((2,)),
         ],
         name="dispatch",
         cost_estimate=pl.CostEstimate(flops=10**8, transcendentals=0, bytes_accessed=2 * 10**6),
@@ -383,50 +379,47 @@
     )(norm_gain[None, :])
 
 
-def scale_body(feat_width, chunk_ref, sum_ref, gain_ref, out_ref):
-    tok = chunk_ref.shape[0]
-    inv = lax.rsqrt(sum_ref[0:1, :] * (1.0 / feat_width) + epsilon)
-    column = jnp.broadcast_to(inv, (tok, tok)).T[:, 0:1]
-    out_ref[...] = (chunk_ref[...].astype(F32) * column * gain_ref[0:1, :]).astype(BF16)
-
-
-def scale(chunk, total, gain, feat_width):
-    return pl.pallas_call(
-        functools.partial(scale_body, feat_width),
-        out_shape=jax.ShapeDtypeStruct(chunk.shape, BF16),
-        in_specs=[vmem()] * 3,
-        out_specs=vmem(),
-        name="scale",
-        cost_estimate=pl.CostEstimate(flops=10**6, transcendentals=0, bytes_accessed=10**6),
-        compiler_params=pltpu.CompilerParams(vmem_limit_bytes=4 * 2**20),
-    )(chunk, total, gain)
-
-
-def finish_body(*refs):
-    *chunks, out_ref, sems = refs
+def finish_body(feat_width, ready, raw, *refs):
+    ways = len(ready) + len(raw)
+    chunks, sums = refs[:ways], refs[ways : ways + len(raw)]
+    gain_ref, out_ref, scratch, sems = refs[ways + len(raw) :]
     me = lax.axis_index("dp")
     tok = chunks[0].shape[0]
-    copies = []
-    for k, chunk in enumerate(chunks):
+
+    def put(source, k):
         rows = pl.ds(pl.multiple_of((me ^ k) * tok, tok), tok)
-        copies.append(pltpu.make_async_copy(chunk, out_ref.at[rows, :], sems.at[k]))
-        copies[-1].start()
+        copy = pltpu.make_async_copy(source, out_ref.at[rows, :], sems.at[k])
+        copy.start()
+        return copy
+
+    copies = [put(chunks[i], k) for i, k in enumerate(ready)]
+    for i, k in enumerate(raw):
+        inv = lax.rsqrt(sums[i][0:1, :] * (1.0 / feat_width) + epsilon)
+        column = jnp.broadcast_to(inv, (tok, tok)).T[:, 0:1]
+        value = chunks[len(ready) + i][...].astype(F32) * column * gain_ref[0:1, :]
+        scratch[i] = value.astype(BF16)
+        copies.append(put(scratch.at[i], k))
     for copy in copies:
         copy.wait()
 
 
-def finish(chunks):
-    tok, width = chunks[0].shape
-    return pl.pallas_call(
-        finish_body,
-        out_shape=jax.ShapeDtypeStruct((tok * len(chunks), width), BF16),
-        in_specs=[vmem()] * len(chunks),
+def finish(ready, raw, sums, gain, feat_width):
+    first = next(iter(ready.values()))
+    tok, width = first.shape
+    ways = len(ready) + len(raw)
+    return pl.pallas_call(
+        functools.partial(finish_body, feat_width, tuple(ready), tuple(raw)),
+        out_shape=jax.ShapeDtypeStruct((tok * ways, width), BF16),
+        in_specs=[vmem()] * (ways + len(raw) + 1),
         out_specs=pl.BlockSpec(memory_space=pltpu.HBM),
-        scratch_shapes=[pltpu.SemaphoreType.DMA((len(chunks),))],
+        scratch_shapes=[
+            pltpu.VMEM((len(raw), tok, width), BF16),
+            pltpu.SemaphoreType.DMA((ways,)),
+        ],
         name="finish",
         cost_estimate=pl.CostEstimate(flops=10**6, transcendentals=0, bytes_accessed=10**6),
-        compiler_params=pltpu.CompilerParams(vmem_limit_bytes=4 * 2**20),
-    )(*chunks)
+        compiler_params=pltpu.CompilerParams(vmem_limit_bytes=8 * 2**20),
+    )(*ready.values(), *raw.values(), *[sums[k] for k in raw], gain)
 
 
 def swap(value, axis, offset):
@@ -489,11 +482,9 @@
         select_away, weights, begun, part, gain_late, [got_late[k] for k in away], chunk,
         feat_width,
     )
-    chunks = swap_each(dict(zip(late, rest)), "dp")
+    ready = swap_each(dict(zip(late, rest)), "dp")
     sums = swap_each({k: total for k in early}, "dp")
-    for k in early:
-        chunks[k] = scale(raw[k], sums[k], gain_own, feat_width)
-    return finish([chunks[k] for k in range(ways)])[None]
+    return finish(ready, raw, sums, gain_own, feat_width)[None]
 
 
 def solution(mesh):

time: 61.6 us -> 62.2 us (level)
    ppermute x20, waiting for transfers between devices: 20.4 us -> 21 us  [swap(): return lax.ppermute(value, axis, [(i, i ^ offset) for i in range(size)])]
  transfers between devices with their start and end apart: 20 -> 20, of which waited for: 5 -> 5; matrix products, arithmetic and copies ran while one was open for 0% -> 0% of each run, Pallas kernels for 12% -> 11%
where the time goes in v8:
time: 62.2 us; the launch traced here: 61.9 us
  starting transfers between devices  25.4 us (41%)
  waiting for transfers between devices  21 us (34%)
  Pallas kernels  9.86 us (16%)
  local copies, waits for them, and re-layouts  5.47 us (9%)
    ppermute x20, starting transfers between devices, swap(): return lax.ppermute(value, axis, [(i, i ^ offset) for i in range(size)])  25.4 us
    ppermute x20, waiting for transfers between devices, swap(): return lax.ppermute(value, axis, [(i, i ^ offset) for i in range(size)])  21 us
    unnamed x18, local copies, waits for them, and re-layouts  5.47 us
    pallas_call x2, Pallas kernels, expert_call(): pl.pallas_call(functools.partial(expert_body, count, chunk, plan), out_sh...  4.75 us
    pallas_call x1, Pallas kernels, dispatch(): pl.pallas_call(functools.partial(dispatch_body, experts, capacity), out_s...  1.57 us
  transfers between devices with their start and end apart: 20, of which 5 were waited for; matrix products, arithmetic and copies ran while one was open for 0% of the time, Pallas kernels for 11%

profile of v8, /device:TPU:0, one launch (start us, length us, event | category | flops | bytes accessed | tf_op | source)
XLA Modules:
  0.0 61.9 jit_solution(12367586391587581363)
XLA Ops:
  0.0 1.6 %dispatch.1 = (bf16[40,2048]{1,0:T(8,128)(2,1)S(1)}, bf16[40,2048]{1,0:T(8,128)(2,1)S(1)}, bf16[40,2048]{1,0:T(8,128)(2,1)S(1)}, bf16[40,2048]{1,0:T(8,128)(2,1)...) custom-call(s32[2,128]{1,0:T(2,128)} %bitcast.25, ...), custom_call_target="tpu_custom_call" | custom-call | flops 100000000 | bytes 2000000 | tf_op jit(solution)/shard_map/dispatch/pallas_call | solution.py:122
  1.6 3.1 %collective-permute-start = (bf16[40,2048]{1,0:T(8,128)(2,1)S(1)}, bf16[40,2048]{1,0:T(8,128)(2,1)S(1)}, u32[]{:S(2)}, u32[]{:S(2)}) collective-permute-start(bf16[40,2048]{1,0:T(8,128)(2,1)S(1)} %get-tuple-element.37), channel_id=1, source_target_pairs={{0,4},{1,5},{2,6},{3,7},{4,0},{5,1},{6,2},{7,3},{8,12},{9,13},{10,... | collective-permute-start | bytes 491528 | tf_op jit(solution)/shard_map/ppermute | solution.py:427
  4.6 1.5 %collective-permute-start.1 = (bf16[40,2048]{1,0:T(8,128)(2,1)S(1)}, bf16[40,2048]{1,0:T(8,128)(2,1)S(1)}, u32[]{:S(2)}, u32[]{:S(2)}) collective-permute-start(bf16[40,2048]{1,0:T(8,128)(2,1)S(1)} %get-tuple-element.38), channel_id=1, source_target_pairs={{0,2},{1,3},{2,0},{3,1},{4,6},{5,7},{6,4},{7,5},{8,10},{9,11},{10,... | collective-permute-start | bytes 491528 | tf_op jit(solution)/shard_map/ppermute | solution.py:427
  6.1 0.0 collective-permute-start.2
  6.1 0.3 collective-permute-start.3
  6.5 0.3 collective-permute-start.4
  6.8 2.3 %collective-permute-done.refs_0_ = bf16[40,2048]{1,0:T(8,128)(2,1)S(1)} collective-permute-done((bf16[40,2048]{1,0:T(8,128)(2,1)S(1)}, bf16[40,2048]{1,0:T(8,128)(2,1)S(1)}, u32[]{:S(2)}, u32[]{:S(2)}) %collective-permute-start) | collective-permute-done | bytes 163872 | tf_op jit(solution)/shard_map/ppermute | solution.py:427
  9.1 3.6 %collective-permute-start.10 = (bf16[40,2048]{1,0:T(8,128)(2,1)S(1)}, bf16[40,2048]{1,0:T(8,128)(2,1)S(1)}, u32[]{:S(2)}, u32[]{:S(2)}) collective-permute-start(bf16[40,2048]{1,0:T(8,128)(2,1)S(1)} %get-tuple-element.50), channel_id=1, source_target_pairs={{0,6},{1,7},{2,4},{3,5},{4,2},{5,3},{6,0},{7,1},{8,14},{9,15},{10,... | collective-permute-start | bytes 491528 | tf_op jit(solution)/shard_map/ppermute | solution.py:427
  12.6 0.0 collective-permute-done.1.refs_1_
  12.6 0.0 collective-permute-start.11
  12.6 0.0 collective-permute-done.2.refs_2_
  12.7 1.6 %collective-permute-done.3.refs_3_ = bf16[40,2048]{1,0:T(8,128)(2,1)S(1)} collective-permute-done((bf16[40,2048]{1,0:T(8,128)(2,1)S(1)}, bf16[40,2048]{1,0:T(8,128)(2,1)S(1)}, u32[]{:S(2)}, u32[]{:S(2)}) %collective-permute-start.3) | collective-permute-done | bytes 163872 | tf_op jit(solution)/shard_map/ppermute | solution.py:427
  14.2 0.0 collective-permute-done.4.refs_4_
  14.2 0.0 copy-start
  14.2 1.8 %copy-done = bf16[1,704,2048]{2,1,0:T(8,128)(2,1)S(1)} copy-done((bf16[1,704,2048]{2,1,0:T(8,128)(2,1)S(1)}, bf16[1,704,2048]{2,1,0:T(8,128)(2,1)}, u32[]{:S(2)}) %copy-start) | copy-done | bytes 2883608
  16.1 0.0 copy-start.2
  16.1 1.8 %copy-done.2 = bf16[1,2048,704]{1,2,0:T(8,128)(2,1)S(1)} copy-done((bf16[1,2048,704]{1,2,0:T(8,128)(2,1)S(1)}, bf16[1,2048,704]{1,2,0:T(8,128)(2,1)}, u32[]{:S(2)}) %copy-start.2) | copy-done | bytes 2883608
  17.9 0.0 copy-start.4
  17.9 1.8 %copy-done.4 = bf16[1,2048,704]{1,2,0:T(8,128)(2,1)S(1)} copy-done((bf16[1,2048,704]{1,2,0:T(8,128)(2,1)S(1)}, bf16[1,2048,704]{1,2,0:T(8,128)(2,1)}, u32[]{:S(2)}) %copy-start.4) | copy-done | bytes 2883608
  19.7 2.7 %shard_map.82 = (bf16[240,704]{1,0:T(8,128)(2,1)}, bf16[40,2048]{1,0:T(8,128)(2,1)S(1)}, bf16[40,2048]{1,0:T(8,128)(2,1)S(1)}, bf16[40,2048]{1,0:T(8,128)(2,1)S(...) custom-call(bf16[40,2048]{1,0:T(8,128)(2,1)S(1)} %collective-permute-done.refs_0_, ...), custom_call_target="tpu_custom_call" | custom-call | flops 1730150400 | bytes 8000000 | tf_op jit(solution)/shard_map/pallas_call | solution.py:219
  22.4 0.9 %collective-permute-start.5 = (bf16[40,2048]{1,0:T(8,128)(2,1)S(1)}, bf16[40,2048]{1,0:T(8,128)(2,1)S(1)}, u32[]{:S(2)}, u32[]{:S(2)}) collective-permute-start(bf16[40,2048]{1,0:T(8,128)(2,1)S(1)} %get-tuple-element.44), channel_id=1, source_target_pairs={{0,1},{1,0},{2,3},{3,2},{4,5},{5,4},{6,7},{7,6},{8,9},{9,8},{10,11... | collective-permute-start | bytes 491528 | tf_op jit(solution)/shard_map/ppermute | solution.py:427
  23.3 1.7 %collective-permute-start.6 = (bf16[40,2048]{1,0:T(8,128)(2,1)S(1)}, bf16[40,2048]{1,0:T(8,128)(2,1)S(1)}, u32[]{:S(2)}, u32[]{:S(2)}) collective-permute-start(bf16[40,2048]{1,0:T(8,128)(2,1)S(1)} %get-tuple-element.45), channel_id=1, source_target_pairs={{0,2},{1,3},{2,0},{3,1},{4,6},{5,7},{6,4},{7,5},{8,10},{9,11},{10,... | collective-permute-start | bytes 491528 | tf_op jit(solution)/shard_map/ppermute | solution.py:427
  25.0 0.0 collective-permute-done.10.refs_0_
  25.0 0.0 collective-permute-done.11.refs_1_
  25.0 0.0 copy-done.1
  25.0 0.0 copy-done.3
  25.0 2.0 %shard_map.83 = (bf16[80,704]{1,0:T(8,128)(2,1)S(1)}, bf16[40,512]{1,0:T(8,128)(2,1)S(1)}, bf16[40,512]{1,0:T(8,128)(2,1)S(1)}) custom-call(bf16[40,2048]{1,0:T(8,128)(2,1)S(1)} %collective-permute-done.10.refs_0_, bf16[40,2048]{1,0:T(8,128)(2,1)S(1)} %collective-permute-done.11.refs_1_, bf16[704,2048]{1,0:T(8,128)(2,1)S(1)} %bitcast.20, ...), custom_call_target="tpu_custom_call" | custom-call | flops 576716800 | bytes 8000000 | tf_op jit(solution)/shard_map/pallas_call | solution.py:219
  27.1 0.0 copy-start.6
  27.1 0.0 copy-start.7
  27.1 0.0 copy-start.8
  27.1 0.1 collective-permute-start.12
  27.2 2.0 %collective-permute-start.13 = (bf16[40,512]{1,0:T(8,128)(2,1)S(1)}, bf16[40,512]{1,0:T(8,128)(2,1)S(1)}, u32[]{:S(2)}, u32[]{:S(2)}) collective-permute-start(bf16[40,512]{1,0:T(8,128)(2,1)S(1)} %get-tuple-element.53), channel_id=1, source_target_pairs={{0,7},{1,6},{2,5},{3,4},{4,3},{5,2},{6,1},{7,0},{8,15},{9,14},{10,... | collective-permute-start | bytes 122888 | tf_op jit(solution)/shard_map/ppermute | solution.py:427
  29.1 1.0 %collective-permute-start.7 = (bf16[40,2048]{1,0:T(8,128)(2,1)S(1)}, bf16[40,2048]{1,0:T(8,128)(2,1)S(1)}, u32[]{:S(2)}, u32[]{:S(2)}) collective-permute-start(bf16[40,2048]{1,0:T(8,128)(2,1)S(1)} %get-tuple-element.46), channel_id=1, source_target_pairs={{0,3},{1,2},{2,1},{3,0},{4,7},{5,6},{6,5},{7,4},{8,11},{9,10},{10,... | collective-permute-start | bytes 491528 | tf_op jit(solution)/shard_map/ppermute | solution.py:427
  30.1 0.5 shard_map.85
  30.6 1.9 %collective-permute-done.12.refs_6_ = bf16[40,512]{1,0:T(8,128)(2,1)S(1)} collective-permute-done((bf16[40,512]{1,0:T(8,128)(2,1)S(1)}, bf16[40,512]{1,0:T(8,128)(2,1)S(1)}, u32[]{:S(2)}, u32[]{:S(2)}) %collective-permute-start.12) | collective-permute-done | bytes 40992 | tf_op jit(solution)/shard_map/ppermute | solution.py:427
  32.5 0.0 collective-permute-start.8
  32.5 0.0 collective-permute-done.13.refs_7_
  32.5 0.2 collective-permute-start.9
  32.7 0.0 collective-permute-done.5.refs_1_
  32.7 1.8 %collective-permute-start.14 = (bf16[40,1536]{1,0:T(8,128)(2,1)S(1)}, bf16[40,1536]{1,0:T(8,128)(2,1)S(1)}, u32[]{:S(2)}, u32[]{:S(2)}) collective-permute-start(bf16[40,1536]{1,0:T(8,128)(2,1)S(1)} %get-tuple-element.56), channel_id=1, source_target_pairs={{0,6},{1,7},{2,4},{3,5},{4,2},{5,3},{6,0},{7,1},{8,14},{9,15},{10,... | collective-permute-start | bytes 368648 | tf_op jit(solution)/shard_map/ppermute | solution.py:427
  34.5 0.0 collective-permute-done.6.refs_2_
  34.5 2.4 %collective-permute-start.15 = (bf16[40,1536]{1,0:T(8,128)(2,1)S(1)}, bf16[40,1536]{1,0:T(8,128)(2,1)S(1)}, u32[]{:S(2)}, u32[]{:S(2)}) collective-permute-start(bf16[40,1536]{1,0:T(8,128)(2,1)S(1)} %get-tuple-element.57), channel_id=1, source_target_pairs={{0,7},{1,6},{2,5},{3,4},{4,3},{5,2},{6,1},{7,0},{8,15},{9,14},{10,... | collective-permute-start | bytes 368648 | tf_op jit(solution)/shard_map/ppermute | solution.py:427
  36.9 0.0 copy-done.6
  36.9 0.0 copy-done.7
  36.9 0.0 copy-done.8
  36.9 0.9 %selector.1 = (bf16[256,320]{1,0:T(8,128)(2,1)S(1)}, bf16[256,240]{1,0:T(8,128)(2,1)S(1)}, bf16[256,80]{1,0:T(8,128)(2,1)S(1)}, f32[2,128,128]{2,1,0:T(8,128)S(1)}) custom-call(s32[2,128]{1,0:T(2,128)S(1)} %bitcast.26, s32[2,128]{1,0:T(2,128)S(1)} %bitcast.27, f32[16]{0:T(128)S(1)} %copy-done.8), custom_call_target="tpu_custom_call" | custom-call | flops 20000000000 | bytes 100000000 | tf_op jit(solution)/shard_map/selector/pallas_call | solution.py:165
  37.8 0.0 copy-done.5
  37.8 0.0 collective-permute-done.7.refs_3_
  37.8 6.4 %collective-permute-done.8.refs_4_ = bf16[40,2048]{1,0:T(8,128)(2,1)S(1)} collective-permute-done((bf16[40,2048]{1,0:T(8,128)(2,1)S(1)}, bf16[40,2048]{1,0:T(8,128)(2,1)S(1)}, u32[]{:S(2)}, u32[]{:S(2)}) %collective-permute-start.8) | collective-permute-done | bytes 163872 | tf_op jit(solution)/shard_map/ppermute | solution.py:427
  44.3 0.0 collective-permute-done.9.refs_5_
  44.3 0.3 combine_early.1
  44.6 0.4 combine_mid.1.begun_ref
  45.0 0.0 collective-permute-done.14.refs_0_
  45.0 0.0 collective-permute-done.15.refs_1_
  45.0 0.6 combine_late.1
  45.6 3.7 %collective-permute-start.16 = (bf16[128,512]{1,0:T(8,128)(2,1)S(1)}, bf16[128,512]{1,0:T(8,128)(2,1)S(1)}, u32[]{:S(2)}, u32[]{:S(2)}) collective-permute-start(bf16[128,512]{1,0:T(8,128)(2,1)S(1)} %get-tuple-element.58), channel_id=1, source_target_pairs={{0,24},{8,16},{16,8},{24,0},{1,25},{9,17},{17,9},{25,1},{2,26},{10... | collective-permute-start | bytes 393224 | tf_op jit(solution)/shard_map/ppermute | solution.py:427
  49.2 0.0 collective-permute-start.17
  49.2 0.8 %collective-permute-start.18 = (bf16[128,512]{1,0:T(8,128)(2,1)S(1)}, bf16[128,512]{1,0:T(8,128)(2,1)S(1)}, u32[]{:S(2)}, u32[]{:S(2)}) collective-permute-start(bf16[128,512]{1,0:T(8,128)(2,1)S(1)} %get-tuple-element.61), channel_id=1, source_target_pairs={{0,16},{8,24},{16,0},{24,8},{1,17},{9,25},{17,1},{25,9},{2,18},{10... | collective-permute-start | bytes 393224 | tf_op jit(solution)/shard_map/ppermute | solution.py:427
  50.0 2.1 %collective-permute-start.19 = (f32[8,128]{1,0:T(8,128)S(1)}, f32[8,128]{1,0:T(8,128)S(1)}, u32[]{:S(2)}, u32[]{:S(2)}) collective-permute-start(f32[8,128]{1,0:T(8,128)S(1)} %get-tuple-element.62), channel_id=1, source_target_pairs={{0,16},{8,24},{16,0},{24,8},{1,17},{9,25},{17,1},{25,9},{2,18},{10... | collective-permute-start | bytes 12296 | tf_op jit(solution)/shard_map/ppermute | solution.py:427
  52.2 8.9 %collective-permute-done.19.refs_4_ = f32[8,128]{1,0:T(8,128)S(1)} collective-permute-done((f32[8,128]{1,0:T(8,128)S(1)}, f32[8,128]{1,0:T(8,128)S(1)}, u32[]{:S(2)}, u32[]{:S(2)}) %collective-permute-start.19) | collective-permute-done | bytes 4128 | tf_op jit(solution)/shard_map/ppermute | solution.py:427
  61.0 0.0 collective-permute-done.16.refs_0_
  61.0 0.0 collective-permute-done.17.refs_1_
  61.0 0.0 collective-permute-done.18.refs_3_
  61.0 0.9 %finish.1 = bf16[512,512]{1,0:T(8,128)(2,1)} custom-call(bf16[128,512]{1,0:T(8,128)(2,1)S(1)} %collective-permute-done.16.refs_0_, bf16[128,512]{1,0:T(8,128)(2,1)S(1)} %collective-permute-done.17.refs_1_, bf16[128,512]{1,0:T(8,128)(2,1)S(1)} %get-tuple-element.60.refs_2_, bf16[128,512]{1,0:T(8,128)(2,1)S(1)} %collective-permute-done.18.refs_3_, ...), custom_call_target="tpu_custom_call" | custom-call | flops 1000000 | bytes 1000000 | tf_op jit(solution)/shard_map/finish/pallas_call | solution.py:410
  (5 shorter events, 0.0 us)
Async XLA Ops:
  1.6 7.5 %collective-permute-start = (bf16[40,2048]{1,0:T(8,128)(2,1)S(1)}, bf16[40,2048]{1,0:T(8,128)(2,1)S(1)}, u32[]{:S(2)}, u32[]{:S(2)}) collective-permute-start(bf16[40,2048]{1,0:T(8,128)(2,1)S(1)} %get-tuple-element.37), channel_id=1, source_target_pairs={{0,4},{1,5},{2,6},{3,7},{4,0},{5,1},{6,2},{7,3},{8,12},{9,13},{10,... | collective-permute-start | bytes 491528 | tf_op jit(solution)/shard_map/ppermute | solution.py:427
  4.6 8.0 %collective-permute-start.1 = (bf16[40,2048]{1,0:T(8,128)(2,1)S(1)}, bf16[40,2048]{1,0:T(8,128)(2,1)S(1)}, u32[]{:S(2)}, u32[]{:S(2)}) collective-permute-start(bf16[40,2048]{1,0:T(8,128)(2,1)S(1)} %get-tuple-element.38), channel_id=1, source_target_pairs={{0,2},{1,3},{2,0},{3,1},{4,6},{5,7},{6,4},{7,5},{8,10},{9,11},{10,... | collective-permute-start | bytes 491528 | tf_op jit(solution)/shard_map/ppermute | solution.py:427
  6.1 6.5 %collective-permute-start.2 = (bf16[40,2048]{1,0:T(8,128)(2,1)S(1)}, bf16[40,2048]{1,0:T(8,128)(2,1)S(1)}, u32[]{:S(2)}, u32[]{:S(2)}) collective-permute-start(bf16[40,2048]{1,0:T(8,128)(2,1)S(1)} %get-tuple-element.39), channel_id=1, source_target_pairs={{0,5},{1,4},{2,7},{3,6},{4,1},{5,0},{6,3},{7,2},{8,13},{9,12},{10,... | collective-permute-start | bytes 491528 | tf_op jit(solution)/shard_map/ppermute | solution.py:427
  6.1 8.1 %collective-permute-start.3 = (bf16[40,2048]{1,0:T(8,128)(2,1)S(1)}, bf16[40,2048]{1,0:T(8,128)(2,1)S(1)}, u32[]{:S(2)}, u32[]{:S(2)}) collective-permute-start(bf16[40,2048]{1,0:T(8,128)(2,1)S(1)} %get-tuple-element.40), channel_id=1, source_target_pairs={{0,3},{1,2},{2,1},{3,0},{4,7},{5,6},{6,5},{7,4},{8,11},{9,10},{10,... | collective-permute-start | bytes 491528 | tf_op jit(solution)/shard_map/ppermute | solution.py:427
  6.5 7.8 %collective-permute-start.4 = (bf16[40,2048]{1,0:T(8,128)(2,1)S(1)}, bf16[40,2048]{1,0:T(8,128)(2,1)S(1)}, u32[]{:S(2)}, u32[]{:S(2)}) collective-permute-start(bf16[40,2048]{1,0:T(8,128)(2,1)S(1)} %get-tuple-element.41), channel_id=1, source_target_pairs={{0,1},{1,0},{2,3},{3,2},{4,5},{5,4},{6,7},{7,6},{8,9},{9,8},{10,11... | collective-permute-start | bytes 491528 | tf_op jit(solution)/shard_map/ppermute | solution.py:427
  9.1 15.9 %collective-permute-start.10 = (bf16[40,2048]{1,0:T(8,128)(2,1)S(1)}, bf16[40,2048]{1,0:T(8,128)(2,1)S(1)}, u32[]{:S(2)}, u32[]{:S(2)}) collective-permute-start(bf16[40,2048]{1,0:T(8,128)(2,1)S(1)} %get-tuple-element.50), channel_id=1, source_target_pairs={{0,6},{1,7},{2,4},{3,5},{4,2},{5,3},{6,0},{7,1},{8,14},{9,15},{10,... | collective-permute-start | bytes 491528 | tf_op jit(solution)/shard_map/ppermute | solution.py:427
  12.6 12.4 %collective-permute-start.11 = (bf16[40,2048]{1,0:T(8,128)(2,1)S(1)}, bf16[40,2048]{1,0:T(8,128)(2,1)S(1)}, u32[]{:S(2)}, u32[]{:S(2)}) collective-permute-start(bf16[40,2048]{1,0:T(8,128)(2,1)S(1)} %get-tuple-element.51), channel_id=1, source_target_pairs={{0,7},{1,6},{2,5},{3,4},{4,3},{5,2},{6,1},{7,0},{8,15},{9,14},{10,... | collective-permute-start | bytes 491528 | tf_op jit(solution)/shard_map/ppermute | solution.py:427
  14.2 1.8 %copy-start = (bf16[1,704,2048]{2,1,0:T(8,128)(2,1)S(1)}, bf16[1,704,2048]{2,1,0:T(8,128)(2,1)}, u32[]{:S(2)}) copy-start(bf16[1,704,2048]{2,1,0:T(8,128)(2,1)} %param.14) | copy-start | bytes 8650756
  16.1 1.8 %copy-start.2 = (bf16[1,2048,704]{1,2,0:T(8,128)(2,1)S(1)}, bf16[1,2048,704]{1,2,0:T(8,128)(2,1)}, u32[]{:S(2)}) copy-start(bf16[1,2048,704]{1,2,0:T(8,128)(2,1)} %param.12) | copy-start | bytes 8650756
  17.9 1.8 %copy-start.4 = (bf16[1,2048,704]{1,2,0:T(8,128)(2,1)S(1)}, bf16[1,2048,704]{1,2,0:T(8,128)(2,1)}, u32[]{:S(2)}) copy-start(bf16[1,2048,704]{1,2,0:T(8,128)(2,1)} %param.13) | copy-start | bytes 8650756
  19.7 5.3 %copy-start.1 = (bf16[1,704,2048]{2,1,0:T(8,128)(2,1)S(1)}, bf16[1,704,2048]{2,1,0:T(8,128)(2,1)}, u32[]{:S(2)}) copy-start(bf16[1,704,2048]{2,1,0:T(8,128)(2,1)} %param.14) | copy-start | bytes 8650756
  19.7 5.3 %copy-start.3 = (bf16[1,2048,704]{1,2,0:T(8,128)(2,1)S(1)}, bf16[1,2048,704]{1,2,0:T(8,128)(2,1)}, u32[]{:S(2)}) copy-start(bf16[1,2048,704]{1,2,0:T(8,128)(2,1)} %param.12) | copy-start | bytes 8650756
  22.4 10.3 %collective-permute-start.5 = (bf16[40,2048]{1,0:T(8,128)(2,1)S(1)}, bf16[40,2048]{1,0:T(8,128)(2,1)S(1)}, u32[]{:S(2)}, u32[]{:S(2)}) collective-permute-start(bf16[40,2048]{1,0:T(8,128)(2,1)S(1)} %get-tuple-element.44), channel_id=1, source_target_pairs={{0,1},{1,0},{2,3},{3,2},{4,5},{5,4},{6,7},{7,6},{8,9},{9,8},{10,11... | collective-permute-start | bytes 491528 | tf_op jit(solution)/shard_map/ppermute | solution.py:427
  23.3 11.2 %collective-permute-start.6 = (bf16[40,2048]{1,0:T(8,128)(2,1)S(1)}, bf16[40,2048]{1,0:T(8,128)(2,1)S(1)}, u32[]{:S(2)}, u32[]{:S(2)}) collective-permute-start(bf16[40,2048]{1,0:T(8,128)(2,1)S(1)} %get-tuple-element.45), channel_id=1, source_target_pairs={{0,2},{1,3},{2,0},{3,1},{4,6},{5,7},{6,4},{7,5},{8,10},{9,11},{10,... | collective-permute-start | bytes 491528 | tf_op jit(solution)/shard_map/ppermute | solution.py:427
  27.1 9.8 %copy-start.6 = (s32[1,128,2]{1,2,0:T(2,128)S(1)}, s32[1,128,2]{1,2,0:T(2,128)}, u32[]{:S(2)}) copy-start(s32[1,128,2]{1,2,0:T(2,128)} %param.9) | copy-start | bytes 3076
  27.1 9.8 %copy-start.7 = (s32[1,128,2]{1,2,0:T(2,128)S(1)}, s32[1,128,2]{1,2,0:T(2,128)}, u32[]{:S(2)}) copy-start(s32[1,128,2]{1,2,0:T(2,128)} %param.10) | copy-start | bytes 3076
  27.1 9.8 %copy-start.8 = (f32[16]{0:T(128)S(1)}, f32[16]{0:T(128)}, u32[]{:S(2)}) copy-start(f32[16]{0:T(128)} %table_ref.1) | copy-start | bytes 196
  27.1 5.4 %collective-permute-start.12 = (bf16[40,512]{1,0:T(8,128)(2,1)S(1)}, bf16[40,512]{1,0:T(8,128)(2,1)S(1)}, u32[]{:S(2)}, u32[]{:S(2)}) collective-permute-start(bf16[40,512]{1,0:T(8,128)(2,1)S(1)} %get-tuple-element.52), channel_id=1, source_target_pairs={{0,6},{1,7},{2,4},{3,5},{4,2},{5,3},{6,0},{7,1},{8,14},{9,15},{10,... | collective-permute-start | bytes 122888 | tf_op jit(solution)/shard_map/ppermute | solution.py:427
  27.2 5.3 %collective-permute-start.13 = (bf16[40,512]{1,0:T(8,128)(2,1)S(1)}, bf16[40,512]{1,0:T(8,128)(2,1)S(1)}, u32[]{:S(2)}, u32[]{:S(2)}) collective-permute-start(bf16[40,512]{1,0:T(8,128)(2,1)S(1)} %get-tuple-element.53), channel_id=1, source_target_pairs={{0,7},{1,6},{2,5},{3,4},{4,3},{5,2},{6,1},{7,0},{8,15},{9,14},{10,... | collective-permute-start | bytes 122888 | tf_op jit(solution)/shard_map/ppermute | solution.py:427
  29.1 8.7 %collective-permute-start.7 = (bf16[40,2048]{1,0:T(8,128)(2,1)S(1)}, bf16[40,2048]{1,0:T(8,128)(2,1)S(1)}, u32[]{:S(2)}, u32[]{:S(2)}) collective-permute-start(bf16[40,2048]{1,0:T(8,128)(2,1)S(1)} %get-tuple-element.46), channel_id=1, source_target_pairs={{0,3},{1,2},{2,1},{3,0},{4,7},{5,6},{6,5},{7,4},{8,11},{9,10},{10,... | collective-permute-start | bytes 491528 | tf_op jit(solution)/shard_map/ppermute | solution.py:427
  32.5 11.8 %collective-permute-start.8 = (bf16[40,2048]{1,0:T(8,128)(2,1)S(1)}, bf16[40,2048]{1,0:T(8,128)(2,1)S(1)}, u32[]{:S(2)}, u32[]{:S(2)}) collective-permute-start(bf16[40,2048]{1,0:T(8,128)(2,1)S(1)} %get-tuple-element.47), channel_id=1, source_target_pairs={{0,4},{1,5},{2,6},{3,7},{4,0},{5,1},{6,2},{7,3},{8,12},{9,13},{10,... | collective-permute-start | bytes 491528 | tf_op jit(solution)/shard_map/ppermute | solution.py:427
  32.5 11.8 %collective-permute-start.9 = (bf16[40,2048]{1,0:T(8,128)(2,1)S(1)}, bf16[40,2048]{1,0:T(8,128)(2,1)S(1)}, u32[]{:S(2)}, u32[]{:S(2)}) collective-permute-start(bf16[40,2048]{1,0:T(8,128)(2,1)S(1)} %get-tuple-element.48), channel_id=1, source_target_pairs={{0,5},{1,4},{2,7},{3,6},{4,1},{5,0},{6,3},{7,2},{8,13},{9,12},{10,... | collective-permute-start | bytes 491528 | tf_op jit(solution)/shard_map/ppermute | solution.py:427
  32.7 12.3 %collective-permute-start.14 = (bf16[40,1536]{1,0:T(8,128)(2,1)S(1)}, bf16[40,1536]{1,0:T(8,128)(2,1)S(1)}, u32[]{:S(2)}, u32[]{:S(2)}) collective-permute-start(bf16[40,1536]{1,0:T(8,128)(2,1)S(1)} %get-tuple-element.56), channel_id=1, source_target_pairs={{0,6},{1,7},{2,4},{3,5},{4,2},{5,3},{6,0},{7,1},{8,14},{9,15},{10,... | collective-permute-start | bytes 368648 | tf_op jit(solution)/shard_map/ppermute | solution.py:427
  34.5 10.5 %collective-permute-start.15 = (bf16[40,1536]{1,0:T(8,128)(2,1)S(1)}, bf16[40,1536]{1,0:T(8,128)(2,1)S(1)}, u32[]{:S(2)}, u32[]{:S(2)}) collective-permute-start(bf16[40,1536]{1,0:T(8,128)(2,1)S(1)} %get-tuple-element.57), channel_id=1, source_target_pairs={{0,7},{1,6},{2,5},{3,4},{4,3},{5,2},{6,1},{7,0},{8,15},{9,14},{10,... | collective-permute-start | bytes 368648 | tf_op jit(solution)/shard_map/ppermute | solution.py:427
  36.9 0.9 %copy-start.5 = (f32[2048]{0:T(1024)S(1)}, f32[2048]{0:T(1024)}, u32[]{:S(2)}) copy-start(f32[2048]{0:T(1024)} %param.15) | copy-start | bytes 24580
  45.6 15.5 %collective-permute-start.16 = (bf16[128,512]{1,0:T(8,128)(2,1)S(1)}, bf16[128,512]{1,0:T(8,128)(2,1)S(1)}, u32[]{:S(2)}, u32[]{:S(2)}) collective-permute-start(bf16[128,512]{1,0:T(8,128)(2,1)S(1)} %get-tuple-element.58), channel_id=1, source_target_pairs={{0,24},{8,16},{16,8},{24,0},{1,25},{9,17},{17,9},{25,1},{2,26},{10... | collective-permute-start | bytes 393224 | tf_op jit(solution)/shard_map/ppermute | solution.py:427
  49.2 11.8 %collective-permute-start.17 = (bf16[128,512]{1,0:T(8,128)(2,1)S(1)}, bf16[128,512]{1,0:T(8,128)(2,1)S(1)}, u32[]{:S(2)}, u32[]{:S(2)}) collective-permute-start(bf16[128,512]{1,0:T(8,128)(2,1)S(1)} %get-tuple-element.59), channel_id=1, source_target_pairs={{0,8},{8,0},{16,24},{24,16},{1,9},{9,1},{17,25},{25,17},{2,10},{10... | collective-permute-start | bytes 393224 | tf_op jit(solution)/shard_map/ppermute | solution.py:427
  49.2 11.8 %collective-permute-start.18 = (bf16[128,512]{1,0:T(8,128)(2,1)S(1)}, bf16[128,512]{1,0:T(8,128)(2,1)S(1)}, u32[]{:S(2)}, u32[]{:S(2)}) collective-permute-start(bf16[128,512]{1,0:T(8,128)(2,1)S(1)} %get-tuple-element.61), channel_id=1, source_target_pairs={{0,16},{8,24},{16,0},{24,8},{1,17},{9,25},{17,1},{25,9},{2,18},{10... | collective-permute-start | bytes 393224 | tf_op jit(solution)/shard_map/ppermute | solution.py:427
  50.0 11.0 %collective-permute-start.19 = (f32[8,128]{1,0:T(8,128)S(1)}, f32[8,128]{1,0:T(8,128)S(1)}, u32[]{:S(2)}, u32[]{:S(2)}) collective-permute-start(f32[8,128]{1,0:T(8,128)S(1)} %get-tuple-element.62), channel_id=1, source_target_pairs={{0,16},{8,24},{16,0},{24,8},{1,17},{9,25},{17,1},{25,9},{2,18},{10... | collective-permute-start | bytes 12296 | tf_op jit(solution)/shard_map/ppermute | solution.py:427

commit v9 on v8

--- a/solution.py
+++ b/solution.py
@@ -92,8 +92,17 @@
     return jnp.where(named, count.astype(jnp.int32), -1), ids
 
 
-def dispatch_body(experts, capacity, route_hbm, tok_hbm, *refs):
-    *out_refs, route_ref, tok_ref, sems = refs
+def pick_rows(pick_ref, tok_ref, out_refs):
+    capacity, tile = out_refs[0].shape[0], 256
+    for col in range(0, tok_ref.shape[1], tile):
+        rows = jnp.dot(pick_ref[...], tok_ref[:, col : col + tile], preferred_element_type=F32)
+        rows = rows.astype(BF16)
+        for j, out in enumerate(out_refs):
+            out[:, col : col + tile] = rows[j * capacity : (j + 1) * capacity, :]
+
+
+def dispatch_body(experts, first, others, route_hbm, tok_hbm, *refs):
+    *out_refs, rest_ref, tok_ref, pick_ref, route_ref, sems = refs
     copies = [
         pltpu.make_async_copy(route_hbm, route_ref, sems.at[0]),
         pltpu.make_async_copy(tok_hbm, tok_ref, sems.at[1]),
@@ -101,38 +110,56 @@
     for copy in copies:
         copy.start()
     me = lax.axis_index("expert")
-    tok, width = tok_ref.shape
+    capacity, tok = out_refs[0].shape[0], tok_ref.shape[0]
     lane = lax.broadcasted_iota(jnp.int32, (capacity, tok), 0)
     copies[0].wait()
     slots, _ = slot_rows(route_ref[...], experts, me)
-    pick = jnp.concatenate(
-        [(lane == slots[j : j + 1, :]).astype(F32) for j in range(experts)], axis=0
-    ).astype(BF16)
+    for ref, offsets in ((pick_ref, first), (rest_ref, others)):
+        for j, k in enumerate(offsets):
+            pick = (lane == slots[k : k + 1, :]).astype(F32).astype(BF16)
+            ref[j * capacity : (j + 1) * capacity, :] = pick
     copies[1].wait()
-    tile = 256
-    for col in range(0, width, tile):
-        rows = jnp.dot(pick, tok_ref[:, col : col + tile], preferred_element_type=F32)
-        rows = rows.astype(BF16)
-        for j in range(experts):
-            out_refs[j][:, col : col + tile] = rows[j * capacity : (j + 1) * capacity, :]
-
-
-def dispatch(route_rows, own_rows, experts, capacity):
-    width = own_rows.shape[1]
-    return pl.pallas_call(
-        functools.partial(dispatch_body, experts, capacity),
-        out_shape=[jax.ShapeDtypeStruct((capacity, width), BF16)] * experts,
+    pick_rows(pick_ref, tok_ref, out_refs)
+
+
+def dispatch(route_rows, own_rows, experts, capacity, first, others):
+    tok, width = own_rows.shape
+    *outs, rest, held = pl.pallas_call(
+        functools.partial(dispatch_body, experts, first, others),
+        out_shape=[jax.ShapeDtypeStruct((capacity, width), BF16)] * len(first)
+        + [
+            jax.ShapeDtypeStruct((capacity * len(others), tok), BF16),
+            jax.ShapeDtypeStruct((tok, width), BF16),
+        ],
         in_specs=[pl.BlockSpec(memory_space=pltpu.HBM)] * 2,
-        out_specs=[vmem()] * experts,
+        out_specs=[vmem()] * (len(first) + 2),
         scratch_shapes=[
+            pltpu.VMEM((capacity * len(first), tok), BF16),
             pltpu.VMEM(route_rows.shape, jnp.int32),
-            pltpu.VMEM(own_rows.shape, BF16),
             pltpu.SemaphoreType.DMA((2,)),
         ],
         name="dispatch",
         cost_estimate=pl.CostEstimate(flops=10**8, transcendentals=0, bytes_accessed=2 * 10**6),
         compiler_params=pltpu.CompilerParams(vmem_limit_bytes=16 * 2**20),
     )(route_rows, own_rows)
+    return dict(zip(first, outs)), rest, held
+
+
+def others_body(rest_ref, tok_ref, *out_refs):
+    pick_rows(rest_ref, tok_ref, out_refs)
+
+
+def dispatch_others(rest, held, capacity, others):
+    outs = pl.pallas_call(
+        others_body,
+        out_shape=[jax.ShapeDtypeStruct((capacity, held.shape[1]), BF16)] * len(others),
+        in_specs=[vmem()] * 2,
+        out_specs=[vmem()] * len(others),
+        name="others",
+        cost_estimate=pl.CostEstimate(flops=10**8, transcendentals=0, bytes_accessed=2 * 10**6),
+        compiler_params=pltpu.CompilerParams(vmem_limit_bytes=8 * 2**20),
+    )(rest, held)
+    return dict(zip(others, outs))
 
 
 def selector_body(experts, capacity, route_ref, code_ref, table_ref, *refs):
@@ -201,9 +228,14 @@
     for j, block in enumerate(blocks):
         x_ref[j * capacity : (j + 1) * capacity, :] = block[...]
     hid = gate_ref.shape[0]
+    over = (((1,), (1,)), ((), ()))
+    few = x_ref.shape[0] <= 128
+    if few:
+        gate = lax.dot_general(gate_ref[...], x_ref[...], over, preferred_element_type=F32)
+        up = lax.dot_general(up_ref[...], x_ref[...], over, preferred_element_type=F32)
+        hid_ref[...] = (gate / (1.0 + jnp.exp(-gate)) * up).T.astype(BF16)
     tile = 256
-    over = (((1,), (1,)), ((), ()))
-    for low in range(0, hid, tile):
+    for low in range(0, 0 if few else hid, tile):
         high = min(hid, low + tile)
         gate = lax.dot_general(x_ref[...], gate_ref[low:high, :], over, preferred_element_type=F32)
         up = lax.dot_general(x_ref[...], up_ref[low:high, :], over, preferred_element_type=F32)
@@ -450,11 +482,12 @@
     late = tuple(k for k in range(ways - 1, -1, -1) if k not in early)
 
     route_rows = routes[0].T
-    blocks = dispatch(
+    blocks, rest, held = dispatch(
         pltpu.with_memory_space_constraint(route_rows, pltpu.HBM),
         pltpu.with_memory_space_constraint(own_rows, pltpu.HBM),
-        experts, capacity,
-    )
+        experts, capacity, CLOSE[:4], CLOSE[4:] + [0] + AWAY,
+    )
+    blocks |= dispatch_others(rest, held, capacity, CLOSE[4:] + [0] + AWAY)
     near = swap_each({k: blocks[k] for k in close}, "expert")
     far = swap_each({k: blocks[k] for k in away}, "expert")
     select, select_close, select_away, weights = selector(route_rows, gate_code[0].T, gate_table, experts, capacity)

time: 62.2 us -> 62 us (level)
  waiting for transfers between devices: 21 us -> 20.1 us
  starting transfers between devices: 25.4 us -> 26.2 us
    ppermute x20, waiting for transfers between devices: 21 us -> 20.1 us  [swap(): return lax.ppermute(value, axis, [(i, i ^ offset) for i in range(size)])]
    ppermute x20, starting transfers between devices: 25.4 us -> 26.2 us  [swap(): return lax.ppermute(value, axis, [(i, i ^ offset) for i in range(size)])]
    pallas_call x1 -> x2, Pallas kernels: 1.57 us -> 1.73 us  [the longest x1 1.41 us: dispatch(): pl.pallas_call(functools.partial(dispatch_body, experts, first, others),...]
  transfers between devices with their start and end apart: 20 -> 20, of which waited for: 5 -> 7; matrix products, arithmetic and copies ran while one was open for 0% -> 0% of each run, Pallas kernels for 11% -> 11%
where the time goes in v9:
time: 62 us; the launch traced here: 61.8 us
  starting transfers between devices  26.2 us (42%)
  waiting for transfers between devices  20.1 us (32%)
  Pallas kernels  9.85 us (16%)
  local copies, waits for them, and re-layouts  5.47 us (9%)
    ppermute x20, starting transfers between devices, swap(): return lax.ppermute(value, axis, [(i, i ^ offset) for i in range(size)])  26.2 us
    ppermute x20, waiting for transfers between devices, swap(): return lax.ppermute(value, axis, [(i, i ^ offset) for i in range(size)])  20.1 us
    unnamed x18, local copies, waits for them, and re-layouts  5.47 us
    pallas_call x2, Pallas kernels, expert_call(): pl.pallas_call(functools.partial(expert_body, count, chunk, plan), out_sh...  4.57 us
    pallas_call x1, Pallas kernels, dispatch(): pl.pallas_call(functools.partial(dispatch_body, experts, first, others),...  1.41 us
  transfers between devices with their start and end apart: 20, of which 7 were waited for; matrix products, arithmetic and copies ran while one was open for 0% of the time, Pallas kernels for 11%

profile of v9, /device:TPU:0, one launch (start us, length us, event | category | flops | bytes accessed | tf_op | source)
XLA Modules:
  0.0 61.8 jit_solution(16356817667400340151)
XLA Ops:
  0.0 1.4 %dispatch.1 = (bf16[40,2048]{1,0:T(8,128)(2,1)S(1)}, bf16[40,2048]{1,0:T(8,128)(2,1)S(1)}, bf16[40,2048]{1,0:T(8,128)(2,1)S(1)}, bf16[40,2048]{1,0:T(8,128)(2,1)...) custom-call(s32[2,128]{1,0:T(2,128)} %bitcast.25, bf16[128,2048]{1,0:T(8,128)(2,1)} %bitcast.28), custom_call_target="tpu_custom_call" | custom-call | flops 100000000 | bytes 2000000 | tf_op jit(solution)/shard_map/dispatch/pallas_call | solution.py:127
  1.4 0.3 others.1
  1.7 0.6 collective-permute-start.4
  2.3 2.6 %collective-permute-start = (bf16[40,2048]{1,0:T(8,128)(2,1)S(1)}, bf16[40,2048]{1,0:T(8,128)(2,1)S(1)}, u32[]{:S(2)}, u32[]{:S(2)}) collective-permute-start(bf16[40,2048]{1,0:T(8,128)(2,1)S(1)} %get-tuple-element.39), channel_id=1, source_target_pairs={{0,4},{1,5},{2,6},{3,7},{4,0},{5,1},{6,2},{7,3},{8,12},{9,13},{10,... | collective-permute-start | bytes 491528 | tf_op jit(solution)/shard_map/ppermute | solution.py:459
  4.9 1.5 %collective-permute-start.1 = (bf16[40,2048]{1,0:T(8,128)(2,1)S(1)}, bf16[40,2048]{1,0:T(8,128)(2,1)S(1)}, u32[]{:S(2)}, u32[]{:S(2)}) collective-permute-start(bf16[40,2048]{1,0:T(8,128)(2,1)S(1)} %get-tuple-element.40), channel_id=1, source_target_pairs={{0,2},{1,3},{2,0},{3,1},{4,6},{5,7},{6,4},{7,5},{8,10},{9,11},{10,... | collective-permute-start | bytes 491528 | tf_op jit(solution)/shard_map/ppermute | solution.py:459
  6.4 0.0 collective-permute-start.2
  6.4 0.3 collective-permute-start.3
  6.7 0.0 collective-permute-done.4.refs_4_
  6.7 2.9 %collective-permute-start.10 = (bf16[40,2048]{1,0:T(8,128)(2,1)S(1)}, bf16[40,2048]{1,0:T(8,128)(2,1)S(1)}, u32[]{:S(2)}, u32[]{:S(2)}) collective-permute-start(bf16[40,2048]{1,0:T(8,128)(2,1)S(1)} %get-tuple-element.54), channel_id=1, source_target_pairs={{0,6},{1,7},{2,4},{3,5},{4,2},{5,3},{6,0},{7,1},{8,14},{9,15},{10,... | collective-permute-start | bytes 491528 | tf_op jit(solution)/shard_map/ppermute | solution.py:459
  9.6 0.3 collective-permute-done.refs_0_
  9.9 1.6 %collective-permute-start.11 = (bf16[40,2048]{1,0:T(8,128)(2,1)S(1)}, bf16[40,2048]{1,0:T(8,128)(2,1)S(1)}, u32[]{:S(2)}, u32[]{:S(2)}) collective-permute-start(bf16[40,2048]{1,0:T(8,128)(2,1)S(1)} %get-tuple-element.55), channel_id=1, source_target_pairs={{0,7},{1,6},{2,5},{3,4},{4,3},{5,2},{6,1},{7,0},{8,15},{9,14},{10,... | collective-permute-start | bytes 491528 | tf_op jit(solution)/shard_map/ppermute | solution.py:459
  11.5 0.4 collective-permute-done.1.refs_1_
  11.9 1.0 %collective-permute-done.2.refs_2_ = bf16[40,2048]{1,0:T(8,128)(2,1)S(1)} collective-permute-done((bf16[40,2048]{1,0:T(8,128)(2,1)S(1)}, bf16[40,2048]{1,0:T(8,128)(2,1)S(1)}, u32[]{:S(2)}, u32[]{:S(2)}) %collective-permute-start.2) | collective-permute-done | bytes 163872 | tf_op jit(solution)/shard_map/ppermute | solution.py:459
  12.9 1.6 %collective-permute-done.3.refs_3_ = bf16[40,2048]{1,0:T(8,128)(2,1)S(1)} collective-permute-done((bf16[40,2048]{1,0:T(8,128)(2,1)S(1)}, bf16[40,2048]{1,0:T(8,128)(2,1)S(1)}, u32[]{:S(2)}, u32[]{:S(2)}) %collective-permute-start.3) | collective-permute-done | bytes 163872 | tf_op jit(solution)/shard_map/ppermute | solution.py:459
  14.5 0.0 copy-start
  14.5 1.8 %copy-done = bf16[1,704,2048]{2,1,0:T(8,128)(2,1)S(1)} copy-done((bf16[1,704,2048]{2,1,0:T(8,128)(2,1)S(1)}, bf16[1,704,2048]{2,1,0:T(8,128)(2,1)}, u32[]{:S(2)}) %copy-start) | copy-done | bytes 2883608
  16.3 0.0 copy-start.2
  16.3 1.8 %copy-done.2 = bf16[1,2048,704]{1,2,0:T(8,128)(2,1)S(1)} copy-done((bf16[1,2048,704]{1,2,0:T(8,128)(2,1)S(1)}, bf16[1,2048,704]{1,2,0:T(8,128)(2,1)}, u32[]{:S(2)}) %copy-start.2) | copy-done | bytes 2883608
  18.1 1.8 %copy-done.4 = bf16[1,2048,704]{1,2,0:T(8,128)(2,1)S(1)} copy-done((bf16[1,2048,704]{1,2,0:T(8,128)(2,1)S(1)}, bf16[1,2048,704]{1,2,0:T(8,128)(2,1)}, u32[]{:S(2)}) %copy-start.4) | copy-done | bytes 2883608
  19.9 2.7 %shard_map.82 = (bf16[240,704]{1,0:T(8,128)(2,1)}, bf16[40,2048]{1,0:T(8,128)(2,1)S(1)}, bf16[40,2048]{1,0:T(8,128)(2,1)S(1)}, bf16[40,2048]{1,0:T(8,128)(2,1)S(...) custom-call(bf16[40,2048]{1,0:T(8,128)(2,1)S(1)} %collective-permute-done.refs_0_, ...), custom_call_target="tpu_custom_call" | custom-call | flops 1730150400 | bytes 8000000 | tf_op jit(solution)/shard_map/pallas_call | solution.py:251
  22.6 1.1 %collective-permute-start.5 = (bf16[40,2048]{1,0:T(8,128)(2,1)S(1)}, bf16[40,2048]{1,0:T(8,128)(2,1)S(1)}, u32[]{:S(2)}, u32[]{:S(2)}) collective-permute-start(bf16[40,2048]{1,0:T(8,128)(2,1)S(1)} %get-tuple-element.48), channel_id=1, source_target_pairs={{0,1},{1,0},{2,3},{3,2},{4,5},{5,4},{6,7},{7,6},{8,9},{9,8},{10,11... | collective-permute-start | bytes 491528 | tf_op jit(solution)/shard_map/ppermute | solution.py:459
  23.7 1.5 %collective-permute-start.6 = (bf16[40,2048]{1,0:T(8,128)(2,1)S(1)}, bf16[40,2048]{1,0:T(8,128)(2,1)S(1)}, u32[]{:S(2)}, u32[]{:S(2)}) collective-permute-start(bf16[40,2048]{1,0:T(8,128)(2,1)S(1)} %get-tuple-element.49), channel_id=1, source_target_pairs={{0,2},{1,3},{2,0},{3,1},{4,6},{5,7},{6,4},{7,5},{8,10},{9,11},{10,... | collective-permute-start | bytes 491528 | tf_op jit(solution)/shard_map/ppermute | solution.py:459
  25.2 0.0 collective-permute-done.10.refs_0_
  25.2 0.0 collective-permute-done.11.refs_1_
  25.2 0.0 copy-done.1
  25.2 0.0 copy-done.3
  25.3 1.9 %shard_map.83 = (bf16[80,704]{1,0:T(8,128)(2,1)S(1)}, bf16[40,512]{1,0:T(8,128)(2,1)S(1)}, bf16[40,512]{1,0:T(8,128)(2,1)S(1)}) custom-call(bf16[40,2048]{1,0:T(8,128)(2,1)S(1)} %collective-permute-done.10.refs_0_, bf16[40,2048]{1,0:T(8,128)(2,1)S(1)} %collective-permute-done.11.refs_1_, bf16[704,2048]{1,0:T(8,128)(2,1)S(1)} %bitcast.20, ...), custom_call_target="tpu_custom_call" | custom-call | flops 576716800 | bytes 8000000 | tf_op jit(solution)/shard_map/pallas_call | solution.py:251
  27.1 0.0 copy-start.6
  27.1 0.0 copy-start.7
  27.1 0.0 copy-start.8
  27.2 0.1 collective-permute-start.12
  27.2 2.0 %collective-permute-start.13 = (bf16[40,512]{1,0:T(8,128)(2,1)S(1)}, bf16[40,512]{1,0:T(8,128)(2,1)S(1)}, u32[]{:S(2)}, u32[]{:S(2)}) collective-permute-start(bf16[40,512]{1,0:T(8,128)(2,1)S(1)} %get-tuple-element.57), channel_id=1, source_target_pairs={{0,7},{1,6},{2,5},{3,4},{4,3},{5,2},{6,1},{7,0},{8,15},{9,14},{10,... | collective-permute-start | bytes 122888 | tf_op jit(solution)/shard_map/ppermute | solution.py:459
  29.2 1.2 %collective-permute-start.7 = (bf16[40,2048]{1,0:T(8,128)(2,1)S(1)}, bf16[40,2048]{1,0:T(8,128)(2,1)S(1)}, u32[]{:S(2)}, u32[]{:S(2)}) collective-permute-start(bf16[40,2048]{1,0:T(8,128)(2,1)S(1)} %get-tuple-element.50), channel_id=1, source_target_pairs={{0,3},{1,2},{2,1},{3,0},{4,7},{5,6},{6,5},{7,4},{8,11},{9,10},{10,... | collective-permute-start | bytes 491528 | tf_op jit(solution)/shard_map/ppermute | solution.py:459
  30.4 0.5 shard_map.85
  30.9 1.5 %collective-permute-done.12.refs_6_ = bf16[40,512]{1,0:T(8,128)(2,1)S(1)} collective-permute-done((bf16[40,512]{1,0:T(8,128)(2,1)S(1)}, bf16[40,512]{1,0:T(8,128)(2,1)S(1)}, u32[]{:S(2)}, u32[]{:S(2)}) %collective-permute-start.12) | collective-permute-done | bytes 40992 | tf_op jit(solution)/shard_map/ppermute | solution.py:459
  32.4 0.0 collective-permute-start.8
  32.4 0.0 collective-permute-done.13.refs_7_
  32.4 0.6 collective-permute-start.9
  33.0 0.0 collective-permute-done.5.refs_1_
  33.0 1.6 %collective-permute-start.14 = (bf16[40,1536]{1,0:T(8,128)(2,1)S(1)}, bf16[40,1536]{1,0:T(8,128)(2,1)S(1)}, u32[]{:S(2)}, u32[]{:S(2)}) collective-permute-start(bf16[40,1536]{1,0:T(8,128)(2,1)S(1)} %get-tuple-element.60), channel_id=1, source_target_pairs={{0,6},{1,7},{2,4},{3,5},{4,2},{5,3},{6,0},{7,1},{8,14},{9,15},{10,... | collective-permute-start | bytes 368648 | tf_op jit(solution)/shard_map/ppermute | solution.py:459
  34.6 0.0 collective-permute-done.6.refs_2_
  34.6 2.2 %collective-permute-start.15 = (bf16[40,1536]{1,0:T(8,128)(2,1)S(1)}, bf16[40,1536]{1,0:T(8,128)(2,1)S(1)}, u32[]{:S(2)}, u32[]{:S(2)}) collective-permute-start(bf16[40,1536]{1,0:T(8,128)(2,1)S(1)} %get-tuple-element.61), channel_id=1, source_target_pairs={{0,7},{1,6},{2,5},{3,4},{4,3},{5,2},{6,1},{7,0},{8,15},{9,14},{10,... | collective-permute-start | bytes 368648 | tf_op jit(solution)/shard_map/ppermute | solution.py:459
  36.8 0.0 copy-done.6
  36.8 0.0 copy-done.7
  36.8 0.0 copy-done.8
  36.8 0.9 %selector.1 = (bf16[256,320]{1,0:T(8,128)(2,1)S(1)}, bf16[256,240]{1,0:T(8,128)(2,1)S(1)}, bf16[256,80]{1,0:T(8,128)(2,1)S(1)}, f32[2,128,128]{2,1,0:T(8,128)S(1)}) custom-call(s32[2,128]{1,0:T(2,128)S(1)} %bitcast.26, s32[2,128]{1,0:T(2,128)S(1)} %bitcast.27, f32[16]{0:T(128)S(1)} %copy-done.8), custom_call_target="tpu_custom_call" | custom-call | flops 20000000000 | bytes 100000000 | tf_op jit(solution)/shard_map/selector/pallas_call | solution.py:192
  37.7 0.0 copy-done.5
  37.7 0.0 collective-permute-done.7.refs_3_
  37.7 6.4 %collective-permute-done.8.refs_4_ = bf16[40,2048]{1,0:T(8,128)(2,1)S(1)} collective-permute-done((bf16[40,2048]{1,0:T(8,128)(2,1)S(1)}, bf16[40,2048]{1,0:T(8,128)(2,1)S(1)}, u32[]{:S(2)}, u32[]{:S(2)}) %collective-permute-start.8) | collective-permute-done | bytes 163872 | tf_op jit(solution)/shard_map/ppermute | solution.py:459
  44.2 0.0 collective-permute-done.9.refs_5_
  44.2 0.3 combine_early.1
  44.5 0.4 combine_mid.1.begun_ref
  44.9 0.0 collective-permute-done.14.refs_0_
  44.9 0.0 collective-permute-done.15.refs_1_
  44.9 0.6 combine_late.1
  45.5 3.6 %collective-permute-start.16 = (bf16[128,512]{1,0:T(8,128)(2,1)S(1)}, bf16[128,512]{1,0:T(8,128)(2,1)S(1)}, u32[]{:S(2)}, u32[]{:S(2)}) collective-permute-start(bf16[128,512]{1,0:T(8,128)(2,1)S(1)} %get-tuple-element.62), channel_id=1, source_target_pairs={{0,24},{8,16},{16,8},{24,0},{1,25},{9,17},{17,9},{25,1},{2,26},{10... | collective-permute-start | bytes 393224 | tf_op jit(solution)/shard_map/ppermute | solution.py:459
  49.1 0.0 collective-permute-start.17
  49.1 0.8 %collective-permute-start.18 = (bf16[128,512]{1,0:T(8,128)(2,1)S(1)}, bf16[128,512]{1,0:T(8,128)(2,1)S(1)}, u32[]{:S(2)}, u32[]{:S(2)}) collective-permute-start(bf16[128,512]{1,0:T(8,128)(2,1)S(1)} %get-tuple-element.65), channel_id=1, source_target_pairs={{0,16},{8,24},{16,0},{24,8},{1,17},{9,25},{17,1},{25,9},{2,18},{10... | collective-permute-start | bytes 393224 | tf_op jit(solution)/shard_map/ppermute | solution.py:459
  49.9 2.1 %collective-permute-start.19 = (f32[8,128]{1,0:T(8,128)S(1)}, f32[8,128]{1,0:T(8,128)S(1)}, u32[]{:S(2)}, u32[]{:S(2)}) collective-permute-start(f32[8,128]{1,0:T(8,128)S(1)} %get-tuple-element.66), channel_id=1, source_target_pairs={{0,16},{8,24},{16,0},{24,8},{1,17},{9,25},{17,1},{25,9},{2,18},{10... | collective-permute-start | bytes 12296 | tf_op jit(solution)/shard_map/ppermute | solution.py:459
  52.1 8.8 %collective-permute-done.19.refs_4_ = f32[8,128]{1,0:T(8,128)S(1)} collective-permute-done((f32[8,128]{1,0:T(8,128)S(1)}, f32[8,128]{1,0:T(8,128)S(1)}, u32[]{:S(2)}, u32[]{:S(2)}) %collective-permute-start.19) | collective-permute-done | bytes 4128 | tf_op jit(solution)/shard_map/ppermute | solution.py:459
  60.9 0.0 collective-permute-done.16.refs_0_
  60.9 0.0 collective-permute-done.17.refs_1_
  60.9 0.0 collective-permute-done.18.refs_3_
  60.9 0.9 %finish.1 = bf16[512,512]{1,0:T(8,128)(2,1)} custom-call(bf16[128,512]{1,0:T(8,128)(2,1)S(1)} %collective-permute-done.16.refs_0_, bf16[128,512]{1,0:T(8,128)(2,1)S(1)} %collective-permute-done.17.refs_1_, bf16[128,512]{1,0:T(8,128)(2,1)S(1)} %get-tuple-element.64.refs_2_, bf16[128,512]{1,0:T(8,128)(2,1)S(1)} %collective-permute-done.18.refs_3_, ...), custom_call_target="tpu_custom_call" | custom-call | flops 1000000 | bytes 1000000 | tf_op jit(solution)/shard_map/finish/pallas_call | solution.py:442
  (6 shorter events, 0.0 us)
Async XLA Ops:
  1.7 5.0 %collective-permute-start.4 = (bf16[40,2048]{1,0:T(8,128)(2,1)S(1)}, bf16[40,2048]{1,0:T(8,128)(2,1)S(1)}, u32[]{:S(2)}, u32[]{:S(2)}) collective-permute-start(bf16[40,2048]{1,0:T(8,128)(2,1)S(1)} %get-tuple-element.45), channel_id=1, source_target_pairs={{0,1},{1,0},{2,3},{3,2},{4,5},{5,4},{6,7},{7,6},{8,9},{9,8},{10,11... | collective-permute-start | bytes 491528 | tf_op jit(solution)/shard_map/ppermute | solution.py:459
  2.3 7.6 %collective-permute-start = (bf16[40,2048]{1,0:T(8,128)(2,1)S(1)}, bf16[40,2048]{1,0:T(8,128)(2,1)S(1)}, u32[]{:S(2)}, u32[]{:S(2)}) collective-permute-start(bf16[40,2048]{1,0:T(8,128)(2,1)S(1)} %get-tuple-element.39), channel_id=1, source_target_pairs={{0,4},{1,5},{2,6},{3,7},{4,0},{5,1},{6,2},{7,3},{8,12},{9,13},{10,... | collective-permute-start | bytes 491528 | tf_op jit(solution)/shard_map/ppermute | solution.py:459
  4.9 7.1 %collective-permute-start.1 = (bf16[40,2048]{1,0:T(8,128)(2,1)S(1)}, bf16[40,2048]{1,0:T(8,128)(2,1)S(1)}, u32[]{:S(2)}, u32[]{:S(2)}) collective-permute-start(bf16[40,2048]{1,0:T(8,128)(2,1)S(1)} %get-tuple-element.40), channel_id=1, source_target_pairs={{0,2},{1,3},{2,0},{3,1},{4,6},{5,7},{6,4},{7,5},{8,10},{9,11},{10,... | collective-permute-start | bytes 491528 | tf_op jit(solution)/shard_map/ppermute | solution.py:459
  6.4 6.5 %collective-permute-start.2 = (bf16[40,2048]{1,0:T(8,128)(2,1)S(1)}, bf16[40,2048]{1,0:T(8,128)(2,1)S(1)}, u32[]{:S(2)}, u32[]{:S(2)}) collective-permute-start(bf16[40,2048]{1,0:T(8,128)(2,1)S(1)} %get-tuple-element.41), channel_id=1, source_target_pairs={{0,5},{1,4},{2,7},{3,6},{4,1},{5,0},{6,3},{7,2},{8,13},{9,12},{10,... | collective-permute-start | bytes 491528 | tf_op jit(solution)/shard_map/ppermute | solution.py:459
  6.4 8.1 %collective-permute-start.3 = (bf16[40,2048]{1,0:T(8,128)(2,1)S(1)}, bf16[40,2048]{1,0:T(8,128)(2,1)S(1)}, u32[]{:S(2)}, u32[]{:S(2)}) collective-permute-start(bf16[40,2048]{1,0:T(8,128)(2,1)S(1)} %get-tuple-element.42), channel_id=1, source_target_pairs={{0,3},{1,2},{2,1},{3,0},{4,7},{5,6},{6,5},{7,4},{8,11},{9,10},{10,... | collective-permute-start | bytes 491528 | tf_op jit(solution)/shard_map/ppermute | solution.py:459
  6.7 18.5 %collective-permute-start.10 = (bf16[40,2048]{1,0:T(8,128)(2,1)S(1)}, bf16[40,2048]{1,0:T(8,128)(2,1)S(1)}, u32[]{:S(2)}, u32[]{:S(2)}) collective-permute-start(bf16[40,2048]{1,0:T(8,128)(2,1)S(1)} %get-tuple-element.54), channel_id=1, source_target_pairs={{0,6},{1,7},{2,4},{3,5},{4,2},{5,3},{6,0},{7,1},{8,14},{9,15},{10,... | collective-permute-start | bytes 491528 | tf_op jit(solution)/shard_map/ppermute | solution.py:459
  9.9 15.3 %collective-permute-start.11 = (bf16[40,2048]{1,0:T(8,128)(2,1)S(1)}, bf16[40,2048]{1,0:T(8,128)(2,1)S(1)}, u32[]{:S(2)}, u32[]{:S(2)}) collective-permute-start(bf16[40,2048]{1,0:T(8,128)(2,1)S(1)} %get-tuple-element.55), channel_id=1, source_target_pairs={{0,7},{1,6},{2,5},{3,4},{4,3},{5,2},{6,1},{7,0},{8,15},{9,14},{10,... | collective-permute-start | bytes 491528 | tf_op jit(solution)/shard_map/ppermute | solution.py:459
  14.5 1.8 %copy-start = (bf16[1,704,2048]{2,1,0:T(8,128)(2,1)S(1)}, bf16[1,704,2048]{2,1,0:T(8,128)(2,1)}, u32[]{:S(2)}) copy-start(bf16[1,704,2048]{2,1,0:T(8,128)(2,1)} %param.14) | copy-start | bytes 8650756
  16.3 1.8 %copy-start.2 = (bf16[1,2048,704]{1,2,0:T(8,128)(2,1)S(1)}, bf16[1,2048,704]{1,2,0:T(8,128)(2,1)}, u32[]{:S(2)}) copy-start(bf16[1,2048,704]{1,2,0:T(8,128)(2,1)} %param.12) | copy-start | bytes 8650756
  18.1 1.8 %copy-start.4 = (bf16[1,2048,704]{1,2,0:T(8,128)(2,1)S(1)}, bf16[1,2048,704]{1,2,0:T(8,128)(2,1)}, u32[]{:S(2)}) copy-start(bf16[1,2048,704]{1,2,0:T(8,128)(2,1)} %param.13) | copy-start | bytes 8650756
  19.9 5.3 %copy-start.1 = (bf16[1,704,2048]{2,1,0:T(8,128)(2,1)S(1)}, bf16[1,704,2048]{2,1,0:T(8,128)(2,1)}, u32[]{:S(2)}) copy-start(bf16[1,704,2048]{2,1,0:T(8,128)(2,1)} %param.14) | copy-start | bytes 8650756
  19.9 5.3 %copy-start.3 = (bf16[1,2048,704]{1,2,0:T(8,128)(2,1)S(1)}, bf16[1,2048,704]{1,2,0:T(8,128)(2,1)}, u32[]{:S(2)}) copy-start(bf16[1,2048,704]{1,2,0:T(8,128)(2,1)} %param.12) | copy-start | bytes 8650756
  22.6 10.3 %collective-permute-start.5 = (bf16[40,2048]{1,0:T(8,128)(2,1)S(1)}, bf16[40,2048]{1,0:T(8,128)(2,1)S(1)}, u32[]{:S(2)}, u32[]{:S(2)}) collective-permute-start(bf16[40,2048]{1,0:T(8,128)(2,1)S(1)} %get-tuple-element.48), channel_id=1, source_target_pairs={{0,1},{1,0},{2,3},{3,2},{4,5},{5,4},{6,7},{7,6},{8,9},{9,8},{10,11... | collective-permute-start | bytes 491528 | tf_op jit(solution)/shard_map/ppermute | solution.py:459
  23.7 10.8 %collective-permute-start.6 = (bf16[40,2048]{1,0:T(8,128)(2,1)S(1)}, bf16[40,2048]{1,0:T(8,128)(2,1)S(1)}, u32[]{:S(2)}, u32[]{:S(2)}) collective-permute-start(bf16[40,2048]{1,0:T(8,128)(2,1)S(1)} %get-tuple-element.49), channel_id=1, source_target_pairs={{0,2},{1,3},{2,0},{3,1},{4,6},{5,7},{6,4},{7,5},{8,10},{9,11},{10,... | collective-permute-start | bytes 491528 | tf_op jit(solution)/shard_map/ppermute | solution.py:459
  27.1 9.7 %copy-start.6 = (s32[1,128,2]{1,2,0:T(2,128)S(1)}, s32[1,128,2]{1,2,0:T(2,128)}, u32[]{:S(2)}) copy-start(s32[1,128,2]{1,2,0:T(2,128)} %param.9) | copy-start | bytes 3076
  27.1 9.7 %copy-start.7 = (s32[1,128,2]{1,2,0:T(2,128)S(1)}, s32[1,128,2]{1,2,0:T(2,128)}, u32[]{:S(2)}) copy-start(s32[1,128,2]{1,2,0:T(2,128)} %param.10) | copy-start | bytes 3076
  27.1 9.7 %copy-start.8 = (f32[16]{0:T(128)S(1)}, f32[16]{0:T(128)}, u32[]{:S(2)}) copy-start(f32[16]{0:T(128)} %table_ref.1) | copy-start | bytes 196
  27.2 5.2 %collective-permute-start.12 = (bf16[40,512]{1,0:T(8,128)(2,1)S(1)}, bf16[40,512]{1,0:T(8,128)(2,1)S(1)}, u32[]{:S(2)}, u32[]{:S(2)}) collective-permute-start(bf16[40,512]{1,0:T(8,128)(2,1)S(1)} %get-tuple-element.56), channel_id=1, source_target_pairs={{0,6},{1,7},{2,4},{3,5},{4,2},{5,3},{6,0},{7,1},{8,14},{9,15},{10,... | collective-permute-start | bytes 122888 | tf_op jit(solution)/shard_map/ppermute | solution.py:459
  27.2 5.2 %collective-permute-start.13 = (bf16[40,512]{1,0:T(8,128)(2,1)S(1)}, bf16[40,512]{1,0:T(8,128)(2,1)S(1)}, u32[]{:S(2)}, u32[]{:S(2)}) collective-permute-start(bf16[40,512]{1,0:T(8,128)(2,1)S(1)} %get-tuple-element.57), channel_id=1, source_target_pairs={{0,7},{1,6},{2,5},{3,4},{4,3},{5,2},{6,1},{7,0},{8,15},{9,14},{10,... | collective-permute-start | bytes 122888 | tf_op jit(solution)/shard_map/ppermute | solution.py:459
  29.2 8.5 %collective-permute-start.7 = (bf16[40,2048]{1,0:T(8,128)(2,1)S(1)}, bf16[40,2048]{1,0:T(8,128)(2,1)S(1)}, u32[]{:S(2)}, u32[]{:S(2)}) collective-permute-start(bf16[40,2048]{1,0:T(8,128)(2,1)S(1)} %get-tuple-element.50), channel_id=1, source_target_pairs={{0,3},{1,2},{2,1},{3,0},{4,7},{5,6},{6,5},{7,4},{8,11},{9,10},{10,... | collective-permute-start | bytes 491528 | tf_op jit(solution)/shard_map/ppermute | solution.py:459
  32.4 11.8 %collective-permute-start.8 = (bf16[40,2048]{1,0:T(8,128)(2,1)S(1)}, bf16[40,2048]{1,0:T(8,128)(2,1)S(1)}, u32[]{:S(2)}, u32[]{:S(2)}) collective-permute-start(bf16[40,2048]{1,0:T(8,128)(2,1)S(1)} %get-tuple-element.51), channel_id=1, source_target_pairs={{0,4},{1,5},{2,6},{3,7},{4,0},{5,1},{6,2},{7,3},{8,12},{9,13},{10,... | collective-permute-start | bytes 491528 | tf_op jit(solution)/shard_map/ppermute | solution.py:459
  32.4 11.8 %collective-permute-start.9 = (bf16[40,2048]{1,0:T(8,128)(2,1)S(1)}, bf16[40,2048]{1,0:T(8,128)(2,1)S(1)}, u32[]{:S(2)}, u32[]{:S(2)}) collective-permute-start(bf16[40,2048]{1,0:T(8,128)(2,1)S(1)} %get-tuple-element.52), channel_id=1, source_target_pairs={{0,5},{1,4},{2,7},{3,6},{4,1},{5,0},{6,3},{7,2},{8,13},{9,12},{10,... | collective-permute-start | bytes 491528 | tf_op jit(solution)/shard_map/ppermute | solution.py:459
  33.0 11.9 %collective-permute-start.14 = (bf16[40,1536]{1,0:T(8,128)(2,1)S(1)}, bf16[40,1536]{1,0:T(8,128)(2,1)S(1)}, u32[]{:S(2)}, u32[]{:S(2)}) collective-permute-start(bf16[40,1536]{1,0:T(8,128)(2,1)S(1)} %get-tuple-element.60), channel_id=1, source_target_pairs={{0,6},{1,7},{2,4},{3,5},{4,2},{5,3},{6,0},{7,1},{8,14},{9,15},{10,... | collective-permute-start | bytes 368648 | tf_op jit(solution)/shard_map/ppermute | solution.py:459
  34.6 10.3 %collective-permute-start.15 = (bf16[40,1536]{1,0:T(8,128)(2,1)S(1)}, bf16[40,1536]{1,0:T(8,128)(2,1)S(1)}, u32[]{:S(2)}, u32[]{:S(2)}) collective-permute-start(bf16[40,1536]{1,0:T(8,128)(2,1)S(1)} %get-tuple-element.61), channel_id=1, source_target_pairs={{0,7},{1,6},{2,5},{3,4},{4,3},{5,2},{6,1},{7,0},{8,15},{9,14},{10,... | collective-permute-start | bytes 368648 | tf_op jit(solution)/shard_map/ppermute | solution.py:459
  36.8 0.9 %copy-start.5 = (f32[2048]{0:T(1024)S(1)}, f32[2048]{0:T(1024)}, u32[]{:S(2)}) copy-start(f32[2048]{0:T(1024)} %param.15) | copy-start | bytes 24580
  45.5 15.4 %collective-permute-start.16 = (bf16[128,512]{1,0:T(8,128)(2,1)S(1)}, bf16[128,512]{1,0:T(8,128)(2,1)S(1)}, u32[]{:S(2)}, u32[]{:S(2)}) collective-permute-start(bf16[128,512]{1,0:T(8,128)(2,1)S(1)} %get-tuple-element.62), channel_id=1, source_target_pairs={{0,24},{8,16},{16,8},{24,0},{1,25},{9,17},{17,9},{25,1},{2,26},{10... | collective-permute-start | bytes 393224 | tf_op jit(solution)/shard_map/ppermute | solution.py:459
  49.1 11.8 %collective-permute-start.17 = (bf16[128,512]{1,0:T(8,128)(2,1)S(1)}, bf16[128,512]{1,0:T(8,128)(2,1)S(1)}, u32[]{:S(2)}, u32[]{:S(2)}) collective-permute-start(bf16[128,512]{1,0:T(8,128)(2,1)S(1)} %get-tuple-element.63), channel_id=1, source_target_pairs={{0,8},{8,0},{16,24},{24,16},{1,9},{9,1},{17,25},{25,17},{2,10},{10... | collective-permute-start | bytes 393224 | tf_op jit(solution)/shard_map/ppermute | solution.py:459
  49.1 11.8 %collective-permute-start.18 = (bf16[128,512]{1,0:T(8,128)(2,1)S(1)}, bf16[128,512]{1,0:T(8,128)(2,1)S(1)}, u32[]{:S(2)}, u32[]{:S(2)}) collective-permute-start(bf16[128,512]{1,0:T(8,128)(2,1)S(1)} %get-tuple-element.65), channel_id=1, source_target_pairs={{0,16},{8,24},{16,0},{24,8},{1,17},{9,25},{17,1},{25,9},{2,18},{10... | collective-permute-start | bytes 393224 | tf_op jit(solution)/shard_map/ppermute | solution.py:459
  49.9 11.0 %collective-permute-start.19 = (f32[8,128]{1,0:T(8,128)S(1)}, f32[8,128]{1,0:T(8,128)S(1)}, u32[]{:S(2)}, u32[]{:S(2)}) collective-permute-start(f32[8,128]{1,0:T(8,128)S(1)} %get-tuple-element.66), channel_id=1, source_target_pairs={{0,16},{8,24},{16,0},{24,8},{1,17},{9,25},{17,1},{25,9},{2,18},{10... | collective-permute-start | bytes 12296 | tf_op jit(solution)/shard_map/ppermute | solution.py:459

commit v10 on v9

--- a/solution.py
+++ b/solution.py
@@ -101,11 +101,12 @@
             out[:, col : col + tile] = rows[j * capacity : (j + 1) * capacity, :]
 
 
-def dispatch_body(experts, first, others, route_hbm, tok_hbm, *refs):
-    *out_refs, rest_ref, tok_ref, pick_ref, route_ref, sems = refs
+def dispatch_body(experts, first, others, route_hbm, code_hbm, tok_hbm, *refs):
+    *out_refs, rest_ref, route_ref, code_ref, tok_ref, pick_ref, sems = refs
     copies = [
         pltpu.make_async_copy(route_hbm, route_ref, sems.at[0]),
         pltpu.make_async_copy(tok_hbm, tok_ref, sems.at[1]),
+        pltpu.make_async_copy(code_hbm, code_ref, sems.at[2]),
     ]
     for copy in copies:
         copy.start()
@@ -120,29 +121,31 @@
             ref[j * capacity : (j + 1) * capacity, :] = pick
     copies[1].wait()
     pick_rows(pick_ref, tok_ref, out_refs)
-
-
-def dispatch(route_rows, own_rows, experts, capacity, first, others):
+    copies[2].wait()
+
+
+def dispatch(route_rows, code_rows, own_rows, experts, capacity, first, others):
     tok, width = own_rows.shape
-    *outs, rest, held = pl.pallas_call(
+    *outs, rest, route_held, code_held, held = pl.pallas_call(
         functools.partial(dispatch_body, experts, first, others),
         out_shape=[jax.ShapeDtypeStruct((capacity, width), BF16)] * len(first)
         + [
             jax.ShapeDtypeStruct((capacity * len(others), tok), BF16),
+            jax.ShapeDtypeStruct(route_rows.shape, jnp.int32),
+            jax.ShapeDtypeStruct(code_rows.shape, jnp.int32),
             jax.ShapeDtypeStruct((tok, width), BF16),
         ],
-        in_specs=[pl.BlockSpec(memory_space=pltpu.HBM)] * 2,
-        out_specs=[vmem()] * (len(first) + 2),
+        in_specs=[pl.BlockSpec(memory_space=pltpu.HBM)] * 3,
+        out_specs=[vmem()] * (len(first) + 4),
         scratch_shapes=[
             pltpu.VMEM((capacity * len(first), tok), BF16),
-            pltpu.VMEM(route_rows.shape, jnp.int32),
-            pltpu.SemaphoreType.DMA((2,)),
+            pltpu.SemaphoreType.DMA((3,)),
         ],
         name="dispatch",
         cost_estimate=pl.CostEstimate(flops=10**8, transcendentals=0, bytes_accessed=2 * 10**6),
         compiler_params=pltpu.CompilerParams(vmem_limit_bytes=16 * 2**20),
-    )(route_rows, own_rows)
-    return dict(zip(first, outs)), rest, held
+    )(route_rows, code_rows, own_rows)
+    return dict(zip(first, outs)), rest, route_held, code_held, held
 
 
 def others_body(rest_ref, tok_ref, *out_refs):
@@ -481,16 +484,18 @@
     early = (ways // 2,)
     late = tuple(k for k in range(ways - 1, -1, -1) if k not in early)
 
-    route_rows = routes[0].T
-    blocks, rest, held = dispatch(
-        pltpu.with_memory_space_constraint(route_rows, pltpu.HBM),
+    blocks, rest, route_rows, code_rows, held = dispatch(
+        pltpu.with_memory_space_constraint(routes[0].T, pltpu.HBM),
+        pltpu.with_memory_space_constraint(gate_code[0].T, pltpu.HBM),
         pltpu.with_memory_space_constraint(own_rows, pltpu.HBM),
         experts, capacity, CLOSE[:4], CLOSE[4:] + [0] + AWAY,
     )
     blocks |= dispatch_others(rest, held, capacity, CLOSE[4:] + [0] + AWAY)
     near = swap_each({k: blocks[k] for k in close}, "expert")
     far = swap_each({k: blocks[k] for k in away}, "expert")
-    select, select_close, select_away, weights = selector(route_rows, gate_code[0].T, gate_table, experts, capacity)
+    select, select_close, select_away, weights = selector(
+        route_rows, code_rows, gate_table, experts, capacity
+    )
     matrices = w_gate[0].T, w_up[0].T, w_down[0]
 
     plan = [(j, early + late) for j in range(len(close))]

time: 62 us -> 62 us (level)
    unnamed x18 -> x14, local copies, waits for them, and re-layouts: 5.47 us -> 5.46 us
where the time goes in v10:
time: 62 us; the launch traced here: 61.8 us
  starting transfers between devices  26.3 us (42%)
  waiting for transfers between devices  20 us (32%)
  Pallas kernels  9.85 us (16%)
  local copies, waits for them, and re-layouts  5.46 us (9%)
    ppermute x20, starting transfers between devices, swap(): return lax.ppermute(value, axis, [(i, i ^ offset) for i in range(size)])  26.3 us
    ppermute x20, waiting for transfers between devices, swap(): return lax.ppermute(value, axis, [(i, i ^ offset) for i in range(size)])  20 us
    unnamed x14, local copies, waits for them, and re-layouts  5.46 us
    pallas_call x2, Pallas kernels, expert_call(): pl.pallas_call(functools.partial(expert_body, count, chunk, plan), out_sh...  4.57 us
    pallas_call x1, Pallas kernels, dispatch(): pl.pallas_call(functools.partial(dispatch_body, experts, first, others),...  1.41 us
  transfers between devices with their start and end apart: 20, of which 7 were waited for; matrix products, arithmetic and copies ran while one was open for 0% of the time, Pallas kernels for 11%

profile of v10, /device:TPU:0, one launch (start us, length us, event | category | flops | bytes accessed | tf_op | source)
XLA Modules:
  0.0 61.8 jit_solution(5506296970401365631)
XLA Ops:
  0.0 1.4 %dispatch.1 = (bf16[40,2048]{1,0:T(8,128)(2,1)S(1)}, bf16[40,2048]{1,0:T(8,128)(2,1)S(1)}, bf16[40,2048]{1,0:T(8,128)(2,1)S(1)}, bf16[40,2048]{1,0:T(8,128)(2,1)...) custom-call(s32[2,128]{1,0:T(2,128)} %bitcast.26, ...), custom_call_target="tpu_custom_call" | custom-call | flops 100000000 | bytes 2000000 | tf_op jit(solution)/shard_map/dispatch/pallas_call | solution.py:129
  1.4 0.3 others.1
  1.7 0.6 collective-permute-start.4
  2.3 2.6 %collective-permute-start = (bf16[40,2048]{1,0:T(8,128)(2,1)S(1)}, bf16[40,2048]{1,0:T(8,128)(2,1)S(1)}, u32[]{:S(2)}, u32[]{:S(2)}) collective-permute-start(bf16[40,2048]{1,0:T(8,128)(2,1)S(1)} %get-tuple-element.43), channel_id=1, source_target_pairs={{0,4},{1,5},{2,6},{3,7},{4,0},{5,1},{6,2},{7,3},{8,12},{9,13},{10,... | collective-permute-start | bytes 491528 | tf_op jit(solution)/shard_map/ppermute | solution.py:462
  4.9 1.5 %collective-permute-start.1 = (bf16[40,2048]{1,0:T(8,128)(2,1)S(1)}, bf16[40,2048]{1,0:T(8,128)(2,1)S(1)}, u32[]{:S(2)}, u32[]{:S(2)}) collective-permute-start(bf16[40,2048]{1,0:T(8,128)(2,1)S(1)} %get-tuple-element.44), channel_id=1, source_target_pairs={{0,2},{1,3},{2,0},{3,1},{4,6},{5,7},{6,4},{7,5},{8,10},{9,11},{10,... | collective-permute-start | bytes 491528 | tf_op jit(solution)/shard_map/ppermute | solution.py:462
  6.4 0.0 collective-permute-start.2
  6.4 0.3 collective-permute-start.3
  6.7 0.0 collective-permute-done.4.refs_4_
  6.7 2.9 %collective-permute-start.10 = (bf16[40,2048]{1,0:T(8,128)(2,1)S(1)}, bf16[40,2048]{1,0:T(8,128)(2,1)S(1)}, u32[]{:S(2)}, u32[]{:S(2)}) collective-permute-start(bf16[40,2048]{1,0:T(8,128)(2,1)S(1)} %get-tuple-element.58), channel_id=1, source_target_pairs={{0,6},{1,7},{2,4},{3,5},{4,2},{5,3},{6,0},{7,1},{8,14},{9,15},{10,... | collective-permute-start | bytes 491528 | tf_op jit(solution)/shard_map/ppermute | solution.py:462
  9.6 0.3 collective-permute-done.refs_0_
  9.9 1.6 %collective-permute-start.11 = (bf16[40,2048]{1,0:T(8,128)(2,1)S(1)}, bf16[40,2048]{1,0:T(8,128)(2,1)S(1)}, u32[]{:S(2)}, u32[]{:S(2)}) collective-permute-start(bf16[40,2048]{1,0:T(8,128)(2,1)S(1)} %get-tuple-element.59), channel_id=1, source_target_pairs={{0,7},{1,6},{2,5},{3,4},{4,3},{5,2},{6,1},{7,0},{8,15},{9,14},{10,... | collective-permute-start | bytes 491528 | tf_op jit(solution)/shard_map/ppermute | solution.py:462
  11.5 0.4 collective-permute-done.1.refs_1_
  12.0 1.0 %collective-permute-done.2.refs_2_ = bf16[40,2048]{1,0:T(8,128)(2,1)S(1)} collective-permute-done((bf16[40,2048]{1,0:T(8,128)(2,1)S(1)}, bf16[40,2048]{1,0:T(8,128)(2,1)S(1)}, u32[]{:S(2)}, u32[]{:S(2)}) %collective-permute-start.2) | collective-permute-done | bytes 163872 | tf_op jit(solution)/shard_map/ppermute | solution.py:462
  12.9 1.6 %collective-permute-done.3.refs_3_ = bf16[40,2048]{1,0:T(8,128)(2,1)S(1)} collective-permute-done((bf16[40,2048]{1,0:T(8,128)(2,1)S(1)}, bf16[40,2048]{1,0:T(8,128)(2,1)S(1)}, u32[]{:S(2)}, u32[]{:S(2)}) %collective-permute-start.3) | collective-permute-done | bytes 163872 | tf_op jit(solution)/shard_map/ppermute | solution.py:462
  14.5 0.0 copy-start
  14.5 1.8 %copy-done = bf16[1,704,2048]{2,1,0:T(8,128)(2,1)S(1)} copy-done((bf16[1,704,2048]{2,1,0:T(8,128)(2,1)S(1)}, bf16[1,704,2048]{2,1,0:T(8,128)(2,1)}, u32[]{:S(2)}) %copy-start) | copy-done | bytes 2883608
  16.3 0.0 copy-start.2
  16.3 1.8 %copy-done.2 = bf16[1,2048,704]{1,2,0:T(8,128)(2,1)S(1)} copy-done((bf16[1,2048,704]{1,2,0:T(8,128)(2,1)S(1)}, bf16[1,2048,704]{1,2,0:T(8,128)(2,1)}, u32[]{:S(2)}) %copy-start.2) | copy-done | bytes 2883608
  18.1 0.0 copy-start.4
  18.1 1.8 %copy-done.4 = bf16[1,2048,704]{1,2,0:T(8,128)(2,1)S(1)} copy-done((bf16[1,2048,704]{1,2,0:T(8,128)(2,1)S(1)}, bf16[1,2048,704]{1,2,0:T(8,128)(2,1)}, u32[]{:S(2)}) %copy-start.4) | copy-done | bytes 2883608
  19.9 0.0 copy-start.1
  19.9 0.0 copy-start.3
  19.9 2.7 %shard_map.82 = (bf16[240,704]{1,0:T(8,128)(2,1)}, bf16[40,2048]{1,0:T(8,128)(2,1)S(1)}, bf16[40,2048]{1,0:T(8,128)(2,1)S(1)}, bf16[40,2048]{1,0:T(8,128)(2,1)S(...) custom-call(bf16[40,2048]{1,0:T(8,128)(2,1)S(1)} %collective-permute-done.refs_0_, ...), custom_call_target="tpu_custom_call" | custom-call | flops 1730150400 | bytes 8000000 | tf_op jit(solution)/shard_map/pallas_call | solution.py:254
  22.6 1.1 %collective-permute-start.5 = (bf16[40,2048]{1,0:T(8,128)(2,1)S(1)}, bf16[40,2048]{1,0:T(8,128)(2,1)S(1)}, u32[]{:S(2)}, u32[]{:S(2)}) collective-permute-start(bf16[40,2048]{1,0:T(8,128)(2,1)S(1)} %get-tuple-element.52), channel_id=1, source_target_pairs={{0,1},{1,0},{2,3},{3,2},{4,5},{5,4},{6,7},{7,6},{8,9},{9,8},{10,11... | collective-permute-start | bytes 491528 | tf_op jit(solution)/shard_map/ppermute | solution.py:462
  23.7 1.5 %collective-permute-start.6 = (bf16[40,2048]{1,0:T(8,128)(2,1)S(1)}, bf16[40,2048]{1,0:T(8,128)(2,1)S(1)}, u32[]{:S(2)}, u32[]{:S(2)}) collective-permute-start(bf16[40,2048]{1,0:T(8,128)(2,1)S(1)} %get-tuple-element.53), channel_id=1, source_target_pairs={{0,2},{1,3},{2,0},{3,1},{4,6},{5,7},{6,4},{7,5},{8,10},{9,11},{10,... | collective-permute-start | bytes 491528 | tf_op jit(solution)/shard_map/ppermute | solution.py:462
  25.2 0.0 collective-permute-done.10.refs_0_
  25.2 0.0 collective-permute-done.11.refs_1_
  25.2 0.0 copy-done.1
  25.2 0.0 copy-done.3
  25.3 1.9 %shard_map.83 = (bf16[80,704]{1,0:T(8,128)(2,1)S(1)}, bf16[40,512]{1,0:T(8,128)(2,1)S(1)}, bf16[40,512]{1,0:T(8,128)(2,1)S(1)}) custom-call(bf16[40,2048]{1,0:T(8,128)(2,1)S(1)} %collective-permute-done.10.refs_0_, bf16[40,2048]{1,0:T(8,128)(2,1)S(1)} %collective-permute-done.11.refs_1_, bf16[704,2048]{1,0:T(8,128)(2,1)S(1)} %bitcast.20, ...), custom_call_target="tpu_custom_call" | custom-call | flops 576716800 | bytes 8000000 | tf_op jit(solution)/shard_map/pallas_call | solution.py:254
  27.1 0.0 copy-start.6
  27.1 0.1 collective-permute-start.12
  27.2 2.0 %collective-permute-start.13 = (bf16[40,512]{1,0:T(8,128)(2,1)S(1)}, bf16[40,512]{1,0:T(8,128)(2,1)S(1)}, u32[]{:S(2)}, u32[]{:S(2)}) collective-permute-start(bf16[40,512]{1,0:T(8,128)(2,1)S(1)} %get-tuple-element.61), channel_id=1, source_target_pairs={{0,7},{1,6},{2,5},{3,4},{4,3},{5,2},{6,1},{7,0},{8,15},{9,14},{10,... | collective-permute-start | bytes 122888 | tf_op jit(solution)/shard_map/ppermute | solution.py:462
  29.2 1.2 %collective-permute-start.7 = (bf16[40,2048]{1,0:T(8,128)(2,1)S(1)}, bf16[40,2048]{1,0:T(8,128)(2,1)S(1)}, u32[]{:S(2)}, u32[]{:S(2)}) collective-permute-start(bf16[40,2048]{1,0:T(8,128)(2,1)S(1)} %get-tuple-element.54), channel_id=1, source_target_pairs={{0,3},{1,2},{2,1},{3,0},{4,7},{5,6},{6,5},{7,4},{8,11},{9,10},{10,... | collective-permute-start | bytes 491528 | tf_op jit(solution)/shard_map/ppermute | solution.py:462
  30.4 0.5 shard_map.85
  30.9 1.5 %collective-permute-done.12.refs_6_ = bf16[40,512]{1,0:T(8,128)(2,1)S(1)} collective-permute-done((bf16[40,512]{1,0:T(8,128)(2,1)S(1)}, bf16[40,512]{1,0:T(8,128)(2,1)S(1)}, u32[]{:S(2)}, u32[]{:S(2)}) %collective-permute-start.12) | collective-permute-done | bytes 40992 | tf_op jit(solution)/shard_map/ppermute | solution.py:462
  32.4 0.0 collective-permute-start.8
  32.4 0.0 collective-permute-done.13.refs_7_
  32.4 0.6 collective-permute-start.9
  33.0 0.0 collective-permute-done.5.refs_1_
  33.0 1.6 %collective-permute-start.14 = (bf16[40,1536]{1,0:T(8,128)(2,1)S(1)}, bf16[40,1536]{1,0:T(8,128)(2,1)S(1)}, u32[]{:S(2)}, u32[]{:S(2)}) collective-permute-start(bf16[40,1536]{1,0:T(8,128)(2,1)S(1)} %get-tuple-element.64), channel_id=1, source_target_pairs={{0,6},{1,7},{2,4},{3,5},{4,2},{5,3},{6,0},{7,1},{8,14},{9,15},{10,... | collective-permute-start | bytes 368648 | tf_op jit(solution)/shard_map/ppermute | solution.py:462
  34.6 0.0 collective-permute-done.6.refs_2_
  34.6 2.2 %collective-permute-start.15 = (bf16[40,1536]{1,0:T(8,128)(2,1)S(1)}, bf16[40,1536]{1,0:T(8,128)(2,1)S(1)}, u32[]{:S(2)}, u32[]{:S(2)}) collective-permute-start(bf16[40,1536]{1,0:T(8,128)(2,1)S(1)} %get-tuple-element.65), channel_id=1, source_target_pairs={{0,7},{1,6},{2,5},{3,4},{4,3},{5,2},{6,1},{7,0},{8,15},{9,14},{10,... | collective-permute-start | bytes 368648 | tf_op jit(solution)/shard_map/ppermute | solution.py:462
  36.8 0.0 copy-done.6
  36.8 0.0 copy-start.5
  36.8 0.9 %selector.1 = (bf16[256,320]{1,0:T(8,128)(2,1)S(1)}, bf16[256,240]{1,0:T(8,128)(2,1)S(1)}, bf16[256,80]{1,0:T(8,128)(2,1)S(1)}, f32[2,128,128]{2,1,0:T(8,128)S(1)}) custom-call(s32[2,128]{1,0:T(2,128)S(1)} %get-tuple-element.38.route_ref, s32[2,128]{1,0:T(2,128)S(1)} %get-tuple-element.39.code_ref, f32[16]{0:T(128)S(1)} %copy-done.6), custom_call_target="tpu_custom_call" | custom-call | flops 20000000000 | bytes 100000000 | tf_op jit(solution)/shard_map/selector/pallas_call | solution.py:195
  37.7 0.0 copy-done.5
  37.7 0.0 collective-permute-done.7.refs_3_
  37.7 6.4 %collective-permute-done.8.refs_4_ = bf16[40,2048]{1,0:T(8,128)(2,1)S(1)} collective-permute-done((bf16[40,2048]{1,0:T(8,128)(2,1)S(1)}, bf16[40,2048]{1,0:T(8,128)(2,1)S(1)}, u32[]{:S(2)}, u32[]{:S(2)}) %collective-permute-start.8) | collective-permute-done | bytes 163872 | tf_op jit(solution)/shard_map/ppermute | solution.py:462
  44.1 0.0 collective-permute-done.9.refs_5_
  44.1 0.3 combine_early.1
  44.5 0.4 combine_mid.1.begun_ref
  44.9 0.0 collective-permute-done.14.refs_0_
  44.9 0.0 collective-permute-done.15.refs_1_
  44.9 0.6 combine_late.1
  45.4 3.7 %collective-permute-start.16 = (bf16[128,512]{1,0:T(8,128)(2,1)S(1)}, bf16[128,512]{1,0:T(8,128)(2,1)S(1)}, u32[]{:S(2)}, u32[]{:S(2)}) collective-permute-start(bf16[128,512]{1,0:T(8,128)(2,1)S(1)} %get-tuple-element.66), channel_id=1, source_target_pairs={{0,24},{8,16},{16,8},{24,0},{1,25},{9,17},{17,9},{25,1},{2,26},{10... | collective-permute-start | bytes 393224 | tf_op jit(solution)/shard_map/ppermute | solution.py:462
  49.1 0.0 collective-permute-start.17
  49.2 0.7 %collective-permute-start.18 = (bf16[128,512]{1,0:T(8,128)(2,1)S(1)}, bf16[128,512]{1,0:T(8,128)(2,1)S(1)}, u32[]{:S(2)}, u32[]{:S(2)}) collective-permute-start(bf16[128,512]{1,0:T(8,128)(2,1)S(1)} %get-tuple-element.69), channel_id=1, source_target_pairs={{0,16},{8,24},{16,0},{24,8},{1,17},{9,25},{17,1},{25,9},{2,18},{10... | collective-permute-start | bytes 393224 | tf_op jit(solution)/shard_map/ppermute | solution.py:462
  49.9 2.2 %collective-permute-start.19 = (f32[8,128]{1,0:T(8,128)S(1)}, f32[8,128]{1,0:T(8,128)S(1)}, u32[]{:S(2)}, u32[]{:S(2)}) collective-permute-start(f32[8,128]{1,0:T(8,128)S(1)} %get-tuple-element.70), channel_id=1, source_target_pairs={{0,16},{8,24},{16,0},{24,8},{1,17},{9,25},{17,1},{25,9},{2,18},{10... | collective-permute-start | bytes 12296 | tf_op jit(solution)/shard_map/ppermute | solution.py:462
  52.1 8.8 %collective-permute-done.19.refs_4_ = f32[8,128]{1,0:T(8,128)S(1)} collective-permute-done((f32[8,128]{1,0:T(8,128)S(1)}, f32[8,128]{1,0:T(8,128)S(1)}, u32[]{:S(2)}, u32[]{:S(2)}) %collective-permute-start.19) | collective-permute-done | bytes 4128 | tf_op jit(solution)/shard_map/ppermute | solution.py:462
  60.9 0.0 collective-permute-done.16.refs_0_
  60.9 0.0 collective-permute-done.17.refs_1_
  60.9 0.0 collective-permute-done.18.refs_3_
  60.9 0.9 %finish.1 = bf16[512,512]{1,0:T(8,128)(2,1)} custom-call(bf16[128,512]{1,0:T(8,128)(2,1)S(1)} %collective-permute-done.16.refs_0_, bf16[128,512]{1,0:T(8,128)(2,1)S(1)} %collective-permute-done.17.refs_1_, bf16[128,512]{1,0:T(8,128)(2,1)S(1)} %get-tuple-element.68.refs_2_, bf16[128,512]{1,0:T(8,128)(2,1)S(1)} %collective-permute-done.18.refs_3_, ...), custom_call_target="tpu_custom_call" | custom-call | flops 1000000 | bytes 1000000 | tf_op jit(solution)/shard_map/finish/pallas_call | solution.py:445
  (2 shorter events, 0.0 us)
Async XLA Ops:
  1.7 5.0 %collective-permute-start.4 = (bf16[40,2048]{1,0:T(8,128)(2,1)S(1)}, bf16[40,2048]{1,0:T(8,128)(2,1)S(1)}, u32[]{:S(2)}, u32[]{:S(2)}) collective-permute-start(bf16[40,2048]{1,0:T(8,128)(2,1)S(1)} %get-tuple-element.49), channel_id=1, source_target_pairs={{0,1},{1,0},{2,3},{3,2},{4,5},{5,4},{6,7},{7,6},{8,9},{9,8},{10,11... | collective-permute-start | bytes 491528 | tf_op jit(solution)/shard_map/ppermute | solution.py:462
  2.3 7.6 %collective-permute-start = (bf16[40,2048]{1,0:T(8,128)(2,1)S(1)}, bf16[40,2048]{1,0:T(8,128)(2,1)S(1)}, u32[]{:S(2)}, u32[]{:S(2)}) collective-permute-start(bf16[40,2048]{1,0:T(8,128)(2,1)S(1)} %get-tuple-element.43), channel_id=1, source_target_pairs={{0,4},{1,5},{2,6},{3,7},{4,0},{5,1},{6,2},{7,3},{8,12},{9,13},{10,... | collective-permute-start | bytes 491528 | tf_op jit(solution)/shard_map/ppermute | solution.py:462
  4.9 7.1 %collective-permute-start.1 = (bf16[40,2048]{1,0:T(8,128)(2,1)S(1)}, bf16[40,2048]{1,0:T(8,128)(2,1)S(1)}, u32[]{:S(2)}, u32[]{:S(2)}) collective-permute-start(bf16[40,2048]{1,0:T(8,128)(2,1)S(1)} %get-tuple-element.44), channel_id=1, source_target_pairs={{0,2},{1,3},{2,0},{3,1},{4,6},{5,7},{6,4},{7,5},{8,10},{9,11},{10,... | collective-permute-start | bytes 491528 | tf_op jit(solution)/shard_map/ppermute | solution.py:462
  6.4 6.6 %collective-permute-start.2 = (bf16[40,2048]{1,0:T(8,128)(2,1)S(1)}, bf16[40,2048]{1,0:T(8,128)(2,1)S(1)}, u32[]{:S(2)}, u32[]{:S(2)}) collective-permute-start(bf16[40,2048]{1,0:T(8,128)(2,1)S(1)} %get-tuple-element.45), channel_id=1, source_target_pairs={{0,5},{1,4},{2,7},{3,6},{4,1},{5,0},{6,3},{7,2},{8,13},{9,12},{10,... | collective-permute-start | bytes 491528 | tf_op jit(solution)/shard_map/ppermute | solution.py:462
  6.4 8.1 %collective-permute-start.3 = (bf16[40,2048]{1,0:T(8,128)(2,1)S(1)}, bf16[40,2048]{1,0:T(8,128)(2,1)S(1)}, u32[]{:S(2)}, u32[]{:S(2)}) collective-permute-start(bf16[40,2048]{1,0:T(8,128)(2,1)S(1)} %get-tuple-element.46), channel_id=1, source_target_pairs={{0,3},{1,2},{2,1},{3,0},{4,7},{5,6},{6,5},{7,4},{8,11},{9,10},{10,... | collective-permute-start | bytes 491528 | tf_op jit(solution)/shard_map/ppermute | solution.py:462
  6.7 18.5 %collective-permute-start.10 = (bf16[40,2048]{1,0:T(8,128)(2,1)S(1)}, bf16[40,2048]{1,0:T(8,128)(2,1)S(1)}, u32[]{:S(2)}, u32[]{:S(2)}) collective-permute-start(bf16[40,2048]{1,0:T(8,128)(2,1)S(1)} %get-tuple-element.58), channel_id=1, source_target_pairs={{0,6},{1,7},{2,4},{3,5},{4,2},{5,3},{6,0},{7,1},{8,14},{9,15},{10,... | collective-permute-start | bytes 491528 | tf_op jit(solution)/shard_map/ppermute | solution.py:462
  9.9 15.3 %collective-permute-start.11 = (bf16[40,2048]{1,0:T(8,128)(2,1)S(1)}, bf16[40,2048]{1,0:T(8,128)(2,1)S(1)}, u32[]{:S(2)}, u32[]{:S(2)}) collective-permute-start(bf16[40,2048]{1,0:T(8,128)(2,1)S(1)} %get-tuple-element.59), channel_id=1, source_target_pairs={{0,7},{1,6},{2,5},{3,4},{4,3},{5,2},{6,1},{7,0},{8,15},{9,14},{10,... | collective-permute-start | bytes 491528 | tf_op jit(solution)/shard_map/ppermute | solution.py:462
  14.5 1.8 %copy-start = (bf16[1,704,2048]{2,1,0:T(8,128)(2,1)S(1)}, bf16[1,704,2048]{2,1,0:T(8,128)(2,1)}, u32[]{:S(2)}) copy-start(bf16[1,704,2048]{2,1,0:T(8,128)(2,1)} %param.14) | copy-start | bytes 8650756
  16.3 1.8 %copy-start.2 = (bf16[1,2048,704]{1,2,0:T(8,128)(2,1)S(1)}, bf16[1,2048,704]{1,2,0:T(8,128)(2,1)}, u32[]{:S(2)}) copy-start(bf16[1,2048,704]{1,2,0:T(8,128)(2,1)} %param.12) | copy-start | bytes 8650756
  18.1 1.8 %copy-start.4 = (bf16[1,2048,704]{1,2,0:T(8,128)(2,1)S(1)}, bf16[1,2048,704]{1,2,0:T(8,128)(2,1)}, u32[]{:S(2)}) copy-start(bf16[1,2048,704]{1,2,0:T(8,128)(2,1)} %param.13) | copy-start | bytes 8650756
  19.9 5.3 %copy-start.1 = (bf16[1,704,2048]{2,1,0:T(8,128)(2,1)S(1)}, bf16[1,704,2048]{2,1,0:T(8,128)(2,1)}, u32[]{:S(2)}) copy-start(bf16[1,704,2048]{2,1,0:T(8,128)(2,1)} %param.14) | copy-start | bytes 8650756
  19.9 5.3 %copy-start.3 = (bf16[1,2048,704]{1,2,0:T(8,128)(2,1)S(1)}, bf16[1,2048,704]{1,2,0:T(8,128)(2,1)}, u32[]{:S(2)}) copy-start(bf16[1,2048,704]{1,2,0:T(8,128)(2,1)} %param.12) | copy-start | bytes 8650756
  22.6 10.3 %collective-permute-start.5 = (bf16[40,2048]{1,0:T(8,128)(2,1)S(1)}, bf16[40,2048]{1,0:T(8,128)(2,1)S(1)}, u32[]{:S(2)}, u32[]{:S(2)}) collective-permute-start(bf16[40,2048]{1,0:T(8,128)(2,1)S(1)} %get-tuple-element.52), channel_id=1, source_target_pairs={{0,1},{1,0},{2,3},{3,2},{4,5},{5,4},{6,7},{7,6},{8,9},{9,8},{10,11... | collective-permute-start | bytes 491528 | tf_op jit(solution)/shard_map/ppermute | solution.py:462
  23.7 10.8 %collective-permute-start.6 = (bf16[40,2048]{1,0:T(8,128)(2,1)S(1)}, bf16[40,2048]{1,0:T(8,128)(2,1)S(1)}, u32[]{:S(2)}, u32[]{:S(2)}) collective-permute-start(bf16[40,2048]{1,0:T(8,128)(2,1)S(1)} %get-tuple-element.53), channel_id=1, source_target_pairs={{0,2},{1,3},{2,0},{3,1},{4,6},{5,7},{6,4},{7,5},{8,10},{9,11},{10,... | collective-permute-start | bytes 491528 | tf_op jit(solution)/shard_map/ppermute | solution.py:462
  27.1 9.7 %copy-start.6 = (f32[16]{0:T(128)S(1)}, f32[16]{0:T(128)}, u32[]{:S(2)}) copy-start(f32[16]{0:T(128)} %table_ref.1) | copy-start | bytes 196
  27.1 5.2 %collective-permute-start.12 = (bf16[40,512]{1,0:T(8,128)(2,1)S(1)}, bf16[40,512]{1,0:T(8,128)(2,1)S(1)}, u32[]{:S(2)}, u32[]{:S(2)}) collective-permute-start(bf16[40,512]{1,0:T(8,128)(2,1)S(1)} %get-tuple-element.60), channel_id=1, source_target_pairs={{0,6},{1,7},{2,4},{3,5},{4,2},{5,3},{6,0},{7,1},{8,14},{9,15},{10,... | collective-permute-start | bytes 122888 | tf_op jit(solution)/shard_map/ppermute | solution.py:462
  27.2 5.2 %collective-permute-start.13 = (bf16[40,512]{1,0:T(8,128)(2,1)S(1)}, bf16[40,512]{1,0:T(8,128)(2,1)S(1)}, u32[]{:S(2)}, u32[]{:S(2)}) collective-permute-start(bf16[40,512]{1,0:T(8,128)(2,1)S(1)} %get-tuple-element.61), channel_id=1, source_target_pairs={{0,7},{1,6},{2,5},{3,4},{4,3},{5,2},{6,1},{7,0},{8,15},{9,14},{10,... | collective-permute-start | bytes 122888 | tf_op jit(solution)/shard_map/ppermute | solution.py:462
  29.2 8.5 %collective-permute-start.7 = (bf16[40,2048]{1,0:T(8,128)(2,1)S(1)}, bf16[40,2048]{1,0:T(8,128)(2,1)S(1)}, u32[]{:S(2)}, u32[]{:S(2)}) collective-permute-start(bf16[40,2048]{1,0:T(8,128)(2,1)S(1)} %get-tuple-element.54), channel_id=1, source_target_pairs={{0,3},{1,2},{2,1},{3,0},{4,7},{5,6},{6,5},{7,4},{8,11},{9,10},{10,... | collective-permute-start | bytes 491528 | tf_op jit(solution)/shard_map/ppermute | solution.py:462
  32.4 11.8 %collective-permute-start.8 = (bf16[40,2048]{1,0:T(8,128)(2,1)S(1)}, bf16[40,2048]{1,0:T(8,128)(2,1)S(1)}, u32[]{:S(2)}, u32[]{:S(2)}) collective-permute-start(bf16[40,2048]{1,0:T(8,128)(2,1)S(1)} %get-tuple-element.55), channel_id=1, source_target_pairs={{0,4},{1,5},{2,6},{3,7},{4,0},{5,1},{6,2},{7,3},{8,12},{9,13},{10,... | collective-permute-start | bytes 491528 | tf_op jit(solution)/shard_map/ppermute | solution.py:462
  32.4 11.8 %collective-permute-start.9 = (bf16[40,2048]{1,0:T(8,128)(2,1)S(1)}, bf16[40,2048]{1,0:T(8,128)(2,1)S(1)}, u32[]{:S(2)}, u32[]{:S(2)}) collective-permute-start(bf16[40,2048]{1,0:T(8,128)(2,1)S(1)} %get-tuple-element.56), channel_id=1, source_target_pairs={{0,5},{1,4},{2,7},{3,6},{4,1},{5,0},{6,3},{7,2},{8,13},{9,12},{10,... | collective-permute-start | bytes 491528 | tf_op jit(solution)/shard_map/ppermute | solution.py:462
  33.0 11.9 %collective-permute-start.14 = (bf16[40,1536]{1,0:T(8,128)(2,1)S(1)}, bf16[40,1536]{1,0:T(8,128)(2,1)S(1)}, u32[]{:S(2)}, u32[]{:S(2)}) collective-permute-start(bf16[40,1536]{1,0:T(8,128)(2,1)S(1)} %get-tuple-element.64), channel_id=1, source_target_pairs={{0,6},{1,7},{2,4},{3,5},{4,2},{5,3},{6,0},{7,1},{8,14},{9,15},{10,... | collective-permute-start | bytes 368648 | tf_op jit(solution)/shard_map/ppermute | solution.py:462
  34.6 10.3 %collective-permute-start.15 = (bf16[40,1536]{1,0:T(8,128)(2,1)S(1)}, bf16[40,1536]{1,0:T(8,128)(2,1)S(1)}, u32[]{:S(2)}, u32[]{:S(2)}) collective-permute-start(bf16[40,1536]{1,0:T(8,128)(2,1)S(1)} %get-tuple-element.65), channel_id=1, source_target_pairs={{0,7},{1,6},{2,5},{3,4},{4,3},{5,2},{6,1},{7,0},{8,15},{9,14},{10,... | collective-permute-start | bytes 368648 | tf_op jit(solution)/shard_map/ppermute | solution.py:462
  36.8 0.9 %copy-start.5 = (f32[2048]{0:T(1024)S(1)}, f32[2048]{0:T(1024)}, u32[]{:S(2)}) copy-start(f32[2048]{0:T(1024)} %param.15) | copy-start | bytes 24580
  45.4 15.4 %collective-permute-start.16 = (bf16[128,512]{1,0:T(8,128)(2,1)S(1)}, bf16[128,512]{1,0:T(8,128)(2,1)S(1)}, u32[]{:S(2)}, u32[]{:S(2)}) collective-permute-start(bf16[128,512]{1,0:T(8,128)(2,1)S(1)} %get-tuple-element.66), channel_id=1, source_target_pairs={{0,24},{8,16},{16,8},{24,0},{1,25},{9,17},{17,9},{25,1},{2,26},{10... | collective-permute-start | bytes 393224 | tf_op jit(solution)/shard_map/ppermute | solution.py:462
  49.1 11.7 %collective-permute-start.17 = (bf16[128,512]{1,0:T(8,128)(2,1)S(1)}, bf16[128,512]{1,0:T(8,128)(2,1)S(1)}, u32[]{:S(2)}, u32[]{:S(2)}) collective-permute-start(bf16[128,512]{1,0:T(8,128)(2,1)S(1)} %get-tuple-element.67), channel_id=1, source_target_pairs={{0,8},{8,0},{16,24},{24,16},{1,9},{9,1},{17,25},{25,17},{2,10},{10... | collective-permute-start | bytes 393224 | tf_op jit(solution)/shard_map/ppermute | solution.py:462
  49.2 11.7 %collective-permute-start.18 = (bf16[128,512]{1,0:T(8,128)(2,1)S(1)}, bf16[128,512]{1,0:T(8,128)(2,1)S(1)}, u32[]{:S(2)}, u32[]{:S(2)}) collective-permute-start(bf16[128,512]{1,0:T(8,128)(2,1)S(1)} %get-tuple-element.69), channel_id=1, source_target_pairs={{0,16},{8,24},{16,0},{24,8},{1,17},{9,25},{17,1},{25,9},{2,18},{10... | collective-permute-start | bytes 393224 | tf_op jit(solution)/shard_map/ppermute | solution.py:462
  49.9 11.0 %collective-permute-start.19 = (f32[8,128]{1,0:T(8,128)S(1)}, f32[8,128]{1,0:T(8,128)S(1)}, u32[]{:S(2)}, u32[]{:S(2)}) collective-permute-start(f32[8,128]{1,0:T(8,128)S(1)} %get-tuple-element.70), channel_id=1, source_target_pairs={{0,16},{8,24},{16,0},{24,8},{1,17},{9,25},{17,1},{25,9},{2,18},{10... | collective-permute-start | bytes 12296 | tf_op jit(solution)/shard_map/ppermute | solution.py:462

commit v11 on v8

--- a/solution.py
+++ b/solution.py
@@ -201,9 +201,14 @@
     for j, block in enumerate(blocks):
         x_ref[j * capacity : (j + 1) * capacity, :] = block[...]
     hid = gate_ref.shape[0]
+    over = (((1,), (1,)), ((), ()))
+    few = x_ref.shape[0] <= 128
+    if few:
+        gate = lax.dot_general(gate_ref[...], x_ref[...], over, preferred_element_type=F32)
+        up = lax.dot_general(up_ref[...], x_ref[...], over, preferred_element_type=F32)
+        hid_ref[...] = (gate / (1.0 + jnp.exp(-gate)) * up).T.astype(BF16)
     tile = 256
-    over = (((1,), (1,)), ((), ()))
-    for low in range(0, hid, tile):
+    for low in range(0, 0 if few else hid, tile):
         high = min(hid, low + tile)
         gate = lax.dot_general(x_ref[...], gate_ref[low:high, :], over, preferred_element_type=F32)
         up = lax.dot_general(x_ref[...], up_ref[low:high, :], over, preferred_element_type=F32)

time: 62.2 us -> 62 us (level)
  no operation moved by 1% of the time
where the time goes in v11:
time: 62 us; the launch traced here: 61.7 us
  starting transfers between devices  25.4 us (41%)
  waiting for transfers between devices  21 us (34%)
  Pallas kernels  9.67 us (16%)
  local copies, waits for them, and re-layouts  5.47 us (9%)
    ppermute x20, starting transfers between devices, swap(): return lax.ppermute(value, axis, [(i, i ^ offset) for i in range(size)])  25.4 us
    ppermute x20, waiting for transfers between devices, swap(): return lax.ppermute(value, axis, [(i, i ^ offset) for i in range(size)])  21 us
    unnamed x18, local copies, waits for them, and re-layouts  5.47 us
    pallas_call x2, Pallas kernels, expert_call(): pl.pallas_call(functools.partial(expert_body, count, chunk, plan), out_sh...  4.56 us
    pallas_call x1, Pallas kernels, dispatch(): pl.pallas_call(functools.partial(dispatch_body, experts, capacity), out_s...  1.57 us
  transfers between devices with their start and end apart: 20, of which 5 were waited for; matrix products, arithmetic and copies ran while one was open for 0% of the time, Pallas kernels for 11%

profile of v11, /device:TPU:0, one launch (start us, length us, event | category | flops | bytes accessed | tf_op | source)
XLA Modules:
  0.0 61.7 jit_solution(11947236750488290457)
XLA Ops:
  0.0 1.6 %dispatch.1 = (bf16[40,2048]{1,0:T(8,128)(2,1)S(1)}, bf16[40,2048]{1,0:T(8,128)(2,1)S(1)}, bf16[40,2048]{1,0:T(8,128)(2,1)S(1)}, bf16[40,2048]{1,0:T(8,128)(2,1)...) custom-call(s32[2,128]{1,0:T(2,128)} %bitcast.25, ...), custom_call_target="tpu_custom_call" | custom-call | flops 100000000 | bytes 2000000 | tf_op jit(solution)/shard_map/dispatch/pallas_call | solution.py:122
  1.6 3.1 %collective-permute-start = (bf16[40,2048]{1,0:T(8,128)(2,1)S(1)}, bf16[40,2048]{1,0:T(8,128)(2,1)S(1)}, u32[]{:S(2)}, u32[]{:S(2)}) collective-permute-start(bf16[40,2048]{1,0:T(8,128)(2,1)S(1)} %get-tuple-element.37), channel_id=1, source_target_pairs={{0,4},{1,5},{2,6},{3,7},{4,0},{5,1},{6,2},{7,3},{8,12},{9,13},{10,... | collective-permute-start | bytes 491528 | tf_op jit(solution)/shard_map/ppermute | solution.py:432
  4.6 1.5 %collective-permute-start.1 = (bf16[40,2048]{1,0:T(8,128)(2,1)S(1)}, bf16[40,2048]{1,0:T(8,128)(2,1)S(1)}, u32[]{:S(2)}, u32[]{:S(2)}) collective-permute-start(bf16[40,2048]{1,0:T(8,128)(2,1)S(1)} %get-tuple-element.38), channel_id=1, source_target_pairs={{0,2},{1,3},{2,0},{3,1},{4,6},{5,7},{6,4},{7,5},{8,10},{9,11},{10,... | collective-permute-start | bytes 491528 | tf_op jit(solution)/shard_map/ppermute | solution.py:432
  6.1 0.0 collective-permute-start.2
  6.1 0.3 collective-permute-start.3
  6.5 0.3 collective-permute-start.4
  6.8 2.3 %collective-permute-done.refs_0_ = bf16[40,2048]{1,0:T(8,128)(2,1)S(1)} collective-permute-done((bf16[40,2048]{1,0:T(8,128)(2,1)S(1)}, bf16[40,2048]{1,0:T(8,128)(2,1)S(1)}, u32[]{:S(2)}, u32[]{:S(2)}) %collective-permute-start) | collective-permute-done | bytes 163872 | tf_op jit(solution)/shard_map/ppermute | solution.py:432
  9.1 3.6 %collective-permute-start.10 = (bf16[40,2048]{1,0:T(8,128)(2,1)S(1)}, bf16[40,2048]{1,0:T(8,128)(2,1)S(1)}, u32[]{:S(2)}, u32[]{:S(2)}) collective-permute-start(bf16[40,2048]{1,0:T(8,128)(2,1)S(1)} %get-tuple-element.50), channel_id=1, source_target_pairs={{0,6},{1,7},{2,4},{3,5},{4,2},{5,3},{6,0},{7,1},{8,14},{9,15},{10,... | collective-permute-start | bytes 491528 | tf_op jit(solution)/shard_map/ppermute | solution.py:432
  12.6 0.0 collective-permute-done.1.refs_1_
  12.6 0.0 collective-permute-start.11
  12.6 0.0 collective-permute-done.2.refs_2_
  12.7 1.6 %collective-permute-done.3.refs_3_ = bf16[40,2048]{1,0:T(8,128)(2,1)S(1)} collective-permute-done((bf16[40,2048]{1,0:T(8,128)(2,1)S(1)}, bf16[40,2048]{1,0:T(8,128)(2,1)S(1)}, u32[]{:S(2)}, u32[]{:S(2)}) %collective-permute-start.3) | collective-permute-done | bytes 163872 | tf_op jit(solution)/shard_map/ppermute | solution.py:432
  14.2 0.0 collective-permute-done.4.refs_4_
  14.2 0.0 copy-start
  14.2 1.8 %copy-done = bf16[1,704,2048]{2,1,0:T(8,128)(2,1)S(1)} copy-done((bf16[1,704,2048]{2,1,0:T(8,128)(2,1)S(1)}, bf16[1,704,2048]{2,1,0:T(8,128)(2,1)}, u32[]{:S(2)}) %copy-start) | copy-done | bytes 2883608
  16.1 0.0 copy-start.2
  16.1 1.8 %copy-done.2 = bf16[1,2048,704]{1,2,0:T(8,128)(2,1)S(1)} copy-done((bf16[1,2048,704]{1,2,0:T(8,128)(2,1)S(1)}, bf16[1,2048,704]{1,2,0:T(8,128)(2,1)}, u32[]{:S(2)}) %copy-start.2) | copy-done | bytes 2883608
  17.9 0.0 copy-start.4
  17.9 1.8 %copy-done.4 = bf16[1,2048,704]{1,2,0:T(8,128)(2,1)S(1)} copy-done((bf16[1,2048,704]{1,2,0:T(8,128)(2,1)S(1)}, bf16[1,2048,704]{1,2,0:T(8,128)(2,1)}, u32[]{:S(2)}) %copy-start.4) | copy-done | bytes 2883608
  19.7 2.7 %shard_map.82 = (bf16[240,704]{1,0:T(8,128)(2,1)}, bf16[40,2048]{1,0:T(8,128)(2,1)S(1)}, bf16[40,2048]{1,0:T(8,128)(2,1)S(1)}, bf16[40,2048]{1,0:T(8,128)(2,1)S(...) custom-call(bf16[40,2048]{1,0:T(8,128)(2,1)S(1)} %collective-permute-done.refs_0_, ...), custom_call_target="tpu_custom_call" | custom-call | flops 1730150400 | bytes 8000000 | tf_op jit(solution)/shard_map/pallas_call | solution.py:224
  22.4 0.9 %collective-permute-start.5 = (bf16[40,2048]{1,0:T(8,128)(2,1)S(1)}, bf16[40,2048]{1,0:T(8,128)(2,1)S(1)}, u32[]{:S(2)}, u32[]{:S(2)}) collective-permute-start(bf16[40,2048]{1,0:T(8,128)(2,1)S(1)} %get-tuple-element.44), channel_id=1, source_target_pairs={{0,1},{1,0},{2,3},{3,2},{4,5},{5,4},{6,7},{7,6},{8,9},{9,8},{10,11... | collective-permute-start | bytes 491528 | tf_op jit(solution)/shard_map/ppermute | solution.py:432
  23.3 1.7 %collective-permute-start.6 = (bf16[40,2048]{1,0:T(8,128)(2,1)S(1)}, bf16[40,2048]{1,0:T(8,128)(2,1)S(1)}, u32[]{:S(2)}, u32[]{:S(2)}) collective-permute-start(bf16[40,2048]{1,0:T(8,128)(2,1)S(1)} %get-tuple-element.45), channel_id=1, source_target_pairs={{0,2},{1,3},{2,0},{3,1},{4,6},{5,7},{6,4},{7,5},{8,10},{9,11},{10,... | collective-permute-start | bytes 491528 | tf_op jit(solution)/shard_map/ppermute | solution.py:432
  25.0 0.0 collective-permute-done.10.refs_0_
  25.0 0.0 collective-permute-done.11.refs_1_
  25.0 0.0 copy-done.1
  25.0 0.0 copy-done.3
  25.0 1.9 %shard_map.83 = (bf16[80,704]{1,0:T(8,128)(2,1)S(1)}, bf16[40,512]{1,0:T(8,128)(2,1)S(1)}, bf16[40,512]{1,0:T(8,128)(2,1)S(1)}) custom-call(bf16[40,2048]{1,0:T(8,128)(2,1)S(1)} %collective-permute-done.10.refs_0_, bf16[40,2048]{1,0:T(8,128)(2,1)S(1)} %collective-permute-done.11.refs_1_, bf16[704,2048]{1,0:T(8,128)(2,1)S(1)} %bitcast.20, ...), custom_call_target="tpu_custom_call" | custom-call | flops 576716800 | bytes 8000000 | tf_op jit(solution)/shard_map/pallas_call | solution.py:224
  26.9 0.0 copy-start.6
  26.9 0.0 copy-start.7
  26.9 0.0 copy-start.8
  26.9 0.1 collective-permute-start.12
  27.0 2.0 %collective-permute-start.13 = (bf16[40,512]{1,0:T(8,128)(2,1)S(1)}, bf16[40,512]{1,0:T(8,128)(2,1)S(1)}, u32[]{:S(2)}, u32[]{:S(2)}) collective-permute-start(bf16[40,512]{1,0:T(8,128)(2,1)S(1)} %get-tuple-element.53), channel_id=1, source_target_pairs={{0,7},{1,6},{2,5},{3,4},{4,3},{5,2},{6,1},{7,0},{8,15},{9,14},{10,... | collective-permute-start | bytes 122888 | tf_op jit(solution)/shard_map/ppermute | solution.py:432
  29.0 1.0 %collective-permute-start.7 = (bf16[40,2048]{1,0:T(8,128)(2,1)S(1)}, bf16[40,2048]{1,0:T(8,128)(2,1)S(1)}, u32[]{:S(2)}, u32[]{:S(2)}) collective-permute-start(bf16[40,2048]{1,0:T(8,128)(2,1)S(1)} %get-tuple-element.46), channel_id=1, source_target_pairs={{0,3},{1,2},{2,1},{3,0},{4,7},{5,6},{6,5},{7,4},{8,11},{9,10},{10,... | collective-permute-start | bytes 491528 | tf_op jit(solution)/shard_map/ppermute | solution.py:432
  29.9 0.5 shard_map.85
  30.5 1.9 %collective-permute-done.12.refs_6_ = bf16[40,512]{1,0:T(8,128)(2,1)S(1)} collective-permute-done((bf16[40,512]{1,0:T(8,128)(2,1)S(1)}, bf16[40,512]{1,0:T(8,128)(2,1)S(1)}, u32[]{:S(2)}, u32[]{:S(2)}) %collective-permute-start.12) | collective-permute-done | bytes 40992 | tf_op jit(solution)/shard_map/ppermute | solution.py:432
  32.3 0.0 collective-permute-start.8
  32.3 0.0 collective-permute-done.13.refs_7_
  32.3 0.2 collective-permute-start.9
  32.5 0.0 collective-permute-done.5.refs_1_
  32.5 1.8 %collective-permute-start.14 = (bf16[40,1536]{1,0:T(8,128)(2,1)S(1)}, bf16[40,1536]{1,0:T(8,128)(2,1)S(1)}, u32[]{:S(2)}, u32[]{:S(2)}) collective-permute-start(bf16[40,1536]{1,0:T(8,128)(2,1)S(1)} %get-tuple-element.56), channel_id=1, source_target_pairs={{0,6},{1,7},{2,4},{3,5},{4,2},{5,3},{6,0},{7,1},{8,14},{9,15},{10,... | collective-permute-start | bytes 368648 | tf_op jit(solution)/shard_map/ppermute | solution.py:432
  34.3 0.0 collective-permute-done.6.refs_2_
  34.3 2.4 %collective-permute-start.15 = (bf16[40,1536]{1,0:T(8,128)(2,1)S(1)}, bf16[40,1536]{1,0:T(8,128)(2,1)S(1)}, u32[]{:S(2)}, u32[]{:S(2)}) collective-permute-start(bf16[40,1536]{1,0:T(8,128)(2,1)S(1)} %get-tuple-element.57), channel_id=1, source_target_pairs={{0,7},{1,6},{2,5},{3,4},{4,3},{5,2},{6,1},{7,0},{8,15},{9,14},{10,... | collective-permute-start | bytes 368648 | tf_op jit(solution)/shard_map/ppermute | solution.py:432
  36.7 0.0 copy-done.6
  36.7 0.0 copy-done.7
  36.7 0.0 copy-done.8
  36.7 0.9 %selector.1 = (bf16[256,320]{1,0:T(8,128)(2,1)S(1)}, bf16[256,240]{1,0:T(8,128)(2,1)S(1)}, bf16[256,80]{1,0:T(8,128)(2,1)S(1)}, f32[2,128,128]{2,1,0:T(8,128)S(1)}) custom-call(s32[2,128]{1,0:T(2,128)S(1)} %bitcast.26, s32[2,128]{1,0:T(2,128)S(1)} %bitcast.27, f32[16]{0:T(128)S(1)} %copy-done.8), custom_call_target="tpu_custom_call" | custom-call | flops 20000000000 | bytes 100000000 | tf_op jit(solution)/shard_map/selector/pallas_call | solution.py:165
  37.6 0.0 copy-done.5
  37.6 0.0 collective-permute-done.7.refs_3_
  37.7 6.4 %collective-permute-done.8.refs_4_ = bf16[40,2048]{1,0:T(8,128)(2,1)S(1)} collective-permute-done((bf16[40,2048]{1,0:T(8,128)(2,1)S(1)}, bf16[40,2048]{1,0:T(8,128)(2,1)S(1)}, u32[]{:S(2)}, u32[]{:S(2)}) %collective-permute-start.8) | collective-permute-done | bytes 163872 | tf_op jit(solution)/shard_map/ppermute | solution.py:432
  44.1 0.0 collective-permute-done.9.refs_5_
  44.1 0.3 combine_early.1
  44.4 0.4 combine_mid.1.begun_ref
  44.8 0.0 collective-permute-done.14.refs_0_
  44.8 0.0 collective-permute-done.15.refs_1_
  44.8 0.6 combine_late.1
  45.4 3.7 %collective-permute-start.16 = (bf16[128,512]{1,0:T(8,128)(2,1)S(1)}, bf16[128,512]{1,0:T(8,128)(2,1)S(1)}, u32[]{:S(2)}, u32[]{:S(2)}) collective-permute-start(bf16[128,512]{1,0:T(8,128)(2,1)S(1)} %get-tuple-element.58), channel_id=1, source_target_pairs={{0,24},{8,16},{16,8},{24,0},{1,25},{9,17},{17,9},{25,1},{2,26},{10... | collective-permute-start | bytes 393224 | tf_op jit(solution)/shard_map/ppermute | solution.py:432
  49.1 0.0 collective-permute-start.17
  49.1 0.8 %collective-permute-start.18 = (bf16[128,512]{1,0:T(8,128)(2,1)S(1)}, bf16[128,512]{1,0:T(8,128)(2,1)S(1)}, u32[]{:S(2)}, u32[]{:S(2)}) collective-permute-start(bf16[128,512]{1,0:T(8,128)(2,1)S(1)} %get-tuple-element.61), channel_id=1, source_target_pairs={{0,16},{8,24},{16,0},{24,8},{1,17},{9,25},{17,1},{25,9},{2,18},{10... | collective-permute-start | bytes 393224 | tf_op jit(solution)/shard_map/ppermute | solution.py:432
  49.8 2.2 %collective-permute-start.19 = (f32[8,128]{1,0:T(8,128)S(1)}, f32[8,128]{1,0:T(8,128)S(1)}, u32[]{:S(2)}, u32[]{:S(2)}) collective-permute-start(f32[8,128]{1,0:T(8,128)S(1)} %get-tuple-element.62), channel_id=1, source_target_pairs={{0,16},{8,24},{16,0},{24,8},{1,17},{9,25},{17,1},{25,9},{2,18},{10... | collective-permute-start | bytes 12296 | tf_op jit(solution)/shard_map/ppermute | solution.py:432
  52.0 8.8 %collective-permute-done.19.refs_4_ = f32[8,128]{1,0:T(8,128)S(1)} collective-permute-done((f32[8,128]{1,0:T(8,128)S(1)}, f32[8,128]{1,0:T(8,128)S(1)}, u32[]{:S(2)}, u32[]{:S(2)}) %collective-permute-start.19) | collective-permute-done | bytes 4128 | tf_op jit(solution)/shard_map/ppermute | solution.py:432
  60.8 0.0 collective-permute-done.16.refs_0_
  60.8 0.0 collective-permute-done.17.refs_1_
  60.9 0.0 collective-permute-done.18.refs_3_
  60.9 0.9 %finish.1 = bf16[512,512]{1,0:T(8,128)(2,1)} custom-call(bf16[128,512]{1,0:T(8,128)(2,1)S(1)} %collective-permute-done.16.refs_0_, bf16[128,512]{1,0:T(8,128)(2,1)S(1)} %collective-permute-done.17.refs_1_, bf16[128,512]{1,0:T(8,128)(2,1)S(1)} %get-tuple-element.60.refs_2_, bf16[128,512]{1,0:T(8,128)(2,1)S(1)} %collective-permute-done.18.refs_3_, ...), custom_call_target="tpu_custom_call" | custom-call | flops 1000000 | bytes 1000000 | tf_op jit(solution)/shard_map/finish/pallas_call | solution.py:415
  (5 shorter events, 0.0 us)
Async XLA Ops:
  1.6 7.5 %collective-permute-start = (bf16[40,2048]{1,0:T(8,128)(2,1)S(1)}, bf16[40,2048]{1,0:T(8,128)(2,1)S(1)}, u32[]{:S(2)}, u32[]{:S(2)}) collective-permute-start(bf16[40,2048]{1,0:T(8,128)(2,1)S(1)} %get-tuple-element.37), channel_id=1, source_target_pairs={{0,4},{1,5},{2,6},{3,7},{4,0},{5,1},{6,2},{7,3},{8,12},{9,13},{10,... | collective-permute-start | bytes 491528 | tf_op jit(solution)/shard_map/ppermute | solution.py:432
  4.6 8.0 %collective-permute-start.1 = (bf16[40,2048]{1,0:T(8,128)(2,1)S(1)}, bf16[40,2048]{1,0:T(8,128)(2,1)S(1)}, u32[]{:S(2)}, u32[]{:S(2)}) collective-permute-start(bf16[40,2048]{1,0:T(8,128)(2,1)S(1)} %get-tuple-element.38), channel_id=1, source_target_pairs={{0,2},{1,3},{2,0},{3,1},{4,6},{5,7},{6,4},{7,5},{8,10},{9,11},{10,... | collective-permute-start | bytes 491528 | tf_op jit(solution)/shard_map/ppermute | solution.py:432
  6.1 6.5 %collective-permute-start.2 = (bf16[40,2048]{1,0:T(8,128)(2,1)S(1)}, bf16[40,2048]{1,0:T(8,128)(2,1)S(1)}, u32[]{:S(2)}, u32[]{:S(2)}) collective-permute-start(bf16[40,2048]{1,0:T(8,128)(2,1)S(1)} %get-tuple-element.39), channel_id=1, source_target_pairs={{0,5},{1,4},{2,7},{3,6},{4,1},{5,0},{6,3},{7,2},{8,13},{9,12},{10,... | collective-permute-start | bytes 491528 | tf_op jit(solution)/shard_map/ppermute | solution.py:432
  6.1 8.1 %collective-permute-start.3 = (bf16[40,2048]{1,0:T(8,128)(2,1)S(1)}, bf16[40,2048]{1,0:T(8,128)(2,1)S(1)}, u32[]{:S(2)}, u32[]{:S(2)}) collective-permute-start(bf16[40,2048]{1,0:T(8,128)(2,1)S(1)} %get-tuple-element.40), channel_id=1, source_target_pairs={{0,3},{1,2},{2,1},{3,0},{4,7},{5,6},{6,5},{7,4},{8,11},{9,10},{10,... | collective-permute-start | bytes 491528 | tf_op jit(solution)/shard_map/ppermute | solution.py:432
  6.5 7.8 %collective-permute-start.4 = (bf16[40,2048]{1,0:T(8,128)(2,1)S(1)}, bf16[40,2048]{1,0:T(8,128)(2,1)S(1)}, u32[]{:S(2)}, u32[]{:S(2)}) collective-permute-start(bf16[40,2048]{1,0:T(8,128)(2,1)S(1)} %get-tuple-element.41), channel_id=1, source_target_pairs={{0,1},{1,0},{2,3},{3,2},{4,5},{5,4},{6,7},{7,6},{8,9},{9,8},{10,11... | collective-permute-start | bytes 491528 | tf_op jit(solution)/shard_map/ppermute | solution.py:432
  9.1 15.9 %collective-permute-start.10 = (bf16[40,2048]{1,0:T(8,128)(2,1)S(1)}, bf16[40,2048]{1,0:T(8,128)(2,1)S(1)}, u32[]{:S(2)}, u32[]{:S(2)}) collective-permute-start(bf16[40,2048]{1,0:T(8,128)(2,1)S(1)} %get-tuple-element.50), channel_id=1, source_target_pairs={{0,6},{1,7},{2,4},{3,5},{4,2},{5,3},{6,0},{7,1},{8,14},{9,15},{10,... | collective-permute-start | bytes 491528 | tf_op jit(solution)/shard_map/ppermute | solution.py:432
  12.6 12.4 %collective-permute-start.11 = (bf16[40,2048]{1,0:T(8,128)(2,1)S(1)}, bf16[40,2048]{1,0:T(8,128)(2,1)S(1)}, u32[]{:S(2)}, u32[]{:S(2)}) collective-permute-start(bf16[40,2048]{1,0:T(8,128)(2,1)S(1)} %get-tuple-element.51), channel_id=1, source_target_pairs={{0,7},{1,6},{2,5},{3,4},{4,3},{5,2},{6,1},{7,0},{8,15},{9,14},{10,... | collective-permute-start | bytes 491528 | tf_op jit(solution)/shard_map/ppermute | solution.py:432
  14.2 1.8 %copy-start = (bf16[1,704,2048]{2,1,0:T(8,128)(2,1)S(1)}, bf16[1,704,2048]{2,1,0:T(8,128)(2,1)}, u32[]{:S(2)}) copy-start(bf16[1,704,2048]{2,1,0:T(8,128)(2,1)} %param.14) | copy-start | bytes 8650756
  16.1 1.8 %copy-start.2 = (bf16[1,2048,704]{1,2,0:T(8,128)(2,1)S(1)}, bf16[1,2048,704]{1,2,0:T(8,128)(2,1)}, u32[]{:S(2)}) copy-start(bf16[1,2048,704]{1,2,0:T(8,128)(2,1)} %param.12) | copy-start | bytes 8650756
  17.9 1.8 %copy-start.4 = (bf16[1,2048,704]{1,2,0:T(8,128)(2,1)S(1)}, bf16[1,2048,704]{1,2,0:T(8,128)(2,1)}, u32[]{:S(2)}) copy-start(bf16[1,2048,704]{1,2,0:T(8,128)(2,1)} %param.13) | copy-start | bytes 8650756
  19.7 5.3 %copy-start.1 = (bf16[1,704,2048]{2,1,0:T(8,128)(2,1)S(1)}, bf16[1,704,2048]{2,1,0:T(8,128)(2,1)}, u32[]{:S(2)}) copy-start(bf16[1,704,2048]{2,1,0:T(8,128)(2,1)} %param.14) | copy-start | bytes 8650756
  19.7 5.3 %copy-start.3 = (bf16[1,2048,704]{1,2,0:T(8,128)(2,1)S(1)}, bf16[1,2048,704]{1,2,0:T(8,128)(2,1)}, u32[]{:S(2)}) copy-start(bf16[1,2048,704]{1,2,0:T(8,128)(2,1)} %param.12) | copy-start | bytes 8650756
  22.4 10.1 %collective-permute-start.5 = (bf16[40,2048]{1,0:T(8,128)(2,1)S(1)}, bf16[40,2048]{1,0:T(8,128)(2,1)S(1)}, u32[]{:S(2)}, u32[]{:S(2)}) collective-permute-start(bf16[40,2048]{1,0:T(8,128)(2,1)S(1)} %get-tuple-element.44), channel_id=1, source_target_pairs={{0,1},{1,0},{2,3},{3,2},{4,5},{5,4},{6,7},{7,6},{8,9},{9,8},{10,11... | collective-permute-start | bytes 491528 | tf_op jit(solution)/shard_map/ppermute | solution.py:432
  23.3 11.1 %collective-permute-start.6 = (bf16[40,2048]{1,0:T(8,128)(2,1)S(1)}, bf16[40,2048]{1,0:T(8,128)(2,1)S(1)}, u32[]{:S(2)}, u32[]{:S(2)}) collective-permute-start(bf16[40,2048]{1,0:T(8,128)(2,1)S(1)} %get-tuple-element.45), channel_id=1, source_target_pairs={{0,2},{1,3},{2,0},{3,1},{4,6},{5,7},{6,4},{7,5},{8,10},{9,11},{10,... | collective-permute-start | bytes 491528 | tf_op jit(solution)/shard_map/ppermute | solution.py:432
  26.9 9.8 %copy-start.6 = (s32[1,128,2]{1,2,0:T(2,128)S(1)}, s32[1,128,2]{1,2,0:T(2,128)}, u32[]{:S(2)}) copy-start(s32[1,128,2]{1,2,0:T(2,128)} %param.9) | copy-start | bytes 3076
  26.9 9.8 %copy-start.7 = (s32[1,128,2]{1,2,0:T(2,128)S(1)}, s32[1,128,2]{1,2,0:T(2,128)}, u32[]{:S(2)}) copy-start(s32[1,128,2]{1,2,0:T(2,128)} %param.10) | copy-start | bytes 3076
  26.9 9.8 %copy-start.8 = (f32[16]{0:T(128)S(1)}, f32[16]{0:T(128)}, u32[]{:S(2)}) copy-start(f32[16]{0:T(128)} %table_ref.1) | copy-start | bytes 196
  26.9 5.4 %collective-permute-start.12 = (bf16[40,512]{1,0:T(8,128)(2,1)S(1)}, bf16[40,512]{1,0:T(8,128)(2,1)S(1)}, u32[]{:S(2)}, u32[]{:S(2)}) collective-permute-start(bf16[40,512]{1,0:T(8,128)(2,1)S(1)} %get-tuple-element.52), channel_id=1, source_target_pairs={{0,6},{1,7},{2,4},{3,5},{4,2},{5,3},{6,0},{7,1},{8,14},{9,15},{10,... | collective-permute-start | bytes 122888 | tf_op jit(solution)/shard_map/ppermute | solution.py:432
  27.0 5.3 %collective-permute-start.13 = (bf16[40,512]{1,0:T(8,128)(2,1)S(1)}, bf16[40,512]{1,0:T(8,128)(2,1)S(1)}, u32[]{:S(2)}, u32[]{:S(2)}) collective-permute-start(bf16[40,512]{1,0:T(8,128)(2,1)S(1)} %get-tuple-element.53), channel_id=1, source_target_pairs={{0,7},{1,6},{2,5},{3,4},{4,3},{5,2},{6,1},{7,0},{8,15},{9,14},{10,... | collective-permute-start | bytes 122888 | tf_op jit(solution)/shard_map/ppermute | solution.py:432
  29.0 8.7 %collective-permute-start.7 = (bf16[40,2048]{1,0:T(8,128)(2,1)S(1)}, bf16[40,2048]{1,0:T(8,128)(2,1)S(1)}, u32[]{:S(2)}, u32[]{:S(2)}) collective-permute-start(bf16[40,2048]{1,0:T(8,128)(2,1)S(1)} %get-tuple-element.46), channel_id=1, source_target_pairs={{0,3},{1,2},{2,1},{3,0},{4,7},{5,6},{6,5},{7,4},{8,11},{9,10},{10,... | collective-permute-start | bytes 491528 | tf_op jit(solution)/shard_map/ppermute | solution.py:432
  32.3 11.8 %collective-permute-start.8 = (bf16[40,2048]{1,0:T(8,128)(2,1)S(1)}, bf16[40,2048]{1,0:T(8,128)(2,1)S(1)}, u32[]{:S(2)}, u32[]{:S(2)}) collective-permute-start(bf16[40,2048]{1,0:T(8,128)(2,1)S(1)} %get-tuple-element.47), channel_id=1, source_target_pairs={{0,4},{1,5},{2,6},{3,7},{4,0},{5,1},{6,2},{7,3},{8,12},{9,13},{10,... | collective-permute-start | bytes 491528 | tf_op jit(solution)/shard_map/ppermute | solution.py:432
  32.3 11.8 %collective-permute-start.9 = (bf16[40,2048]{1,0:T(8,128)(2,1)S(1)}, bf16[40,2048]{1,0:T(8,128)(2,1)S(1)}, u32[]{:S(2)}, u32[]{:S(2)}) collective-permute-start(bf16[40,2048]{1,0:T(8,128)(2,1)S(1)} %get-tuple-element.48), channel_id=1, source_target_pairs={{0,5},{1,4},{2,7},{3,6},{4,1},{5,0},{6,3},{7,2},{8,13},{9,12},{10,... | collective-permute-start | bytes 491528 | tf_op jit(solution)/shard_map/ppermute | solution.py:432
  32.5 12.3 %collective-permute-start.14 = (bf16[40,1536]{1,0:T(8,128)(2,1)S(1)}, bf16[40,1536]{1,0:T(8,128)(2,1)S(1)}, u32[]{:S(2)}, u32[]{:S(2)}) collective-permute-start(bf16[40,1536]{1,0:T(8,128)(2,1)S(1)} %get-tuple-element.56), channel_id=1, source_target_pairs={{0,6},{1,7},{2,4},{3,5},{4,2},{5,3},{6,0},{7,1},{8,14},{9,15},{10,... | collective-permute-start | bytes 368648 | tf_op jit(solution)/shard_map/ppermute | solution.py:432
  34.3 10.5 %collective-permute-start.15 = (bf16[40,1536]{1,0:T(8,128)(2,1)S(1)}, bf16[40,1536]{1,0:T(8,128)(2,1)S(1)}, u32[]{:S(2)}, u32[]{:S(2)}) collective-permute-start(bf16[40,1536]{1,0:T(8,128)(2,1)S(1)} %get-tuple-element.57), channel_id=1, source_target_pairs={{0,7},{1,6},{2,5},{3,4},{4,3},{5,2},{6,1},{7,0},{8,15},{9,14},{10,... | collective-permute-start | bytes 368648 | tf_op jit(solution)/shard_map/ppermute | solution.py:432
  36.7 0.9 %copy-start.5 = (f32[2048]{0:T(1024)S(1)}, f32[2048]{0:T(1024)}, u32[]{:S(2)}) copy-start(f32[2048]{0:T(1024)} %param.15) | copy-start | bytes 24580
  45.4 15.5 %collective-permute-start.16 = (bf16[128,512]{1,0:T(8,128)(2,1)S(1)}, bf16[128,512]{1,0:T(8,128)(2,1)S(1)}, u32[]{:S(2)}, u32[]{:S(2)}) collective-permute-start(bf16[128,512]{1,0:T(8,128)(2,1)S(1)} %get-tuple-element.58), channel_id=1, source_target_pairs={{0,24},{8,16},{16,8},{24,0},{1,25},{9,17},{17,9},{25,1},{2,26},{10... | collective-permute-start | bytes 393224 | tf_op jit(solution)/shard_map/ppermute | solution.py:432
  49.1 11.8 %collective-permute-start.17 = (bf16[128,512]{1,0:T(8,128)(2,1)S(1)}, bf16[128,512]{1,0:T(8,128)(2,1)S(1)}, u32[]{:S(2)}, u32[]{:S(2)}) collective-permute-start(bf16[128,512]{1,0:T(8,128)(2,1)S(1)} %get-tuple-element.59), channel_id=1, source_target_pairs={{0,8},{8,0},{16,24},{24,16},{1,9},{9,1},{17,25},{25,17},{2,10},{10... | collective-permute-start | bytes 393224 | tf_op jit(solution)/shard_map/ppermute | solution.py:432
  49.1 11.8 %collective-permute-start.18 = (bf16[128,512]{1,0:T(8,128)(2,1)S(1)}, bf16[128,512]{1,0:T(8,128)(2,1)S(1)}, u32[]{:S(2)}, u32[]{:S(2)}) collective-permute-start(bf16[128,512]{1,0:T(8,128)(2,1)S(1)} %get-tuple-element.61), channel_id=1, source_target_pairs={{0,16},{8,24},{16,0},{24,8},{1,17},{9,25},{17,1},{25,9},{2,18},{10... | collective-permute-start | bytes 393224 | tf_op jit(solution)/shard_map/ppermute | solution.py:432
  49.8 11.0 %collective-permute-start.19 = (f32[8,128]{1,0:T(8,128)S(1)}, f32[8,128]{1,0:T(8,128)S(1)}, u32[]{:S(2)}, u32[]{:S(2)}) collective-permute-start(f32[8,128]{1,0:T(8,128)S(1)} %get-tuple-element.62), channel_id=1, source_target_pairs={{0,16},{8,24},{16,0},{24,8},{1,17},{9,25},{17,1},{25,9},{2,18},{10... | collective-permute-start | bytes 12296 | tf_op jit(solution)/shard_map/ppermute | solution.py:432

commit v12 on v11

--- a/solution.py
+++ b/solution.py
@@ -119,20 +119,18 @@
 
 def dispatch(route_rows, own_rows, experts, capacity):
     width = own_rows.shape[1]
-    return pl.pallas_call(
+    *blocks, route_held = pl.pallas_call(
         functools.partial(dispatch_body, experts, capacity),
-        out_shape=[jax.ShapeDtypeStruct((capacity, width), BF16)] * experts,
+        out_shape=[jax.ShapeDtypeStruct((capacity, width), BF16)] * experts
+        + [jax.ShapeDtypeStruct(route_rows.shape, jnp.int32)],
         in_specs=[pl.BlockSpec(memory_space=pltpu.HBM)] * 2,
-        out_specs=[vmem()] * experts,
-        scratch_shapes=[
-            pltpu.VMEM(route_rows.shape, jnp.int32),
-            pltpu.VMEM(own_rows.shape, BF16),
-            pltpu.SemaphoreType.DMA((2,)),
-        ],
+        out_specs=[vmem()] * (experts + 1),
+        scratch_shapes=[pltpu.VMEM(own_rows.shape, BF16), pltpu.SemaphoreType.DMA((2,))],
         name="dispatch",
         cost_estimate=pl.CostEstimate(flops=10**8, transcendentals=0, bytes_accessed=2 * 10**6),
         compiler_params=pltpu.CompilerParams(vmem_limit_bytes=16 * 2**20),
     )(route_rows, own_rows)
+    return blocks, route_held
 
 
 def selector_body(experts, capacity, route_ref, code_ref, table_ref, *refs):
@@ -454,9 +452,8 @@
     early = (ways // 2,)
     late = tuple(k for k in range(ways - 1, -1, -1) if k not in early)
 
-    route_rows = routes[0].T
-    blocks = dispatch(
-        pltpu.with_memory_space_constraint(route_rows, pltpu.HBM),
+    blocks, route_rows = dispatch(
+        pltpu.with_memory_space_constraint(routes[0].T, pltpu.HBM),
         pltpu.with_memory_space_constraint(own_rows, pltpu.HBM),
         experts, capacity,
     )

time: 62 us -> 61.9 us (level)
    unnamed x18 -> x16, local copies, waits for them, and re-layouts: 5.47 us -> 5.47 us
where the time goes in v12:
time: 61.9 us; the launch traced here: 61.7 us
  starting transfers between devices  25.4 us (41%)
  waiting for transfers between devices  21 us (34%)
  Pallas kernels  9.66 us (16%)
  local copies, waits for them, and re-layouts  5.47 us (9%)
    ppermute x20, starting transfers between devices, swap(): return lax.ppermute(value, axis, [(i, i ^ offset) for i in range(size)])  25.4 us
    ppermute x20, waiting for transfers between devices, swap(): return lax.ppermute(value, axis, [(i, i ^ offset) for i in range(size)])  21 us
    unnamed x16, local copies, waits for them, and re-layouts  5.47 us
    pallas_call x2, Pallas kernels, expert_call(): pl.pallas_call(functools.partial(expert_body, count, chunk, plan), out_sh...  4.56 us
    pallas_call x1, Pallas kernels, dispatch(): pl.pallas_call(functools.partial(dispatch_body, experts, capacity), out_s...  1.57 us
  transfers between devices with their start and end apart: 20, of which 5 were waited for; matrix products, arithmetic and copies ran while one was open for 0% of the time, Pallas kernels for 11%

profile of v12, /device:TPU:0, one launch (start us, length us, event | category | flops | bytes accessed | tf_op | source)
XLA Modules:
  0.0 61.7 jit_solution(2090775157128973130)
XLA Ops:
  0.0 1.6 %dispatch.1 = (bf16[40,2048]{1,0:T(8,128)(2,1)S(1)}, bf16[40,2048]{1,0:T(8,128)(2,1)S(1)}, bf16[40,2048]{1,0:T(8,128)(2,1)S(1)}, bf16[40,2048]{1,0:T(8,128)(2,1)...) custom-call(s32[2,128]{1,0:T(2,128)} %bitcast.27, ...), custom_call_target="tpu_custom_call" | custom-call | flops 100000000 | bytes 2000000 | tf_op jit(solution)/shard_map/dispatch/pallas_call | solution.py:122
  1.6 3.1 %collective-permute-start = (bf16[40,2048]{1,0:T(8,128)(2,1)S(1)}, bf16[40,2048]{1,0:T(8,128)(2,1)S(1)}, u32[]{:S(2)}, u32[]{:S(2)}) collective-permute-start(bf16[40,2048]{1,0:T(8,128)(2,1)S(1)} %get-tuple-element.39), channel_id=1, source_target_pairs={{0,4},{1,5},{2,6},{3,7},{4,0},{5,1},{6,2},{7,3},{8,12},{9,13},{10,... | collective-permute-start | bytes 491528 | tf_op jit(solution)/shard_map/ppermute | solution.py:430
  4.6 1.5 %collective-permute-start.1 = (bf16[40,2048]{1,0:T(8,128)(2,1)S(1)}, bf16[40,2048]{1,0:T(8,128)(2,1)S(1)}, u32[]{:S(2)}, u32[]{:S(2)}) collective-permute-start(bf16[40,2048]{1,0:T(8,128)(2,1)S(1)} %get-tuple-element.40), channel_id=1, source_target_pairs={{0,2},{1,3},{2,0},{3,1},{4,6},{5,7},{6,4},{7,5},{8,10},{9,11},{10,... | collective-permute-start | bytes 491528 | tf_op jit(solution)/shard_map/ppermute | solution.py:430
  6.1 0.0 collective-permute-start.2
  6.1 0.3 collective-permute-start.3
  6.5 0.3 collective-permute-start.4
  6.8 2.3 %collective-permute-done.refs_0_ = bf16[40,2048]{1,0:T(8,128)(2,1)S(1)} collective-permute-done((bf16[40,2048]{1,0:T(8,128)(2,1)S(1)}, bf16[40,2048]{1,0:T(8,128)(2,1)S(1)}, u32[]{:S(2)}, u32[]{:S(2)}) %collective-permute-start) | collective-permute-done | bytes 163872 | tf_op jit(solution)/shard_map/ppermute | solution.py:430
  9.1 3.6 %collective-permute-start.10 = (bf16[40,2048]{1,0:T(8,128)(2,1)S(1)}, bf16[40,2048]{1,0:T(8,128)(2,1)S(1)}, u32[]{:S(2)}, u32[]{:S(2)}) collective-permute-start(bf16[40,2048]{1,0:T(8,128)(2,1)S(1)} %get-tuple-element.52), channel_id=1, source_target_pairs={{0,6},{1,7},{2,4},{3,5},{4,2},{5,3},{6,0},{7,1},{8,14},{9,15},{10,... | collective-permute-start | bytes 491528 | tf_op jit(solution)/shard_map/ppermute | solution.py:430
  12.6 0.0 collective-permute-done.1.refs_1_
  12.6 0.0 collective-permute-start.11
  12.6 0.0 collective-permute-done.2.refs_2_
  12.7 1.6 %collective-permute-done.3.refs_3_ = bf16[40,2048]{1,0:T(8,128)(2,1)S(1)} collective-permute-done((bf16[40,2048]{1,0:T(8,128)(2,1)S(1)}, bf16[40,2048]{1,0:T(8,128)(2,1)S(1)}, u32[]{:S(2)}, u32[]{:S(2)}) %collective-permute-start.3) | collective-permute-done | bytes 163872 | tf_op jit(solution)/shard_map/ppermute | solution.py:430
  14.2 0.0 collective-permute-done.4.refs_4_
  14.2 0.0 copy-start
  14.2 1.8 %copy-done = bf16[1,704,2048]{2,1,0:T(8,128)(2,1)S(1)} copy-done((bf16[1,704,2048]{2,1,0:T(8,128)(2,1)S(1)}, bf16[1,704,2048]{2,1,0:T(8,128)(2,1)}, u32[]{:S(2)}) %copy-start) | copy-done | bytes 2883608
  16.1 0.0 copy-start.2
  16.1 1.8 %copy-done.2 = bf16[1,2048,704]{1,2,0:T(8,128)(2,1)S(1)} copy-done((bf16[1,2048,704]{1,2,0:T(8,128)(2,1)S(1)}, bf16[1,2048,704]{1,2,0:T(8,128)(2,1)}, u32[]{:S(2)}) %copy-start.2) | copy-done | bytes 2883608
  17.9 0.0 copy-start.4
  17.9 1.8 %copy-done.4 = bf16[1,2048,704]{1,2,0:T(8,128)(2,1)S(1)} copy-done((bf16[1,2048,704]{1,2,0:T(8,128)(2,1)S(1)}, bf16[1,2048,704]{1,2,0:T(8,128)(2,1)}, u32[]{:S(2)}) %copy-start.4) | copy-done | bytes 2883608
  19.7 0.0 copy-start.1
  19.7 0.0 copy-start.3
  19.7 2.7 %shard_map.82 = (bf16[240,704]{1,0:T(8,128)(2,1)}, bf16[40,2048]{1,0:T(8,128)(2,1)S(1)}, bf16[40,2048]{1,0:T(8,128)(2,1)S(1)}, bf16[40,2048]{1,0:T(8,128)(2,1)S(...) custom-call(bf16[40,2048]{1,0:T(8,128)(2,1)S(1)} %collective-permute-done.refs_0_, ...), custom_call_target="tpu_custom_call" | custom-call | flops 1730150400 | bytes 8000000 | tf_op jit(solution)/shard_map/pallas_call | solution.py:222
  22.4 0.9 %collective-permute-start.5 = (bf16[40,2048]{1,0:T(8,128)(2,1)S(1)}, bf16[40,2048]{1,0:T(8,128)(2,1)S(1)}, u32[]{:S(2)}, u32[]{:S(2)}) collective-permute-start(bf16[40,2048]{1,0:T(8,128)(2,1)S(1)} %get-tuple-element.46), channel_id=1, source_target_pairs={{0,1},{1,0},{2,3},{3,2},{4,5},{5,4},{6,7},{7,6},{8,9},{9,8},{10,11... | collective-permute-start | bytes 491528 | tf_op jit(solution)/shard_map/ppermute | solution.py:430
  23.3 1.7 %collective-permute-start.6 = (bf16[40,2048]{1,0:T(8,128)(2,1)S(1)}, bf16[40,2048]{1,0:T(8,128)(2,1)S(1)}, u32[]{:S(2)}, u32[]{:S(2)}) collective-permute-start(bf16[40,2048]{1,0:T(8,128)(2,1)S(1)} %get-tuple-element.47), channel_id=1, source_target_pairs={{0,2},{1,3},{2,0},{3,1},{4,6},{5,7},{6,4},{7,5},{8,10},{9,11},{10,... | collective-permute-start | bytes 491528 | tf_op jit(solution)/shard_map/ppermute | solution.py:430
  25.0 0.0 collective-permute-done.10.refs_0_
  25.0 0.0 collective-permute-done.11.refs_1_
  25.0 0.0 copy-done.1
  25.0 0.0 copy-done.3
  25.0 1.9 %shard_map.83 = (bf16[80,704]{1,0:T(8,128)(2,1)S(1)}, bf16[40,512]{1,0:T(8,128)(2,1)S(1)}, bf16[40,512]{1,0:T(8,128)(2,1)S(1)}) custom-call(bf16[40,2048]{1,0:T(8,128)(2,1)S(1)} %collective-permute-done.10.refs_0_, bf16[40,2048]{1,0:T(8,128)(2,1)S(1)} %collective-permute-done.11.refs_1_, bf16[704,2048]{1,0:T(8,128)(2,1)S(1)} %bitcast.20, ...), custom_call_target="tpu_custom_call" | custom-call | flops 576716800 | bytes 8000000 | tf_op jit(solution)/shard_map/pallas_call | solution.py:222
  26.9 0.0 copy-start.6
  26.9 0.0 copy-start.7
  26.9 0.1 collective-permute-start.12
  27.0 2.0 %collective-permute-start.13 = (bf16[40,512]{1,0:T(8,128)(2,1)S(1)}, bf16[40,512]{1,0:T(8,128)(2,1)S(1)}, u32[]{:S(2)}, u32[]{:S(2)}) collective-permute-start(bf16[40,512]{1,0:T(8,128)(2,1)S(1)} %get-tuple-element.55), channel_id=1, source_target_pairs={{0,7},{1,6},{2,5},{3,4},{4,3},{5,2},{6,1},{7,0},{8,15},{9,14},{10,... | collective-permute-start | bytes 122888 | tf_op jit(solution)/shard_map/ppermute | solution.py:430
  29.0 1.0 %collective-permute-start.7 = (bf16[40,2048]{1,0:T(8,128)(2,1)S(1)}, bf16[40,2048]{1,0:T(8,128)(2,1)S(1)}, u32[]{:S(2)}, u32[]{:S(2)}) collective-permute-start(bf16[40,2048]{1,0:T(8,128)(2,1)S(1)} %get-tuple-element.48), channel_id=1, source_target_pairs={{0,3},{1,2},{2,1},{3,0},{4,7},{5,6},{6,5},{7,4},{8,11},{9,10},{10,... | collective-permute-start | bytes 491528 | tf_op jit(solution)/shard_map/ppermute | solution.py:430
  29.9 0.5 shard_map.85
  30.4 1.9 %collective-permute-done.12.refs_6_ = bf16[40,512]{1,0:T(8,128)(2,1)S(1)} collective-permute-done((bf16[40,512]{1,0:T(8,128)(2,1)S(1)}, bf16[40,512]{1,0:T(8,128)(2,1)S(1)}, u32[]{:S(2)}, u32[]{:S(2)}) %collective-permute-start.12) | collective-permute-done | bytes 40992 | tf_op jit(solution)/shard_map/ppermute | solution.py:430
  32.3 0.0 collective-permute-start.8
  32.3 0.0 collective-permute-done.13.refs_7_
  32.3 0.2 collective-permute-start.9
  32.5 0.0 collective-permute-done.5.refs_1_
  32.5 1.8 %collective-permute-start.14 = (bf16[40,1536]{1,0:T(8,128)(2,1)S(1)}, bf16[40,1536]{1,0:T(8,128)(2,1)S(1)}, u32[]{:S(2)}, u32[]{:S(2)}) collective-permute-start(bf16[40,1536]{1,0:T(8,128)(2,1)S(1)} %get-tuple-element.58), channel_id=1, source_target_pairs={{0,6},{1,7},{2,4},{3,5},{4,2},{5,3},{6,0},{7,1},{8,14},{9,15},{10,... | collective-permute-start | bytes 368648 | tf_op jit(solution)/shard_map/ppermute | solution.py:430
  34.3 0.0 collective-permute-done.6.refs_2_
  34.3 2.4 %collective-permute-start.15 = (bf16[40,1536]{1,0:T(8,128)(2,1)S(1)}, bf16[40,1536]{1,0:T(8,128)(2,1)S(1)}, u32[]{:S(2)}, u32[]{:S(2)}) collective-permute-start(bf16[40,1536]{1,0:T(8,128)(2,1)S(1)} %get-tuple-element.59), channel_id=1, source_target_pairs={{0,7},{1,6},{2,5},{3,4},{4,3},{5,2},{6,1},{7,0},{8,15},{9,14},{10,... | collective-permute-start | bytes 368648 | tf_op jit(solution)/shard_map/ppermute | solution.py:430
  36.7 0.0 copy-done.6
  36.7 0.0 copy-done.7
  36.7 0.9 %selector.1 = (bf16[256,320]{1,0:T(8,128)(2,1)S(1)}, bf16[256,240]{1,0:T(8,128)(2,1)S(1)}, bf16[256,80]{1,0:T(8,128)(2,1)S(1)}, f32[2,128,128]{2,1,0:T(8,128)S(1)}) custom-call(s32[2,128]{1,0:T(2,128)S(1)} %get-tuple-element.35.route_ref, s32[2,128]{1,0:T(2,128)S(1)} %bitcast.25, f32[16]{0:T(128)S(1)} %copy-done.7), custom_call_target="tpu_custom_call" | custom-call | flops 20000000000 | bytes 100000000 | tf_op jit(solution)/shard_map/selector/pallas_call | solution.py:163
  37.6 0.0 copy-done.5
  37.6 0.0 collective-permute-done.7.refs_3_
  37.6 6.4 %collective-permute-done.8.refs_4_ = bf16[40,2048]{1,0:T(8,128)(2,1)S(1)} collective-permute-done((bf16[40,2048]{1,0:T(8,128)(2,1)S(1)}, bf16[40,2048]{1,0:T(8,128)(2,1)S(1)}, u32[]{:S(2)}, u32[]{:S(2)}) %collective-permute-start.8) | collective-permute-done | bytes 163872 | tf_op jit(solution)/shard_map/ppermute | solution.py:430
  44.1 0.0 collective-permute-done.9.refs_5_
  44.1 0.3 combine_early.1
  44.4 0.4 combine_mid.1.begun_ref
  44.8 0.0 collective-permute-done.14.refs_0_
  44.8 0.0 collective-permute-done.15.refs_1_
  44.8 0.6 combine_late.1
  45.4 3.7 %collective-permute-start.16 = (bf16[128,512]{1,0:T(8,128)(2,1)S(1)}, bf16[128,512]{1,0:T(8,128)(2,1)S(1)}, u32[]{:S(2)}, u32[]{:S(2)}) collective-permute-start(bf16[128,512]{1,0:T(8,128)(2,1)S(1)} %get-tuple-element.60), channel_id=1, source_target_pairs={{0,24},{8,16},{16,8},{24,0},{1,25},{9,17},{17,9},{25,1},{2,26},{10... | collective-permute-start | bytes 393224 | tf_op jit(solution)/shard_map/ppermute | solution.py:430
  49.0 0.0 collective-permute-start.17
  49.0 0.8 %collective-permute-start.18 = (bf16[128,512]{1,0:T(8,128)(2,1)S(1)}, bf16[128,512]{1,0:T(8,128)(2,1)S(1)}, u32[]{:S(2)}, u32[]{:S(2)}) collective-permute-start(bf16[128,512]{1,0:T(8,128)(2,1)S(1)} %get-tuple-element.63), channel_id=1, source_target_pairs={{0,16},{8,24},{16,0},{24,8},{1,17},{9,25},{17,1},{25,9},{2,18},{10... | collective-permute-start | bytes 393224 | tf_op jit(solution)/shard_map/ppermute | solution.py:430
  49.8 2.1 %collective-permute-start.19 = (f32[8,128]{1,0:T(8,128)S(1)}, f32[8,128]{1,0:T(8,128)S(1)}, u32[]{:S(2)}, u32[]{:S(2)}) collective-permute-start(f32[8,128]{1,0:T(8,128)S(1)} %get-tuple-element.64), channel_id=1, source_target_pairs={{0,16},{8,24},{16,0},{24,8},{1,17},{9,25},{17,1},{25,9},{2,18},{10... | collective-permute-start | bytes 12296 | tf_op jit(solution)/shard_map/ppermute | solution.py:430
  52.0 8.8 %collective-permute-done.19.refs_4_ = f32[8,128]{1,0:T(8,128)S(1)} collective-permute-done((f32[8,128]{1,0:T(8,128)S(1)}, f32[8,128]{1,0:T(8,128)S(1)}, u32[]{:S(2)}, u32[]{:S(2)}) %collective-permute-start.19) | collective-permute-done | bytes 4128 | tf_op jit(solution)/shard_map/ppermute | solution.py:430
  60.8 0.0 collective-permute-done.16.refs_0_
  60.8 0.0 collective-permute-done.17.refs_1_
  60.8 0.0 collective-permute-done.18.refs_3_
  60.8 0.9 %finish.1 = bf16[512,512]{1,0:T(8,128)(2,1)} custom-call(bf16[128,512]{1,0:T(8,128)(2,1)S(1)} %collective-permute-done.16.refs_0_, bf16[128,512]{1,0:T(8,128)(2,1)S(1)} %collective-permute-done.17.refs_1_, bf16[128,512]{1,0:T(8,128)(2,1)S(1)} %get-tuple-element.62.refs_2_, bf16[128,512]{1,0:T(8,128)(2,1)S(1)} %collective-permute-done.18.refs_3_, ...), custom_call_target="tpu_custom_call" | custom-call | flops 1000000 | bytes 1000000 | tf_op jit(solution)/shard_map/finish/pallas_call | solution.py:413
  (3 shorter events, 0.0 us)
Async XLA Ops:
  1.6 7.5 %collective-permute-start = (bf16[40,2048]{1,0:T(8,128)(2,1)S(1)}, bf16[40,2048]{1,0:T(8,128)(2,1)S(1)}, u32[]{:S(2)}, u32[]{:S(2)}) collective-permute-start(bf16[40,2048]{1,0:T(8,128)(2,1)S(1)} %get-tuple-element.39), channel_id=1, source_target_pairs={{0,4},{1,5},{2,6},{3,7},{4,0},{5,1},{6,2},{7,3},{8,12},{9,13},{10,... | collective-permute-start | bytes 491528 | tf_op jit(solution)/shard_map/ppermute | solution.py:430
  4.6 8.0 %collective-permute-start.1 = (bf16[40,2048]{1,0:T(8,128)(2,1)S(1)}, bf16[40,2048]{1,0:T(8,128)(2,1)S(1)}, u32[]{:S(2)}, u32[]{:S(2)}) collective-permute-start(bf16[40,2048]{1,0:T(8,128)(2,1)S(1)} %get-tuple-element.40), channel_id=1, source_target_pairs={{0,2},{1,3},{2,0},{3,1},{4,6},{5,7},{6,4},{7,5},{8,10},{9,11},{10,... | collective-permute-start | bytes 491528 | tf_op jit(solution)/shard_map/ppermute | solution.py:430
  6.1 6.5 %collective-permute-start.2 = (bf16[40,2048]{1,0:T(8,128)(2,1)S(1)}, bf16[40,2048]{1,0:T(8,128)(2,1)S(1)}, u32[]{:S(2)}, u32[]{:S(2)}) collective-permute-start(bf16[40,2048]{1,0:T(8,128)(2,1)S(1)} %get-tuple-element.41), channel_id=1, source_target_pairs={{0,5},{1,4},{2,7},{3,6},{4,1},{5,0},{6,3},{7,2},{8,13},{9,12},{10,... | collective-permute-start | bytes 491528 | tf_op jit(solution)/shard_map/ppermute | solution.py:430
  6.1 8.1 %collective-permute-start.3 = (bf16[40,2048]{1,0:T(8,128)(2,1)S(1)}, bf16[40,2048]{1,0:T(8,128)(2,1)S(1)}, u32[]{:S(2)}, u32[]{:S(2)}) collective-permute-start(bf16[40,2048]{1,0:T(8,128)(2,1)S(1)} %get-tuple-element.42), channel_id=1, source_target_pairs={{0,3},{1,2},{2,1},{3,0},{4,7},{5,6},{6,5},{7,4},{8,11},{9,10},{10,... | collective-permute-start | bytes 491528 | tf_op jit(solution)/shard_map/ppermute | solution.py:430
  6.5 7.8 %collective-permute-start.4 = (bf16[40,2048]{1,0:T(8,128)(2,1)S(1)}, bf16[40,2048]{1,0:T(8,128)(2,1)S(1)}, u32[]{:S(2)}, u32[]{:S(2)}) collective-permute-start(bf16[40,2048]{1,0:T(8,128)(2,1)S(1)} %get-tuple-element.43), channel_id=1, source_target_pairs={{0,1},{1,0},{2,3},{3,2},{4,5},{5,4},{6,7},{7,6},{8,9},{9,8},{10,11... | collective-permute-start | bytes 491528 | tf_op jit(solution)/shard_map/ppermute | solution.py:430
  9.1 15.9 %collective-permute-start.10 = (bf16[40,2048]{1,0:T(8,128)(2,1)S(1)}, bf16[40,2048]{1,0:T(8,128)(2,1)S(1)}, u32[]{:S(2)}, u32[]{:S(2)}) collective-permute-start(bf16[40,2048]{1,0:T(8,128)(2,1)S(1)} %get-tuple-element.52), channel_id=1, source_target_pairs={{0,6},{1,7},{2,4},{3,5},{4,2},{5,3},{6,0},{7,1},{8,14},{9,15},{10,... | collective-permute-start | bytes 491528 | tf_op jit(solution)/shard_map/ppermute | solution.py:430
  12.6 12.4 %collective-permute-start.11 = (bf16[40,2048]{1,0:T(8,128)(2,1)S(1)}, bf16[40,2048]{1,0:T(8,128)(2,1)S(1)}, u32[]{:S(2)}, u32[]{:S(2)}) collective-permute-start(bf16[40,2048]{1,0:T(8,128)(2,1)S(1)} %get-tuple-element.53), channel_id=1, source_target_pairs={{0,7},{1,6},{2,5},{3,4},{4,3},{5,2},{6,1},{7,0},{8,15},{9,14},{10,... | collective-permute-start | bytes 491528 | tf_op jit(solution)/shard_map/ppermute | solution.py:430
  14.2 1.8 %copy-start = (bf16[1,704,2048]{2,1,0:T(8,128)(2,1)S(1)}, bf16[1,704,2048]{2,1,0:T(8,128)(2,1)}, u32[]{:S(2)}) copy-start(bf16[1,704,2048]{2,1,0:T(8,128)(2,1)} %param.14) | copy-start | bytes 8650756
  16.1 1.8 %copy-start.2 = (bf16[1,2048,704]{1,2,0:T(8,128)(2,1)S(1)}, bf16[1,2048,704]{1,2,0:T(8,128)(2,1)}, u32[]{:S(2)}) copy-start(bf16[1,2048,704]{1,2,0:T(8,128)(2,1)} %param.12) | copy-start | bytes 8650756
  17.9 1.8 %copy-start.4 = (bf16[1,2048,704]{1,2,0:T(8,128)(2,1)S(1)}, bf16[1,2048,704]{1,2,0:T(8,128)(2,1)}, u32[]{:S(2)}) copy-start(bf16[1,2048,704]{1,2,0:T(8,128)(2,1)} %param.13) | copy-start | bytes 8650756
  19.7 5.3 %copy-start.1 = (bf16[1,704,2048]{2,1,0:T(8,128)(2,1)S(1)}, bf16[1,704,2048]{2,1,0:T(8,128)(2,1)}, u32[]{:S(2)}) copy-start(bf16[1,704,2048]{2,1,0:T(8,128)(2,1)} %param.14) | copy-start | bytes 8650756
  19.7 5.3 %copy-start.3 = (bf16[1,2048,704]{1,2,0:T(8,128)(2,1)S(1)}, bf16[1,2048,704]{1,2,0:T(8,128)(2,1)}, u32[]{:S(2)}) copy-start(bf16[1,2048,704]{1,2,0:T(8,128)(2,1)} %param.12) | copy-start | bytes 8650756
  22.4 10.1 %collective-permute-start.5 = (bf16[40,2048]{1,0:T(8,128)(2,1)S(1)}, bf16[40,2048]{1,0:T(8,128)(2,1)S(1)}, u32[]{:S(2)}, u32[]{:S(2)}) collective-permute-start(bf16[40,2048]{1,0:T(8,128)(2,1)S(1)} %get-tuple-element.46), channel_id=1, source_target_pairs={{0,1},{1,0},{2,3},{3,2},{4,5},{5,4},{6,7},{7,6},{8,9},{9,8},{10,11... | collective-permute-start | bytes 491528 | tf_op jit(solution)/shard_map/ppermute | solution.py:430
  23.3 11.0 %collective-permute-start.6 = (bf16[40,2048]{1,0:T(8,128)(2,1)S(1)}, bf16[40,2048]{1,0:T(8,128)(2,1)S(1)}, u32[]{:S(2)}, u32[]{:S(2)}) collective-permute-start(bf16[40,2048]{1,0:T(8,128)(2,1)S(1)} %get-tuple-element.47), channel_id=1, source_target_pairs={{0,2},{1,3},{2,0},{3,1},{4,6},{5,7},{6,4},{7,5},{8,10},{9,11},{10,... | collective-permute-start | bytes 491528 | tf_op jit(solution)/shard_map/ppermute | solution.py:430
  26.9 9.8 %copy-start.6 = (s32[1,128,2]{1,2,0:T(2,128)S(1)}, s32[1,128,2]{1,2,0:T(2,128)}, u32[]{:S(2)}) copy-start(s32[1,128,2]{1,2,0:T(2,128)} %param.10) | copy-start | bytes 3076
  26.9 9.8 %copy-start.7 = (f32[16]{0:T(128)S(1)}, f32[16]{0:T(128)}, u32[]{:S(2)}) copy-start(f32[16]{0:T(128)} %table_ref.1) | copy-start | bytes 196
  26.9 5.4 %collective-permute-start.12 = (bf16[40,512]{1,0:T(8,128)(2,1)S(1)}, bf16[40,512]{1,0:T(8,128)(2,1)S(1)}, u32[]{:S(2)}, u32[]{:S(2)}) collective-permute-start(bf16[40,512]{1,0:T(8,128)(2,1)S(1)} %get-tuple-element.54), channel_id=1, source_target_pairs={{0,6},{1,7},{2,4},{3,5},{4,2},{5,3},{6,0},{7,1},{8,14},{9,15},{10,... | collective-permute-start | bytes 122888 | tf_op jit(solution)/shard_map/ppermute | solution.py:430
  27.0 5.3 %collective-permute-start.13 = (bf16[40,512]{1,0:T(8,128)(2,1)S(1)}, bf16[40,512]{1,0:T(8,128)(2,1)S(1)}, u32[]{:S(2)}, u32[]{:S(2)}) collective-permute-start(bf16[40,512]{1,0:T(8,128)(2,1)S(1)} %get-tuple-element.55), channel_id=1, source_target_pairs={{0,7},{1,6},{2,5},{3,4},{4,3},{5,2},{6,1},{7,0},{8,15},{9,14},{10,... | collective-permute-start | bytes 122888 | tf_op jit(solution)/shard_map/ppermute | solution.py:430
  29.0 8.7 %collective-permute-start.7 = (bf16[40,2048]{1,0:T(8,128)(2,1)S(1)}, bf16[40,2048]{1,0:T(8,128)(2,1)S(1)}, u32[]{:S(2)}, u32[]{:S(2)}) collective-permute-start(bf16[40,2048]{1,0:T(8,128)(2,1)S(1)} %get-tuple-element.48), channel_id=1, source_target_pairs={{0,3},{1,2},{2,1},{3,0},{4,7},{5,6},{6,5},{7,4},{8,11},{9,10},{10,... | collective-permute-start | bytes 491528 | tf_op jit(solution)/shard_map/ppermute | solution.py:430
  32.3 11.8 %collective-permute-start.8 = (bf16[40,2048]{1,0:T(8,128)(2,1)S(1)}, bf16[40,2048]{1,0:T(8,128)(2,1)S(1)}, u32[]{:S(2)}, u32[]{:S(2)}) collective-permute-start(bf16[40,2048]{1,0:T(8,128)(2,1)S(1)} %get-tuple-element.49), channel_id=1, source_target_pairs={{0,4},{1,5},{2,6},{3,7},{4,0},{5,1},{6,2},{7,3},{8,12},{9,13},{10,... | collective-permute-start | bytes 491528 | tf_op jit(solution)/shard_map/ppermute | solution.py:430
  32.3 11.8 %collective-permute-start.9 = (bf16[40,2048]{1,0:T(8,128)(2,1)S(1)}, bf16[40,2048]{1,0:T(8,128)(2,1)S(1)}, u32[]{:S(2)}, u32[]{:S(2)}) collective-permute-start(bf16[40,2048]{1,0:T(8,128)(2,1)S(1)} %get-tuple-element.50), channel_id=1, source_target_pairs={{0,5},{1,4},{2,7},{3,6},{4,1},{5,0},{6,3},{7,2},{8,13},{9,12},{10,... | collective-permute-start | bytes 491528 | tf_op jit(solution)/shard_map/ppermute | solution.py:430
  32.5 12.3 %collective-permute-start.14 = (bf16[40,1536]{1,0:T(8,128)(2,1)S(1)}, bf16[40,1536]{1,0:T(8,128)(2,1)S(1)}, u32[]{:S(2)}, u32[]{:S(2)}) collective-permute-start(bf16[40,1536]{1,0:T(8,128)(2,1)S(1)} %get-tuple-element.58), channel_id=1, source_target_pairs={{0,6},{1,7},{2,4},{3,5},{4,2},{5,3},{6,0},{7,1},{8,14},{9,15},{10,... | collective-permute-start | bytes 368648 | tf_op jit(solution)/shard_map/ppermute | solution.py:430
  34.3 10.5 %collective-permute-start.15 = (bf16[40,1536]{1,0:T(8,128)(2,1)S(1)}, bf16[40,1536]{1,0:T(8,128)(2,1)S(1)}, u32[]{:S(2)}, u32[]{:S(2)}) collective-permute-start(bf16[40,1536]{1,0:T(8,128)(2,1)S(1)} %get-tuple-element.59), channel_id=1, source_target_pairs={{0,7},{1,6},{2,5},{3,4},{4,3},{5,2},{6,1},{7,0},{8,15},{9,14},{10,... | collective-permute-start | bytes 368648 | tf_op jit(solution)/shard_map/ppermute | solution.py:430
  36.7 0.9 %copy-start.5 = (f32[2048]{0:T(1024)S(1)}, f32[2048]{0:T(1024)}, u32[]{:S(2)}) copy-start(f32[2048]{0:T(1024)} %param.15) | copy-start | bytes 24580
  45.4 15.4 %collective-permute-start.16 = (bf16[128,512]{1,0:T(8,128)(2,1)S(1)}, bf16[128,512]{1,0:T(8,128)(2,1)S(1)}, u32[]{:S(2)}, u32[]{:S(2)}) collective-permute-start(bf16[128,512]{1,0:T(8,128)(2,1)S(1)} %get-tuple-element.60), channel_id=1, source_target_pairs={{0,24},{8,16},{16,8},{24,0},{1,25},{9,17},{17,9},{25,1},{2,26},{10... | collective-permute-start | bytes 393224 | tf_op jit(solution)/shard_map/ppermute | solution.py:430
  49.0 11.8 %collective-permute-start.17 = (bf16[128,512]{1,0:T(8,128)(2,1)S(1)}, bf16[128,512]{1,0:T(8,128)(2,1)S(1)}, u32[]{:S(2)}, u32[]{:S(2)}) collective-permute-start(bf16[128,512]{1,0:T(8,128)(2,1)S(1)} %get-tuple-element.61), channel_id=1, source_target_pairs={{0,8},{8,0},{16,24},{24,16},{1,9},{9,1},{17,25},{25,17},{2,10},{10... | collective-permute-start | bytes 393224 | tf_op jit(solution)/shard_map/ppermute | solution.py:430
  49.0 11.8 %collective-permute-start.18 = (bf16[128,512]{1,0:T(8,128)(2,1)S(1)}, bf16[128,512]{1,0:T(8,128)(2,1)S(1)}, u32[]{:S(2)}, u32[]{:S(2)}) collective-permute-start(bf16[128,512]{1,0:T(8,128)(2,1)S(1)} %get-tuple-element.63), channel_id=1, source_target_pairs={{0,16},{8,24},{16,0},{24,8},{1,17},{9,25},{17,1},{25,9},{2,18},{10... | collective-permute-start | bytes 393224 | tf_op jit(solution)/shard_map/ppermute | solution.py:430
  49.8 11.0 %collective-permute-start.19 = (f32[8,128]{1,0:T(8,128)S(1)}, f32[8,128]{1,0:T(8,128)S(1)}, u32[]{:S(2)}, u32[]{:S(2)}) collective-permute-start(f32[8,128]{1,0:T(8,128)S(1)} %get-tuple-element.64), channel_id=1, source_target_pairs={{0,16},{8,24},{16,0},{24,8},{1,17},{9,25},{17,1},{25,9},{2,18},{10... | collective-permute-start | bytes 12296 | tf_op jit(solution)/shard_map/ppermute | solution.py:430
